TPU v7x, 32 devices: a whole 2x2x4 slice. The times are simulated.
32 devices in a mesh: dp: 8 (over z, x), fsdp: 4 (over y, core).
Axes of the slice: x: 2, y: 2, z: 4, core: 2. Of those that a mesh axis runs over, the one named last changes fastest.
Arguments:
- tokens: bfloat16 [32, 512, 1536], P(('dp', 'fsdp')), may hold values from -6 to 6
- seg_ids: int32 [16, 4], replicated, may hold values from 0 to 3
- timesteps: int32 [16], replicated, may hold values from 0 to 999
- labels: int32 [16], replicated, may hold values from 0 to 999
- cotangent: bfloat16 [32, 512, 1536], P(('dp', 'fsdp')), may hold values from -6 to 6
- mod_weight: bfloat16 [1536, 9216], P(('dp', 'fsdp')), may hold values from -0.15625 to 0.15625
- class_table: bfloat16 [1000, 1536], P(None, ('dp', 'fsdp')), may hold values from -6 to 6
- attn_kernel: bfloat16 [9, 1536], P(None, ('dp', 'fsdp')), may hold values from -2 to 2
- qkv_weight: bfloat16 [1536, 4608], P(('dp', 'fsdp')), may hold values from -0.15625 to 0.15625
- proj_weight: bfloat16 [1536, 1536], P(('dp', 'fsdp')), may hold values from -1.25 to 1.25
- up_weight: bfloat16 [1536, 6144], P(('dp', 'fsdp')), may hold values from -0.15625 to 0.15625
- ffn_kernel: bfloat16 [9, 6144], P(None, ('dp', 'fsdp')), may hold values from -2 to 2
- down_weight: bfloat16 [6144, 1536], P(('dp', 'fsdp')), may hold values from -0.078125 to 0.078125
Outputs:
- layer_out: bfloat16 [32, 512, 1536], P(('dp', 'fsdp'))
- input_grad: float32 [32, 512, 1536], P(('dp', 'fsdp'))
- mod_grad: float32 [1536, 9216], P(('dp', 'fsdp'))
- table_grad: float32 [1000, 1536], P(None, ('dp', 'fsdp'))
- attn_kernel_grad: float32 [9, 1536], P(None, ('dp', 'fsdp'))
- qkv_grad: float32 [1536, 4608], P(('dp', 'fsdp'))
- proj_grad: float32 [1536, 1536], P(('dp', 'fsdp'))
- up_grad: float32 [1536, 6144], P(('dp', 'fsdp'))
- ffn_kernel_grad: float32 [9, 6144], P(None, ('dp', 'fsdp'))
- down_grad: float32 [6144, 1536], P(('dp', 'fsdp'))
- shift_grad: float32 [32, 1536], P(('dp', 'fsdp'))
All inputs are finite; a program needn't handle non-finite values.
Results may differ from a plain program's by a relative error of at most 0.018.
The roundings to bfloat16 on the way count: a program that leaves them out, or rounds other values in their place, can miss the bound.
Values may be sent and summed in bfloat16 or wider, within the bound.
A program may use at most 448 MiB of HBM per device.

v0:
```python
import math

import jax
import jax.numpy as jnp
from jax import lax
from jax.sharding import PartitionSpec as P

D = 1536
HEAD = 64
SIDE = 32


highest = lax.Precision.HIGHEST
ln_epsilon = 1e-06
masked_score = -1000000000.0


def from_partner(x, axis, distance):
    return lax.ppermute(x, axis, [(i, i ^ 1 << distance) for i in range(lax.axis_size(axis))])


def layer_norm(values):
    average = jnp.mean(values, axis=-1, keepdims=True)
    centred = values - average
    variance = jnp.mean(centred * centred, axis=-1, keepdims=True)
    return centred * lax.rsqrt(variance + ln_epsilon)


def modulate(grid_values, shift_by, scale_by):
    return layer_norm(grid_values) * (1.0 + scale_by[:, None, :]) + shift_by[:, None, :]


def sinusoid(steps_in):
    halfway = D // 2
    frequency = jnp.exp(-math.log(10000.0) * jnp.arange(halfway, dtype=jnp.float32) / halfway)
    angles = steps_in.astype(jnp.float32)[..., None] * frequency
    return jnp.concatenate([jnp.cos(angles), jnp.sin(angles)], axis=-1)


def gelu_tanh(values):
    return jax.nn.gelu(values, approximate=True)


def with_rims(grid_values, half_bit):
    leaving = jnp.where(half_bit == 0, grid_values[:, -1], grid_values[:, 0])
    arriving = from_partner(leaving.astype(jnp.bfloat16), "fsdp", 0).astype(leaving.dtype)
    blank = jnp.zeros_like(arriving)
    above = jnp.where(half_bit == 0, blank, arriving)
    below = jnp.where(half_bit == 0, arriving, blank)
    framed = jnp.concatenate([above[:, None], grid_values, below[:, None]], axis=1)
    return jnp.pad(framed, ((0, 0), (0, 0), (1, 1), (0, 0)))


def depthwise(framed, kernel):
    row_count = framed.shape[1] - 2
    result = jnp.zeros((framed.shape[0], row_count, SIDE, framed.shape[3]), jnp.float32)
    for tap_index in range(9):
        row_shift = tap_index // 3
        column_shift = tap_index % 3
        result = result + framed[
            :, row_shift : row_shift + row_count, column_shift : column_shift + SIDE
        ] * kernel[tap_index].astype(jnp.float32)
    return result


def kernel_grad(framed, upstream):
    row_count = upstream.shape[1]
    tap_sums = []
    for tap_index in range(9):
        row_shift = tap_index // 3
        column_shift = tap_index % 3
        tap_sums.append(
            jnp.sum(
                framed[:, row_shift : row_shift + row_count, column_shift : column_shift + SIDE]
                * upstream,
                axis=(0, 1, 2),
            )
        )
    return jnp.stack(tap_sums)


def to_phases(grid_values):
    pieces, row_count, last_width = (
        grid_values.shape[0],
        grid_values.shape[1],
        grid_values.shape[-1],
    )
    split_grid = grid_values.reshape(pieces, row_count // 2, 2, SIDE // 2, 2, last_width)
    return split_grid.transpose(0, 2, 4, 1, 3, 5).reshape(
        pieces, 4, row_count // 2 * (SIDE // 2), last_width
    )


def from_phases(grouped, row_count):
    pieces, last_width = (grouped.shape[0], grouped.shape[-1])
    split_grid = grouped.reshape(pieces, 2, 2, row_count // 2, SIDE // 2, last_width)
    return split_grid.transpose(0, 3, 1, 4, 2, 5).reshape(pieces, row_count, SIDE, last_width)


def on_device(
    tokens,
    seg_ids,
    timesteps,
    labels,
    cotangent,
    mod_weight,
    class_table,
    attn_kernel,
    qkv_weight,
    proj_weight,
    up_weight,
    ffn_kernel,
    down_weight,
):
    pieces, half_tokens, model_width = tokens.shape
    half_rows = half_tokens // SIDE
    head_count = model_width // HEAD
    group_len = half_rows // 2 * (SIDE // 2)
    score_scale = HEAD ** (-0.5)
    device_rank = lax.axis_index("dp") * lax.axis_size("fsdp") + lax.axis_index("fsdp")
    half_bit = lax.axis_index("fsdp") % 2
    first_canvas = device_rank // 2 * pieces
    step_here = lax.dynamic_slice_in_dim(timesteps, first_canvas, pieces)
    label_here = lax.dynamic_slice_in_dim(labels, first_canvas, pieces)
    quadrant_here = lax.dynamic_slice_in_dim(seg_ids, first_canvas, pieces, 0)
    mod_full, table_full, kernel_full, qkv_full, proj_full = (
        lax.all_gather(mod_weight, ("dp", "fsdp"), axis=0, tiled=True),
        lax.all_gather(class_table, ("dp", "fsdp"), axis=1, tiled=True),
        lax.all_gather(attn_kernel, ("dp", "fsdp"), axis=1, tiled=True),
        lax.all_gather(qkv_weight, ("dp", "fsdp"), axis=0, tiled=True),
        lax.all_gather(proj_weight, ("dp", "fsdp"), axis=0, tiled=True),
    )
    picks = label_here[:, None] == jnp.arange(table_full.shape[0])[None, :]
    cond = sinusoid(step_here) + jnp.dot(
        picks.astype(jnp.bfloat16), table_full, preferred_element_type=jnp.float32
    )
    lift_value, lift_pull = jax.vjp(jax.nn.silu, cond)
    lifted = lift_value.astype(jnp.bfloat16)
    mods = jnp.dot(lifted, mod_full, preferred_element_type=jnp.float32)
    shift_a, scale_a, gate_a, shift_f, scale_f, gate_f = jnp.split(mods, 6, axis=1)
    source = tokens.astype(jnp.float32)
    normed_a, norm_pull_a = jax.vjp(modulate, source, shift_a, scale_a)
    normed_rims = with_rims(normed_a.reshape(pieces, half_rows, SIDE, model_width), half_bit)
    convolved = (
        depthwise(normed_rims, kernel_full)
        .reshape(pieces * half_tokens, model_width)
        .astype(jnp.bfloat16)
    )
    qkv = jnp.dot(convolved, qkv_full, preferred_element_type=jnp.float32).astype(jnp.bfloat16)

    def phased(block_in):
        return to_phases(block_in.reshape(pieces, half_rows, SIDE, model_width)).reshape(
            pieces, 4, group_len, head_count, HEAD
        )

    def tokens_of(block_in):
        return from_phases(block_in.reshape(pieces, 4, group_len, model_width), half_rows).reshape(
            pieces * half_tokens, model_width
        )

    column_quads = jnp.arange(SIDE) // (SIDE // 2)

    def segment_groups(row_quad):
        quadrants = 2 * row_quad + column_quads
        matches = quadrants[None, :, None] == jnp.arange(4)[None, None, :]
        segment_cols = jnp.sum(jnp.where(matches, quadrant_here[:, None, :], 0), axis=2)
        grid_ids = jnp.broadcast_to(segment_cols[:, None, :, None], (pieces, half_rows, SIDE, 1))
        return to_phases(grid_ids)[..., 0]

    segment_near = segment_groups(half_bit)
    segment_keys = jnp.concatenate([segment_near, segment_groups(1 - half_bit)], axis=2)
    allowed = segment_near[:, :, None, :, None] == segment_keys[:, :, None, None, :]
    queries = phased(qkv[:, :model_width])
    near_keys = phased(qkv[:, model_width : 2 * model_width])
    near_values = phased(qkv[:, 2 * model_width :])
    far_keys, far_values = from_partner((near_keys, near_values), "fsdp", 0)
    keys_all = jnp.concatenate([near_keys, far_keys], axis=2)
    values_all = jnp.concatenate([near_values, far_values], axis=2)

    def scores_of():
        raw_scores = (
            jnp.einsum("cpqhe,cpkhe->cphqk", queries, keys_all, preferred_element_type=jnp.float32)
            * score_scale
        )
        return jnp.where(allowed, raw_scores, masked_score)

    scores = scores_of()
    row_max = jnp.max(scores, axis=-1, keepdims=True)
    exp_scores = jnp.exp(scores - row_max)
    row_total = jnp.sum(exp_scores, axis=-1, keepdims=True)
    probs = (exp_scores / row_total).astype(jnp.bfloat16)
    log_total = row_max + jnp.log(row_total)
    attended_ph = jnp.einsum(
        "cphqk,cpkhe->cpqhe", probs, values_all, preferred_element_type=jnp.float32
    ).astype(jnp.bfloat16)
    attended = tokens_of(attended_ph)
    branch_a = jnp.dot(attended, proj_full, preferred_element_type=jnp.float32).reshape(
        pieces, half_tokens, model_width
    )
    middle = source + gate_a[:, None, :] * branch_a
    normed_f, norm_pull_f = jax.vjp(modulate, middle, shift_f, scale_f)
    normed_low = normed_f.reshape(pieces * half_tokens, model_width).astype(jnp.bfloat16)
    up_full, ffn_full, down_full = (
        lax.all_gather(up_weight, ("dp", "fsdp"), axis=0, tiled=True),
        lax.all_gather(ffn_kernel, ("dp", "fsdp"), axis=1, tiled=True),
        lax.all_gather(down_weight, ("dp", "fsdp"), axis=0, tiled=True),
    )
    hidden = jnp.dot(normed_low, up_full, preferred_element_type=jnp.float32)
    hidden_rims = with_rims(hidden.reshape(pieces, half_rows, SIDE, -1), half_bit)
    widened = depthwise(hidden_rims, ffn_full)
    gelu_value, gelu_pull = jax.vjp(gelu_tanh, widened)
    activated = gelu_value.reshape(pieces * half_tokens, -1).astype(jnp.bfloat16)
    branch_f = jnp.dot(activated, down_full, preferred_element_type=jnp.float32).reshape(
        pieces, half_tokens, model_width
    )
    layer_out = (middle + gate_f[:, None, :] * branch_f).astype(jnp.bfloat16)
    upstream = cotangent.astype(jnp.float32)
    grad_gate_f = jnp.sum(upstream * branch_f, axis=1)
    grad_branch_f = (
        (upstream * gate_f[:, None, :])
        .reshape(pieces * half_tokens, model_width)
        .astype(jnp.bfloat16)
    )
    down_grad = jnp.dot(activated.T, grad_branch_f, preferred_element_type=jnp.float32)
    grad_activated = jnp.dot(grad_branch_f, down_full.T, preferred_element_type=jnp.float32)
    (grad_widened,) = gelu_pull(grad_activated.reshape(widened.shape))
    ffn_kernel_grad = kernel_grad(hidden_rims, grad_widened)
    grad_hidden = (
        depthwise(with_rims(grad_widened, half_bit), ffn_full[::-1])
        .reshape(pieces * half_tokens, -1)
        .astype(jnp.bfloat16)
    )
    up_grad = jnp.dot(normed_low.T, grad_hidden, preferred_element_type=jnp.float32)
    grad_normed_f = jnp.dot(grad_hidden, up_full.T, preferred_element_type=jnp.float32).reshape(
        pieces, half_tokens, model_width
    )
    grad_middle, grad_shift_f, grad_scale_f = norm_pull_f(grad_normed_f)
    grad_middle = grad_middle + upstream
    up_share, down_share = (
        lax.psum_scatter(up_grad, ("dp", "fsdp"), scatter_dimension=0, tiled=True),
        lax.psum_scatter(down_grad, ("dp", "fsdp"), scatter_dimension=0, tiled=True),
    )
    grad_gate_a = jnp.sum(grad_middle * branch_a, axis=1)
    grad_branch_a = (
        (grad_middle * gate_a[:, None, :])
        .reshape(pieces * half_tokens, model_width)
        .astype(jnp.bfloat16)
    )
    proj_grad = jnp.dot(attended.T, grad_branch_a, preferred_element_type=jnp.float32)
    grad_attended = jnp.dot(grad_branch_a, proj_full.T, preferred_element_type=jnp.float32).astype(
        jnp.bfloat16
    )
    grad_attended_ph = phased(grad_attended)
    soft_weights = jnp.exp(scores_of() - log_total)
    soft_low = soft_weights.astype(jnp.bfloat16)
    grad_values_all = jnp.einsum(
        "cphqk,cpqhe->cpkhe", soft_low, grad_attended_ph, preferred_element_type=jnp.float32
    )
    grad_probs = jnp.einsum(
        "cpqhe,cpkhe->cphqk", grad_attended_ph, values_all, preferred_element_type=jnp.float32
    )
    row_delta = jnp.sum(grad_probs * soft_weights, axis=-1, keepdims=True)
    grad_scores = (soft_weights * (grad_probs - row_delta)).astype(jnp.bfloat16)
    grad_queries = (
        jnp.einsum("cphqk,cpkhe->cpqhe", grad_scores, keys_all, preferred_element_type=jnp.float32)
        * score_scale
    ).astype(jnp.bfloat16)
    grad_keys_all = (
        jnp.einsum("cphqk,cpqhe->cpkhe", grad_scores, queries, preferred_element_type=jnp.float32)
        * score_scale
    )
    back_keys, back_values = (
        from_partner(grad_keys_all[:, :, group_len:].astype(jnp.bfloat16), "fsdp", 0).astype(
            jnp.float32
        ),
        from_partner(grad_values_all[:, :, group_len:].astype(jnp.bfloat16), "fsdp", 0).astype(
            jnp.float32
        ),
    )
    grad_keys = (grad_keys_all[:, :, :group_len] + back_keys).astype(jnp.bfloat16)
    grad_values = (grad_values_all[:, :, :group_len] + back_values).astype(jnp.bfloat16)
    grad_qkv = jnp.concatenate(
        [tokens_of(grad_queries), tokens_of(grad_keys), tokens_of(grad_values)], axis=1
    )
    qkv_grad = jnp.dot(convolved.T, grad_qkv, preferred_element_type=jnp.float32)
    grad_convolved = jnp.dot(grad_qkv, qkv_full.T, preferred_element_type=jnp.float32).reshape(
        pieces, half_rows, SIDE, model_width
    )
    attn_kernel_grad = kernel_grad(normed_rims, grad_convolved)
    grad_normed_a = depthwise(with_rims(grad_convolved, half_bit), kernel_full[::-1]).reshape(
        pieces, half_tokens, model_width
    )
    grad_source, grad_shift_a, grad_scale_a = norm_pull_a(grad_normed_a)
    input_grad = grad_source + grad_middle
    grad_mods = jnp.concatenate(
        [grad_shift_a, grad_scale_a, grad_gate_a, grad_shift_f, grad_scale_f, grad_gate_f], axis=1
    )
    far_mods = from_partner(grad_mods.astype(jnp.bfloat16), "fsdp", 0).astype(grad_mods.dtype)
    shared_mods = (grad_mods + far_mods).astype(jnp.bfloat16) * 0.5
    (cond_grad,) = lift_pull(jnp.dot(shared_mods, mod_full.T, preferred_element_type=jnp.float32))
    mod_grad = jnp.dot(lifted.T, shared_mods, preferred_element_type=jnp.float32)
    table_grad = jnp.dot(picks.astype(jnp.float32).T, cond_grad, precision=highest)
    mod_share, qkv_share, proj_share = (
        lax.psum_scatter(mod_grad, ("dp", "fsdp"), scatter_dimension=0, tiled=True),
        lax.psum_scatter(qkv_grad, ("dp", "fsdp"), scatter_dimension=0, tiled=True),
        lax.psum_scatter(proj_grad, ("dp", "fsdp"), scatter_dimension=0, tiled=True),
    )
    ffn_share, kernel_share, table_share = (
        lax.psum_scatter(ffn_kernel_grad, ("dp", "fsdp"), scatter_dimension=1, tiled=True),
        lax.psum_scatter(attn_kernel_grad, ("dp", "fsdp"), scatter_dimension=1, tiled=True),
        lax.psum_scatter(table_grad, ("dp", "fsdp"), scatter_dimension=1, tiled=True),
    )
    return (
        layer_out,
        input_grad,
        mod_share,
        table_share,
        kernel_share,
        qkv_share,
        proj_share,
        up_share,
        ffn_share,
        down_share,
        grad_shift_f,
    )


def solution(mesh):
    return jax.shard_map(
        on_device,
        mesh=mesh,
        in_specs=(
            P(("dp", "fsdp"), None, None),
            P(),
            P(),
            P(),
            P(("dp", "fsdp"), None, None),
            P(("dp", "fsdp"), None),
            P(None, ("dp", "fsdp")),
            P(None, ("dp", "fsdp")),
            P(("dp", "fsdp"), None),
            P(("dp", "fsdp"), None),
            P(("dp", "fsdp"), None),
            P(None, ("dp", "fsdp")),
            P(("dp", "fsdp"), None),
        ),
        out_specs=(
            P(("dp", "fsdp"), None, None),
            P(("dp", "fsdp"), None, None),
            P(("dp", "fsdp"), None),
            P(None, ("dp", "fsdp")),
            P(None, ("dp", "fsdp")),
            P(("dp", "fsdp"), None),
            P(("dp", "fsdp"), None),
            P(("dp", "fsdp"), None),
            P(None, ("dp", "fsdp")),
            P(("dp", "fsdp"), None),
            P(("dp", "fsdp"), None),
        ),
        check_vma=False,
    )
```

profile of v0, /device:TPU:0, one launch (start us, length us, event | category | flops | bytes accessed | tf_op | source)
XLA Modules:
  0.0 2852.9 jit_solution(13260515725783024636)
XLA Ops:
  16.0 44.1 %all-gather = bf16[32,48,9]{1,2,0:T(8,128)(2,1)S(1)} all-gather(bf16[1,48,9]{1,2,0:T(8,128)(2,1)} %bitcast.327), channel_id=1, replica_groups=mesh['dp'=8,'fsdp'=4] {'dp','fsdp'}, dimensions={0}, use_global_device_ids=true | all-gather | bytes 28512 | tf_op jit(solution)/shard_map/all_gather | solution.py:129
  60.3 38.2 %all-gather.1 = bf16[32,192,9]{1,2,0:T(8,128)(2,1)S(1)} all-gather(bf16[1,192,9]{1,2,0:T(8,128)(2,1)S(1)} %bitcast.326), channel_id=1, replica_groups=mesh['dp'=8,'fsdp'=4] {'dp','fsdp'}, dimensions={0}, use_global_device_ids=true | all-gather | bytes 114048 | tf_op jit(solution)/shard_map/all_gather | solution.py:205
  104.0 140.0 %all-gather.11.cloned.1.call-done = bf16[1536,9216]{1,0:T(8,128)(2,1)} async-done(((bf16[48,9216]{1,0:T(8,128)(2,1)}), bf16[1536,9216]{1,0:T(8,128)(2,1)}) %all-gather.11.cloned.1.call-update) | async-done | bytes 28311568 | tf_op jit(solution)/shard_map/all_gather | solution.py:127
  244.0 11.2 fusion.134
  265.1 82.5 %all-gather.13.cloned.1.call-done = bf16[1536,4608]{1,0:T(8,128)(2,1)} async-done(((bf16[48,4608]{1,0:T(8,128)(2,1)}), bf16[1536,4608]{1,0:T(8,128)(2,1)}) %all-gather.13.cloned.1.call-update) | async-done | bytes 14155792 | tf_op jit(solution)/shard_map/all_gather | solution.py:130
  347.6 10.7 convolution_convert_fusion
  447.5 90.1 %all-gather.17.cloned.1.call-done = bf16[1536,6144]{1,0:T(8,128)(2,1)} async-done(((bf16[48,6144]{1,0:T(8,128)(2,1)}), bf16[1536,6144]{1,0:T(8,128)(2,1)}) %all-gather.17.cloned.1.call-update) | async-done | bytes 18874384 | tf_op jit(solution)/shard_map/all_gather | solution.py:204
  537.6 14.4 fusion.126
  554.0 8.4 select_maximum_fusion.2
  562.4 47.9 %multiply_convert_fusion.1 = (bf16[1,16,32,6144]{3,2,1,0:T(8,128)(2,1)}, f32[1,16,32,6144]{3,2,1,0:T(8,128)}) fusion(f32[6144]{0:T(1024)S(1)} %bitcast.299, f32[1,18,34,6144]{3,2,1,0:T(8,128)} %select_maximum_fusion.2, f32[6144]{0:T(1024)S(1)} %bitcast.301, f32[1,1,32,6144]{3,2,1,0:T(8,128)S(1)} %get-tuple-element.74, f32[1,16,32,6144]{3,2,1,0:T(8,128)} %bitcast.269, ...), kind=kLoop, calls=%fused_computation.56 | loop fusion | flops 88080384 | bytes 108748800 | tf_op jit(solution)/shard_map/convert_element_type | solution.py:212
  610.4 52.2 %all-gather.19.cloned.1.call-done = bf16[6144,1536]{1,0:T(8,128)(2,1)} async-done(((bf16[192,1536]{1,0:T(8,128)(2,1)}), bf16[6144,1536]{1,0:T(8,128)(2,1)}) %all-gather.19.cloned.1.call-update) | async-done | bytes 18874384 | tf_op jit(solution)/shard_map/all_gather | solution.py:206
  662.6 56.0 %multiply_reduce_fusion = (f32[6144]{0:T(1024)}, f32[6144]{0:T(1024)}, f32[6144]{0:T(1024)}, f32[6144]{0:T(1024)}, f32[6144]{0:T(1024)}, /*index=5*/f32[6144]{0:...) fusion(f32[1,18,34,6144]{3,2,1,0:T(8,128)} %select_maximum_fusion.2, ...), kind=kOutput, calls=%fused_computation.44 | convolution fusion | flops 9786304512 | bytes 148070400 | tf_op jit(solution)/shard_map/dot_general | solution.py:225
  721.9 11.4 select_maximum_fusion
  733.3 43.1 %fusion.10 = bf16[1,16,32,6144]{3,2,1,0:T(8,128)(2,1)} fusion(f32[1,18,34,6144]{3,2,1,0:T(8,128)} %select_maximum_fusion, f32[1,1,32,6144]{3,2,1,0:T(8,128)S(1)} %get-tuple-element.72, f32[1,16,32,6144]{3,2,1,0:T(8,128)} %get-tuple-element.95, f32[1,1,32,6144]{3,2,1,0:T(8,128)S(1)} %get-tuple-element.71, f32[6144]{0:T(1024)S(1)} %bitcast.300, ...), kind=kLoop, calls=%fused_computation.20 | loop fusion | flops 62914560 | bytes 96165888 | tf_op jit(solution)/shard_map/convert_element_type | solution.py:231
  776.4 17.4 fusion.58
  823.5 11.6 multiply_reduce_fusion.9
  835.1 8.9 multiply_convert_fusion
  901.9 19.6 multiply_reduce_fusion.10
  938.8 21.1 fusion.44
  962.6 12.9 convolution_reduce_fusion.1
  980.6 8.4 fusion.81
  990.3 14.9 fusion.135
  1006.6 19.2 fusion.71
  1027.8 19.1 fusion.124
  1047.6 18.2 broadcast_multiply_fusion
  1068.0 59.5 %reduce-scatter.25.cloned.1.call-done = f32[48,9]{1,0:T(8,128)} async-done(((f32[1536,9]{1,0:T(8,128)}), f32[48,9]{1,0:T(8,128)}) %reduce-scatter.25.cloned.1.call-update) | async-done | bytes 1744
  1128.9 118.8 %reduce-scatter.15.cloned.1.call-done = f32[1000,48]{0,1:T(8,128)} async-done(((f32[1000,1536]{0,1:T(8,128)}), f32[1000,48]{0,1:T(8,128)}) %reduce-scatter.15.cloned.1.call-update) | async-done | bytes 192016 | tf_op jit(solution)/shard_map/reduce_scatter | solution.py:311
  1247.7 141.7 %reduce-scatter.19.cloned.1.call-done = f32[48,1536]{1,0:T(8,128)} async-done(((f32[1536,1536]{1,0:T(8,128)}), f32[48,1536]{1,0:T(8,128)}) %reduce-scatter.19.cloned.1.call-update) | async-done | bytes 294928 | tf_op jit(solution)/shard_map/reduce_scatter | solution.py:306
  1389.5 268.6 %reduce-scatter.17.cloned.1.call-done = f32[48,4608]{1,0:T(8,128)} async-done(((f32[1536,4608]{1,0:T(8,128)}), f32[48,4608]{1,0:T(8,128)}) %reduce-scatter.17.cloned.1.call-update) | async-done | bytes 884752 | tf_op jit(solution)/shard_map/reduce_scatter | solution.py:305
  1658.1 355.2 %reduce-scatter.23.cloned.1.call-done = f32[192,1536]{1,0:T(8,128)} async-done(((f32[6144,1536]{1,0:T(8,128)}), f32[192,1536]{1,0:T(8,128)}) %reduce-scatter.23.cloned.1.call-update) | async-done | bytes 1179664 | tf_op jit(solution)/shard_map/reduce_scatter | solution.py:241
  2013.3 355.2 %reduce-scatter.21.cloned.1.call-done = f32[48,6144]{1,0:T(8,128)} async-done(((f32[1536,6144]{1,0:T(8,128)}), f32[48,6144]{1,0:T(8,128)}) %reduce-scatter.21.cloned.1.call-update) | async-done | bytes 1179664 | tf_op jit(solution)/shard_map/reduce_scatter | solution.py:240
  2368.5 477.3 %reduce-scatter.13.cloned.1.call-done = f32[48,9216]{1,0:T(8,128)} async-done(((f32[1536,9216]{1,0:T(8,128)}), f32[48,9216]{1,0:T(8,128)}) %reduce-scatter.13.cloned.1.call-update) | async-done | bytes 1769488 | tf_op jit(solution)/shard_map/reduce_scatter | solution.py:304
  (394 shorter events, 238.3 us)
Async XLA Ops:
  7.2 93.3 %all-gather.9.cloned.1.call-start = ((), (), s32[]{:S(2)}) async-start(), calls=%async_computation.8 | async-start | bytes 3244032 | tf_op jit(solution)/shard_map/all_gather | solution.py:128
  8.0 236.0 %all-gather.11.cloned.1.call-start = ((), (), s32[]{:S(2)}) async-start(), calls=%async_computation.9 | async-start | bytes 29196288 | tf_op jit(solution)/shard_map/all_gather | solution.py:127
  8.7 338.9 %all-gather.13.cloned.1.call-start = ((), (), s32[]{:S(2)}) async-start(), calls=%async_computation.10 | async-start | bytes 14598144 | tf_op jit(solution)/shard_map/all_gather | solution.py:130
  9.4 428.2 %all-gather.15.cloned.1.call-start = ((), (), s32[]{:S(2)}) async-start(), calls=%async_computation.11 | async-start | bytes 4866048 | tf_op jit(solution)/shard_map/all_gather | solution.py:131
  10.0 527.5 %all-gather.17.cloned.1.call-start = ((), (), s32[]{:S(2)}) async-start(), calls=%async_computation.12 | async-start | bytes 19464192 | tf_op jit(solution)/shard_map/all_gather | solution.py:204
  10.6 652.0 %all-gather.19.cloned.1.call-start = ((), (), s32[]{:S(2)}) async-start(), calls=%async_computation.13 | async-start | bytes 19464192 | tf_op jit(solution)/shard_map/all_gather | solution.py:206
  11.2 1054.6 %reduce-scatter.27.cloned.1.call-start = ((), (), s32[]{:S(2)}) async-start(), calls=%async_computation.21 | async-start | bytes 3244032
  99.0 159.8 %copy-start.41 = (f32[1536]{0:T(1024)}, f32[1536]{0:T(1024)S(1)}, u32[]{:S(2)}) copy-start(f32[1536]{0:T(1024)S(1)} %get-tuple-element.39) | copy-start | bytes 18436
  99.0 159.8 %copy-start.43 = (f32[1536]{0:T(1024)}, f32[1536]{0:T(1024)S(1)}, u32[]{:S(2)}) copy-start(f32[1536]{0:T(1024)S(1)} %get-tuple-element.40) | copy-start | bytes 18436
  99.0 159.8 %copy-start.45 = (f32[1536]{0:T(1024)}, f32[1536]{0:T(1024)S(1)}, u32[]{:S(2)}) copy-start(f32[1536]{0:T(1024)S(1)} %get-tuple-element.41) | copy-start | bytes 18436
  99.0 159.8 %copy-start.47 = (f32[1536]{0:T(1024)}, f32[1536]{0:T(1024)S(1)}, u32[]{:S(2)}) copy-start(f32[1536]{0:T(1024)S(1)} %get-tuple-element.42) | copy-start | bytes 18436
  99.0 159.8 %copy-start.49 = (f32[1536]{0:T(1024)}, f32[1536]{0:T(1024)S(1)}, u32[]{:S(2)}) copy-start(f32[1536]{0:T(1024)S(1)} %get-tuple-element.43) | copy-start | bytes 18436
  99.0 159.8 %copy-start.51 = (f32[1536]{0:T(1024)}, f32[1536]{0:T(1024)S(1)}, u32[]{:S(2)}) copy-start(f32[1536]{0:T(1024)S(1)} %get-tuple-element.44) | copy-start | bytes 18436
  99.0 159.8 %copy-start.53 = (f32[1536]{0:T(1024)}, f32[1536]{0:T(1024)S(1)}, u32[]{:S(2)}) copy-start(f32[1536]{0:T(1024)S(1)} %get-tuple-element.45) | copy-start | bytes 18436
  255.9 281.6 %copy-start.70 = (f32[1536]{0:T(1024)}, f32[1536]{0:T(1024)S(1)}, u32[]{:S(2)}) copy-start(f32[1536]{0:T(1024)S(1)} %get-tuple-element.49) | copy-start | bytes 18436
  256.6 1.4 collective-permute-start
  377.1 28.3 collective-permute-start.2
  388.1 27.8 collective-permute-start.1
  552.1 1.8 collective-permute-start.3
  720.0 1.8 collective-permute-start.4
  823.2 42.3 %collective-permute-start.6 = (bf16[1,4,128,24,64]{2,4,3,1,0:T(8,128)(2,1)}, bf16[1,4,128,24,64]{2,4,3,1,0:T(8,128)(2,1)}, u32[]{:S(2)}, u32[]{:S(2)}) collective-permute-start(bf16[1,4,128,24,64]{2,4,3,1,0:T(8,128)(2,1)} %slice.555), channel_id=1, source_target_pairs={{0,1},{1,0},{2,3},{3,2},{4,5},{5,4},{6,7},{7,6},{8,9},{9,8},{10,11... | collective-permute-start | bytes 4718600 | tf_op jit(solution)/shard_map/ppermute | solution.py:19
  849.2 31.5 %collective-permute-start.5 = (bf16[1,4,128,24,64]{2,4,3,1,0:T(8,128)(2,1)}, bf16[1,4,128,24,64]{2,4,3,1,0:T(8,128)(2,1)}, u32[]{:S(2)}, u32[]{:S(2)}) collective-permute-start(bf16[1,4,128,24,64]{2,4,3,1,0:T(8,128)(2,1)} %slice.556), channel_id=1, source_target_pairs={{0,1},{1,0},{2,3},{3,2},{4,5},{5,4},{6,7},{7,6},{8,9},{9,8},{10,11... | collective-permute-start | bytes 4718600 | tf_op jit(solution)/shard_map/ppermute | solution.py:19
  922.1 6.5 collective-permute-start.7
  926.5 201.0 %reduce-scatter.25.cloned.1.call-start = ((), (), s32[]{:S(2)}) async-start(), calls=%async_computation.20 | async-start | bytes 811008
  960.0 2.6 collective-permute-start.8
  962.5 285.2 %reduce-scatter.15.cloned.1.call-start = ((), (), s32[]{:S(2)}) async-start(), calls=%async_computation.15 | async-start | bytes 6488064 | tf_op jit(solution)/shard_map/reduce_scatter | solution.py:311
  978.7 410.8 %reduce-scatter.19.cloned.1.call-start = ((), (), s32[]{:S(2)}) async-start(), calls=%async_computation.17 | async-start | bytes 9732096 | tf_op jit(solution)/shard_map/reduce_scatter | solution.py:306
  989.0 669.1 %reduce-scatter.17.cloned.1.call-start = ((), (), s32[]{:S(2)}) async-start(), calls=%async_computation.16 | async-start | bytes 29196288 | tf_op jit(solution)/shard_map/reduce_scatter | solution.py:305
  1005.2 1008.1 %reduce-scatter.23.cloned.1.call-start = ((), (), s32[]{:S(2)}) async-start(), calls=%async_computation.19 | async-start | bytes 38928384 | tf_op jit(solution)/shard_map/reduce_scatter | solution.py:241
  1025.9 1342.6 %reduce-scatter.21.cloned.1.call-start = ((), (), s32[]{:S(2)}) async-start(), calls=%async_computation.18 | async-start | bytes 38928384 | tf_op jit(solution)/shard_map/reduce_scatter | solution.py:240
  1046.9 1798.9 %reduce-scatter.13.cloned.1.call-start = ((), (), s32[]{:S(2)}) async-start(), calls=%async_computation.14 | async-start | bytes 58392576 | tf_op jit(solution)/shard_map/reduce_scatter | solution.py:304
  1065.8 1780.1 %copy-start.1 = (s32[16,4]{0,1:T(4,128)S(1)}, s32[16,4]{0,1:T(4,128)}, u32[]{:S(2)}) copy-start(s32[16,4]{0,1:T(4,128)} %param.14) | copy-start | bytes 772
  (95 other events, 2096.5 us)
Sparse Core Ops, SparseCore 0:
  10.9 62.2 all-gather.8
  76.2 167.7 all-gather.10
  246.9 100.6 all-gather.12
  350.4 62.0 all-gather.14
  415.2 122.2 all-gather.16
  540.3 122.1 all-gather.18
  926.6 100.4 reduce-scatter.26
  1032.2 95.2 reduce-scatter.24
  1133.7 113.9 reduce-scatter.14
  1254.0 135.3 reduce-scatter.18
  1396.5 261.5 reduce-scatter.16
  1664.9 348.3 reduce-scatter.22
  2020.3 348.1 reduce-scatter.20
  2375.3 470.4 reduce-scatter.12
where the time goes:
time: 2860 us; the launch traced here: 2850 us
  waiting for transfers between devices  2150 us (75%)
  matrix products  277 us (10%)
  other arithmetic  182 us (6%)
  local copies, waits for them, and re-layouts  142 us (5%)
  blocking collectives  82.3 us (3%)
    reduce_scatter x1, waiting for transfers between devices, on_device(): lax.psum_scatter(mod_grad, ('dp', 'fsdp'), scatter_dimension=0, tiled=True)  477 us
    reduce_scatter x1, waiting for transfers between devices, on_device(): lax.psum_scatter(down_grad, ('dp', 'fsdp'), scatter_dimension=0, tiled=True)  355 us
    reduce_scatter x1, waiting for transfers between devices, on_device(): lax.psum_scatter(up_grad, ('dp', 'fsdp'), scatter_dimension=0, tiled=True)  355 us
    reduce_scatter x1, waiting for transfers between devices, on_device(): lax.psum_scatter(qkv_grad, ('dp', 'fsdp'), scatter_dimension=0, tiled=True)  269 us
    reduce_scatter x1, waiting for transfers between devices, on_device(): lax.psum_scatter(proj_grad, ('dp', 'fsdp'), scatter_dimension=0, tiled=True)  142 us
    all_gather x1, waiting for transfers between devices, on_device(): lax.all_gather(mod_weight, ('dp', 'fsdp'), axis=0, tiled=True)  140 us
    reduce_scatter x1, waiting for transfers between devices, on_device(): lax.psum_scatter(table_grad, ('dp', 'fsdp'), scatter_dimension=1, tiled=T...  119 us
    all_gather x1, waiting for transfers between devices, on_device(): lax.all_gather(up_weight, ('dp', 'fsdp'), axis=0, tiled=True)  90.1 us
  transfers between devices with their start and end apart: 23, of which 14 were waited for; matrix products, arithmetic and copies ran while one was open for 14% of the time, Pallas kernels for 0%

commit v1 on v0

v1 whole, which is shorter than its diff:
```python
import functools
import math

import jax
import jax.numpy as jnp
from jax import lax
from jax.experimental import pallas as pl
from jax.experimental.pallas import tpu as pltpu
from jax.sharding import PartitionSpec as P

HEAD = 64
SIDE = 32
HALF_SIDE = SIDE // 2
STRIP = HALF_SIDE
PLANE = HALF_SIDE * HALF_SIDE
PADDED = PLANE + 2 * STRIP
TILE = 256
CHUNKS = 3

highest = lax.Precision.HIGHEST
ln_epsilon = 1e-06
masked_score = -1000000000.0
low = jnp.bfloat16
full = jnp.float32
AXES = ("dp", "fsdp")


def device_count():
    return lax.axis_size("dp") * lax.axis_size("fsdp")


def swap(x, bit):
    return lax.ppermute(x, AXES, [(i, i ^ 1 << bit) for i in range(device_count())])


def swap_core(x):
    return swap(x, 0)


def gather_order(chip_bits, colour):
    order = list(range(chip_bits - 1, -1, -1))
    if colour and chip_bits > 1:
        order[-1], order[-2] = order[-2], order[-1]
    return order


def gather_pieces(shard, order):
    pieces = [shard[None]]
    for step, bit in enumerate(order):
        pieces = pieces + [swap(piece, bit + 1) for piece in pieces]
        if len(pieces) == 4 and step + 1 < len(order):
            pieces = [jnp.concatenate(pieces, axis=0)]
    return pieces


def assemble_body(steps, chip_ref, *refs):
    *piece_refs, out_ref = refs
    which = pl.program_id(0) // steps
    top = chip_ref[1]
    for index, piece_ref in enumerate(piece_refs):

        @pl.when(which == index)
        def _():
            for k in range(4):
                out_ref[jnp.bitwise_xor(top, (k & 1) << 1 | k >> 1), 0] = piece_ref[k]


def assemble(pieces, order, chip):
    chips = sum(piece.shape[0] for piece in pieces)
    rows, columns = pieces[0].shape[1:]
    if chips < 4 or len(pieces) * pieces[0].shape[0] != chips or pieces[0].shape[0] % 4:
        raise ValueError("unexpected mesh")
    rest = len(order) - 2
    steps = pieces[0].shape[0] // 4
    chip_words = jnp.stack([jnp.bitwise_and(chip, (1 << rest) - 1), chip >> rest]).astype(jnp.int32)

    def out_map(step, words):
        at = words[0]
        for position, bit in enumerate(order[2:]):
            at = jnp.bitwise_xor(at, jnp.bitwise_and(step >> position, 1) << bit)
        return (0, at, 0, 0)

    def piece_map(index):
        return lambda step, words: (jnp.clip(step - index * steps, 0, steps - 1), 0, 0)

    out = pl.pallas_call(
        functools.partial(assemble_body, steps),
        grid_spec=pltpu.PrefetchScalarGridSpec(
            num_scalar_prefetch=1,
            grid=(chips // 4,),
            in_specs=[
                pl.BlockSpec((4, rows, columns), piece_map(index)) for index in range(len(pieces))
            ],
            out_specs=pl.BlockSpec((4, 1, rows, columns), out_map),
        ),
        out_shape=jax.ShapeDtypeStruct((4, chips // 4, rows, columns), pieces[0].dtype),
        cost_estimate=pl.CostEstimate(
            flops=0, bytes_accessed=4 * chips * rows * columns, transcendentals=0
        ),
        name="assemble",
    )(chip_words, *pieces)
    return out.reshape(chips, rows, columns)


def gather_weights(shard, colour, chip, chip_bits):
    order = gather_order(chip_bits, colour)
    return assemble(gather_pieces(shard, order), order, chip)


def at_bit(array, axis, bit):
    return lax.dynamic_index_in_dim(array, bit, axis, keepdims=False)


def scatter_sum(parts, colour, chip, chip_bits, sent=low):
    order = gather_order(chip_bits, colour)[::-1]
    left = list(range(chip_bits - 1, -1, -1))
    held = [parts.reshape((2,) * chip_bits + parts.shape[1:])]
    for bit in order:
        axis = left.index(bit)
        left.remove(bit)
        mine = jnp.bitwise_and(chip >> bit, 1)
        leaving = sum(at_bit(h, axis, 1 - mine).astype(full) for h in held).astype(sent)
        staying = sum(at_bit(h, axis, mine).astype(full) for h in held).astype(sent)
        held = [staying, swap(leaving, bit + 1)]
    return held[0].astype(full) + held[1].astype(full)


def gather_rows(row, chip, chip_bits):
    order = gather_order(chip_bits, 0)
    held = row[None]
    for bit in order:
        held = jnp.concatenate([held, swap(held, bit + 1)], axis=0)
    places = jnp.arange(1 << chip_bits)
    position = jnp.zeros_like(places)
    apart = jnp.bitwise_xor(places, chip)
    for step, bit in enumerate(order):
        position = position + (jnp.bitwise_and(apart >> bit, 1) << step)
    pick = position[:, None] == places[None, :]
    return jnp.dot(pick.astype(held.dtype), held, preferred_element_type=full).astype(held.dtype)


def to_phases(block_in, row_count):
    width = block_in.shape[-1]
    split_grid = block_in.reshape(row_count // 2, 2, HALF_SIDE, 2, width)
    return split_grid.transpose(1, 3, 0, 2, 4).reshape(4, row_count // 2 * HALF_SIDE, width)


def from_phases(block_in, row_count):
    width = block_in.shape[-1]
    split_grid = block_in.reshape(2, 2, row_count // 2, HALF_SIDE, width)
    return split_grid.transpose(2, 0, 3, 1, 4).reshape(row_count * SIDE, width)


def in_core_order(mine, other, core):
    return jnp.where(core == 0, mine, other), jnp.where(core == 0, other, mine)


def join_halves(mine, other, core):
    return jnp.stack(in_core_order(mine, other, core), axis=1).reshape(-1, mine.shape[-1])


def half_of(joined, which):
    width = joined.shape[-1]
    return at_bit(joined.reshape(4, 2, -1, width), 1, which)


def layer_norm(values):
    average = jnp.mean(values, axis=-1, keepdims=True)
    centred = values - average
    variance = jnp.mean(centred * centred, axis=-1, keepdims=True)
    return centred * lax.rsqrt(variance + ln_epsilon)


def modulate(values, shift_by, scale_by):
    return layer_norm(values) * (1.0 + scale_by) + shift_by


def sinusoid(steps_in, width):
    halfway = width // 2
    frequency = jnp.exp(-math.log(10000.0) * jnp.arange(halfway, dtype=jnp.float32) / halfway)
    angles = steps_in.astype(jnp.float32)[..., None] * frequency
    return jnp.concatenate([jnp.cos(angles), jnp.sin(angles)], axis=-1)


def depthwise(framed, kernel):
    row_count = framed.shape[0] - 2
    result = jnp.zeros((row_count, SIDE, framed.shape[2]), jnp.float32)
    for tap in range(9):
        r, s = divmod(tap, 3)
        result = result + framed[r : r + row_count, s : s + SIDE] * kernel[tap].astype(full)
    return result


def kernel_grad(framed, upstream):
    row_count = upstream.shape[0]
    sums = []
    for tap in range(9):
        r, s = divmod(tap, 3)
        sums.append(jnp.sum(framed[r : r + row_count, s : s + SIDE] * upstream, axis=(0, 1)))
    return jnp.stack(sums)


def softmax_of(query, key, allowed):
    raw = lax.dot_general(query, key, (((1,), (1,)), ((), ())), preferred_element_type=full)
    scores = jnp.where(allowed, raw * HEAD ** (-0.5), masked_score)
    shifted = jnp.exp(scores - jnp.max(scores, axis=-1, keepdims=True))
    return shifted / jnp.sum(shifted, axis=-1, keepdims=True)


def head_lanes(shape, head):
    lanes = lax.broadcasted_iota(jnp.int32, shape, 1)
    return jnp.logical_and(lanes >= head * HEAD, lanes < (head + 1) * HEAD)


def attend_body(mask_ref, qkv_ref, out_ref):
    allowed = mask_ref[...] > 0.5

    @pl.loop(0, 4)
    def _(phase):
        rows = pl.ds(pl.multiple_of(phase * PLANE, PLANE), PLANE)
        query = qkv_ref[rows, :128]
        key = qkv_ref[rows, 128:256]
        value = qkv_ref[rows, 256:]
        total = None
        for head in range(2):
            here = head_lanes(key.shape, head)
            probs = softmax_of(query, jnp.where(here, key, jnp.zeros_like(key)), allowed)
            part = jnp.dot(
                probs.astype(low),
                jnp.where(here, value, jnp.zeros_like(value)),
                preferred_element_type=full,
            )
            total = part if total is None else total + part
        out_ref[rows, :] = total.astype(low)


def attend_back_body(mask_ref, qkv_ref, grad_ref, out_ref):
    allowed = mask_ref[...] > 0.5

    @pl.loop(0, 4)
    def _(phase):
        rows = pl.ds(pl.multiple_of(phase * PLANE, PLANE), PLANE)
        query = qkv_ref[rows, :128]
        key = qkv_ref[rows, 128:256]
        value = qkv_ref[rows, 256:]
        grad = grad_ref[rows, :]
        by_rows = (((0,), (0,)), ((), ()))
        totals = [None, None, None]
        for head in range(2):
            here = head_lanes(key.shape, head)
            blank = jnp.zeros_like(key)
            key_here = jnp.where(here, key, blank)
            query_here = jnp.where(here, query, blank)
            value_here = jnp.where(here, value, blank)
            grad_here = jnp.where(here, grad, blank)
            weights = softmax_of(query, key_here, allowed)
            grad_probs = lax.dot_general(
                grad, value_here, (((1,), (1,)), ((), ())), preferred_element_type=full
            )
            delta = jnp.sum(grad_probs * weights, axis=-1, keepdims=True)
            grad_scores = (weights * (grad_probs - delta)).astype(low)
            parts = (
                jnp.dot(grad_scores, key_here, preferred_element_type=full),
                lax.dot_general(grad_scores, query_here, by_rows, preferred_element_type=full),
                lax.dot_general(
                    weights.astype(low), grad_here, by_rows, preferred_element_type=full
                ),
            )
            totals = [p if t is None else t + p for t, p in zip(totals, parts)]
        out_ref[rows, :128] = (totals[0] * HEAD ** (-0.5)).astype(low)
        out_ref[rows, 128:256] = (totals[1] * HEAD ** (-0.5)).astype(low)
        out_ref[rows, 256:] = totals[2].astype(low)


def attend(mask, qkv):
    tokens, width = qkv.shape
    pairs = width // 384
    return pl.pallas_call(
        attend_body,
        grid=(pairs,),
        in_specs=[
            pl.BlockSpec((PLANE, PLANE), lambda j: (0, 0)),
            pl.BlockSpec((tokens, 384), lambda j: (0, j)),
        ],
        out_specs=pl.BlockSpec((tokens, 128), lambda j: (0, j)),
        out_shape=jax.ShapeDtypeStruct((tokens, pairs * 128), low),
        cost_estimate=pl.CostEstimate(
            flops=pairs * 2 * 4 * 4 * PLANE * PLANE * 256,
            bytes_accessed=8 * tokens * pairs * 128,
            transcendentals=pairs * 8 * PLANE * PLANE,
        ),
        name="attend",
    )(mask, qkv)


def attend_back(mask, qkv, grad):
    tokens, width = qkv.shape
    pairs = width // 384
    return pl.pallas_call(
        attend_back_body,
        grid=(pairs,),
        in_specs=[
            pl.BlockSpec((PLANE, PLANE), lambda j: (0, 0)),
            pl.BlockSpec((tokens, 384), lambda j: (0, j)),
            pl.BlockSpec((tokens, 128), lambda j: (0, j)),
        ],
        out_specs=pl.BlockSpec((tokens, 384), lambda j: (0, j)),
        out_shape=jax.ShapeDtypeStruct((tokens, width), low),
        cost_estimate=pl.CostEstimate(
            flops=pairs * 2 * 4 * 10 * PLANE * PLANE * 256,
            bytes_accessed=14 * tokens * pairs * 128,
            transcendentals=pairs * 8 * PLANE * PLANE,
        ),
        name="attend_back",
    )(mask, qkv, grad)


def strip_at(ref, row_phase, column_phase, row):
    start = pl.multiple_of((row + 1) * STRIP, STRIP)
    return ref[2 * row_phase + column_phase, pl.ds(start, STRIP), :]


def near_strips(ref, row):
    tokens = lax.broadcasted_iota(jnp.int32, (STRIP, ref.shape[-1]), 0)
    loaded = {}
    for row_phase, at in ((1, row - 1), (0, row), (1, row), (0, row + 1)):
        even = strip_at(ref, row_phase, 0, at)
        odd = strip_at(ref, row_phase, 1, at)
        before = jnp.where(tokens == 0, 0.0, pltpu.roll(odd, 1, 0))
        after = jnp.where(tokens == STRIP - 1, 0.0, pltpu.roll(even, STRIP - 1, 0))
        loaded[len(loaded)] = ((before, even, odd), (even, odd, after))
    return {0: (loaded[0], loaded[1], loaded[2]), 1: (loaded[1], loaded[2], loaded[3])}


def conv_strip(near, kernel, row_phase, column_phase):
    total = None
    for i in range(3):
        for j in range(3):
            term = near[row_phase][i][column_phase][j] * kernel[3 * i + j : 3 * i + j + 1, :]
            total = term if total is None else total + term
    return total


def feed_body(
    norm_ref,
    norm_t_ref,
    grad_ref,
    up_ref,
    down_ref,
    kernel_ref,
    branch_ref,
    back_ref,
    up_grad_ref,
    down_grad_ref,
    kernel_grad_ref,
    branch_acc,
    back_acc,
    hidden,
    widened_grad,
    act_grad,
    act,
    hidden_grad,
):
    step = pl.program_id(0)
    by_columns = (((1,), (1,)), ((), ()))
    width = up_ref.shape[1]

    @pl.when(step == 0)
    def _():
        blank = jnp.zeros((STRIP, width), full)
        for plane in range(4):
            for ref in (hidden, widened_grad):
                ref[plane, pl.ds(0, STRIP), :] = blank
                ref[plane, pl.ds(PLANE + STRIP, STRIP), :] = blank
        branch_acc[...] = jnp.zeros_like(branch_acc)
        back_acc[...] = jnp.zeros_like(back_acc)

    @pl.loop(0, 4)
    def _(plane):
        rows = pl.ds(pl.multiple_of(plane * PLANE, PLANE), PLANE)
        hidden[plane, pl.ds(STRIP, PLANE), :] = jnp.dot(
            norm_ref[rows, :], up_ref[...], preferred_element_type=full
        )
        act_grad[rows, :] = lax.dot_general(
            grad_ref[rows, :], down_ref[...], by_columns, preferred_element_type=full
        )

    kernel = kernel_ref[...]

    def forward_strip(row, sums):
        near = near_strips(hidden, row)
        sums = list(sums)
        for row_phase in range(2):
            for column_phase in range(2):
                plane = 2 * row_phase + column_phase
                wide = conv_strip(near, kernel, row_phase, column_phase)
                square = wide * wide
                bend = math.sqrt(2.0 / math.pi) * (wide + 0.044715 * wide * square)
                curve = jnp.tanh(bend)
                half = 0.5 * (1.0 + curve)
                slope = half + 0.5 * wide * (1.0 - curve * curve) * (
                    math.sqrt(2.0 / math.pi) * (1.0 + 3 * 0.044715 * square)
                )
                at = pl.ds(pl.multiple_of(plane * PLANE + row * STRIP, STRIP), STRIP)
                act[at, :] = (wide * half).astype(low)
                grad_here = slope * act_grad[at, :]
                widened_grad[plane, pl.ds(pl.multiple_of((row + 1) * STRIP, STRIP), STRIP), :] = (
                    grad_here
                )
                for i in range(3):
                    for j in range(3):
                        product = near[row_phase][i][column_phase][j] * grad_here
                        sums[3 * i + j] = sums[3 * i + j] + (product[:8] + product[8:])
        return tuple(sums)

    sums = lax.fori_loop(
        0, HALF_SIDE, forward_strip, tuple(jnp.zeros((8, width), full) for _ in range(9))
    )
    kernel_grad_ref[...] = jnp.concatenate(
        [jnp.sum(s, axis=0, keepdims=True) for s in sums] + [jnp.zeros((7, width), full)], axis=0
    )

    flipped = [kernel[8 - t : 9 - t, :] for t in range(9)]
    flipped = jnp.concatenate(flipped, axis=0)

    @pl.loop(0, HALF_SIDE)
    def _(row):
        near = near_strips(widened_grad, row)
        for row_phase in range(2):
            for column_phase in range(2):
                plane = 2 * row_phase + column_phase
                at = pl.ds(pl.multiple_of(plane * PLANE + row * STRIP, STRIP), STRIP)
                hidden_grad[at, :] = conv_strip(near, flipped, row_phase, column_phase).astype(low)

    @pl.loop(0, 4)
    def _(plane):
        rows = pl.ds(pl.multiple_of(plane * PLANE, PLANE), PLANE)
        branch_acc[rows, :] += jnp.dot(act[rows, :], down_ref[...], preferred_element_type=full)
        back_acc[rows, :] += lax.dot_general(
            hidden_grad[rows, :], up_ref[...], by_columns, preferred_element_type=full
        )

    model = norm_t_ref.shape[0]

    @pl.loop(0, model // TILE)
    def _(tile):
        rows = pl.ds(pl.multiple_of(tile * TILE, TILE), TILE)
        up_grad_ref[rows, :] = jnp.dot(
            norm_t_ref[rows, :], hidden_grad[...], preferred_element_type=full
        ).astype(low)

    down_grad_ref[...] = lax.dot_general(
        act[...], grad_ref[...], (((0,), (0,)), ((), ())), preferred_element_type=full
    ).astype(low)

    @pl.when(step == pl.num_programs(0) - 1)
    def _():
        branch_ref[...] = branch_acc[...].astype(low)
        back_ref[...] = back_acc[...].astype(low)


def feed_forward(norm, norm_t, grad, up, down, kernel):
    tokens, model = norm.shape
    channels = up.shape[1]
    width = TILE
    whole = lambda j: (0, 0)
    once = pl.Buffered(1)
    return pl.pallas_call(
        feed_body,
        grid=(channels // width,),
        in_specs=[
            pl.BlockSpec((tokens, model), whole, pipeline_mode=once),
            pl.BlockSpec((model, tokens), whole, pipeline_mode=once),
            pl.BlockSpec((tokens, model), whole, pipeline_mode=once),
            pl.BlockSpec((model, width), lambda j: (0, j)),
            pl.BlockSpec((width, model), lambda j: (j, 0)),
            pl.BlockSpec((16, width), lambda j: (0, j)),
        ],
        out_specs=[
            pl.BlockSpec((tokens, model), whole),
            pl.BlockSpec((tokens, model), whole),
            pl.BlockSpec((model, width), lambda j: (0, j)),
            pl.BlockSpec((width, model), lambda j: (j, 0)),
            pl.BlockSpec((16, width), lambda j: (0, j)),
        ],
        out_shape=[
            jax.ShapeDtypeStruct((tokens, model), low),
            jax.ShapeDtypeStruct((tokens, model), low),
            jax.ShapeDtypeStruct((model, channels), low),
            jax.ShapeDtypeStruct((channels, model), low),
            jax.ShapeDtypeStruct((16, channels), full),
        ],
        scratch_shapes=[
            pltpu.VMEM((tokens, model), full),
            pltpu.VMEM((tokens, model), full),
            pltpu.VMEM((4, PADDED, width), full),
            pltpu.VMEM((4, PADDED, width), full),
            pltpu.VMEM((tokens, width), full),
            pltpu.VMEM((tokens, width), low),
            pltpu.VMEM((tokens, width), low),
        ],
        compiler_params=pltpu.CompilerParams(vmem_limit_bytes=62 * 1024 * 1024),
        cost_estimate=pl.CostEstimate(
            flops=12 * tokens * model * channels,
            bytes_accessed=8 * model * channels + 10 * tokens * model,
            transcendentals=tokens * channels,
        ),
        name="feed_forward",
    )(norm, norm_t, grad, up, down, kernel)


def on_device(
    tokens,
    seg_ids,
    timesteps,
    labels,
    cotangent,
    mod_weight,
    class_table,
    attn_kernel,
    qkv_weight,
    proj_weight,
    up_weight,
    ffn_kernel,
    down_weight,
):
    devices = device_count()
    chips = devices // 2
    chip_bits = chips.bit_length() - 1
    rank = lax.axis_index("dp") * lax.axis_size("fsdp") + lax.axis_index("fsdp")
    core = rank % 2
    chip = rank // 2
    _, half_tokens, model = tokens.shape
    half_rows = half_tokens // SIDE
    class_count = class_table.shape[0]
    part = model // devices
    share = down_weight.shape[0]
    piece = share // CHUNKS
    pairs = model // HEAD // 4

    picks = labels[:, None] == jnp.arange(class_count)[None, :]
    angles_here = lax.dynamic_slice_in_dim(sinusoid(timesteps, model), rank * part, part, axis=1)
    cond = angles_here + jnp.dot(picks.astype(low), class_table, preferred_element_type=full)
    lift_value, lift_pull = jax.vjp(jax.nn.silu, cond)
    lifted = lift_value.astype(low)
    mods_part = jnp.dot(lifted, mod_weight, preferred_element_type=full)
    mods_half = scatter_sum(mods_part, 0, chip, chip_bits, sent=full)
    mods = mods_half + swap_core(mods_half)
    shift_a, scale_a, gate_a, shift_f, scale_f, gate_f = jnp.split(mods, 6)

    def halves_of(array, axis):
        return at_bit(array, axis, core), at_bit(array, axis, 1 - core)

    def row_pair(array, axis):
        kept, leaving = halves_of(array, axis)
        arriving = swap_core(leaving)
        return jnp.concatenate(in_core_order(kept, arriving, core), axis=0)

    qkv_split = qkv_weight.reshape(part, 3, 2, pairs, 128).transpose(0, 2, 3, 1, 4)
    qkv_rows = row_pair(qkv_split.reshape(part, 2, pairs * 384), 1)
    qkv_half = pairs * 384 // 2
    up_split = up_weight.reshape(part, chips, 2, CHUNKS, piece).transpose(0, 2, 3, 1, 4)
    up_rows = row_pair(up_split.reshape(part, 2, CHUNKS, chips * piece), 1)
    proj_there = [(r, r % chips * 2 + r // chips) for r in range(devices)]
    proj_back = [(b, a) for a, b in proj_there]
    proj_rows = lax.ppermute(proj_weight, AXES, proj_there)

    qkv_full = jnp.concatenate(
        [
            gather_weights(qkv_rows[:, :qkv_half], 0, chip, chip_bits).reshape(model, qkv_half),
            gather_weights(qkv_rows[:, qkv_half:], 1, chip, chip_bits).reshape(model, qkv_half),
        ],
        axis=1,
    )
    proj_halves = [
        gather_weights(proj_rows[:, : model // 2], 0, chip, chip_bits).reshape(-1, model // 2),
        gather_weights(proj_rows[:, model // 2 :], 1, chip, chip_bits).reshape(-1, model // 2),
    ]
    proj_full = jnp.concatenate(proj_halves, axis=1)
    up_full = [
        gather_weights(up_rows[:, t], 0, chip, chip_bits).reshape(model, -1)
        for t in range(CHUNKS)
    ]
    down_full = [
        gather_weights(down_weight[t * piece : (t + 1) * piece], 1, chip, chip_bits).reshape(
            -1, model
        )
        for t in range(CHUNKS)
    ]

    tap_count = 9 * (share + part)
    tap_words = jnp.concatenate([ffn_kernel.reshape(-1), attn_kernel.reshape(-1)])
    tap_rows = -(-tap_count // 2048) * 16
    tap_words = jnp.pad(tap_words, (0, tap_rows * 128 - tap_count)).reshape(tap_rows, 128)
    taps = lax.all_gather(tap_words, AXES, axis=0, tiled=True).reshape(devices, -1)
    ffn_taps = taps[:, : 9 * share].reshape(chips, 2, 9, share)
    ffn_taps = at_bit(ffn_taps, 1, core).reshape(chips, 9, CHUNKS, piece)
    ffn_taps = ffn_taps.transpose(2, 1, 0, 3).reshape(CHUNKS, 9, chips * piece).astype(full)
    ffn_taps = jnp.pad(ffn_taps, ((0, 0), (0, 7), (0, 0)))
    attn_taps = taps[:, 9 * share : tap_count].reshape(devices, 9, part)
    attn_taps = attn_taps.transpose(1, 0, 2).reshape(9, model)

    mine = tokens[0]
    canvas = jnp.concatenate(in_core_order(mine, swap_core(mine), core), axis=0)
    grad_mine = to_phases(cotangent[0], half_rows)
    grad_ph = join_halves(grad_mine, swap_core(grad_mine), core)

    normed_all = modulate(canvas.astype(full), shift_a, scale_a).reshape(SIDE, SIDE, model)
    normed_pad = jnp.pad(normed_all, ((1, 1), (1, 1), (0, 0)))
    convolved = depthwise(normed_pad, attn_taps).astype(low)
    convolved = to_phases(convolved.reshape(SIDE * SIDE, model), SIDE).reshape(SIDE * SIDE, model)

    qkv = jnp.dot(convolved, qkv_full, preferred_element_type=full).astype(low)

    spot = jnp.arange(PLANE)
    quadrant = 2 * (spot // (PLANE // 2)) + spot % HALF_SIDE // (HALF_SIDE // 2)
    quadrants_here = at_bit(seg_ids, 0, chip)
    segment = jnp.sum(
        jnp.where(quadrant[:, None] == jnp.arange(4)[None, :], quadrants_here[None, :], 0), axis=1
    )
    mask = (segment[:, None] == segment[None, :]).astype(full)

    attended = attend(mask, qkv)
    branch_part = jnp.dot(attended, proj_full, preferred_element_type=full)
    branch_a = half_of(branch_part, core) + swap_core(
        half_of(branch_part, 1 - core).astype(low)
    ).astype(full)
    source_ph = to_phases(mine, half_rows).astype(full)
    middle = source_ph + gate_a * branch_a
    normed_f, norm_pull_f = jax.vjp(modulate, middle, shift_f, scale_f)
    normed_low = normed_f.astype(low)
    norm = join_halves(normed_low, swap_core(normed_low), core)
    norm_t = norm.T
    grad_branch_f = (grad_ph.astype(full) * gate_f).astype(low)

    branch_sum, back_sum = 0.0, 0.0
    up_shares, down_shares, tap_grads = [], [], []
    for t in range(CHUNKS):
        branch, back, up_grad, down_grad, tap_grad = feed_forward(
            norm, norm_t, grad_branch_f, up_full[t], down_full[t], ffn_taps[t]
        )
        both = jnp.stack([branch, back]).reshape(2, 4, 2, -1, model)
        staying = at_bit(both, 2, core)
        arriving = swap_core(at_bit(both, 2, 1 - core))
        total = staying.astype(full) + arriving.astype(full)
        branch_sum = branch_sum + total[0]
        back_sum = back_sum + total[1]
        up_shares.append(
            scatter_sum(up_grad.reshape(chips, 2 * part, -1), 0, chip, chip_bits)
        )
        down_shares.append(scatter_sum(down_grad.reshape(chips, piece, model), 1, chip, chip_bits))
        tap_grads.append(tap_grad[:9].reshape(9, chips, piece))

    upstream = to_phases(cotangent[0], half_rows).astype(full)
    layer_out = (middle + gate_f * branch_sum).astype(low)
    layer_out = from_phases(layer_out, half_rows)[None]
    grad_gate_f = jnp.sum(upstream * branch_sum, axis=(0, 1))
    grad_middle, grad_shift_f, grad_scale_f = norm_pull_f(back_sum)
    grad_middle = grad_middle + upstream

    grad_gate_a = jnp.sum(grad_middle * branch_a, axis=(0, 1))
    grad_branch_mine = (grad_middle * gate_a).astype(low)
    grad_branch_a = join_halves(grad_branch_mine, swap_core(grad_branch_mine), core)
    grad_attended = jnp.dot(grad_branch_a, proj_full.T, preferred_element_type=full).astype(low)
    proj_grad = jnp.dot(attended.T, grad_branch_a, preferred_element_type=full).astype(low)
    proj_grad = proj_grad.reshape(chips, -1, model)
    proj_share = jnp.concatenate(
        [
            scatter_sum(proj_grad[..., : model // 2], 0, chip, chip_bits),
            scatter_sum(proj_grad[..., model // 2 :], 1, chip, chip_bits),
        ],
        axis=1,
    )
    proj_share = lax.ppermute(proj_share, AXES, proj_back)

    grad_qkv = attend_back(mask, qkv, grad_attended)
    qkv_grad = jnp.dot(convolved.T, grad_qkv, preferred_element_type=full).astype(low)
    qkv_grad = qkv_grad.reshape(chips, 2 * part, -1)
    qkv_share = jnp.concatenate(
        [
            scatter_sum(qkv_grad[..., :qkv_half], 0, chip, chip_bits),
            scatter_sum(qkv_grad[..., qkv_half:], 1, chip, chip_bits),
        ],
        axis=1,
    )

    grad_conv_part = jnp.dot(grad_qkv, qkv_full.T, preferred_element_type=full)
    grad_conv_part = from_phases(grad_conv_part.reshape(4, PLANE, model), SIDE)
    grad_conv_part = jnp.pad(
        grad_conv_part.reshape(SIDE, SIDE, model), ((1, 1), (0, 0), (0, 0))
    )

    def rows_near(array, which):
        return lax.dynamic_slice_in_dim(array, which * half_rows, half_rows + 2, axis=0)

    grad_conv = rows_near(grad_conv_part, core) + swap_core(
        rows_near(grad_conv_part, 1 - core).astype(low)
    ).astype(full)
    normed_near = rows_near(normed_pad, core)
    attn_tap_grad = kernel_grad(normed_near, grad_conv[1:-1])
    grad_normed_a = depthwise(
        jnp.pad(grad_conv, ((0, 0), (1, 1), (0, 0))), attn_taps[::-1]
    ).reshape(half_tokens, model)
    _, norm_pull_a = jax.vjp(modulate, mine.astype(full), shift_a, scale_a)
    grad_source, grad_shift_a, grad_scale_a = norm_pull_a(grad_normed_a)
    input_grad = grad_source + from_phases(grad_middle, half_rows)

    grad_mods = jnp.concatenate(
        [grad_shift_a, grad_scale_a, grad_gate_a, grad_shift_f, grad_scale_f, grad_gate_f]
    )
    grad_mods = (grad_mods + swap_core(grad_mods)).astype(low)
    grad_mods_all = gather_rows(grad_mods, chip, chip_bits)
    mod_grad = jnp.dot(lifted.T, grad_mods_all, preferred_element_type=full)
    (cond_grad,) = lift_pull(jnp.dot(grad_mods_all, mod_weight.T, preferred_element_type=full))
    table_grad = jnp.dot(picks.astype(full).T, cond_grad, precision=highest)

    ffn_tap_grad = jnp.concatenate(tap_grads, axis=2).transpose(1, 0, 2)
    attn_split = attn_tap_grad.reshape(9, chips, 2, part)
    attn_kept, attn_leaving = halves_of(attn_split, 2)
    attn_tap_grad = (attn_kept + swap_core(attn_leaving)).transpose(1, 0, 2)
    tap_parts = jnp.concatenate(
        [ffn_tap_grad.reshape(chips, -1), attn_tap_grad.reshape(chips, -1)], axis=1
    )
    tap_share = scatter_sum(tap_parts, 0, chip, chip_bits, sent=full)
    ffn_share = tap_share[: 9 * share].reshape(9, share)
    kernel_share = tap_share[9 * share :].reshape(9, part)

    def row_split(array, axis):
        pair = array.reshape((2, part) + array.shape[1:])
        kept, leaving = halves_of(pair, 0)
        arriving = swap_core(leaving)
        return jnp.stack(in_core_order(kept, arriving, core), axis=axis)

    up_all = jnp.stack(up_shares, axis=1).reshape(2 * part, CHUNKS, chips, piece)
    up_share = row_split(up_all.transpose(0, 2, 1, 3), 2).reshape(part, -1)
    down_share = jnp.concatenate(down_shares, axis=0)
    qkv_all = qkv_share.reshape(2 * part, pairs, 3, 128).transpose(0, 2, 1, 3)
    qkv_out = row_split(qkv_all, 2).reshape(part, -1)

    return (
        layer_out,
        input_grad[None],
        mod_grad,
        table_grad,
        kernel_share,
        qkv_out,
        proj_share,
        up_share,
        ffn_share,
        down_share,
        grad_shift_f[None],
    )


def solution(mesh):
    return jax.shard_map(
        on_device,
        mesh=mesh,
        in_specs=(
            P(AXES, None, None),
            P(),
            P(),
            P(),
            P(AXES, None, None),
            P(AXES, None),
            P(None, AXES),
            P(None, AXES),
            P(AXES, None),
            P(AXES, None),
            P(AXES, None),
            P(None, AXES),
            P(AXES, None),
        ),
        out_specs=(
            P(AXES, None, None),
            P(AXES, None, None),
            P(AXES, None),
            P(None, AXES),
            P(None, AXES),
            P(AXES, None),
            P(AXES, None),
            P(AXES, None),
            P(None, AXES),
            P(AXES, None),
            P(AXES, None),
        ),
        check_vma=False,
    )
```

time: 2860 us -> 1310 us (0.46)
  waiting for transfers between devices: 2150 us -> 352 us
  Pallas kernels: 0 us -> 247 us
  matrix products: 277 us -> 50 us
  starting transfers between devices: 3.7 us -> 144 us
  local copies, waits for them, and re-layouts: 142 us -> 231 us
  other arithmetic: 182 us -> 226 us
  blocking collectives: 82.3 us -> 41.7 us
    reduce_scatter x6 -> x0, waiting for transfers between devices: 1720 us -> none  [the longest x1 477 us: on_device(): lax.psum_scatter(mod_grad, ('dp', 'fsdp'), scatter_dimension=0, tiled=True)]
    all_gather x6 -> x0, waiting for transfers between devices: 365 us -> none  [the longest x1 140 us: on_device(): lax.all_gather(mod_weight, ('dp', 'fsdp'), axis=0, tiled=True)]
    ppermute x9 -> x130, waiting for transfers between devices: 3.7 us -> 352 us  [the longest x128 352 us: swap(): lax.ppermute(x, AXES, [(i, i ^ 1 << bit) for i in range(device_count())])]
    pallas_call x0 -> x15, Pallas kernels: none -> 247 us  [the longest x3 157 us: feed_forward(): pl.pallas_call(feed_body, grid=(channels // width,), in_specs=[pl.BlockSp...]
    dot_general x21 -> x12, matrix products: 277 us -> 50 us  [the longest x1 12.8 us: on_device(): qkv = jnp.dot(convolved, qkv_full, preferred_element_type=full).astype(low)]
    ppermute x9 -> x130, starting transfers between devices: 2.59 us -> 144 us  [the longest x128 140 us: swap(): lax.ppermute(x, AXES, [(i, i ^ 1 << bit) for i in range(device_count())])]
    unnamed x16 -> x0, waiting for transfers between devices: 63.3 us -> none
    all_gather x2 -> x1, blocking collectives: 82.3 us -> 41.7 us  [on_device(): lax.all_gather(tap_words, AXES, axis=0, tiled=True).reshape(devices, -1)]
  transfers between devices with their start and end apart: 23 -> 130, of which waited for: 14 -> 54; matrix products, arithmetic and copies ran while one was open for 14% -> 35% of each run, Pallas kernels for 0% -> 11%
where the time goes in v1:
time: 1310 us; the launch traced here: 1290 us
  waiting for transfers between devices  352 us (27%)
  Pallas kernels  247 us (19%)
  local copies, waits for them, and re-layouts  231 us (18%)
  other arithmetic  226 us (17%)
  starting transfers between devices  144 us (11%)
  matrix products  50 us (4%)
  blocking collectives  41.7 us (3%)
    ppermute x128, waiting for transfers between devices, swap(): lax.ppermute(x, AXES, [(i, i ^ 1 << bit) for i in range(device_count())])  352 us
    pallas_call x3, Pallas kernels, feed_forward(): pl.pallas_call(feed_body, grid=(channels // width,), in_specs=[pl.BlockSp...  157 us
    ppermute x128, starting transfers between devices, swap(): lax.ppermute(x, AXES, [(i, i ^ 1 << bit) for i in range(device_count())])  140 us
    pallas_call x10, Pallas kernels, assemble(): pl.pallas_call(functools.partial(assemble_body, steps), grid_spec=pltpu.P...  45.9 us
    unnamed x334, local copies, waits for them, and re-layouts  44.3 us
    all_gather x1, blocking collectives, on_device(): lax.all_gather(tap_words, AXES, axis=0, tiled=True).reshape(devices, -1)  41.7 us
    convert_element_type x20, other arithmetic, scatter_sum(): sum((at_bit(h, axis, mine).astype(full) for h in held)).astype(sent)  36.8 us
    pallas_call x1, Pallas kernels, attend_back(): pl.pallas_call(attend_back_body, grid=(pairs,), in_specs=[pl.BlockSpec((P...  28.9 us
  transfers between devices with their start and end apart: 130, of which 54 were waited for; matrix products, arithmetic and copies ran while one was open for 35% of the time, Pallas kernels for 11%

profile of v1, /device:TPU:0, one launch (start us, length us, event | category | flops | bytes accessed | tf_op | source)
XLA Modules:
  0.0 1294.4 jit_solution(14238841802809098660)
XLA Ops:
  28.5 41.7 %all_gather.3 = bf16[1024,128]{1,0:T(8,128)(2,1)} all-gather(bf16[32,128]{1,0:T(8,128)(2,1)S(1)} %fusion.195), channel_id=1, replica_groups=mesh['dp'=8,'fsdp'=4] {'dp','fsdp'}, dimensions={0}, use_global_device_ids=true | all-gather | bytes 270336 | tf_op jit(solution)/shard_map/all_gather | solution.py:595
  137.6 9.0 collective-permute-done.28
  210.3 16.2 %collective-permute-done.16.refs_1_ = bf16[4,96,1152]{2,1,0:T(8,128)(2,1)} collective-permute-done((bf16[4,96,1152]{2,1,0:T(8,128)(2,1)S(1)}, bf16[4,96,1152]{2,1,0:T(8,128)(2,1)}, u32[]{:S(2)}, u32[]{:S(2)}) %collective-permute-start.16) | collective-permute-done | bytes 884768 | tf_op jit(solution)/shard_map/ppermute | solution.py:33
  228.4 25.3 %fusion.9 = bf16[32,32,1536]{2,1,0:T(8,128)(2,1)} fusion(f32[32,32,1536]{2,1,0:T(8,128)} %multiply_add_fusion, f32[1536]{0:T(1024)S(1)} %copy-done.121, f32[1536]{0:T(1024)S(1)} %copy-done.119, f32[1536]{0:T(1024)S(1)} %copy-done.117, f32[1536]{0:T(1024)S(1)} %copy-done.115, f32[1536]{0:T(1024)S(1)} %copy-done.113, f32[1536]{0:T(1024)S(1)} %copy-done.111, ...), kind=kLoop, calls=%fused_computation.43 | loop fusion | flops 28311552 | bytes 9492480 | tf_op jit(solution)/shard_map/convert_element_type | solution.py:610
  280.4 12.8 convolution_convert_fusion.2.qkv_ref
  293.2 15.4 %attend.1 = bf16[1024,768]{1,0:T(8,128)(2,1)} custom-call(f32[256,256]{1,0:T(8,128)} %compare_convert_fusion.mask_ref, bf16[1024,2304]{1,0:T(8,128)(2,1)} %convolution_convert_fusion.2.qkv_ref), custom_call_target="tpu_custom_call" | custom-call | flops 3221225472 | bytes 6291456 | tf_op jit(solution)/shard_map/attend/pallas_call | solution.py:278
  389.1 11.1 collective-permute-done.39.refs_1_
  402.3 14.9 %collective-permute-done.52.refs_1_ = bf16[4,96,1024]{2,1,0:T(8,128)(2,1)} collective-permute-done((bf16[4,96,1024]{2,1,0:T(8,128)(2,1)}, bf16[4,96,1024]{2,1,0:T(8,128)(2,1)}, u32[]{:S(2)}, u32[]{:S(2)}) %collective-permute-start.52) | collective-permute-done | bytes 786464 | tf_op jit(solution)/shard_map/ppermute | solution.py:33
  418.7 15.4 %collective-permute-done.65.refs_1_ = bf16[4,96,1024]{2,1,0:T(8,128)(2,1)} collective-permute-done((bf16[4,96,1024]{2,1,0:T(8,128)(2,1)S(1)}, bf16[4,96,1024]{2,1,0:T(8,128)(2,1)}, u32[]{:S(2)}, u32[]{:S(2)}) %collective-permute-start.65) | collective-permute-done | bytes 786464 | tf_op jit(solution)/shard_map/ppermute | solution.py:33
  437.7 13.2 %collective-permute-done.47.refs_3_ = bf16[4,64,1536]{2,1,0:T(8,128)(2,1)S(1)} collective-permute-done((bf16[4,64,1536]{2,1,0:T(8,128)(2,1)S(1)}, bf16[4,64,1536]{2,1,0:T(8,128)(2,1)S(1)}, u32[]{:S(2)}, u32[]{:S(2)}) %collective-permute-start.47) | collective-permute-done | bytes 786464 | tf_op jit(solution)/shard_map/ppermute | solution.py:33
  452.4 15.3 %collective-permute-done.60.refs_3_ = bf16[4,64,1536]{2,1,0:T(8,128)(2,1)S(1)} collective-permute-done((bf16[4,64,1536]{2,1,0:T(8,128)(2,1)}, bf16[4,64,1536]{2,1,0:T(8,128)(2,1)S(1)}, u32[]{:S(2)}, u32[]{:S(2)}) %collective-permute-start.60) | collective-permute-done | bytes 786464 | tf_op jit(solution)/shard_map/ppermute | solution.py:33
  469.3 13.6 %collective-permute-done.73.refs_3_ = bf16[4,64,1536]{2,1,0:T(8,128)(2,1)S(1)} collective-permute-done((bf16[4,64,1536]{2,1,0:T(8,128)(2,1)}, bf16[4,64,1536]{2,1,0:T(8,128)(2,1)S(1)}, u32[]{:S(2)}, u32[]{:S(2)}) %collective-permute-start.73) | collective-permute-done | bytes 786464 | tf_op jit(solution)/shard_map/ppermute | solution.py:33
  528.6 8.6 copy.315
  547.9 52.5 %feed_forward.3 = (bf16[1024,1536]{1,0:T(8,128)(2,1)}, bf16[1024,1536]{1,0:T(8,128)(2,1)}, bf16[1536,1024]{1,0:T(8,128)(2,1)}, bf16[1024,1536]{1,0:T(8,128)(2,1)}, f32[16,1024]{1,0:T(8,128)}) custom-call(bf16[1024,1536]{1,0:T(8,128)(2,1)} %copy.322.norm_ref, bf16[1536,1024]{1,0:T(8,128)(2,1)} %bitcast.656, bf16[1024,1536]{1,0:T(8,128)(2,1)} %fusion.17.grad_ref, ...), custom_call_target="tpu_custom_call" | custom-call | flops 19327352832 | bytes 28311552 | tf_op jit(solution)/shard_map/feed_forward/pallas_call | solution.py:468
  605.1 52.2 %feed_forward.4 = (bf16[1024,1536]{1,0:T(8,128)(2,1)}, bf16[1024,1536]{1,0:T(8,128)(2,1)}, bf16[1536,1024]{1,0:T(8,128)(2,1)}, bf16[1024,1536]{1,0:T(8,128)(2,1)}, f32[16,1024]{1,0:T(8,128)}) custom-call(bf16[1024,1536]{1,0:T(8,128)(2,1)} %copy.322.norm_ref, bf16[1536,1024]{1,0:T(8,128)(2,1)} %bitcast.657, bf16[1024,1536]{1,0:T(8,128)(2,1)} %fusion.17.grad_ref, ...), custom_call_target="tpu_custom_call" | custom-call | flops 19327352832 | bytes 28311552 | tf_op jit(solution)/shard_map/feed_forward/pallas_call | solution.py:468
  669.6 52.1 %feed_forward.5 = (bf16[1024,1536]{1,0:T(8,128)(2,1)}, bf16[1024,1536]{1,0:T(8,128)(2,1)}, bf16[1536,1024]{1,0:T(8,128)(2,1)}, bf16[1024,1536]{1,0:T(8,128)(2,1)}, f32[16,1024]{1,0:T(8,128)}) custom-call(bf16[1024,1536]{1,0:T(8,128)(2,1)} %copy.322.norm_ref, bf16[1536,1024]{1,0:T(8,128)(2,1)} %bitcast.658, bf16[1024,1536]{1,0:T(8,128)(2,1)} %fusion.17.grad_ref, ...), custom_call_target="tpu_custom_call" | custom-call | flops 19327352832 | bytes 28311552 | tf_op jit(solution)/shard_map/feed_forward/pallas_call | solution.py:468
  758.2 13.7 %collective-permute-done.113 = bf16[2,2,2,96,1024]{4,3,2,1,0:T(8,128)(2,1)} collective-permute-done((bf16[2,2,2,96,1024]{4,3,2,1,0:T(8,128)(2,1)}, bf16[2,2,2,96,1024]{4,3,2,1,0:T(8,128)(2,1)}, u32[]{:S(2)}, u32[]{:S(2)}) %collective-permute-start.113) | collective-permute-done | bytes 1572896 | tf_op jit(solution)/shard_map/ppermute | solution.py:33
  819.1 10.9 collective-permute-done.114
  864.4 11.2 collective-permute-done.115
  897.4 11.3 collective-permute-done.108
  908.8 12.5 collective-permute-done.112
  921.4 14.8 %collective-permute-done.116 = bf16[96,1024]{0,1:T(8,128)(2,1)S(1)} collective-permute-done((bf16[96,1024]{0,1:T(8,128)(2,1)S(1)}, bf16[96,1024]{0,1:T(8,128)(2,1)S(1)}, u32[]{:S(2)}, u32[]{:S(2)}) %collective-permute-start.116) | collective-permute-done | bytes 196640 | tf_op jit(solution)/shard_map/ppermute | solution.py:33
  1006.3 28.9 %attend_back.1 = bf16[1024,2304]{1,0:T(8,128)(2,1)} custom-call(f32[256,256]{1,0:T(8,128)} %compare_convert_fusion.mask_ref, bf16[1024,2304]{1,0:T(8,128)(2,1)} %convolution_convert_fusion.2.qkv_ref, bf16[1024,768]{1,0:T(8,128)(2,1)} %convolution_convert_fusion.4.grad_ref), custom_call_target="tpu_custom_call" | custom-call | flops 8053063680 | bytes 11010048 | tf_op jit(solution)/shard_map/attend_back/pallas_call | solution.py:299
  1035.3 10.7 convolution_convert_fusion
  1046.1 9.6 fusion.18
  1061.2 11.1 collective-permute-done.96
  1077.9 10.4 copy.453
  1088.3 8.6 reshape_reshape.73
  1098.0 8.8 collective-permute-start.98
  1106.7 9.1 collective-permute-done.101
  1188.0 19.4 %multiply_reduce_fusion.3 = (f32[1536]{0:T(1024)S(1)}, f32[16,32]{1,0:T(8,128)}, f32[1536]{0:T(1024)S(1)}) fusion(f32[16,32,1536]{2,1,0:T(8,128)} %bitcast.673, f32[16,32]{1,0:T(8,128)} %div.113, f32[16,32]{1,0:T(8,128)S(1)} %get-tuple-element.183, f32[16,32]{1,0:T(8,128)S(1)} %get-tuple-element.182, f32[1536]{0:T(1024)S(1)} %copy-done.96, ...), kind=kLoop, calls=%fused_computation.149 | loop fusion | flops 22016512 | bytes 16224256 | tf_op jit(solution)/shard_map/transpose(jvp())/reduce_sum | solution.py:175
  1260.7 10.7 collective-permute-done.89
  (853 shorter events, 720.0 us)
Async XLA Ops:
  2.7 120.9 %collective-permute-start.42 = (bf16[1,64,1536]{2,1,0:T(8,128)(2,1)}, bf16[1,64,1536]{2,1,0:T(8,128)(2,1)}, u32[]{:S(2)}, u32[]{:S(2)}) collective-permute-start(bf16[1,64,1536]{2,1,0:T(8,128)(2,1)} %get-tuple-element.147), channel_id=1, source_target_pairs={{0,16},{1,17},{2,18},{3,19},{4,20},{5,21},{6,22},{7,23},{8,24},{9,... | collective-permute-start | bytes 589832 | tf_op jit(solution)/shard_map/ppermute | solution.py:33
  6.7 119.3 %collective-permute-start.43 = (bf16[1,64,1536]{2,1,0:T(8,128)(2,1)}, bf16[1,64,1536]{2,1,0:T(8,128)(2,1)}, u32[]{:S(2)}, u32[]{:S(2)}) collective-permute-start(bf16[1,64,1536]{2,1,0:T(8,128)(2,1)} %get-tuple-element.147), channel_id=1, source_target_pairs={{0,8},{1,9},{2,10},{3,11},{4,12},{5,13},{6,14},{7,15},{8,0},{9,1},... | collective-permute-start | bytes 589832 | tf_op jit(solution)/shard_map/ppermute | solution.py:33
  15.2 103.0 %collective-permute-start.35 = (bf16[48,3,1024]{2,0,1:T(8,128)(2,1)}, bf16[48,3,1024]{2,0,1:T(8,128)(2,1)}, u32[]{:S(2)}, u32[]{:S(2)}) collective-permute-start(bf16[48,3,1024]{2,0,1:T(8,128)(2,1)} %dynamic-slice_bitcast_fusion.4), channel_id=1, source_target_pairs={{0,1},{1,0},{2,3},{3,2},{4,5},{5,4},{6,7},{7,6},{8,9},{9,8},{10,11... | collective-permute-start | bytes 884744 | tf_op jit(solution)/shard_map/ppermute | solution.py:33
  19.1 82.9 %collective-permute-start.6 = (bf16[48,2304]{1,0:T(8,128)(2,1)}, bf16[48,2304]{1,0:T(8,128)(2,1)}, u32[]{:S(2)}, u32[]{:S(2)}) collective-permute-start(bf16[48,2304]{1,0:T(8,128)(2,1)} %dynamic-slice_bitcast_fusion.5), channel_id=1, source_target_pairs={{0,1},{1,0},{2,3},{3,2},{4,5},{5,4},{6,7},{7,6},{8,9},{9,8},{10,11... | collective-permute-start | bytes 663560 | tf_op jit(solution)/shard_map/ppermute | solution.py:33
  19.6 81.1 %collective-permute-start.19 = (bf16[48,1536]{1,0:T(8,128)(2,1)}, bf16[48,1536]{1,0:T(8,128)(2,1)}, u32[]{:S(2)}, u32[]{:S(2)}) collective-permute-start(bf16[48,1536]{1,0:T(8,128)(2,1)} %param.22), channel_id=1, source_target_pairs={{0,0},{1,2},{2,4},{3,6},{4,8},{5,10},{6,12},{7,14},{8,16},{9,18},{... | collective-permute-start | bytes 442376 | tf_op jit(solution)/shard_map/ppermute | solution.py:566
  100.7 88.1 %collective-permute-start.5 = (bf16[512,1536]{1,0:T(8,128)(2,1)S(1)}, bf16[512,1536]{1,0:T(8,128)(2,1)}, u32[]{:S(2)}, u32[]{:S(2)}) collective-permute-start(bf16[512,1536]{1,0:T(8,128)(2,1)S(1)} %bitcast.643), channel_id=1, source_target_pairs={{0,1},{1,0},{2,3},{3,2},{4,5},{5,4},{6,7},{7,6},{8,9},{9,8},{10,11... | collective-permute-start | bytes 4718600 | tf_op jit(solution)/shard_map/ppermute | solution.py:33
  174.3 97.7 %collective-permute-start.55 = (bf16[1,64,1536]{2,1,0:T(8,128)(2,1)}, bf16[1,64,1536]{2,1,0:T(8,128)(2,1)}, u32[]{:S(2)}, u32[]{:S(2)}) collective-permute-start(bf16[1,64,1536]{2,1,0:T(8,128)(2,1)} %get-tuple-element.149), channel_id=1, source_target_pairs={{0,16},{1,17},{2,18},{3,19},{4,20},{5,21},{6,22},{7,23},{8,24},{9,... | collective-permute-start | bytes 589832 | tf_op jit(solution)/shard_map/ppermute | solution.py:33
  178.7 93.6 %collective-permute-start.68 = (bf16[1,64,1536]{2,1,0:T(8,128)(2,1)S(1)}, bf16[1,64,1536]{2,1,0:T(8,128)(2,1)}, u32[]{:S(2)}, u32[]{:S(2)}) collective-permute-start(bf16[1,64,1536]{2,1,0:T(8,128)(2,1)S(1)} %copy-done.72), channel_id=1, source_target_pairs={{0,16},{1,17},{2,18},{3,19},{4,20},{5,21},{6,22},{7,23},{8,24},{9,... | collective-permute-start | bytes 589832 | tf_op jit(solution)/shard_map/ppermute | solution.py:33
  208.0 66.0 %collective-permute-start.17 = (bf16[4,96,1152]{2,1,0:T(8,128)(2,1)S(1)}, bf16[4,96,1152]{2,1,0:T(8,128)(2,1)}, u32[]{:S(2)}, u32[]{:S(2)}) collective-permute-start(bf16[4,96,1152]{2,1,0:T(8,128)(2,1)S(1)} %pad_maximum_fusion.11.refs_0_), channel_id=1, source_target_pairs={{0,4},{1,5},{2,6},{3,7},{4,0},{5,1},{6,2},{7,3},{8,12},{9,13},{10,... | collective-permute-start | bytes 2654216 | tf_op jit(solution)/shard_map/ppermute | solution.py:33
  209.9 55.4 %collective-permute-start.12 = (bf16[4,96,1152]{2,1,0:T(8,128)(2,1)}, bf16[4,96,1152]{2,1,0:T(8,128)(2,1)}, u32[]{:S(2)}, u32[]{:S(2)}) collective-permute-start(bf16[4,96,1152]{2,1,0:T(8,128)(2,1)} %collective-permute-done.10.refs_1_), channel_id=1, source_target_pairs={{0,2},{1,3},{2,0},{3,1},{4,6},{5,7},{6,4},{7,5},{8,10},{9,11},{10,... | collective-permute-start | bytes 2654216 | tf_op jit(solution)/shard_map/ppermute | solution.py:33
  323.8 61.1 %collective-permute-start.32 = (bf16[4,128,1536]{2,1,0:T(8,128)(2,1)}, bf16[4,128,1536]{2,1,0:T(8,128)(2,1)}, u32[]{:S(2)}, u32[]{:S(2)}) collective-permute-start(bf16[4,128,1536]{2,1,0:T(8,128)(2,1)} %fusion.83), channel_id=1, source_target_pairs={{0,1},{1,0},{2,3},{3,2},{4,5},{5,4},{6,7},{7,6},{8,9},{9,8},{10,11... | collective-permute-start | bytes 4718600 | tf_op jit(solution)/shard_map/ppermute | solution.py:33
  370.2 67.2 %collective-permute-start.34 = (bf16[4,128,1536]{2,1,0:T(8,128)(2,1)S(1)}, bf16[4,128,1536]{2,1,0:T(8,128)(2,1)S(1)}, u32[]{:S(2)}, u32[]{:S(2)}) collective-permute-start(bf16[4,128,1536]{2,1,0:T(8,128)(2,1)S(1)} %bitcast.648), channel_id=1, source_target_pairs={{0,1},{1,0},{2,3},{3,2},{4,5},{5,4},{6,7},{7,6},{8,9},{9,8},{10,11... | collective-permute-start | bytes 4718600 | tf_op jit(solution)/shard_map/ppermute | solution.py:33
  400.3 50.6 %collective-permute-start.47 = (bf16[4,64,1536]{2,1,0:T(8,128)(2,1)S(1)}, bf16[4,64,1536]{2,1,0:T(8,128)(2,1)S(1)}, u32[]{:S(2)}, u32[]{:S(2)}) collective-permute-start(bf16[4,64,1536]{2,1,0:T(8,128)(2,1)S(1)} %copy-done.62), channel_id=1, source_target_pairs={{0,4},{1,5},{2,6},{3,7},{4,0},{5,1},{6,2},{7,3},{8,12},{9,13},{10,... | collective-permute-start | bytes 2359304 | tf_op jit(solution)/shard_map/ppermute | solution.py:33
  401.7 66.0 %collective-permute-start.60 = (bf16[4,64,1536]{2,1,0:T(8,128)(2,1)}, bf16[4,64,1536]{2,1,0:T(8,128)(2,1)S(1)}, u32[]{:S(2)}, u32[]{:S(2)}) collective-permute-start(bf16[4,64,1536]{2,1,0:T(8,128)(2,1)} %collective-permute-done.58.refs_1_), channel_id=1, source_target_pairs={{0,4},{1,5},{2,6},{3,7},{4,0},{5,1},{6,2},{7,3},{8,12},{9,13},{10,... | collective-permute-start | bytes 2359304 | tf_op jit(solution)/shard_map/ppermute | solution.py:33
  417.2 65.6 %collective-permute-start.73 = (bf16[4,64,1536]{2,1,0:T(8,128)(2,1)}, bf16[4,64,1536]{2,1,0:T(8,128)(2,1)S(1)}, u32[]{:S(2)}, u32[]{:S(2)}) collective-permute-start(bf16[4,64,1536]{2,1,0:T(8,128)(2,1)} %collective-permute-done.71.refs_1_), channel_id=1, source_target_pairs={{0,4},{1,5},{2,6},{3,7},{4,0},{5,1},{6,2},{7,3},{8,12},{9,13},{10,... | collective-permute-start | bytes 2359304 | tf_op jit(solution)/shard_map/ppermute | solution.py:33
  434.1 50.8 %collective-permute-start.41 = (bf16[4,96,1024]{2,1,0:T(8,128)(2,1)S(1)}, bf16[4,96,1024]{2,1,0:T(8,128)(2,1)S(1)}, u32[]{:S(2)}, u32[]{:S(2)}) collective-permute-start(bf16[4,96,1024]{2,1,0:T(8,128)(2,1)S(1)} %collective-permute-done.39.refs_1_), channel_id=1, source_target_pairs={{0,2},{1,3},{2,0},{3,1},{4,6},{5,7},{6,4},{7,5},{8,10},{9,11},{10,... | collective-permute-start | bytes 2359304 | tf_op jit(solution)/shard_map/ppermute | solution.py:33
  437.4 85.9 %collective-permute-start.33 = (bf16[4,128,1536]{2,1,0:T(8,128)(2,1)}, bf16[4,128,1536]{2,1,0:T(8,128)(2,1)}, u32[]{:S(2)}, u32[]{:S(2)}) collective-permute-start(bf16[4,128,1536]{2,1,0:T(8,128)(2,1)} %add_convert_fusion), channel_id=1, source_target_pairs={{0,1},{1,0},{2,3},{3,2},{4,5},{5,4},{6,7},{7,6},{8,9},{9,8},{10,11... | collective-permute-start | bytes 4718600 | tf_op jit(solution)/shard_map/ppermute | solution.py:33
  450.8 57.5 %collective-permute-start.53 = (bf16[4,96,1024]{2,1,0:T(8,128)(2,1)}, bf16[4,96,1024]{2,1,0:T(8,128)(2,1)S(1)}, u32[]{:S(2)}, u32[]{:S(2)}) collective-permute-start(bf16[4,96,1024]{2,1,0:T(8,128)(2,1)} %pad_maximum_fusion.16.refs_0_), channel_id=1, source_target_pairs={{0,2},{1,3},{2,0},{3,1},{4,6},{5,7},{6,4},{7,5},{8,10},{9,11},{10,... | collective-permute-start | bytes 2359304 | tf_op jit(solution)/shard_map/ppermute | solution.py:33
  663.6 89.8 %collective-permute-start.118 = (bf16[2,2,2,64,1536]{4,3,1,0,2:T(8,128)(2,1)}, bf16[2,2,2,64,1536]{4,3,1,0,2:T(8,128)(2,1)}, u32[]{:S(2)}, u32[]{:S(2)}) collective-permute-start(bf16[2,2,2,64,1536]{4,3,1,0,2:T(8,128)(2,1)} %copy_bitcast_fusion.5), channel_id=1, source_target_pairs={{0,4},{1,5},{2,6},{3,7},{4,0},{5,1},{6,2},{7,3},{8,12},{9,13},{10,... | collective-permute-start | bytes 4718600 | tf_op jit(solution)/shard_map/ppermute | solution.py:33
  666.1 118.5 %collective-permute-start.122 = (bf16[2,2,2,64,1536]{4,3,1,0,2:T(8,128)(2,1)}, bf16[2,2,2,64,1536]{4,3,1,0,2:T(8,128)(2,1)}, u32[]{:S(2)}, u32[]{:S(2)}) collective-permute-start(bf16[2,2,2,64,1536]{4,3,1,0,2:T(8,128)(2,1)} %copy_bitcast_fusion.4), channel_id=1, source_target_pairs={{0,4},{1,5},{2,6},{3,7},{4,0},{5,1},{6,2},{7,3},{8,12},{9,13},{10,... | collective-permute-start | bytes 4718600 | tf_op jit(solution)/shard_map/ppermute | solution.py:33
  666.9 79.5 %collective-permute-start.105 = (bf16[2,2,2,96,1024]{4,3,2,1,0:T(8,128)(2,1)}, bf16[2,2,2,96,1024]{4,3,2,1,0:T(8,128)(2,1)}, u32[]{:S(2)}, u32[]{:S(2)}) collective-permute-start(bf16[2,2,2,96,1024]{4,3,2,1,0:T(8,128)(2,1)} %dynamic-slice_bitcast_fusion.2), channel_id=1, source_target_pairs={{0,2},{1,3},{2,0},{3,1},{4,6},{5,7},{6,4},{7,5},{8,10},{9,11},{10,... | collective-permute-start | bytes 4718600 | tf_op jit(solution)/shard_map/ppermute | solution.py:33
  669.2 87.6 %collective-permute-start.109 = (bf16[2,2,2,96,1024]{4,3,2,1,0:T(8,128)(2,1)}, bf16[2,2,2,96,1024]{4,3,2,1,0:T(8,128)(2,1)}, u32[]{:S(2)}, u32[]{:S(2)}) collective-permute-start(bf16[2,2,2,96,1024]{4,3,2,1,0:T(8,128)(2,1)} %dynamic-slice_bitcast_fusion.1), channel_id=1, source_target_pairs={{0,2},{1,3},{2,0},{3,1},{4,6},{5,7},{6,4},{7,5},{8,10},{9,11},{10,... | collective-permute-start | bytes 4718600 | tf_op jit(solution)/shard_map/ppermute | solution.py:33
  753.4 187.8 %collective-permute-start.48 = (bf16[2,4,128,1536]{3,2,1,0:T(8,128)(2,1)}, bf16[2,4,128,1536]{3,2,1,0:T(8,128)(2,1)}, u32[]{:S(2)}, u32[]{:S(2)}) collective-permute-start(bf16[2,4,128,1536]{3,2,1,0:T(8,128)(2,1)} %fusion.51), channel_id=1, source_target_pairs={{0,1},{1,0},{2,3},{3,2},{4,5},{5,4},{6,7},{7,6},{8,9},{9,8},{10,11... | collective-permute-start | bytes 9437192 | tf_op jit(solution)/shard_map/ppermute | solution.py:33
  756.8 49.3 %collective-permute-start.119 = (bf16[2,2,64,1536]{3,2,1,0:T(8,128)(2,1)}, bf16[2,2,64,1536]{3,2,1,0:T(8,128)(2,1)}, u32[]{:S(2)}, u32[]{:S(2)}) collective-permute-start(bf16[2,2,64,1536]{3,2,1,0:T(8,128)(2,1)} %get-tuple-element.90), channel_id=1, source_target_pairs={{0,2},{1,3},{2,0},{3,1},{4,6},{5,7},{6,4},{7,5},{8,10},{9,11},{10,... | collective-permute-start | bytes 2359304 | tf_op jit(solution)/shard_map/ppermute | solution.py:33
  800.8 147.2 %collective-permute-start.61 = (bf16[2,4,128,1536]{3,2,1,0:T(8,128)(2,1)}, bf16[2,4,128,1536]{3,2,1,0:T(8,128)(2,1)}, u32[]{:S(2)}, u32[]{:S(2)}) collective-permute-start(bf16[2,4,128,1536]{3,2,1,0:T(8,128)(2,1)} %fusion.47), channel_id=1, source_target_pairs={{0,1},{1,0},{2,3},{3,2},{4,5},{5,4},{6,7},{7,6},{8,9},{9,8},{10,11... | collective-permute-start | bytes 9437192 | tf_op jit(solution)/shard_map/ppermute | solution.py:33
  864.4 86.7 %collective-permute-start.74 = (bf16[2,4,128,1536]{3,2,1,0:T(8,128)(2,1)}, bf16[2,4,128,1536]{3,2,1,0:T(8,128)(2,1)}, u32[]{:S(2)}, u32[]{:S(2)}) collective-permute-start(bf16[2,4,128,1536]{3,2,1,0:T(8,128)(2,1)} %fusion.43), channel_id=1, source_target_pairs={{0,1},{1,0},{2,3},{3,2},{4,5},{5,4},{6,7},{7,6},{8,9},{9,8},{10,11... | collective-permute-start | bytes 9437192 | tf_op jit(solution)/shard_map/ppermute | solution.py:33
  886.1 83.4 %collective-permute-start.121 = (bf16[64,1536]{1,0:T(8,128)(2,1)}, bf16[64,1536]{1,0:T(8,128)(2,1)S(1)}, u32[]{:S(2)}, u32[]{:S(2)}) collective-permute-start(bf16[64,1536]{1,0:T(8,128)(2,1)} %fusion.142), channel_id=1, source_target_pairs={{0,16},{1,17},{2,18},{3,19},{4,20},{5,21},{6,22},{7,23},{8,24},{9,... | collective-permute-start | bytes 589832 | tf_op jit(solution)/shard_map/ppermute | solution.py:33
  948.0 192.6 %collective-permute-start.117 = (f32[48,16,3,64]{3,1,2,0:T(8,128)}, f32[48,16,3,64]{3,1,2,0:T(8,128)}, u32[]{:S(2)}, u32[]{:S(2)}) collective-permute-start(f32[48,16,3,64]{3,1,2,0:T(8,128)} %dynamic-slice_bitcast_fusion.3), channel_id=1, source_target_pairs={{0,1},{1,0},{2,3},{3,2},{4,5},{5,4},{6,7},{7,6},{8,9},{9,8},{10,11... | collective-permute-start | bytes 1769480 | tf_op jit(solution)/shard_map/ppermute | solution.py:33
  1061.1 88.6 %collective-permute-start.87 = (bf16[2,2,2,96,1152]{4,3,1,0,2:T(8,128)(2,1)}, bf16[2,2,2,96,1152]{4,3,1,0,2:T(8,128)(2,1)S(1)}, u32[]{:S(2)}, u32[]{:S(2)}) collective-permute-start(bf16[2,2,2,96,1152]{4,3,1,0,2:T(8,128)(2,1)} %copy_bitcast_fusion.2), channel_id=1, source_target_pairs={{0,2},{1,3},{2,0},{3,1},{4,6},{5,7},{6,4},{7,5},{8,10},{9,11},{10,... | collective-permute-start | bytes 5308424 | tf_op jit(solution)/shard_map/ppermute | solution.py:33
  1077.9 79.6 %collective-permute-start.91 = (bf16[2,2,2,96,1152]{4,3,1,0,2:T(8,128)(2,1)}, bf16[2,2,2,96,1152]{4,3,1,0,2:T(8,128)(2,1)}, u32[]{:S(2)}, u32[]{:S(2)}) collective-permute-start(bf16[2,2,2,96,1152]{4,3,1,0,2:T(8,128)(2,1)} %copy_bitcast_fusion.1), channel_id=1, source_target_pairs={{0,4},{1,5},{2,6},{3,7},{4,0},{5,1},{6,2},{7,3},{8,12},{9,13},{10,... | collective-permute-start | bytes 5308424 | tf_op jit(solution)/shard_map/ppermute | solution.py:33
  1153.1 102.1 %collective-permute-start.88 = (bf16[2,2,96,1152]{3,2,1,0:T(8,128)(2,1)}, bf16[2,2,96,1152]{3,2,1,0:T(8,128)(2,1)}, u32[]{:S(2)}, u32[]{:S(2)}) collective-permute-start(bf16[2,2,96,1152]{3,2,1,0:T(8,128)(2,1)} %get-tuple-element.86), channel_id=1, source_target_pairs={{0,4},{1,5},{2,6},{3,7},{4,0},{5,1},{6,2},{7,3},{8,12},{9,13},{10,... | collective-permute-start | bytes 2654216 | tf_op jit(solution)/shard_map/ppermute | solution.py:33
  1160.4 97.7 %collective-permute-start.92 = (bf16[2,2,96,1152]{3,2,1,0:T(8,128)(2,1)}, bf16[2,2,96,1152]{3,2,1,0:T(8,128)(2,1)}, u32[]{:S(2)}, u32[]{:S(2)}) collective-permute-start(bf16[2,2,96,1152]{3,2,1,0:T(8,128)(2,1)} %get-tuple-element.88), channel_id=1, source_target_pairs={{0,2},{1,3},{2,0},{3,1},{4,6},{5,7},{6,4},{7,5},{8,10},{9,11},{10,... | collective-permute-start | bytes 2654216 | tf_op jit(solution)/shard_map/ppermute | solution.py:33
  (250 other events, 4160.3 us)

commit v2 on v1

--- a/solution.py
+++ b/solution.py
@@ -44,13 +44,45 @@
     return order
 
 
-def gather_pieces(shard, order):
-    pieces = [shard[None]]
-    for step, bit in enumerate(order):
-        pieces = pieces + [swap(piece, bit + 1) for piece in pieces]
-        if len(pieces) == 4 and step + 1 < len(order):
-            pieces = [jnp.concatenate(pieces, axis=0)]
-    return pieces
+class Flow:
+    def __init__(self, steps):
+        self.steps = steps
+        self.wanted = next(steps)
+        self.result = None
+
+    def arrive(self, array):
+        try:
+            self.wanted = self.steps.send(array)
+        except StopIteration as end:
+            self.wanted, self.result = None, end.value
+
+
+class Slots:
+    def __init__(self, token):
+        self.token = token
+
+    def finish(self, flows):
+        while any(flow.wanted is not None for flow in flows):
+            self(flows)
+
+    def __call__(self, flows, work=lambda: ()):
+        flows = [flow for flow in flows if flow.wanted is not None]
+        wanted = [flow.wanted for flow in flows]
+        leaving, self.token = lax.optimization_barrier(([w[0] for w in wanted], self.token))
+        arriving = [swap(array, bit + 1) for array, (_, bit) in zip(leaving, wanted)]
+        arriving, result, self.token = lax.optimization_barrier((arriving, work(), self.token))
+        for flow, array in zip(flows, arriving):
+            flow.arrive(array)
+        return result
+
+
+def gather_steps(shard, order):
+    held = shard[None]
+    for bit in order[:-1]:
+        arriving = yield held, bit
+        held = jnp.concatenate([held, arriving], axis=0)
+    arriving = yield held, order[-1]
+    return held, arriving
 
 
 def assemble_body(steps, chip_ref, *refs):
@@ -102,17 +134,19 @@
     return out.reshape(chips, rows, columns)
 
 
-def gather_weights(shard, colour, chip, chip_bits):
-    order = gather_order(chip_bits, colour)
-    return assemble(gather_pieces(shard, order), order, chip)
+def gather_flow(shard, colour, chip_bits):
+    return Flow(gather_steps(shard, gather_order(chip_bits, colour)))
+
+
+def gathered(flow, colour, chip, chip_bits):
+    return assemble(flow.result, gather_order(chip_bits, colour), chip)
 
 
 def at_bit(array, axis, bit):
     return lax.dynamic_index_in_dim(array, bit, axis, keepdims=False)
 
 
-def scatter_sum(parts, colour, chip, chip_bits, sent=low):
-    order = gather_order(chip_bits, colour)[::-1]
+def scatter_steps(parts, order, chip, chip_bits, sent):
     left = list(range(chip_bits - 1, -1, -1))
     held = [parts.reshape((2,) * chip_bits + parts.shape[1:])]
     for bit in order:
@@ -121,15 +155,29 @@
         mine = jnp.bitwise_and(chip >> bit, 1)
         leaving = sum(at_bit(h, axis, 1 - mine).astype(full) for h in held).astype(sent)
         staying = sum(at_bit(h, axis, mine).astype(full) for h in held).astype(sent)
-        held = [staying, swap(leaving, bit + 1)]
+        arriving = yield leaving, bit
+        held = [staying, arriving]
     return held[0].astype(full) + held[1].astype(full)
 
 
-def gather_rows(row, chip, chip_bits):
+def scatter_flow(parts, colour, chip, chip_bits, sent=low):
+    order = gather_order(chip_bits, colour)[::-1]
+    return Flow(scatter_steps(parts, order, chip, chip_bits, sent))
+
+
+def scatter_sum(parts, colour, chip, chip_bits, sent=low):
+    flow = scatter_flow(parts, colour, chip, chip_bits, sent)
+    while flow.wanted is not None:
+        array, bit = flow.wanted
+        flow.arrive(swap(array, bit + 1))
+    return flow.result
+
+
+def gather_rows(row, chip, chip_bits, first_bit=1):
     order = gather_order(chip_bits, 0)
     held = row[None]
     for bit in order:
-        held = jnp.concatenate([held, swap(held, bit + 1)], axis=0)
+        held = jnp.concatenate([held, swap(held, bit + first_bit)], axis=0)
     places = jnp.arange(1 << chip_bits)
     position = jnp.zeros_like(places)
     apart = jnp.bitwise_xor(places, chip)
@@ -342,14 +390,18 @@
 
 
 def feed_body(
+    core_ref,
     norm_ref,
     norm_t_ref,
     grad_ref,
     up_ref,
     down_ref,
     kernel_ref,
-    branch_ref,
-    back_ref,
+    up_held_ref,
+    down_held_ref,
+    kernel_held_ref,
+    staying_ref,
+    leaving_ref,
     up_grad_ref,
     down_grad_ref,
     kernel_grad_ref,
@@ -455,58 +507,76 @@
 
     @pl.when(step == pl.num_programs(0) - 1)
     def _():
-        branch_ref[...] = branch_acc[...].astype(low)
-        back_ref[...] = back_acc[...].astype(low)
-
-
-def feed_forward(norm, norm_t, grad, up, down, kernel):
+        for ref, which in ((staying_ref, core_ref[0]), (leaving_ref, 1 - core_ref[0])):
+            for index, acc in enumerate((branch_acc, back_acc)):
+                for plane in range(4):
+                    start = plane * PLANE + pl.multiple_of(which * (PLANE // 2), PLANE // 2)
+                    ref[index, plane] = acc[pl.ds(start, PLANE // 2), :].astype(low)
+
+
+def feed_forward(norm, norm_t, grad, up, down, kernel, core, first, count, held=None):
     tokens, model = norm.shape
     channels = up.shape[1]
     width = TILE
-    whole = lambda j: (0, 0)
+    whole = lambda j, words: (0, 0)
+    half = lambda j, words: (0, 0, 0, 0)
+    across = lambda j, words: (0, first + j)
+    down_rows = lambda j, words: (first + j, 0)
     once = pl.Buffered(1)
+    grads = [
+        jax.ShapeDtypeStruct((model, channels), low),
+        jax.ShapeDtypeStruct((channels, model), low),
+        jax.ShapeDtypeStruct((16, channels), full),
+    ]
+    halves = jax.ShapeDtypeStruct((2, 4, PLANE // 2, model), low)
+    body = feed_body
+    if held is None:
+        held = ()
+
+        def body(*refs):
+            feed_body(*refs[:7], None, None, None, *refs[7:])
+
     return pl.pallas_call(
-        feed_body,
-        grid=(channels // width,),
-        in_specs=[
-            pl.BlockSpec((tokens, model), whole, pipeline_mode=once),
-            pl.BlockSpec((model, tokens), whole, pipeline_mode=once),
-            pl.BlockSpec((tokens, model), whole, pipeline_mode=once),
-            pl.BlockSpec((model, width), lambda j: (0, j)),
-            pl.BlockSpec((width, model), lambda j: (j, 0)),
-            pl.BlockSpec((16, width), lambda j: (0, j)),
-        ],
-        out_specs=[
-            pl.BlockSpec((tokens, model), whole),
-            pl.BlockSpec((tokens, model), whole),
-            pl.BlockSpec((model, width), lambda j: (0, j)),
-            pl.BlockSpec((width, model), lambda j: (j, 0)),
-            pl.BlockSpec((16, width), lambda j: (0, j)),
-        ],
-        out_shape=[
-            jax.ShapeDtypeStruct((tokens, model), low),
-            jax.ShapeDtypeStruct((tokens, model), low),
-            jax.ShapeDtypeStruct((model, channels), low),
-            jax.ShapeDtypeStruct((channels, model), low),
-            jax.ShapeDtypeStruct((16, channels), full),
-        ],
-        scratch_shapes=[
-            pltpu.VMEM((tokens, model), full),
-            pltpu.VMEM((tokens, model), full),
-            pltpu.VMEM((4, PADDED, width), full),
-            pltpu.VMEM((4, PADDED, width), full),
-            pltpu.VMEM((tokens, width), full),
-            pltpu.VMEM((tokens, width), low),
-            pltpu.VMEM((tokens, width), low),
-        ],
+        body,
+        grid_spec=pltpu.PrefetchScalarGridSpec(
+            num_scalar_prefetch=1,
+            grid=(count,),
+            in_specs=[
+                pl.BlockSpec((tokens, model), whole, pipeline_mode=once),
+                pl.BlockSpec((model, tokens), whole, pipeline_mode=once),
+                pl.BlockSpec((tokens, model), whole, pipeline_mode=once),
+                pl.BlockSpec((model, width), across),
+                pl.BlockSpec((width, model), down_rows),
+                pl.BlockSpec((16, width), across),
+            ]
+            + [pl.BlockSpec(memory_space=pl.ANY)] * len(held),
+            out_specs=[
+                pl.BlockSpec(halves.shape, half),
+                pl.BlockSpec(halves.shape, half),
+                pl.BlockSpec((model, width), across),
+                pl.BlockSpec((width, model), down_rows),
+                pl.BlockSpec((16, width), across),
+            ],
+            scratch_shapes=[
+                pltpu.VMEM((tokens, model), full),
+                pltpu.VMEM((tokens, model), full),
+                pltpu.VMEM((4, PADDED, width), full),
+                pltpu.VMEM((4, PADDED, width), full),
+                pltpu.VMEM((tokens, width), full),
+                pltpu.VMEM((tokens, width), low),
+                pltpu.VMEM((tokens, width), low),
+            ],
+        ),
+        out_shape=[halves, halves] + grads,
+        input_output_aliases={7 + i: 2 + i for i in range(len(held))},
         compiler_params=pltpu.CompilerParams(vmem_limit_bytes=62 * 1024 * 1024),
         cost_estimate=pl.CostEstimate(
-            flops=12 * tokens * model * channels,
-            bytes_accessed=8 * model * channels + 10 * tokens * model,
-            transcendentals=tokens * channels,
+            flops=12 * tokens * model * count * width,
+            bytes_accessed=8 * model * count * width + 10 * tokens * model,
+            transcendentals=tokens * count * width,
         ),
         name="feed_forward",
-    )(norm, norm_t, grad, up, down, kernel)
+    )(core[None].astype(jnp.int32), norm, norm_t, grad, up, down, kernel, *held)
 
 
 def on_device(
@@ -538,6 +608,27 @@
     piece = share // CHUNKS
     pairs = model // HEAD // 4
 
+    def halves_of(array, axis):
+        return at_bit(array, axis, core), at_bit(array, axis, 1 - core)
+
+    def row_pair(array, axis):
+        kept, leaving = halves_of(array, axis)
+        arriving = swap_core(leaving)
+        return jnp.concatenate(in_core_order(kept, arriving, core), axis=0)
+
+    qkv_split = qkv_weight.reshape(part, 3, 2, pairs, 128).transpose(0, 2, 3, 1, 4)
+    qkv_rows = row_pair(qkv_split.reshape(part, 2, pairs * 384), 1)
+    qkv_half = pairs * 384 // 2
+    up_split = up_weight.reshape(part, chips, 2, CHUNKS, piece).transpose(0, 2, 3, 1, 4)
+    up_rows = row_pair(up_split.reshape(part, 2, CHUNKS, chips * piece), 1)
+    proj_there = [(r, r % chips * 2 + r // chips) for r in range(devices)]
+    proj_back = [(b, a) for a, b in proj_there]
+    proj_rows = lax.ppermute(proj_weight, AXES, proj_there)
+    mine = tokens[0]
+    canvas = jnp.concatenate(in_core_order(mine, swap_core(mine), core), axis=0)
+    grad_mine = to_phases(cotangent[0], half_rows)
+    grad_ph = join_halves(grad_mine, swap_core(grad_mine), core)
+
     picks = labels[:, None] == jnp.arange(class_count)[None, :]
     angles_here = lax.dynamic_slice_in_dim(sinusoid(timesteps, model), rank * part, part, axis=1)
     cond = angles_here + jnp.dot(picks.astype(low), class_table, preferred_element_type=full)
@@ -548,69 +639,16 @@
     mods = mods_half + swap_core(mods_half)
     shift_a, scale_a, gate_a, shift_f, scale_f, gate_f = jnp.split(mods, 6)
 
-    def halves_of(array, axis):
-        return at_bit(array, axis, core), at_bit(array, axis, 1 - core)
-
-    def row_pair(array, axis):
-        kept, leaving = halves_of(array, axis)
-        arriving = swap_core(leaving)
-        return jnp.concatenate(in_core_order(kept, arriving, core), axis=0)
-
-    qkv_split = qkv_weight.reshape(part, 3, 2, pairs, 128).transpose(0, 2, 3, 1, 4)
-    qkv_rows = row_pair(qkv_split.reshape(part, 2, pairs * 384), 1)
-    qkv_half = pairs * 384 // 2
-    up_split = up_weight.reshape(part, chips, 2, CHUNKS, piece).transpose(0, 2, 3, 1, 4)
-    up_rows = row_pair(up_split.reshape(part, 2, CHUNKS, chips * piece), 1)
-    proj_there = [(r, r % chips * 2 + r // chips) for r in range(devices)]
-    proj_back = [(b, a) for a, b in proj_there]
-    proj_rows = lax.ppermute(proj_weight, AXES, proj_there)
-
-    qkv_full = jnp.concatenate(
-        [
-            gather_weights(qkv_rows[:, :qkv_half], 0, chip, chip_bits).reshape(model, qkv_half),
-            gather_weights(qkv_rows[:, qkv_half:], 1, chip, chip_bits).reshape(model, qkv_half),
-        ],
-        axis=1,
-    )
-    proj_halves = [
-        gather_weights(proj_rows[:, : model // 2], 0, chip, chip_bits).reshape(-1, model // 2),
-        gather_weights(proj_rows[:, model // 2 :], 1, chip, chip_bits).reshape(-1, model // 2),
-    ]
-    proj_full = jnp.concatenate(proj_halves, axis=1)
-    up_full = [
-        gather_weights(up_rows[:, t], 0, chip, chip_bits).reshape(model, -1)
-        for t in range(CHUNKS)
-    ]
-    down_full = [
-        gather_weights(down_weight[t * piece : (t + 1) * piece], 1, chip, chip_bits).reshape(
-            -1, model
-        )
-        for t in range(CHUNKS)
-    ]
-
     tap_count = 9 * (share + part)
     tap_words = jnp.concatenate([ffn_kernel.reshape(-1), attn_kernel.reshape(-1)])
-    tap_rows = -(-tap_count // 2048) * 16
-    tap_words = jnp.pad(tap_words, (0, tap_rows * 128 - tap_count)).reshape(tap_rows, 128)
-    taps = lax.all_gather(tap_words, AXES, axis=0, tiled=True).reshape(devices, -1)
+    tap_words = jnp.pad(tap_words, (0, -tap_count % 128))
+    taps = gather_rows(tap_words, rank, chip_bits + 1, 0)
     ffn_taps = taps[:, : 9 * share].reshape(chips, 2, 9, share)
     ffn_taps = at_bit(ffn_taps, 1, core).reshape(chips, 9, CHUNKS, piece)
     ffn_taps = ffn_taps.transpose(2, 1, 0, 3).reshape(CHUNKS, 9, chips * piece).astype(full)
     ffn_taps = jnp.pad(ffn_taps, ((0, 0), (0, 7), (0, 0)))
     attn_taps = taps[:, 9 * share : tap_count].reshape(devices, 9, part)
     attn_taps = attn_taps.transpose(1, 0, 2).reshape(9, model)
-
-    mine = tokens[0]
-    canvas = jnp.concatenate(in_core_order(mine, swap_core(mine), core), axis=0)
-    grad_mine = to_phases(cotangent[0], half_rows)
-    grad_ph = join_halves(grad_mine, swap_core(grad_mine), core)
-
-    normed_all = modulate(canvas.astype(full), shift_a, scale_a).reshape(SIDE, SIDE, model)
-    normed_pad = jnp.pad(normed_all, ((1, 1), (1, 1), (0, 0)))
-    convolved = depthwise(normed_pad, attn_taps).astype(low)
-    convolved = to_phases(convolved.reshape(SIDE * SIDE, model), SIDE).reshape(SIDE * SIDE, model)
-
-    qkv = jnp.dot(convolved, qkv_full, preferred_element_type=full).astype(low)
 
     spot = jnp.arange(PLANE)
     quadrant = 2 * (spot // (PLANE // 2)) + spot % HALF_SIDE // (HALF_SIDE // 2)
@@ -620,90 +658,189 @@
     )
     mask = (segment[:, None] == segment[None, :]).astype(full)
 
-    attended = attend(mask, qkv)
-    branch_part = jnp.dot(attended, proj_full, preferred_element_type=full)
-    branch_a = half_of(branch_part, core) + swap_core(
-        half_of(branch_part, 1 - core).astype(low)
-    ).astype(full)
+    slot = Slots(jnp.zeros((8, 128), full))
+    flow = lambda shard, colour: gather_flow(shard, colour, chip_bits)
+    sums = lambda parts, colour: scatter_flow(parts, colour, chip, chip_bits)
+    joined = lambda flows: [
+        gathered(f, colour, chip, chip_bits) for colour, f in enumerate(flows)
+    ]
+    qkv_flows = [flow(qkv_rows[:, :qkv_half], 0), flow(qkv_rows[:, qkv_half:], 1)]
+    proj_flows = [flow(proj_rows[:, : model // 2], 0), flow(proj_rows[:, model // 2 :], 1)]
+    feed_flows = [
+        [flow(up_rows[:, t], 0), flow(down_weight[t * piece : (t + 1) * piece], 1)]
+        for t in range(CHUNKS)
+    ]
+
+    slot(qkv_flows)
+    slot(qkv_flows)
+
+    def prepare():
+        normed = modulate(canvas.astype(full), shift_a, scale_a).reshape(SIDE, SIDE, model)
+        normed = jnp.pad(normed, ((1, 1), (1, 1), (0, 0)))
+        return normed, depthwise(normed, attn_taps).astype(low)
+
+    normed_pad, convolved = slot(qkv_flows + proj_flows, prepare)
+    convolved = slot(
+        qkv_flows + proj_flows, lambda: to_phases(convolved.reshape(SIDE * SIDE, model), SIDE)
+    ).reshape(SIDE * SIDE, model)
+
+    def project_in():
+        weight = jnp.concatenate(
+            [array.reshape(model, qkv_half) for array in joined(qkv_flows)], axis=1
+        )
+        return weight, jnp.dot(convolved, weight, preferred_element_type=full).astype(low)
+
+    slot.finish(qkv_flows)
+    qkv_full, qkv = slot(proj_flows + feed_flows[0], project_in)
+    attended = slot(proj_flows + feed_flows[0], lambda: attend(mask, qkv))
+
+    def project_out():
+        weight = jnp.concatenate(
+            [array.reshape(-1, model // 2) for array in joined(proj_flows)], axis=1
+        )
+        branch_part = jnp.dot(attended, weight, preferred_element_type=full)
+        branch = half_of(branch_part, core) + swap_core(
+            half_of(branch_part, 1 - core).astype(low)
+        ).astype(full)
+        return weight, branch
+
     source_ph = to_phases(mine, half_rows).astype(full)
-    middle = source_ph + gate_a * branch_a
-    normed_f, norm_pull_f = jax.vjp(modulate, middle, shift_f, scale_f)
-    normed_low = normed_f.astype(low)
-    norm = join_halves(normed_low, swap_core(normed_low), core)
-    norm_t = norm.T
-    grad_branch_f = (grad_ph.astype(full) * gate_f).astype(low)
-
-    branch_sum, back_sum = 0.0, 0.0
-    up_shares, down_shares, tap_grads = [], [], []
-    for t in range(CHUNKS):
-        branch, back, up_grad, down_grad, tap_grad = feed_forward(
-            norm, norm_t, grad_branch_f, up_full[t], down_full[t], ffn_taps[t]
+    slot.finish(proj_flows)
+    proj_full, branch_a = slot(feed_flows[0] + feed_flows[1], project_out)
+
+    def enter_feed():
+        middle = source_ph + gate_a * branch_a
+        normed_low = modulate(middle, shift_f, scale_f).astype(low)
+        norm = join_halves(normed_low, swap_core(normed_low), core)
+        return middle, norm, norm.T, (grad_ph.astype(full) * gate_f).astype(low)
+
+    middle, norm, norm_t, grad_branch_f = slot(feed_flows[0] + feed_flows[1], enter_feed)
+
+    kept = []
+    grads = [None] * CHUNKS
+
+    def feed(t, first, count):
+        def work():
+            if first == 0:
+                feed_weights[t] = [
+                    array.reshape(shape)
+                    for array, shape in zip(joined(feed_flows[t]), ((model, -1), (-1, model)))
+                ]
+            staying, leaving, *grads_now = feed_forward(
+                norm, norm_t, grad_branch_f, *feed_weights[t], ffn_taps[t], core, first, count,
+                grads[t],
+            )
+            return feed_weights[t], staying, leaving, grads_now
+
+        return work
+
+    feed_weights = [None] * CHUNKS
+    back_flows = [None] * CHUNKS
+
+    def run_feed(flows, t, first, count):
+        slot.finish(feed_flows[t])
+        feed_weights[t], staying, leaving, grads[t] = slot(flows, feed(t, first, count))
+        kept.append((staying, leaving))
+
+    blocks = chips * piece // TILE
+    run_feed(feed_flows[1] + feed_flows[2], 0, 0, 1)
+    run_feed(feed_flows[1] + feed_flows[2], 0, 1, blocks - 1)
+    run_feed(feed_flows[2], 1, 0, 1)
+    run_feed(feed_flows[2], 1, 1, blocks - 1)
+
+    def begin_back(t):
+        back_flows[t] = [
+            sums(grads[t][0].reshape(chips, 2 * part, -1), 0),
+            sums(grads[t][1].reshape(chips, piece, model), 1),
+        ]
+
+    begin_back(0)
+    begin_back(1)
+    run_feed(back_flows[0], 2, 0, blocks - 1)
+    run_feed(back_flows[0], 2, blocks - 1, 1)
+    begin_back(2)
+
+    upstream = to_phases(cotangent[0], half_rows).astype(full)
+
+    def leave_feed():
+        total = sum(
+            staying.astype(full) + swap_core(leaving).astype(full) for staying, leaving in kept
         )
-        both = jnp.stack([branch, back]).reshape(2, 4, 2, -1, model)
-        staying = at_bit(both, 2, core)
-        arriving = swap_core(at_bit(both, 2, 1 - core))
-        total = staying.astype(full) + arriving.astype(full)
-        branch_sum = branch_sum + total[0]
-        back_sum = back_sum + total[1]
-        up_shares.append(
-            scatter_sum(up_grad.reshape(chips, 2 * part, -1), 0, chip, chip_bits)
+        branch_sum, back_sum = total[0], total[1]
+        layer_out = from_phases((middle + gate_f * branch_sum).astype(low), half_rows)
+        grad_gate_f = jnp.sum(upstream * branch_sum, axis=(0, 1))
+        _, norm_pull_f = jax.vjp(modulate, middle, shift_f, scale_f)
+        grad_middle, grad_shift_f, grad_scale_f = norm_pull_f(back_sum)
+        grad_middle = grad_middle + upstream
+        grad_gate_a = jnp.sum(grad_middle * branch_a, axis=(0, 1))
+        grad_branch_mine = (grad_middle * gate_a).astype(low)
+        return (
+            layer_out, grad_middle, grad_branch_mine,
+            grad_gate_f, grad_shift_f, grad_scale_f, grad_gate_a,
         )
-        down_shares.append(scatter_sum(down_grad.reshape(chips, piece, model), 1, chip, chip_bits))
-        tap_grads.append(tap_grad[:9].reshape(9, chips, piece))
-
-    upstream = to_phases(cotangent[0], half_rows).astype(full)
-    layer_out = (middle + gate_f * branch_sum).astype(low)
-    layer_out = from_phases(layer_out, half_rows)[None]
-    grad_gate_f = jnp.sum(upstream * branch_sum, axis=(0, 1))
-    grad_middle, grad_shift_f, grad_scale_f = norm_pull_f(back_sum)
-    grad_middle = grad_middle + upstream
-
-    grad_gate_a = jnp.sum(grad_middle * branch_a, axis=(0, 1))
-    grad_branch_mine = (grad_middle * gate_a).astype(low)
-    grad_branch_a = join_halves(grad_branch_mine, swap_core(grad_branch_mine), core)
-    grad_attended = jnp.dot(grad_branch_a, proj_full.T, preferred_element_type=full).astype(low)
-    proj_grad = jnp.dot(attended.T, grad_branch_a, preferred_element_type=full).astype(low)
+
+    (
+        layer_out, grad_middle, grad_branch_mine,
+        grad_gate_f, grad_shift_f, grad_scale_f, grad_gate_a,
+    ) = slot(back_flows[0] + back_flows[1], leave_feed)
+    layer_out = layer_out[None]
+
+    def enter_attend():
+        grad_branch_a = join_halves(grad_branch_mine, swap_core(grad_branch_mine), core)
+        grad_attended = jnp.dot(grad_branch_a, proj_full.T, preferred_element_type=full)
+        proj_grad = jnp.dot(attended.T, grad_branch_a, preferred_element_type=full)
+        return grad_attended.astype(low), proj_grad.astype(low)
+
+    grad_attended, proj_grad = slot(back_flows[0] + back_flows[1], enter_attend)
     proj_grad = proj_grad.reshape(chips, -1, model)
-    proj_share = jnp.concatenate(
-        [
-            scatter_sum(proj_grad[..., : model // 2], 0, chip, chip_bits),
-            scatter_sum(proj_grad[..., model // 2 :], 1, chip, chip_bits),
-        ],
-        axis=1,
+    proj_flows = [sums(proj_grad[..., : model // 2], 0), sums(proj_grad[..., model // 2 :], 1)]
+    grad_qkv = slot(
+        back_flows[1] + back_flows[2], lambda: attend_back(mask, qkv, grad_attended)
     )
-    proj_share = lax.ppermute(proj_share, AXES, proj_back)
-
-    grad_qkv = attend_back(mask, qkv, grad_attended)
-    qkv_grad = jnp.dot(convolved.T, grad_qkv, preferred_element_type=full).astype(low)
+    qkv_grad = slot(
+        back_flows[1] + back_flows[2],
+        lambda: jnp.dot(convolved.T, grad_qkv, preferred_element_type=full).astype(low),
+    )
     qkv_grad = qkv_grad.reshape(chips, 2 * part, -1)
-    qkv_share = jnp.concatenate(
-        [
-            scatter_sum(qkv_grad[..., :qkv_half], 0, chip, chip_bits),
-            scatter_sum(qkv_grad[..., qkv_half:], 1, chip, chip_bits),
-        ],
-        axis=1,
-    )
-
-    grad_conv_part = jnp.dot(grad_qkv, qkv_full.T, preferred_element_type=full)
-    grad_conv_part = from_phases(grad_conv_part.reshape(4, PLANE, model), SIDE)
-    grad_conv_part = jnp.pad(
-        grad_conv_part.reshape(SIDE, SIDE, model), ((1, 1), (0, 0), (0, 0))
-    )
+    qkv_flows = [sums(qkv_grad[..., :qkv_half], 0), sums(qkv_grad[..., qkv_half:], 1)]
 
     def rows_near(array, which):
         return lax.dynamic_slice_in_dim(array, which * half_rows, half_rows + 2, axis=0)
 
-    grad_conv = rows_near(grad_conv_part, core) + swap_core(
-        rows_near(grad_conv_part, 1 - core).astype(low)
-    ).astype(full)
-    normed_near = rows_near(normed_pad, core)
-    attn_tap_grad = kernel_grad(normed_near, grad_conv[1:-1])
-    grad_normed_a = depthwise(
-        jnp.pad(grad_conv, ((0, 0), (1, 1), (0, 0))), attn_taps[::-1]
-    ).reshape(half_tokens, model)
-    _, norm_pull_a = jax.vjp(modulate, mine.astype(full), shift_a, scale_a)
-    grad_source, grad_shift_a, grad_scale_a = norm_pull_a(grad_normed_a)
-    input_grad = grad_source + from_phases(grad_middle, half_rows)
+    def leave_attend():
+        grad_conv_part = jnp.dot(grad_qkv, qkv_full.T, preferred_element_type=full)
+        grad_conv_part = from_phases(grad_conv_part.reshape(4, PLANE, model), SIDE)
+        grad_conv_part = jnp.pad(
+            grad_conv_part.reshape(SIDE, SIDE, model), ((1, 1), (0, 0), (0, 0))
+        )
+        return rows_near(grad_conv_part, core) + swap_core(
+            rows_near(grad_conv_part, 1 - core).astype(low)
+        ).astype(full)
+
+    grad_conv = slot(qkv_flows + back_flows[2], leave_attend)
+
+    def leave_block():
+        attn_tap_grad = kernel_grad(rows_near(normed_pad, core), grad_conv[1:-1])
+        grad_normed_a = depthwise(
+            jnp.pad(grad_conv, ((0, 0), (1, 1), (0, 0))), attn_taps[::-1]
+        ).reshape(half_tokens, model)
+        _, norm_pull_a = jax.vjp(modulate, mine.astype(full), shift_a, scale_a)
+        grad_source, grad_shift_a, grad_scale_a = norm_pull_a(grad_normed_a)
+        input_grad = grad_source + from_phases(grad_middle, half_rows)
+        return attn_tap_grad, input_grad, grad_shift_a, grad_scale_a
+
+    attn_tap_grad, input_grad, grad_shift_a, grad_scale_a = slot(
+        qkv_flows + back_flows[2], leave_block
+    )
+    slot(qkv_flows + proj_flows)
+    slot(qkv_flows + proj_flows)
+    slot.finish(sum(back_flows, proj_flows + qkv_flows))
+    up_shares = [flows[0].result for flows in back_flows]
+    down_shares = [flows[1].result for flows in back_flows]
+    tap_grads = [g[2][:9].reshape(9, chips, piece) for g in grads]
+    qkv_share = jnp.concatenate([f.result for f in qkv_flows], axis=1)
+    proj_share = jnp.concatenate([f.result for f in proj_flows], axis=1)
+    proj_share = lax.ppermute(proj_share, AXES, proj_back)
 
     grad_mods = jnp.concatenate(
         [grad_shift_a, grad_scale_a, grad_gate_a, grad_shift_f, grad_scale_f, grad_gate_f]

time: 1310 us -> 1140 us (0.87)
  waiting for transfers between devices: 352 us -> 145 us
  other arithmetic: 226 us -> 282 us
  blocking collectives: 41.7 us -> 0 us
  Pallas kernels: 247 us -> 279 us
  starting transfers between devices: 144 us -> 124 us
    ppermute x128 -> x116, waiting for transfers between devices: 352 us -> 145 us  [swap(): lax.ppermute(x, AXES, [(i, i ^ 1 << bit) for i in range(device_count())])]
    all_gather x1 -> x0, blocking collectives: 41.7 us -> none  [on_device(): lax.all_gather(tap_words, AXES, axis=0, tiled=True).reshape(devices, -1)]
    concatenate x15 -> x39, other arithmetic: 16.2 us -> 57.5 us  [the longest x28 47.5 us: gather_steps(): held = jnp.concatenate([held, arriving], axis=0)]
    pallas_call x3 -> x6, Pallas kernels: 157 us -> 182 us  [feed_forward(): pl.pallas_call(body, grid_spec=pltpu.PrefetchScalarGridSpec(num_scalar_pr...]
    optimization_barrier x0 -> x7, local copies, waits for them, and re-layouts: none -> 21.5 us  [__call__(): lax.optimization_barrier((arriving, work(), self.token))]
    ppermute x128 -> x116, starting transfers between devices: 140 us -> 121 us  [swap(): lax.ppermute(x, AXES, [(i, i ^ 1 << bit) for i in range(device_count())])]
    unnamed x334 -> x277, local copies, waits for them, and re-layouts: 44.3 us -> 25.1 us
    dynamic_slice x18 -> x13, local copies, waits for them, and re-layouts: 25.3 us -> 7.55 us  [at_bit(): return lax.dynamic_index_in_dim(array, bit, axis, keepdims=False)]
  transfers between devices with their start and end apart: 130 -> 118, of which waited for: 54 -> 32; matrix products, arithmetic and copies ran while one was open for 35% -> 44% of each run, Pallas kernels for 11% -> 25%
where the time goes in v2:
time: 1140 us; the launch traced here: 1120 us
  other arithmetic  282 us (25%)
  Pallas kernels  279 us (24%)
  local copies, waits for them, and re-layouts  230 us (20%)
  waiting for transfers between devices  145 us (13%)
  starting transfers between devices  124 us (11%)
  matrix products  53.6 us (5%)
    pallas_call x6, Pallas kernels, feed_forward(): pl.pallas_call(body, grid_spec=pltpu.PrefetchScalarGridSpec(num_scalar_pr...  182 us
    ppermute x116, waiting for transfers between devices, swap(): lax.ppermute(x, AXES, [(i, i ^ 1 << bit) for i in range(device_count())])  145 us
    ppermute x116, starting transfers between devices, swap(): lax.ppermute(x, AXES, [(i, i ^ 1 << bit) for i in range(device_count())])  121 us
    pallas_call x10, Pallas kernels, assemble(): pl.pallas_call(functools.partial(assemble_body, steps), grid_spec=pltpu.P...  52.1 us
    concatenate x28, other arithmetic, gather_steps(): held = jnp.concatenate([held, arriving], axis=0)  47.5 us
    convert_element_type x20, other arithmetic, scatter_steps(): sum((at_bit(h, axis, mine).astype(full) for h in held)).astype(sent)  41.8 us
    pallas_call x1, Pallas kernels, attend_back(): pl.pallas_call(attend_back_body, grid=(pairs,), in_specs=[pl.BlockSpec((P...  29 us
    reduce_sum x3, other arithmetic, modulate(): return layer_norm(values) * (1.0 + scale_by) + shift_by  25.7 us
  transfers between devices with their start and end apart: 118, of which 32 were waited for; matrix products, arithmetic and copies ran while one was open for 44% of the time, Pallas kernels for 25%

profile of v2, /device:TPU:0, one launch (start us, length us, event | category | flops | bytes accessed | tf_op | source)
XLA Modules:
  0.0 1116.5 jit_solution(5031231606258325495)
XLA Ops:
  51.8 11.2 %collective-permute-done.3 = bf16[1,96,1152]{2,1,0:T(8,128)(2,1)S(1)} collective-permute-done((bf16[1,96,1152]{2,1,0:T(8,128)(2,1)S(1)}, bf16[1,96,1152]{2,1,0:T(8,128)(2,1)S(1)}, u32[]{:S(2)}, u32[]{:S(2)}) %collective-permute-start.3) | collective-permute-done | bytes 221216 | tf_op jit(solution)/shard_map/ppermute | solution.py:33
  78.8 7.5 collective-permute-done.5
  86.3 7.3 collective-permute-done.6
  110.3 6.5 multiply_add_fusion
  116.9 24.8 %add_convert_fusion = bf16[32,32,1536]{2,1,0:T(8,128)(2,1)} fusion(f32[32,32,1536]{2,1,0:T(8,128)} %multiply_add_fusion, f32[1536]{0:T(1024)S(1)} %reshape.963, f32[1536]{0:T(1024)S(1)} %reshape.962, f32[1536]{0:T(1024)S(1)} %reshape.961, f32[1536]{0:T(1024)S(1)} %reshape.960, f32[1536]{0:T(1024)S(1)} %copy-done.94, f32[1536]{0:T(1024)S(1)} %copy-done.96, ...), kind=kLoop, calls=%fused_computation.9 | loop fusion | flops 28311552 | bytes 9492480 | tf_op jit(solution)/shard_map/convert_element_type | solution.py:680
  141.6 7.3 pad.23
  178.8 7.6 reshape_reshape.57
  211.7 12.7 %convolution_convert_fusion.2.qkv_ref = bf16[1024,2304]{1,0:T(8,128)(2,1)} fusion(bf16[1024,1536]{1,0:T(8,128)(2,1)} %bitcast.645, bf16[1536,1152]{1,0:T(8,128)(2,1)} %bitcast.606, bf16[1536,1152]{1,0:T(8,128)(2,1)} %bitcast.608), kind=kOutput, calls=%fused_computation.12 | convolution fusion | flops 7264272384 | bytes 14942208 | tf_op jit(solution)/shard_map/dot_general | solution.py:691
  224.4 6.5 pad_maximum_fusion
  243.2 15.4 %attend.1 = bf16[1024,768]{1,0:T(8,128)(2,1)} custom-call(f32[256,256]{1,0:T(8,128)} %compare_convert_fusion.mask_ref, bf16[1024,2304]{1,0:T(8,128)(2,1)} %convolution_convert_fusion.2.qkv_ref), custom_call_target="tpu_custom_call" | custom-call | flops 3221225472 | bytes 6291456 | tf_op jit(solution)/shard_map/attend/pallas_call | solution.py:326
  297.5 10.2 collective-permute-done.36
  329.0 8.6 copy.316
  343.8 12.5 %collective-permute-done.39.refs_1_ = bf16[8,96,1024]{2,1,0:T(8,128)(2,1)} collective-permute-done((bf16[8,96,1024]{2,1,0:T(8,128)(2,1)S(1)}, bf16[8,96,1024]{2,1,0:T(8,128)(2,1)}, u32[]{:S(2)}, u32[]{:S(2)}) %collective-permute-start.39) | collective-permute-done | bytes 1572896 | tf_op jit(solution)/shard_map/ppermute | solution.py:33
  382.9 19.2 %feed_forward.6 = (bf16[2,4,128,1536]{3,2,1,0:T(8,128)(2,1)}, bf16[2,4,128,1536]{3,2,1,0:T(8,128)(2,1)}, bf16[1536,1024]{1,0:T(8,128)(2,1)}, bf16[1024,1536]{1,0:T(8,128)(2,1)}, f32[16,1024]{1,0:T(8,128)}) custom-call(s32[1]{0:T(128)} %bitcast.48.refs_0_.core_ref, bf16[1024,1536]{1,0:T(8,128)(2,1)} %copy.322.refs_1_.norm_ref, bf16[1536,1024]{1,0:T(8,128)(2,1)} %bitcast.597, ...), custom_call_target="tpu_custom_call" | custom-call | flops 4831838208 | bytes 18874368 | tf_op jit(solution)/shard_map/feed_forward/pallas_call | solution.py:539
  414.2 41.3 %feed_forward.7 = (bf16[2,4,128,1536]{3,2,1,0:T(8,128)(2,1)}, bf16[2,4,128,1536]{3,2,1,0:T(8,128)(2,1)}, bf16[1536,1024]{1,0:T(8,128)(2,1)}, bf16[1024,1536]{1,0:T(8,128)(2,1)}, f32[16,1024]{1,0:T(8,128)}) custom-call(s32[1]{0:T(128)} %bitcast.48.refs_0_.core_ref, ...), custom_call_target="tpu_custom_call", output_to_operand_aliasing={{2}: (7, {}), {3}: (8, {}), {4}: (9, {})} | custom-call | flops 14495514624 | bytes 25165824 | tf_op jit(solution)/shard_map/feed_forward/pallas_call | solution.py:539
  472.8 19.2 %feed_forward.8 = (bf16[2,4,128,1536]{3,2,1,0:T(8,128)(2,1)}, bf16[2,4,128,1536]{3,2,1,0:T(8,128)(2,1)}, bf16[1536,1024]{1,0:T(8,128)(2,1)}, bf16[1024,1536]{1,0:T(8,128)(2,1)}, f32[16,1024]{1,0:T(8,128)}) custom-call(s32[1]{0:T(128)} %bitcast.48.refs_0_.core_ref, bf16[1024,1536]{1,0:T(8,128)(2,1)} %copy.322.refs_1_.norm_ref, bf16[1536,1024]{1,0:T(8,128)(2,1)} %bitcast.599, ...), custom_call_target="tpu_custom_call" | custom-call | flops 4831838208 | bytes 18874368 | tf_op jit(solution)/shard_map/feed_forward/pallas_call | solution.py:539
  504.0 41.7 %feed_forward.9 = (bf16[2,4,128,1536]{3,2,1,0:T(8,128)(2,1)}, bf16[2,4,128,1536]{3,2,1,0:T(8,128)(2,1)}, bf16[1536,1024]{1,0:T(8,128)(2,1)}, bf16[1024,1536]{1,0:T(8,128)(2,1)}, f32[16,1024]{1,0:T(8,128)}) custom-call(s32[1]{0:T(128)} %bitcast.48.refs_0_.core_ref, ...), custom_call_target="tpu_custom_call", output_to_operand_aliasing={{2}: (7, {}), {3}: (8, {}), {4}: (9, {})} | custom-call | flops 14495514624 | bytes 25165824 | tf_op jit(solution)/shard_map/feed_forward/pallas_call | solution.py:539
  556.5 41.4 %feed_forward.10 = (bf16[2,4,128,1536]{3,2,1,0:T(8,128)(2,1)}, bf16[2,4,128,1536]{3,2,1,0:T(8,128)(2,1)}, bf16[1536,1024]{1,0:T(8,128)(2,1)}, bf16[1024,1536]{1,0:T(8,128)(2,1)}, f32[16,1024]{1,0:T(8,128)}) custom-call(s32[1]{0:T(128)} %bitcast.48.refs_0_.core_ref, bf16[1024,1536]{1,0:T(8,128)(2,1)} %copy.322.refs_1_.norm_ref, bf16[1536,1024]{1,0:T(8,128)(2,1)} %bitcast.601, ...), custom_call_target="tpu_custom_call" | custom-call | flops 14495514624 | bytes 25165824 | tf_op jit(solution)/shard_map/feed_forward/pallas_call | solution.py:539
  606.0 19.3 %feed_forward.11 = (bf16[2,4,128,1536]{3,2,1,0:T(8,128)(2,1)}, bf16[2,4,128,1536]{3,2,1,0:T(8,128)(2,1)}, bf16[1536,1024]{1,0:T(8,128)(2,1)}, bf16[1024,1536]{1,0:T(8,128)(2,1)}, f32[16,1024]{1,0:T(8,128)}) custom-call(s32[1]{0:T(128)} %bitcast.48.refs_0_.core_ref, ...), custom_call_target="tpu_custom_call", output_to_operand_aliasing={{2}: (7, {}), {3}: (8, {}), {4}: (9, {})} | custom-call | flops 4831838208 | bytes 18874368 | tf_op jit(solution)/shard_map/feed_forward/pallas_call | solution.py:539
  667.6 14.6 %add_add_fusion = f32[2,4,128,1536]{3,2,1,0:T(8,128)S(1)} fusion(bf16[2,4,128,1536]{3,2,1,0:T(8,128)(2,1)} %collective-permute-done.70, bf16[2,4,128,1536]{3,2,1,0:T(8,128)(2,1)} %get-tuple-element.486, bf16[2,4,128,1536]{3,2,1,0:T(8,128)(2,1)} %collective-permute-done.69, bf16[2,4,128,1536]{3,2,1,0:T(8,128)(2,1)} %get-tuple-element.484, ...), kind=kLoop, calls=%fused_computation.8 | loop fusion | flops 36175872 | bytes 44040192 | tf_op jit(solution)/shard_map/add | solution.py:766
  772.3 29.0 %attend_back.1 = bf16[1024,2304]{1,0:T(8,128)(2,1)} custom-call(f32[256,256]{1,0:T(8,128)} %compare_convert_fusion.mask_ref, bf16[1024,2304]{1,0:T(8,128)(2,1)} %convolution_convert_fusion.2.qkv_ref, bf16[1024,768]{1,0:T(8,128)(2,1)} %convolution_convert_fusion.5.grad_ref), custom_call_target="tpu_custom_call" | custom-call | flops 8053063680 | bytes 11010048 | tf_op jit(solution)/shard_map/attend_back/pallas_call | solution.py:347
  826.5 11.7 %convolution_convert_fusion = bf16[1536,2304]{1,0:T(8,128)(2,1)} fusion(bf16[1024,1536]{1,0:T(8,128)(2,1)S(1)} %bitcast.646, bf16[1024,2304]{1,0:T(8,128)(2,1)} %attend_back.1), kind=kOutput, calls=%fused_computation | convolution fusion | flops 7251296256 | bytes 14942208 | tf_op jit(solution)/shard_map/dot_general | solution.py:802
  838.3 9.7 fusion.173
  847.9 10.4 copy.431
  858.4 8.4 reshape_reshape.75
  871.6 6.5 fusion.170
  896.3 6.8 collective-permute-done.86
  903.1 7.4 collective-permute-done.87
  910.5 16.0 %collective-permute-done.84 = bf16[2,2,2,96,1152]{4,3,1,0,2:T(8,128)(2,1)S(1)} collective-permute-done((bf16[2,2,2,96,1152]{4,3,1,0,2:T(8,128)(2,1)S(1)}, bf16[2,2,2,96,1152]{4,3,1,0,2:T(8,128)(2,1)S(1)}, u32[]{:S(2)}, u32[]{:S(2)}) %collective-permute-start.84) | collective-permute-done | bytes 1769504 | tf_op jit(solution)/shard_map/ppermute | solution.py:33
  949.3 19.4 %multiply_reduce_fusion.1 = (f32[1536]{0:T(1024)}, f32[16,32]{1,0:T(8,128)S(1)}, f32[1536]{0:T(1024)}) fusion(f32[16,32,1536]{2,1,0:T(8,128)} %bitcast.625, f32[16,32]{1,0:T(8,128)} %div.121, f32[16,32]{1,0:T(8,128)S(1)} %get-tuple-element.712, f32[16,32]{1,0:T(8,128)S(1)} %get-tuple-element.711, f32[1536]{0:T(1024)S(1)} %copy-done.82, f32[1536]{0:T(1024)} %reshape.955, ...), kind=kLoop, calls=%fused_computation.82 | loop fusion | flops 22016512 | bytes 16226304 | tf_op jit(solution)/shard_map/transpose(jvp())/reduce_sum | solution.py:223
  975.1 14.7 %fusion.26 = (f32[1536]{0:T(1024)S(1)}, f32[1536]{0:T(1024)S(1)}, f32[1536]{0:T(1024)S(1)}, f32[1536]{0:T(1024)S(1)}, f32[1536]{0:T(1024)S(1)}, /*index=5*/f32[1...) fusion(f32[34,34,1536]{2,1,0:T(8,128)} %pad.23, s32[]{:T(128)S(6)} %add.1182, s32[]{:T(128)S(6)} %add.1176, ...), kind=kLoop, calls=%fused_computation.54 | loop fusion | flops 14141952 | bytes 31512596 | tf_op jit(solution)/shard_map/reduce_sum | solution.py:247
  1011.7 12.4 %collective-permute-done.94 = bf16[1,9216]{1,0:T(2,128)(2,1)S(1)} collective-permute-done((bf16[1,9216]{1,0:T(2,128)(2,1)S(1)}, bf16[1,9216]{1,0:T(2,128)(2,1)S(1)}, u32[]{:S(2)}, u32[]{:S(2)}) %collective-permute-start.94) | collective-permute-done | bytes 18464 | tf_op jit(solution)/shard_map/ppermute | solution.py:33
  (805 shorter events, 626.0 us)
Async XLA Ops:
  6.1 70.8 %collective-permute-start.1 = (bf16[48,1536]{1,0:T(8,128)(2,1)}, bf16[48,1536]{1,0:T(8,128)(2,1)}, u32[]{:S(2)}, u32[]{:S(2)}) collective-permute-start(bf16[48,1536]{1,0:T(8,128)(2,1)} %param.22), channel_id=1, source_target_pairs={{0,0},{1,2},{2,4},{3,6},{4,8},{5,10},{6,12},{7,14},{8,16},{9,18},{... | collective-permute-start | bytes 442376 | tf_op jit(solution)/shard_map/ppermute | solution.py:626
  9.0 91.8 %collective-permute-start.11 = (bf16[512,1536]{1,0:T(8,128)(2,1)S(1)}, bf16[512,1536]{1,0:T(8,128)(2,1)}, u32[]{:S(2)}, u32[]{:S(2)}) collective-permute-start(bf16[512,1536]{1,0:T(8,128)(2,1)S(1)} %bitcast.596), channel_id=1, source_target_pairs={{0,1},{1,0},{2,3},{3,2},{4,5},{5,4},{6,7},{7,6},{8,9},{9,8},{10,11... | collective-permute-start | bytes 4718600 | tf_op jit(solution)/shard_map/ppermute | solution.py:33
  95.7 53.3 %collective-permute-start.7 = (bf16[4,96,1152]{2,1,0:T(8,128)(2,1)}, bf16[4,96,1152]{2,1,0:T(8,128)(2,1)}, u32[]{:S(2)}, u32[]{:S(2)}) collective-permute-start(bf16[4,96,1152]{2,1,0:T(8,128)(2,1)} %pad_maximum_fusion.14), channel_id=1, source_target_pairs={{0,4},{1,5},{2,6},{3,7},{4,0},{5,1},{6,2},{7,3},{8,12},{9,13},{10,... | collective-permute-start | bytes 2654216 | tf_op jit(solution)/shard_map/ppermute | solution.py:33
  96.0 53.0 %collective-permute-start.8 = (bf16[4,96,1152]{2,1,0:T(8,128)(2,1)}, bf16[4,96,1152]{2,1,0:T(8,128)(2,1)}, u32[]{:S(2)}, u32[]{:S(2)}) collective-permute-start(bf16[4,96,1152]{2,1,0:T(8,128)(2,1)} %pad_maximum_fusion.15), channel_id=1, source_target_pairs={{0,2},{1,3},{2,0},{3,1},{4,6},{5,7},{6,4},{7,5},{8,10},{9,11},{10,... | collective-permute-start | bytes 2654216 | tf_op jit(solution)/shard_map/ppermute | solution.py:33
  97.8 51.2 %collective-permute-start.9 = (bf16[1,48,768]{2,1,0:T(8,128)(2,1)S(1)}, bf16[1,48,768]{2,1,0:T(8,128)(2,1)}, u32[]{:S(2)}, u32[]{:S(2)}) collective-permute-start(bf16[1,48,768]{2,1,0:T(8,128)(2,1)S(1)} %get-tuple-element.312), channel_id=1, source_target_pairs={{0,16},{1,17},{2,18},{3,19},{4,20},{5,21},{6,22},{7,23},{8,24},{9,... | collective-permute-start | bytes 221192 | tf_op jit(solution)/shard_map/ppermute | solution.py:33
  100.1 48.9 %collective-permute-start.10 = (bf16[1,48,768]{2,1,0:T(8,128)(2,1)S(1)}, bf16[1,48,768]{2,1,0:T(8,128)(2,1)}, u32[]{:S(2)}, u32[]{:S(2)}) collective-permute-start(bf16[1,48,768]{2,1,0:T(8,128)(2,1)S(1)} %get-tuple-element.313), channel_id=1, source_target_pairs={{0,16},{1,17},{2,18},{3,19},{4,20},{5,21},{6,22},{7,23},{8,24},{9,... | collective-permute-start | bytes 221192 | tf_op jit(solution)/shard_map/ppermute | solution.py:33
  172.4 111.4 %collective-permute-start.44 = (bf16[4,128,1536]{2,1,0:T(8,128)(2,1)}, bf16[4,128,1536]{2,1,0:T(8,128)(2,1)}, u32[]{:S(2)}, u32[]{:S(2)}) collective-permute-start(bf16[4,128,1536]{2,1,0:T(8,128)(2,1)} %bitcast.39), channel_id=1, source_target_pairs={{0,1},{1,0},{2,3},{3,2},{4,5},{5,4},{6,7},{7,6},{8,9},{9,8},{10,11... | collective-permute-start | bytes 4718600 | tf_op jit(solution)/shard_map/ppermute | solution.py:33
  410.7 44.9 %collective-permute-start.49 = (bf16[8,96,1024]{2,1,0:T(8,128)(2,1)}, bf16[8,96,1024]{2,1,0:T(8,128)(2,1)}, u32[]{:S(2)}, u32[]{:S(2)}) collective-permute-start(bf16[8,96,1024]{2,1,0:T(8,128)(2,1)} %pad_maximum_fusion.9.refs_0_), channel_id=1, source_target_pairs={{0,2},{1,3},{2,0},{3,1},{4,6},{5,7},{6,4},{7,5},{8,10},{9,11},{10,... | collective-permute-start | bytes 4718600 | tf_op jit(solution)/shard_map/ppermute | solution.py:33
  411.0 44.6 %collective-permute-start.50 = (bf16[8,64,1536]{2,1,0:T(8,128)(2,1)}, bf16[8,64,1536]{2,1,0:T(8,128)(2,1)}, u32[]{:S(2)}, u32[]{:S(2)}) collective-permute-start(bf16[8,64,1536]{2,1,0:T(8,128)(2,1)} %pad_maximum_fusion.10.refs_0_), channel_id=1, source_target_pairs={{0,4},{1,5},{2,6},{3,7},{4,0},{5,1},{6,2},{7,3},{8,12},{9,13},{10,... | collective-permute-start | bytes 4718600 | tf_op jit(solution)/shard_map/ppermute | solution.py:33
  412.2 43.3 %collective-permute-start.51 = (bf16[2,96,1024]{2,1,0:T(8,128)(2,1)}, bf16[2,96,1024]{2,1,0:T(8,128)(2,1)}, u32[]{:S(2)}, u32[]{:S(2)}) collective-permute-start(bf16[2,96,1024]{2,1,0:T(8,128)(2,1)} %pad_maximum_fusion.32), channel_id=1, source_target_pairs={{0,8},{1,9},{2,10},{3,11},{4,12},{5,13},{6,14},{7,15},{8,0},{9,1},... | collective-permute-start | bytes 1179656 | tf_op jit(solution)/shard_map/ppermute | solution.py:33
  412.2 43.4 %collective-permute-start.52 = (bf16[2,64,1536]{2,1,0:T(8,128)(2,1)}, bf16[2,64,1536]{2,1,0:T(8,128)(2,1)S(1)}, u32[]{:S(2)}, u32[]{:S(2)}) collective-permute-start(bf16[2,64,1536]{2,1,0:T(8,128)(2,1)} %pad_maximum_fusion.33), channel_id=1, source_target_pairs={{0,8},{1,9},{2,10},{3,11},{4,12},{5,13},{6,14},{7,15},{8,0},{9,1},... | collective-permute-start | bytes 1179656 | tf_op jit(solution)/shard_map/ppermute | solution.py:33
  462.0 163.9 %collective-permute-start.65 = (bf16[2,4,128,1536]{3,2,1,0:T(8,128)(2,1)}, bf16[2,4,128,1536]{3,2,1,0:T(8,128)(2,1)}, u32[]{:S(2)}, u32[]{:S(2)}) collective-permute-start(bf16[2,4,128,1536]{3,2,1,0:T(8,128)(2,1)} %get-tuple-element.477), channel_id=1, source_target_pairs={{0,1},{1,0},{2,3},{3,2},{4,5},{5,4},{6,7},{7,6},{8,9},{9,8},{10,11... | collective-permute-start | bytes 9437192 | tf_op jit(solution)/shard_map/ppermute | solution.py:33
  497.3 48.4 %collective-permute-start.55 = (bf16[8,96,1024]{2,1,0:T(8,128)(2,1)}, bf16[8,96,1024]{2,1,0:T(8,128)(2,1)}, u32[]{:S(2)}, u32[]{:S(2)}) collective-permute-start(bf16[8,96,1024]{2,1,0:T(8,128)(2,1)} %pad_maximum_fusion.11.refs_0_), channel_id=1, source_target_pairs={{0,2},{1,3},{2,0},{3,1},{4,6},{5,7},{6,4},{7,5},{8,10},{9,11},{10,... | collective-permute-start | bytes 4718600 | tf_op jit(solution)/shard_map/ppermute | solution.py:33
  497.6 48.2 %collective-permute-start.56 = (bf16[8,64,1536]{2,1,0:T(8,128)(2,1)}, bf16[8,64,1536]{2,1,0:T(8,128)(2,1)}, u32[]{:S(2)}, u32[]{:S(2)}) collective-permute-start(bf16[8,64,1536]{2,1,0:T(8,128)(2,1)} %pad_maximum_fusion.12.refs_0_), channel_id=1, source_target_pairs={{0,4},{1,5},{2,6},{3,7},{4,0},{5,1},{6,2},{7,3},{8,12},{9,13},{10,... | collective-permute-start | bytes 4718600 | tf_op jit(solution)/shard_map/ppermute | solution.py:33
  501.5 96.5 %collective-permute-start.57 = (bf16[2,2,2,96,1024]{4,3,2,1,0:T(8,128)(2,1)}, bf16[2,2,2,96,1024]{4,3,2,1,0:T(8,128)(2,1)}, u32[]{:S(2)}, u32[]{:S(2)}) collective-permute-start(bf16[2,2,2,96,1024]{4,3,2,1,0:T(8,128)(2,1)} %dynamic-slice_bitcast_fusion.2), channel_id=1, source_target_pairs={{0,2},{1,3},{2,0},{3,1},{4,6},{5,7},{6,4},{7,5},{8,10},{9,11},{10,... | collective-permute-start | bytes 4718600 | tf_op jit(solution)/shard_map/ppermute | solution.py:33
  502.3 95.7 %collective-permute-start.58 = (bf16[2,2,2,64,1536]{4,3,1,0,2:T(8,128)(2,1)}, bf16[2,2,2,64,1536]{4,3,1,0,2:T(8,128)(2,1)}, u32[]{:S(2)}, u32[]{:S(2)}) collective-permute-start(bf16[2,2,2,64,1536]{4,3,1,0,2:T(8,128)(2,1)} %copy_bitcast_fusion.5), channel_id=1, source_target_pairs={{0,4},{1,5},{2,6},{3,7},{4,0},{5,1},{6,2},{7,3},{8,12},{9,13},{10,... | collective-permute-start | bytes 4718600 | tf_op jit(solution)/shard_map/ppermute | solution.py:33
  605.5 57.6 %collective-permute-start.66 = (bf16[2,4,128,1536]{3,2,1,0:T(8,128)(2,1)}, bf16[2,4,128,1536]{3,2,1,0:T(8,128)(2,1)}, u32[]{:S(2)}, u32[]{:S(2)}) collective-permute-start(bf16[2,4,128,1536]{3,2,1,0:T(8,128)(2,1)} %get-tuple-element.479), channel_id=1, source_target_pairs={{0,1},{1,0},{2,3},{3,2},{4,5},{5,4},{6,7},{7,6},{8,9},{9,8},{10,11... | collective-permute-start | bytes 9437192 | tf_op jit(solution)/shard_map/ppermute | solution.py:33
  605.5 57.6 %collective-permute-start.67 = (bf16[2,4,128,1536]{3,2,1,0:T(8,128)(2,1)}, bf16[2,4,128,1536]{3,2,1,0:T(8,128)(2,1)}, u32[]{:S(2)}, u32[]{:S(2)}) collective-permute-start(bf16[2,4,128,1536]{3,2,1,0:T(8,128)(2,1)} %get-tuple-element.481), channel_id=1, source_target_pairs={{0,1},{1,0},{2,3},{3,2},{4,5},{5,4},{6,7},{7,6},{8,9},{9,8},{10,11... | collective-permute-start | bytes 9437192 | tf_op jit(solution)/shard_map/ppermute | solution.py:33
  625.9 41.8 %collective-permute-start.70 = (bf16[2,4,128,1536]{3,2,1,0:T(8,128)(2,1)}, bf16[2,4,128,1536]{3,2,1,0:T(8,128)(2,1)}, u32[]{:S(2)}, u32[]{:S(2)}) collective-permute-start(bf16[2,4,128,1536]{3,2,1,0:T(8,128)(2,1)} %get-tuple-element.487), channel_id=1, source_target_pairs={{0,1},{1,0},{2,3},{3,2},{4,5},{5,4},{6,7},{7,6},{8,9},{9,8},{10,11... | collective-permute-start | bytes 9437192 | tf_op jit(solution)/shard_map/ppermute | solution.py:33
  749.6 57.6 %collective-permute-start.78 = (bf16[2,2,2,96,1024]{4,3,2,1,0:T(8,128)(2,1)}, bf16[2,2,2,96,1024]{4,3,2,1,0:T(8,128)(2,1)}, u32[]{:S(2)}, u32[]{:S(2)}) collective-permute-start(bf16[2,2,2,96,1024]{4,3,2,1,0:T(8,128)(2,1)} %dynamic-slice_bitcast_fusion), channel_id=1, source_target_pairs={{0,2},{1,3},{2,0},{3,1},{4,6},{5,7},{6,4},{7,5},{8,10},{9,11},{10,... | collective-permute-start | bytes 4718600 | tf_op jit(solution)/shard_map/ppermute | solution.py:33
  749.7 57.5 %collective-permute-start.79 = (bf16[2,2,2,64,1536]{4,3,1,0,2:T(8,128)(2,1)}, bf16[2,2,2,64,1536]{4,3,1,0,2:T(8,128)(2,1)}, u32[]{:S(2)}, u32[]{:S(2)}) collective-permute-start(bf16[2,2,2,64,1536]{4,3,1,0,2:T(8,128)(2,1)} %copy_bitcast_fusion.3), channel_id=1, source_target_pairs={{0,4},{1,5},{2,6},{3,7},{4,0},{5,1},{6,2},{7,3},{8,12},{9,13},{10,... | collective-permute-start | bytes 4718600 | tf_op jit(solution)/shard_map/ppermute | solution.py:33
  820.5 51.1 %collective-permute-start.80 = (bf16[96,1024]{0,1:T(8,128)(2,1)}, bf16[96,1024]{0,1:T(8,128)(2,1)}, u32[]{:S(2)}, u32[]{:S(2)}) collective-permute-start(bf16[96,1024]{0,1:T(8,128)(2,1)} %fusion.87), channel_id=1, source_target_pairs={{0,16},{1,17},{2,18},{3,19},{4,20},{5,21},{6,22},{7,23},{8,24},{9,... | collective-permute-start | bytes 589832 | tf_op jit(solution)/shard_map/ppermute | solution.py:33
  821.2 50.3 %collective-permute-start.81 = (bf16[64,1536]{1,0:T(8,128)(2,1)}, bf16[64,1536]{1,0:T(8,128)(2,1)}, u32[]{:S(2)}, u32[]{:S(2)}) collective-permute-start(bf16[64,1536]{1,0:T(8,128)(2,1)} %fusion.101), channel_id=1, source_target_pairs={{0,16},{1,17},{2,18},{3,19},{4,20},{5,21},{6,22},{7,23},{8,24},{9,... | collective-permute-start | bytes 589832 | tf_op jit(solution)/shard_map/ppermute | solution.py:33
  823.5 48.1 %collective-permute-start.82 = (bf16[2,2,96,1024]{3,2,1,0:T(8,128)(2,1)}, bf16[2,2,96,1024]{3,2,1,0:T(8,128)(2,1)}, u32[]{:S(2)}, u32[]{:S(2)}) collective-permute-start(bf16[2,2,96,1024]{3,2,1,0:T(8,128)(2,1)} %fusion.46), channel_id=1, source_target_pairs={{0,4},{1,5},{2,6},{3,7},{4,0},{5,1},{6,2},{7,3},{8,12},{9,13},{10,... | collective-permute-start | bytes 2359304 | tf_op jit(solution)/shard_map/ppermute | solution.py:33
  824.6 47.0 %collective-permute-start.83 = (bf16[2,2,64,1536]{3,2,1,0:T(8,128)(2,1)}, bf16[2,2,64,1536]{3,2,1,0:T(8,128)(2,1)}, u32[]{:S(2)}, u32[]{:S(2)}) collective-permute-start(bf16[2,2,64,1536]{3,2,1,0:T(8,128)(2,1)} %get-tuple-element.520), channel_id=1, source_target_pairs={{0,2},{1,3},{2,0},{3,1},{4,6},{5,7},{6,4},{7,5},{8,10},{9,11},{10,... | collective-permute-start | bytes 2359304 | tf_op jit(solution)/shard_map/ppermute | solution.py:33
  931.1 58.9 %collective-permute-start.89 = (bf16[2,2,96,1152]{3,2,1,0:T(8,128)(2,1)}, bf16[2,2,96,1152]{3,2,1,0:T(8,128)(2,1)}, u32[]{:S(2)}, u32[]{:S(2)}) collective-permute-start(bf16[2,2,96,1152]{3,2,1,0:T(8,128)(2,1)} %get-tuple-element.534), channel_id=1, source_target_pairs={{0,4},{1,5},{2,6},{3,7},{4,0},{5,1},{6,2},{7,3},{8,12},{9,13},{10,... | collective-permute-start | bytes 2654216 | tf_op jit(solution)/shard_map/ppermute | solution.py:33
  931.8 58.3 %collective-permute-start.90 = (bf16[2,2,96,1152]{3,2,1,0:T(8,128)(2,1)}, bf16[2,2,96,1152]{3,2,1,0:T(8,128)(2,1)}, u32[]{:S(2)}, u32[]{:S(2)}) collective-permute-start(bf16[2,2,96,1152]{3,2,1,0:T(8,128)(2,1)} %get-tuple-element.535), channel_id=1, source_target_pairs={{0,2},{1,3},{2,0},{3,1},{4,6},{5,7},{6,4},{7,5},{8,10},{9,11},{10,... | collective-permute-start | bytes 2654216 | tf_op jit(solution)/shard_map/ppermute | solution.py:33
  933.1 57.0 %collective-permute-start.91 = (bf16[96,1024]{0,1:T(8,128)(2,1)}, bf16[96,1024]{0,1:T(8,128)(2,1)}, u32[]{:S(2)}, u32[]{:S(2)}) collective-permute-start(bf16[96,1024]{0,1:T(8,128)(2,1)} %fusion.88), channel_id=1, source_target_pairs={{0,16},{1,17},{2,18},{3,19},{4,20},{5,21},{6,22},{7,23},{8,24},{9,... | collective-permute-start | bytes 589832 | tf_op jit(solution)/shard_map/ppermute | solution.py:33
  933.8 56.3 %collective-permute-start.92 = (bf16[64,1536]{1,0:T(8,128)(2,1)}, bf16[64,1536]{1,0:T(8,128)(2,1)S(1)}, u32[]{:S(2)}, u32[]{:S(2)}) collective-permute-start(bf16[64,1536]{1,0:T(8,128)(2,1)} %fusion.102), channel_id=1, source_target_pairs={{0,16},{1,17},{2,18},{3,19},{4,20},{5,21},{6,22},{7,23},{8,24},{9,... | collective-permute-start | bytes 589832 | tf_op jit(solution)/shard_map/ppermute | solution.py:33
  1003.7 55.4 %collective-permute-start.103 = (bf16[2,96,1152]{2,1,0:T(8,128)(2,1)}, bf16[2,96,1152]{2,1,0:T(8,128)(2,1)}, u32[]{:S(2)}, u32[]{:S(2)}) collective-permute-start(bf16[2,96,1152]{2,1,0:T(8,128)(2,1)} %get-tuple-element.555), channel_id=1, source_target_pairs={{0,8},{1,9},{2,10},{3,11},{4,12},{5,13},{6,14},{7,15},{8,0},{9,1},... | collective-permute-start | bytes 1327112 | tf_op jit(solution)/shard_map/ppermute | solution.py:33
  1003.7 55.4 %collective-permute-start.104 = (bf16[2,96,1152]{2,1,0:T(8,128)(2,1)}, bf16[2,96,1152]{2,1,0:T(8,128)(2,1)}, u32[]{:S(2)}, u32[]{:S(2)}) collective-permute-start(bf16[2,96,1152]{2,1,0:T(8,128)(2,1)} %get-tuple-element.556), channel_id=1, source_target_pairs={{0,8},{1,9},{2,10},{3,11},{4,12},{5,13},{6,14},{7,15},{8,0},{9,1},... | collective-permute-start | bytes 1327112 | tf_op jit(solution)/shard_map/ppermute | solution.py:33
  1005.7 53.4 %collective-permute-start.105 = (bf16[2,2,2,48,768]{4,3,1,0,2:T(8,128)(2,1)}, bf16[2,2,2,48,768]{4,3,1,0,2:T(8,128)(2,1)}, u32[]{:S(2)}, u32[]{:S(2)}) collective-permute-start(bf16[2,2,2,48,768]{4,3,1,0,2:T(8,128)(2,1)} %copy_bitcast_fusion.7), channel_id=1, source_target_pairs={{0,2},{1,3},{2,0},{3,1},{4,6},{5,7},{6,4},{7,5},{8,10},{9,11},{10,... | collective-permute-start | bytes 1769480 | tf_op jit(solution)/shard_map/ppermute | solution.py:33
  (219 other events, 3556.3 us)

commit v3 on v2

--- a/solution.py
+++ b/solution.py
@@ -228,24 +228,6 @@
     frequency = jnp.exp(-math.log(10000.0) * jnp.arange(halfway, dtype=jnp.float32) / halfway)
     angles = steps_in.astype(jnp.float32)[..., None] * frequency
     return jnp.concatenate([jnp.cos(angles), jnp.sin(angles)], axis=-1)
-
-
-def depthwise(framed, kernel):
-    row_count = framed.shape[0] - 2
-    result = jnp.zeros((row_count, SIDE, framed.shape[2]), jnp.float32)
-    for tap in range(9):
-        r, s = divmod(tap, 3)
-        result = result + framed[r : r + row_count, s : s + SIDE] * kernel[tap].astype(full)
-    return result
-
-
-def kernel_grad(framed, upstream):
-    row_count = upstream.shape[0]
-    sums = []
-    for tap in range(9):
-        r, s = divmod(tap, 3)
-        sums.append(jnp.sum(framed[r : r + row_count, s : s + SIDE] * upstream, axis=(0, 1)))
-    return jnp.stack(sums)
 
 
 def softmax_of(query, key, allowed):
@@ -579,6 +561,258 @@
     )(core[None].astype(jnp.int32), norm, norm_t, grad, up, down, kernel, *held)
 
 
+def token_stats(x_ref, average, scale):
+    @pl.loop(0, x_ref.shape[0] // STRIP)
+    def _(strip):
+        rows = pl.ds(pl.multiple_of(strip * STRIP, STRIP), STRIP)
+        values = x_ref[rows, :].astype(full)
+        mean = jnp.mean(values, axis=-1, keepdims=True)
+        centred = values - mean
+        variance = jnp.mean(centred * centred, axis=-1, keepdims=True)
+        average[rows, :] = jnp.broadcast_to(mean, (STRIP, 128))
+        scale[rows, :] = jnp.broadcast_to(lax.rsqrt(variance + ln_epsilon), (STRIP, 128))
+
+
+def normed_strip(x_ref, average, scale, rows, columns):
+    width = columns.size
+    wide = lambda ref: jnp.concatenate([ref[rows, :]] * (width // 128), axis=1)
+    return (x_ref[rows, columns].astype(full) - wide(average)) * wide(scale)
+
+
+def frame_zeros(refs):
+    for ref in refs:
+        blank = jnp.zeros((STRIP, ref.shape[-1]), full)
+        for plane in range(4):
+            ref[plane, pl.ds(0, STRIP), :] = blank
+            ref[plane, pl.ds(ref.shape[1] - STRIP, STRIP), :] = blank
+
+
+def conv_in_body(x_ref, kernel_ref, mods_ref, out_ref, average, scale, normed):
+    step = pl.program_id(0)
+    width = out_ref.shape[1]
+    columns = pl.ds(pl.multiple_of(step * width, width), width)
+
+    @pl.when(step == 0)
+    def _():
+        token_stats(x_ref, average, scale)
+        frame_zeros([normed])
+
+    shift_by = mods_ref[0:1, :]
+    scale_by = 1.0 + mods_ref[1:2, :]
+
+    @pl.loop(0, HALF_SIDE)
+    def _(row):
+        for plane in range(4):
+            rows = pl.ds(pl.multiple_of(plane * PLANE + row * STRIP, STRIP), STRIP)
+            normed[plane, pl.ds(pl.multiple_of((row + 1) * STRIP, STRIP), STRIP), :] = (
+                normed_strip(x_ref, average, scale, rows, columns) * scale_by + shift_by
+            )
+
+    kernel = kernel_ref[...]
+
+    @pl.loop(0, HALF_SIDE)
+    def _(row):
+        near = near_strips(normed, row)
+        for row_phase in range(2):
+            for column_phase in range(2):
+                plane = 2 * row_phase + column_phase
+                at = pl.ds(pl.multiple_of(plane * PLANE + row * STRIP, STRIP), STRIP)
+                out_ref[at, :] = conv_strip(near, kernel, row_phase, column_phase).astype(low)
+
+
+def conv_in(canvas, kernel, mods):
+    tokens, model = canvas.shape
+    return pl.pallas_call(
+        conv_in_body,
+        grid=(model // TILE,),
+        in_specs=[
+            pl.BlockSpec((tokens, model), lambda j: (0, 0), pipeline_mode=pl.Buffered(1)),
+            pl.BlockSpec((16, TILE), lambda j: (0, j)),
+            pl.BlockSpec((8, TILE), lambda j: (0, j)),
+        ],
+        out_specs=pl.BlockSpec((tokens, TILE), lambda j: (0, j)),
+        out_shape=jax.ShapeDtypeStruct((tokens, model), low),
+        scratch_shapes=[
+            pltpu.VMEM((tokens, 128), full),
+            pltpu.VMEM((tokens, 128), full),
+            pltpu.VMEM((4, PADDED, TILE), full),
+        ],
+        cost_estimate=pl.CostEstimate(
+            flops=30 * tokens * model, bytes_accessed=4 * tokens * model, transcendentals=tokens
+        ),
+        name="conv_in",
+    )(canvas, kernel, mods)
+
+
+def conv_back_body(
+    core_ref,
+    x_ref,
+    kept_ref,
+    arriving_ref,
+    kernel_ref,
+    mods_ref,
+    middle_ref,
+    out_ref,
+    kernel_grad_ref,
+    mods_grad_ref,
+    average,
+    scale,
+    normed,
+    upstream,
+    held,
+    sum_plain,
+    sum_normed,
+):
+    step = pl.program_id(0)
+    core = core_ref[0]
+    width = kept_ref.shape[1]
+    near_rows = x_ref.shape[0] // 4 // STRIP
+    own_rows = near_rows - 1
+    columns = pl.ds(pl.multiple_of(step * width, width), width)
+
+    def near_at(plane, row):
+        return pl.ds(pl.multiple_of((plane * near_rows + row) * STRIP, STRIP), STRIP)
+
+    def own_at(plane, row):
+        return pl.ds(pl.multiple_of((plane * own_rows + row) * STRIP, STRIP), STRIP)
+
+    @pl.when(step == 0)
+    def _():
+        token_stats(x_ref, average, scale)
+        frame_zeros([normed, upstream])
+        sum_plain[...] = jnp.zeros_like(sum_plain)
+        sum_normed[...] = jnp.zeros_like(sum_normed)
+
+    shift_by = mods_ref[0:1, :]
+    scale_by = 1.0 + mods_ref[1:2, :]
+
+    @pl.loop(0, near_rows)
+    def _(row):
+        for plane in range(4):
+            rows = near_at(plane, row)
+            padded = pl.ds(pl.multiple_of((row + 1) * STRIP, STRIP), STRIP)
+            normed[plane, padded, :] = (
+                normed_strip(x_ref, average, scale, rows, columns) * scale_by + shift_by
+            )
+            upstream[plane, padded, :] = kept_ref[rows, :].astype(full) + arriving_ref[
+                rows, :
+            ].astype(full)
+
+    kernel = kernel_ref[...]
+    flipped = jnp.concatenate([kernel[8 - t : 9 - t, :] for t in range(9)], axis=0)
+
+    def kernel_strip(row, sums):
+        near = near_strips(normed, row + core)
+        sums = list(sums)
+        for row_phase in range(2):
+            for column_phase in range(2):
+                grad_here = strip_at(upstream, row_phase, column_phase, row + core)
+                for i in range(3):
+                    for j in range(3):
+                        product = near[row_phase][i][column_phase][j] * grad_here
+                        sums[3 * i + j] = sums[3 * i + j] + (product[:8] + product[8:])
+        return tuple(sums)
+
+    def fold(sums, rows):
+        return jnp.concatenate(
+            [jnp.sum(s, axis=0, keepdims=True) for s in sums]
+            + [jnp.zeros((rows - len(sums), width), full)],
+            axis=0,
+        )
+
+    blank = jnp.zeros((8, width), full)
+    kernel_grad_ref[...] = fold(lax.fori_loop(0, own_rows, kernel_strip, (blank,) * 9), 16)
+
+    def input_strip(row, sums):
+        near = near_strips(upstream, row + core)
+        shift_sum, scale_sum = sums
+        for row_phase in range(2):
+            for column_phase in range(2):
+                plane = 2 * row_phase + column_phase
+                grad = conv_strip(near, flipped, row_phase, column_phase)
+                plain = normed_strip(x_ref, average, scale, near_at(plane, row + core), columns)
+                shift_sum = shift_sum + (grad[:8] + grad[8:])
+                product = grad * plain
+                scale_sum = scale_sum + (product[:8] + product[8:])
+                scaled = grad * scale_by
+                rows = own_at(plane, row)
+                held[step, rows, :] = scaled
+                product = scaled * plain
+                sum_plain[rows, :] += sum(scaled[:, k : k + 128] for k in range(0, width, 128))
+                sum_normed[rows, :] += sum(product[:, k : k + 128] for k in range(0, width, 128))
+        return shift_sum, scale_sum
+
+    mods_grad_ref[...] = fold(lax.fori_loop(0, own_rows, input_strip, (blank,) * 2), 8)
+
+    @pl.when(step == pl.num_programs(0) - 1)
+    def _():
+        model = x_ref.shape[1]
+
+        @pl.loop(0, own_rows)
+        def _(row):
+            for plane in range(4):
+                rows = own_at(plane, row)
+                near = near_at(plane, row + core)
+                mean_plain = jnp.sum(sum_plain[rows, :], axis=-1, keepdims=True) / model
+                mean_normed = jnp.sum(sum_normed[rows, :], axis=-1, keepdims=True) / model
+                for block in range(model // width):
+                    at = pl.ds(block * width, width)
+                    plain = normed_strip(x_ref, average, scale, near, at)
+                    spread = jnp.concatenate([scale[near, :]] * (width // 128), axis=1)
+                    out_ref[rows, at] = middle_ref[rows, at] + spread * (
+                        held[block, rows, :] - mean_plain - plain * mean_normed
+                    )
+
+
+def conv_back(core, x_near, kept, arriving, kernel, mods, grad_middle):
+    near_tokens, model = x_near.shape
+    own_tokens = grad_middle.shape[0]
+    once = pl.Buffered(1)
+    whole = lambda j, words: (0, 0)
+    across = lambda j, words: (0, j)
+    padded = near_tokens // 4 + 2 * STRIP
+    return pl.pallas_call(
+        conv_back_body,
+        grid_spec=pltpu.PrefetchScalarGridSpec(
+            num_scalar_prefetch=1,
+            grid=(model // TILE,),
+            in_specs=[
+                pl.BlockSpec((near_tokens, model), whole, pipeline_mode=once),
+                pl.BlockSpec((near_tokens, TILE), across),
+                pl.BlockSpec((near_tokens, TILE), across),
+                pl.BlockSpec((16, TILE), across),
+                pl.BlockSpec((8, TILE), across),
+                pl.BlockSpec((own_tokens, model), whole, pipeline_mode=once),
+            ],
+            out_specs=[
+                pl.BlockSpec((own_tokens, model), whole),
+                pl.BlockSpec((16, TILE), across),
+                pl.BlockSpec((8, TILE), across),
+            ],
+            scratch_shapes=[
+                pltpu.VMEM((near_tokens, 128), full),
+                pltpu.VMEM((near_tokens, 128), full),
+                pltpu.VMEM((4, padded, TILE), full),
+                pltpu.VMEM((4, padded, TILE), full),
+                pltpu.VMEM((model // TILE, own_tokens, TILE), full),
+                pltpu.VMEM((own_tokens, 128), full),
+                pltpu.VMEM((own_tokens, 128), full),
+            ],
+        ),
+        out_shape=[
+            jax.ShapeDtypeStruct((own_tokens, model), full),
+            jax.ShapeDtypeStruct((16, model), full),
+            jax.ShapeDtypeStruct((8, model), full),
+        ],
+        cost_estimate=pl.CostEstimate(
+            flops=70 * own_tokens * model,
+            bytes_accessed=14 * own_tokens * model,
+            transcendentals=near_tokens,
+        ),
+        name="conv_back",
+    )(core[None].astype(jnp.int32), x_near, kept, arriving, kernel, mods, grad_middle)
+
+
 def on_device(
     tokens,
     seg_ids,
@@ -624,8 +858,8 @@
     proj_there = [(r, r % chips * 2 + r // chips) for r in range(devices)]
     proj_back = [(b, a) for a, b in proj_there]
     proj_rows = lax.ppermute(proj_weight, AXES, proj_there)
-    mine = tokens[0]
-    canvas = jnp.concatenate(in_core_order(mine, swap_core(mine), core), axis=0)
+    mine = to_phases(tokens[0], half_rows)
+    canvas = join_halves(mine, swap_core(mine), core)
     grad_mine = to_phases(cotangent[0], half_rows)
     grad_ph = join_halves(grad_mine, swap_core(grad_mine), core)
 
@@ -648,7 +882,8 @@
     ffn_taps = ffn_taps.transpose(2, 1, 0, 3).reshape(CHUNKS, 9, chips * piece).astype(full)
     ffn_taps = jnp.pad(ffn_taps, ((0, 0), (0, 7), (0, 0)))
     attn_taps = taps[:, 9 * share : tap_count].reshape(devices, 9, part)
-    attn_taps = attn_taps.transpose(1, 0, 2).reshape(9, model)
+    attn_taps = attn_taps.transpose(1, 0, 2).reshape(9, model).astype(full)
+    attn_taps = jnp.pad(attn_taps, ((0, 7), (0, 0)))
 
     spot = jnp.arange(PLANE)
     quadrant = 2 * (spot // (PLANE // 2)) + spot % HALF_SIDE // (HALF_SIDE // 2)
@@ -674,15 +909,9 @@
     slot(qkv_flows)
     slot(qkv_flows)
 
-    def prepare():
-        normed = modulate(canvas.astype(full), shift_a, scale_a).reshape(SIDE, SIDE, model)
-        normed = jnp.pad(normed, ((1, 1), (1, 1), (0, 0)))
-        return normed, depthwise(normed, attn_taps).astype(low)
-
-    normed_pad, convolved = slot(qkv_flows + proj_flows, prepare)
-    convolved = slot(
-        qkv_flows + proj_flows, lambda: to_phases(convolved.reshape(SIDE * SIDE, model), SIDE)
-    ).reshape(SIDE * SIDE, model)
+    mods_a = jnp.concatenate([shift_a[None], scale_a[None], jnp.zeros((6, model), full)], axis=0)
+    convolved = slot(qkv_flows + proj_flows, lambda: conv_in(canvas, attn_taps, mods_a))
+    slot(qkv_flows + proj_flows)
 
     def project_in():
         weight = jnp.concatenate(
@@ -704,7 +933,7 @@
         ).astype(full)
         return weight, branch
 
-    source_ph = to_phases(mine, half_rows).astype(full)
+    source_ph = mine.astype(full)
     slot.finish(proj_flows)
     proj_full, branch_a = slot(feed_flows[0] + feed_flows[1], project_out)
 
@@ -805,29 +1034,25 @@
     qkv_flows = [sums(qkv_grad[..., :qkv_half], 0), sums(qkv_grad[..., qkv_half:], 1)]
 
     def rows_near(array, which):
-        return lax.dynamic_slice_in_dim(array, which * half_rows, half_rows + 2, axis=0)
+        size = PLANE // 2 + STRIP
+        near = lax.dynamic_slice_in_dim(
+            array.reshape(4, PLANE, model), which * (PLANE - size), size, axis=1
+        )
+        return near.reshape(4 * size, model)
 
     def leave_attend():
-        grad_conv_part = jnp.dot(grad_qkv, qkv_full.T, preferred_element_type=full)
-        grad_conv_part = from_phases(grad_conv_part.reshape(4, PLANE, model), SIDE)
-        grad_conv_part = jnp.pad(
-            grad_conv_part.reshape(SIDE, SIDE, model), ((1, 1), (0, 0), (0, 0))
+        part_here = jnp.dot(grad_qkv, qkv_full.T, preferred_element_type=full).astype(low)
+        return rows_near(part_here, core), swap_core(rows_near(part_here, 1 - core))
+
+    grad_conv = slot(qkv_flows + back_flows[2], leave_attend)
+
+    def leave_block():
+        input_grad, attn_tap_grad, mods_grad = conv_back(
+            core, rows_near(canvas, core), *grad_conv, attn_taps, mods_a,
+            grad_middle.reshape(half_tokens, model),
         )
-        return rows_near(grad_conv_part, core) + swap_core(
-            rows_near(grad_conv_part, 1 - core).astype(low)
-        ).astype(full)
-
-    grad_conv = slot(qkv_flows + back_flows[2], leave_attend)
-
-    def leave_block():
-        attn_tap_grad = kernel_grad(rows_near(normed_pad, core), grad_conv[1:-1])
-        grad_normed_a = depthwise(
-            jnp.pad(grad_conv, ((0, 0), (1, 1), (0, 0))), attn_taps[::-1]
-        ).reshape(half_tokens, model)
-        _, norm_pull_a = jax.vjp(modulate, mine.astype(full), shift_a, scale_a)
-        grad_source, grad_shift_a, grad_scale_a = norm_pull_a(grad_normed_a)
-        input_grad = grad_source + from_phases(grad_middle, half_rows)
-        return attn_tap_grad, input_grad, grad_shift_a, grad_scale_a
+        input_grad = from_phases(input_grad.reshape(4, -1, model), half_rows)
+        return attn_tap_grad[:9], input_grad, mods_grad[0], mods_grad[1]
 
     attn_tap_grad, input_grad, grad_shift_a, grad_scale_a = slot(
         qkv_flows + back_flows[2], leave_block

time: 1140 us -> 1040 us (0.912)
  other arithmetic: 282 us -> 182 us
  local copies, waits for them, and re-layouts: 230 us -> 167 us
  Pallas kernels: 279 us -> 322 us
  waiting for transfers between devices: 145 us -> 183 us
    pallas_call x0 -> x2, Pallas kernels: none -> 43.8 us  [the longest x1 22.9 us: conv_in(): pl.pallas_call(conv_in_body, grid=(model // TILE,), in_specs=[pl.BlockSpe...]
    ppermute x116, waiting for transfers between devices: 145 us -> 183 us  [swap(): lax.ppermute(x, AXES, [(i, i ^ 1 << bit) for i in range(device_count())])]
    convert_element_type x4 -> x0, other arithmetic: 32.4 us -> none  [the longest x1 24.8 us: prepare(): return (normed, depthwise(normed, attn_taps).astype(low))]
    reduce_sum x3 -> x2, other arithmetic: 25.7 us -> 4.38 us  [modulate(): return layer_norm(values) * (1.0 + scale_by) + shift_by]
    add x4 -> x0, other arithmetic: 19.5 us -> none  [the longest x1 6.49 us: modulate(): return layer_norm(values) * (1.0 + scale_by) + shift_by]
    another operation x12 -> x0, local copies, waits for them, and re-layouts: 19 us -> none  [the longest x1 10.4 us: from_phases(): split_grid = block_in.reshape(2, 2, row_count // 2, HALF_SIDE, width)]
    reduce_sum x1 -> x0, other arithmetic: 14.7 us -> none  [kernel_grad(): jnp.sum(framed[r:r + row_count, s:s + SIDE] * upstream, axis=(0, 1))]
    convert_element_type x12 -> x3, local copies, waits for them, and re-layouts: 14.6 us -> 0.32 us  [on_device(): attn_taps = attn_taps.transpose(1, 0, 2).reshape(9, model).astype(full)]
  transfers between devices with their start and end apart: 118 -> 118, of which waited for: 32 -> 41; matrix products, arithmetic and copies ran while one was open for 44% -> 32% of each run, Pallas kernels for 25% -> 31%
where the time goes in v3:
time: 1040 us; the launch traced here: 1020 us
  Pallas kernels  322 us (31%)
  waiting for transfers between devices  183 us (18%)
  other arithmetic  182 us (18%)
  local copies, waits for them, and re-layouts  167 us (16%)
  starting transfers between devices  116 us (11%)
  matrix products  52 us (5%)
    ppermute x116, waiting for transfers between devices, swap(): lax.ppermute(x, AXES, [(i, i ^ 1 << bit) for i in range(device_count())])  183 us
    pallas_call x6, Pallas kernels, feed_forward(): pl.pallas_call(body, grid_spec=pltpu.PrefetchScalarGridSpec(num_scalar_pr...  182 us
    ppermute x116, starting transfers between devices, swap(): lax.ppermute(x, AXES, [(i, i ^ 1 << bit) for i in range(device_count())])  112 us
    pallas_call x10, Pallas kernels, assemble(): pl.pallas_call(functools.partial(assemble_body, steps), grid_spec=pltpu.P...  52.1 us
    concatenate x28, other arithmetic, gather_steps(): held = jnp.concatenate([held, arriving], axis=0)  47 us
    convert_element_type x20, other arithmetic, scatter_steps(): sum((at_bit(h, axis, mine).astype(full) for h in held)).astype(sent)  43.4 us
    pallas_call x1, Pallas kernels, attend_back(): pl.pallas_call(attend_back_body, grid=(pairs,), in_specs=[pl.BlockSpec((P...  29 us
    unnamed x247, local copies, waits for them, and re-layouts  25.2 us
  transfers between devices with their start and end apart: 118, of which 41 were waited for; matrix products, arithmetic and copies ran while one was open for 32% of the time, Pallas kernels for 31%

profile of v3, /device:TPU:0, one launch (start us, length us, event | category | flops | bytes accessed | tf_op | source)
XLA Modules:
  0.0 1024.8 jit_solution(16062911941321478408)
XLA Ops:
  49.8 6.0 collective-permute-done.3
  68.3 9.7 collective-permute-done.5
  78.0 9.0 collective-permute-done.6
  97.5 22.9 %conv_in.1 = bf16[1024,1536]{1,0:T(8,128)(2,1)} custom-call(bf16[1024,1536]{1,0:T(8,128)(2,1)} %bitcast.600, f32[16,1536]{1,0:T(8,128)} %pad_convert_fusion.1.kernel_ref, f32[8,1536]{1,0:T(8,128)} %maximum_maximum_fusion.mods_ref), custom_call_target="tpu_custom_call" | custom-call | flops 47185920 | bytes 6291456 | tf_op jit(solution)/shard_map/conv_in/pallas_call | solution.py:625
  149.8 14.9 %collective-permute-done.22.refs_1_ = bf16[8,96,1152]{2,1,0:T(8,128)(2,1)} collective-permute-done((bf16[8,96,1152]{2,1,0:T(8,128)(2,1)}, bf16[8,96,1152]{2,1,0:T(8,128)(2,1)}, u32[]{:S(2)}, u32[]{:S(2)}) %collective-permute-start.22) | collective-permute-done | bytes 1769504 | tf_op jit(solution)/shard_map/ppermute | solution.py:33
  174.1 5.7 assemble.10
  179.8 5.6 assemble.11
  185.4 13.1 %convolution_convert_fusion.2.qkv_ref = bf16[1024,2304]{1,0:T(8,128)(2,1)} fusion(bf16[1024,1536]{1,0:T(8,128)(2,1)} %conv_in.1, bf16[1536,1152]{1,0:T(8,128)(2,1)} %bitcast.604, bf16[1536,1152]{1,0:T(8,128)(2,1)} %bitcast.602), kind=kOutput, calls=%fused_computation.6 | convolution fusion | flops 7264272384 | bytes 14942208 | tf_op jit(solution)/shard_map/dot_general | solution.py:920
  198.5 6.6 pad_maximum_fusion
  216.8 15.4 %attend.1 = bf16[1024,768]{1,0:T(8,128)(2,1)} custom-call(f32[256,256]{1,0:T(8,128)} %compare_convert_fusion.mask_ref, bf16[1024,2304]{1,0:T(8,128)(2,1)} %convolution_convert_fusion.2.qkv_ref), custom_call_target="tpu_custom_call" | custom-call | flops 3221225472 | bytes 6291456 | tf_op jit(solution)/shard_map/attend/pallas_call | solution.py:308
  267.3 7.6 collective-permute-done.36
  299.0 8.7 copy.329
  307.6 6.1 reshape.704
  313.8 13.0 %collective-permute-done.39.refs_1_ = bf16[8,96,1024]{2,1,0:T(8,128)(2,1)} collective-permute-done((bf16[8,96,1024]{2,1,0:T(8,128)(2,1)}, bf16[8,96,1024]{2,1,0:T(8,128)(2,1)}, u32[]{:S(2)}, u32[]{:S(2)}) %collective-permute-start.39) | collective-permute-done | bytes 1572896 | tf_op jit(solution)/shard_map/ppermute | solution.py:33
  352.2 19.2 %feed_forward.6 = (bf16[2,4,128,1536]{3,2,1,0:T(8,128)(2,1)}, bf16[2,4,128,1536]{3,2,1,0:T(8,128)(2,1)}, bf16[1536,1024]{1,0:T(8,128)(2,1)}, bf16[1024,1536]{1,0:T(8,128)(2,1)}, f32[16,1024]{1,0:T(8,128)}) custom-call(s32[1]{0:T(128)} %bitcast.47.refs_0_.core_ref, bf16[1024,1536]{1,0:T(8,128)(2,1)} %copy.335.refs_1_.norm_ref, bf16[1536,1024]{1,0:T(8,128)(2,1)} %bitcast.590, ...), custom_call_target="tpu_custom_call" | custom-call | flops 4831838208 | bytes 18874368 | tf_op jit(solution)/shard_map/feed_forward/pallas_call | solution.py:521
  384.5 41.5 %feed_forward.7 = (bf16[2,4,128,1536]{3,2,1,0:T(8,128)(2,1)}, bf16[2,4,128,1536]{3,2,1,0:T(8,128)(2,1)}, bf16[1536,1024]{1,0:T(8,128)(2,1)}, bf16[1024,1536]{1,0:T(8,128)(2,1)}, f32[16,1024]{1,0:T(8,128)}) custom-call(s32[1]{0:T(128)} %bitcast.47.refs_0_.core_ref, ...), custom_call_target="tpu_custom_call", output_to_operand_aliasing={{2}: (7, {}), {3}: (8, {}), {4}: (9, {})} | custom-call | flops 14495514624 | bytes 25165824 | tf_op jit(solution)/shard_map/feed_forward/pallas_call | solution.py:521
  442.3 19.1 %feed_forward.8 = (bf16[2,4,128,1536]{3,2,1,0:T(8,128)(2,1)}, bf16[2,4,128,1536]{3,2,1,0:T(8,128)(2,1)}, bf16[1536,1024]{1,0:T(8,128)(2,1)}, bf16[1024,1536]{1,0:T(8,128)(2,1)}, f32[16,1024]{1,0:T(8,128)}) custom-call(s32[1]{0:T(128)} %bitcast.47.refs_0_.core_ref, bf16[1024,1536]{1,0:T(8,128)(2,1)} %copy.335.refs_1_.norm_ref, bf16[1536,1024]{1,0:T(8,128)(2,1)} %bitcast.592, ...), custom_call_target="tpu_custom_call" | custom-call | flops 4831838208 | bytes 18874368 | tf_op jit(solution)/shard_map/feed_forward/pallas_call | solution.py:521
  473.3 41.5 %feed_forward.9 = (bf16[2,4,128,1536]{3,2,1,0:T(8,128)(2,1)}, bf16[2,4,128,1536]{3,2,1,0:T(8,128)(2,1)}, bf16[1536,1024]{1,0:T(8,128)(2,1)}, bf16[1024,1536]{1,0:T(8,128)(2,1)}, f32[16,1024]{1,0:T(8,128)}) custom-call(s32[1]{0:T(128)} %bitcast.47.refs_0_.core_ref, ...), custom_call_target="tpu_custom_call", output_to_operand_aliasing={{2}: (7, {}), {3}: (8, {}), {4}: (9, {})} | custom-call | flops 14495514624 | bytes 25165824 | tf_op jit(solution)/shard_map/feed_forward/pallas_call | solution.py:521
  525.6 41.3 %feed_forward.10 = (bf16[2,4,128,1536]{3,2,1,0:T(8,128)(2,1)}, bf16[2,4,128,1536]{3,2,1,0:T(8,128)(2,1)}, bf16[1536,1024]{1,0:T(8,128)(2,1)}, bf16[1024,1536]{1,0:T(8,128)(2,1)}, f32[16,1024]{1,0:T(8,128)}) custom-call(s32[1]{0:T(128)} %bitcast.47.refs_0_.core_ref, bf16[1024,1536]{1,0:T(8,128)(2,1)} %copy.335.refs_1_.norm_ref, bf16[1536,1024]{1,0:T(8,128)(2,1)} %bitcast.594, ...), custom_call_target="tpu_custom_call" | custom-call | flops 14495514624 | bytes 25165824 | tf_op jit(solution)/shard_map/feed_forward/pallas_call | solution.py:521
  575.9 19.4 %feed_forward.11 = (bf16[2,4,128,1536]{3,2,1,0:T(8,128)(2,1)}, bf16[2,4,128,1536]{3,2,1,0:T(8,128)(2,1)}, bf16[1536,1024]{1,0:T(8,128)(2,1)}, bf16[1024,1536]{1,0:T(8,128)(2,1)}, f32[16,1024]{1,0:T(8,128)}) custom-call(s32[1]{0:T(128)} %bitcast.47.refs_0_.core_ref, ...), custom_call_target="tpu_custom_call", output_to_operand_aliasing={{2}: (7, {}), {3}: (8, {}), {4}: (9, {})} | custom-call | flops 4831838208 | bytes 18874368 | tf_op jit(solution)/shard_map/feed_forward/pallas_call | solution.py:521
  618.1 14.4 %add_add_fusion = f32[2,4,128,1536]{3,2,1,0:T(8,128)S(1)} fusion(bf16[2,4,128,1536]{3,2,1,0:T(8,128)(2,1)} %collective-permute-done.70, bf16[2,4,128,1536]{3,2,1,0:T(8,128)(2,1)} %get-tuple-element.487, bf16[2,4,128,1536]{3,2,1,0:T(8,128)(2,1)} %collective-permute-done.69, bf16[2,4,128,1536]{3,2,1,0:T(8,128)(2,1)} %get-tuple-element.485, ...), kind=kLoop, calls=%fused_computation.5 | loop fusion | flops 36175872 | bytes 44040192 | tf_op jit(solution)/shard_map/add | solution.py:995
  646.6 6.3 collective-permute-done.63
  708.8 29.0 %attend_back.1 = bf16[1024,2304]{1,0:T(8,128)(2,1)} custom-call(f32[256,256]{1,0:T(8,128)} %compare_convert_fusion.mask_ref, bf16[1024,2304]{1,0:T(8,128)(2,1)} %convolution_convert_fusion.2.qkv_ref, bf16[1024,768]{1,0:T(8,128)(2,1)} %convolution_convert_fusion.6.grad_ref), custom_call_target="tpu_custom_call" | custom-call | flops 8053063680 | bytes 11010048 | tf_op jit(solution)/shard_map/attend_back/pallas_call | solution.py:329
  748.6 10.9 %convolution_convert_fusion.3 = bf16[1024,1536]{1,0:T(8,128)(2,1)} fusion(bf16[1024,2304]{1,0:T(8,128)(2,1)S(1)} %copy-done.116, bf16[1536,2304]{1,0:T(8,128)(2,1)} %pad_maximum_fusion), kind=kOutput, calls=%fused_computation.10 | convolution fusion | flops 7249330176 | bytes 14942208 | tf_op jit(solution)/shard_map/dot_general | solution.py:1044
  759.5 10.0 convolution_convert_fusion
  782.3 6.2 collective-permute-done.81
  824.8 8.2 collective-permute-done.87
  833.0 9.6 collective-permute-done.86
  842.5 5.8 collective-permute-done.84
  864.1 20.9 %conv_back.1 = (f32[512,1536]{1,0:T(8,128)}, f32[16,1536]{1,0:T(8,128)}, f32[8,1536]{1,0:T(8,128)}) custom-call(s32[1]{0:T(128)} %bitcast.47.refs_0_.core_ref, bf16[576,1536]{1,0:T(8,128)(2,1)} %bitcast.625, bf16[576,1536]{1,0:T(8,128)(2,1)} %bitcast.626, bf16[576,1536]{1,0:T(8,128)(2,1)} %collective-permute-done.88.arriving_ref, ...), custom_call_target="tpu_custom_call" | custom-call | flops 55050240 | bytes 11010048 | tf_op jit(solution)/shard_map/conv_back/pallas_call | solution.py:774
  885.0 6.0 copy.372
  920.8 12.6 %collective-permute-done.94 = bf16[1,9216]{1,0:T(2,128)(2,1)S(1)} collective-permute-done((bf16[1,9216]{1,0:T(2,128)(2,1)S(1)}, bf16[1,9216]{1,0:T(2,128)(2,1)S(1)}, u32[]{:S(2)}, u32[]{:S(2)}) %collective-permute-start.94) | collective-permute-done | bytes 18464 | tf_op jit(solution)/shard_map/ppermute | solution.py:33
  (736 shorter events, 556.0 us)
Async XLA Ops:
  6.6 42.4 %collective-permute-start.1 = (bf16[48,1536]{1,0:T(8,128)(2,1)}, bf16[48,1536]{1,0:T(8,128)(2,1)}, u32[]{:S(2)}, u32[]{:S(2)}) collective-permute-start(bf16[48,1536]{1,0:T(8,128)(2,1)} %param.22), channel_id=1, source_target_pairs={{0,0},{1,2},{2,4},{3,6},{4,8},{5,10},{6,12},{7,14},{8,16},{9,18},{... | collective-permute-start | bytes 442376 | tf_op jit(solution)/shard_map/ppermute | solution.py:860
  26.2 67.5 %collective-permute-start.11 = (bf16[4,128,1536]{2,1,0:T(8,128)(2,1)S(1)}, bf16[4,128,1536]{2,1,0:T(8,128)(2,1)}, u32[]{:S(2)}, u32[]{:S(2)}) collective-permute-start(bf16[4,128,1536]{2,1,0:T(8,128)(2,1)S(1)} %bitcast.610), channel_id=1, source_target_pairs={{0,1},{1,0},{2,3},{3,2},{4,5},{5,4},{6,7},{7,6},{8,9},{9,8},{10,11... | collective-permute-start | bytes 4718600 | tf_op jit(solution)/shard_map/ppermute | solution.py:33
  125.4 39.3 %collective-permute-start.22 = (bf16[8,96,1152]{2,1,0:T(8,128)(2,1)}, bf16[8,96,1152]{2,1,0:T(8,128)(2,1)}, u32[]{:S(2)}, u32[]{:S(2)}) collective-permute-start(bf16[8,96,1152]{2,1,0:T(8,128)(2,1)} %get-tuple-element.322.refs_0_), channel_id=1, source_target_pairs={{0,2},{1,3},{2,0},{3,1},{4,6},{5,7},{6,4},{7,5},{8,10},{9,11},{10,... | collective-permute-start | bytes 5308424 | tf_op jit(solution)/shard_map/ppermute | solution.py:33
  126.4 39.1 %collective-permute-start.23 = (bf16[8,96,1152]{2,1,0:T(8,128)(2,1)}, bf16[8,96,1152]{2,1,0:T(8,128)(2,1)}, u32[]{:S(2)}, u32[]{:S(2)}) collective-permute-start(bf16[8,96,1152]{2,1,0:T(8,128)(2,1)} %get-tuple-element.323.refs_0_), channel_id=1, source_target_pairs={{0,4},{1,5},{2,6},{3,7},{4,0},{5,1},{6,2},{7,3},{8,12},{9,13},{10,... | collective-permute-start | bytes 5308424 | tf_op jit(solution)/shard_map/ppermute | solution.py:33
  137.9 115.8 %collective-permute-start.44 = (bf16[4,128,1536]{2,1,0:T(8,128)(2,1)S(1)}, bf16[4,128,1536]{2,1,0:T(8,128)(2,1)}, u32[]{:S(2)}, u32[]{:S(2)}) collective-permute-start(bf16[4,128,1536]{2,1,0:T(8,128)(2,1)S(1)} %bitcast.596), channel_id=1, source_target_pairs={{0,1},{1,0},{2,3},{3,2},{4,5},{5,4},{6,7},{7,6},{8,9},{9,8},{10,11... | collective-permute-start | bytes 4718600 | tf_op jit(solution)/shard_map/ppermute | solution.py:33
  289.6 37.2 %collective-permute-start.39 = (bf16[8,96,1024]{2,1,0:T(8,128)(2,1)}, bf16[8,96,1024]{2,1,0:T(8,128)(2,1)}, u32[]{:S(2)}, u32[]{:S(2)}) collective-permute-start(bf16[8,96,1024]{2,1,0:T(8,128)(2,1)} %pad_maximum_fusion.8.refs_0_), channel_id=1, source_target_pairs={{0,2},{1,3},{2,0},{3,1},{4,6},{5,7},{6,4},{7,5},{8,10},{9,11},{10,... | collective-permute-start | bytes 4718600 | tf_op jit(solution)/shard_map/ppermute | solution.py:33
  290.9 36.6 %collective-permute-start.40 = (bf16[8,64,1536]{2,1,0:T(8,128)(2,1)S(1)}, bf16[8,64,1536]{2,1,0:T(8,128)(2,1)}, u32[]{:S(2)}, u32[]{:S(2)}) collective-permute-start(bf16[8,64,1536]{2,1,0:T(8,128)(2,1)S(1)} %pad_maximum_fusion.9.refs_0_), channel_id=1, source_target_pairs={{0,4},{1,5},{2,6},{3,7},{4,0},{5,1},{6,2},{7,3},{8,12},{9,13},{10,... | collective-permute-start | bytes 4718600 | tf_op jit(solution)/shard_map/ppermute | solution.py:33
  331.5 40.0 %collective-permute-start.45 = (bf16[4,96,1024]{2,1,0:T(8,128)(2,1)}, bf16[4,96,1024]{2,1,0:T(8,128)(2,1)}, u32[]{:S(2)}, u32[]{:S(2)}) collective-permute-start(bf16[4,96,1024]{2,1,0:T(8,128)(2,1)} %pad_maximum_fusion.21), channel_id=1, source_target_pairs={{0,4},{1,5},{2,6},{3,7},{4,0},{5,1},{6,2},{7,3},{8,12},{9,13},{10,... | collective-permute-start | bytes 2359304 | tf_op jit(solution)/shard_map/ppermute | solution.py:33
  332.0 39.5 %collective-permute-start.46 = (bf16[4,64,1536]{2,1,0:T(8,128)(2,1)}, bf16[4,64,1536]{2,1,0:T(8,128)(2,1)}, u32[]{:S(2)}, u32[]{:S(2)}) collective-permute-start(bf16[4,64,1536]{2,1,0:T(8,128)(2,1)} %pad_maximum_fusion.22), channel_id=1, source_target_pairs={{0,2},{1,3},{2,0},{3,1},{4,6},{5,7},{6,4},{7,5},{8,10},{9,11},{10,... | collective-permute-start | bytes 2359304 | tf_op jit(solution)/shard_map/ppermute | solution.py:33
  380.0 46.0 %collective-permute-start.49 = (bf16[8,96,1024]{2,1,0:T(8,128)(2,1)}, bf16[8,96,1024]{2,1,0:T(8,128)(2,1)}, u32[]{:S(2)}, u32[]{:S(2)}) collective-permute-start(bf16[8,96,1024]{2,1,0:T(8,128)(2,1)} %pad_maximum_fusion.10.refs_0_), channel_id=1, source_target_pairs={{0,2},{1,3},{2,0},{3,1},{4,6},{5,7},{6,4},{7,5},{8,10},{9,11},{10,... | collective-permute-start | bytes 4718600 | tf_op jit(solution)/shard_map/ppermute | solution.py:33
  381.0 45.0 %collective-permute-start.50 = (bf16[8,64,1536]{2,1,0:T(8,128)(2,1)}, bf16[8,64,1536]{2,1,0:T(8,128)(2,1)}, u32[]{:S(2)}, u32[]{:S(2)}) collective-permute-start(bf16[8,64,1536]{2,1,0:T(8,128)(2,1)} %pad_maximum_fusion.11.refs_0_), channel_id=1, source_target_pairs={{0,4},{1,5},{2,6},{3,7},{4,0},{5,1},{6,2},{7,3},{8,12},{9,13},{10,... | collective-permute-start | bytes 4718600 | tf_op jit(solution)/shard_map/ppermute | solution.py:33
  382.5 43.5 %collective-permute-start.51 = (bf16[2,96,1024]{2,1,0:T(8,128)(2,1)}, bf16[2,96,1024]{2,1,0:T(8,128)(2,1)}, u32[]{:S(2)}, u32[]{:S(2)}) collective-permute-start(bf16[2,96,1024]{2,1,0:T(8,128)(2,1)} %pad_maximum_fusion.33), channel_id=1, source_target_pairs={{0,8},{1,9},{2,10},{3,11},{4,12},{5,13},{6,14},{7,15},{8,0},{9,1},... | collective-permute-start | bytes 1179656 | tf_op jit(solution)/shard_map/ppermute | solution.py:33
  383.0 42.9 %collective-permute-start.52 = (bf16[2,64,1536]{2,1,0:T(8,128)(2,1)}, bf16[2,64,1536]{2,1,0:T(8,128)(2,1)S(1)}, u32[]{:S(2)}, u32[]{:S(2)}) collective-permute-start(bf16[2,64,1536]{2,1,0:T(8,128)(2,1)} %pad_maximum_fusion.34), channel_id=1, source_target_pairs={{0,8},{1,9},{2,10},{3,11},{4,12},{5,13},{6,14},{7,15},{8,0},{9,1},... | collective-permute-start | bytes 1179656 | tf_op jit(solution)/shard_map/ppermute | solution.py:33
  431.5 164.4 %collective-permute-start.65 = (bf16[2,4,128,1536]{3,2,1,0:T(8,128)(2,1)}, bf16[2,4,128,1536]{3,2,1,0:T(8,128)(2,1)}, u32[]{:S(2)}, u32[]{:S(2)}) collective-permute-start(bf16[2,4,128,1536]{3,2,1,0:T(8,128)(2,1)} %get-tuple-element.478), channel_id=1, source_target_pairs={{0,1},{1,0},{2,3},{3,2},{4,5},{5,4},{6,7},{7,6},{8,9},{9,8},{10,11... | collective-permute-start | bytes 9437192 | tf_op jit(solution)/shard_map/ppermute | solution.py:33
  466.6 48.3 %collective-permute-start.55 = (bf16[8,96,1024]{2,1,0:T(8,128)(2,1)}, bf16[8,96,1024]{2,1,0:T(8,128)(2,1)}, u32[]{:S(2)}, u32[]{:S(2)}) collective-permute-start(bf16[8,96,1024]{2,1,0:T(8,128)(2,1)} %pad_maximum_fusion.12.refs_0_), channel_id=1, source_target_pairs={{0,2},{1,3},{2,0},{3,1},{4,6},{5,7},{6,4},{7,5},{8,10},{9,11},{10,... | collective-permute-start | bytes 4718600 | tf_op jit(solution)/shard_map/ppermute | solution.py:33
  467.5 47.4 %collective-permute-start.56 = (bf16[8,64,1536]{2,1,0:T(8,128)(2,1)}, bf16[8,64,1536]{2,1,0:T(8,128)(2,1)}, u32[]{:S(2)}, u32[]{:S(2)}) collective-permute-start(bf16[8,64,1536]{2,1,0:T(8,128)(2,1)} %pad_maximum_fusion.13.refs_0_), channel_id=1, source_target_pairs={{0,4},{1,5},{2,6},{3,7},{4,0},{5,1},{6,2},{7,3},{8,12},{9,13},{10,... | collective-permute-start | bytes 4718600 | tf_op jit(solution)/shard_map/ppermute | solution.py:33
  471.7 95.2 %collective-permute-start.57 = (bf16[2,2,2,96,1024]{4,3,2,1,0:T(8,128)(2,1)}, bf16[2,2,2,96,1024]{4,3,2,1,0:T(8,128)(2,1)}, u32[]{:S(2)}, u32[]{:S(2)}) collective-permute-start(bf16[2,2,2,96,1024]{4,3,2,1,0:T(8,128)(2,1)} %dynamic-slice_bitcast_fusion.2), channel_id=1, source_target_pairs={{0,2},{1,3},{2,0},{3,1},{4,6},{5,7},{6,4},{7,5},{8,10},{9,11},{10,... | collective-permute-start | bytes 4718600 | tf_op jit(solution)/shard_map/ppermute | solution.py:33
  472.5 94.4 %collective-permute-start.58 = (bf16[2,2,2,64,1536]{4,3,1,0,2:T(8,128)(2,1)}, bf16[2,2,2,64,1536]{4,3,1,0,2:T(8,128)(2,1)}, u32[]{:S(2)}, u32[]{:S(2)}) collective-permute-start(bf16[2,2,2,64,1536]{4,3,1,0,2:T(8,128)(2,1)} %copy_bitcast_fusion.4), channel_id=1, source_target_pairs={{0,4},{1,5},{2,6},{3,7},{4,0},{5,1},{6,2},{7,3},{8,12},{9,13},{10,... | collective-permute-start | bytes 4718600 | tf_op jit(solution)/shard_map/ppermute | solution.py:33
  575.4 39.0 %collective-permute-start.66 = (bf16[2,4,128,1536]{3,2,1,0:T(8,128)(2,1)}, bf16[2,4,128,1536]{3,2,1,0:T(8,128)(2,1)}, u32[]{:S(2)}, u32[]{:S(2)}) collective-permute-start(bf16[2,4,128,1536]{3,2,1,0:T(8,128)(2,1)} %get-tuple-element.480), channel_id=1, source_target_pairs={{0,1},{1,0},{2,3},{3,2},{4,5},{5,4},{6,7},{7,6},{8,9},{9,8},{10,11... | collective-permute-start | bytes 9437192 | tf_op jit(solution)/shard_map/ppermute | solution.py:33
  575.4 39.6 %collective-permute-start.67 = (bf16[2,4,128,1536]{3,2,1,0:T(8,128)(2,1)}, bf16[2,4,128,1536]{3,2,1,0:T(8,128)(2,1)}, u32[]{:S(2)}, u32[]{:S(2)}) collective-permute-start(bf16[2,4,128,1536]{3,2,1,0:T(8,128)(2,1)} %get-tuple-element.482), channel_id=1, source_target_pairs={{0,1},{1,0},{2,3},{3,2},{4,5},{5,4},{6,7},{7,6},{8,9},{9,8},{10,11... | collective-permute-start | bytes 9437192 | tf_op jit(solution)/shard_map/ppermute | solution.py:33
  746.9 47.0 %collective-permute-start.82 = (bf16[2,2,96,1024]{3,2,1,0:T(8,128)(2,1)}, bf16[2,2,96,1024]{3,2,1,0:T(8,128)(2,1)}, u32[]{:S(2)}, u32[]{:S(2)}) collective-permute-start(bf16[2,2,96,1024]{3,2,1,0:T(8,128)(2,1)} %fusion.13), channel_id=1, source_target_pairs={{0,4},{1,5},{2,6},{3,7},{4,0},{5,1},{6,2},{7,3},{8,12},{9,13},{10,... | collective-permute-start | bytes 2359304 | tf_op jit(solution)/shard_map/ppermute | solution.py:33
  747.5 46.4 %collective-permute-start.83 = (bf16[2,2,64,1536]{3,2,1,0:T(8,128)(2,1)}, bf16[2,2,64,1536]{3,2,1,0:T(8,128)(2,1)}, u32[]{:S(2)}, u32[]{:S(2)}) collective-permute-start(bf16[2,2,64,1536]{3,2,1,0:T(8,128)(2,1)} %get-tuple-element.521), channel_id=1, source_target_pairs={{0,2},{1,3},{2,0},{3,1},{4,6},{5,7},{6,4},{7,5},{8,10},{9,11},{10,... | collective-permute-start | bytes 2359304 | tf_op jit(solution)/shard_map/ppermute | solution.py:33
  779.6 62.9 %collective-permute-start.88 = (bf16[576,1536]{1,0:T(8,128)(2,1)}, bf16[576,1536]{1,0:T(8,128)(2,1)}, u32[]{:S(2)}, u32[]{:S(2)}) collective-permute-start(bf16[576,1536]{1,0:T(8,128)(2,1)} %bitcast.122), channel_id=1, source_target_pairs={{0,1},{1,0},{2,3},{3,2},{4,5},{5,4},{6,7},{7,6},{8,9},{9,8},{10,11... | collective-permute-start | bytes 5308424 | tf_op jit(solution)/shard_map/ppermute | solution.py:33
  807.6 40.7 %collective-permute-start.84 = (bf16[2,2,2,96,1152]{4,3,1,0,2:T(8,128)(2,1)}, bf16[2,2,2,96,1152]{4,3,1,0,2:T(8,128)(2,1)}, u32[]{:S(2)}, u32[]{:S(2)}) collective-permute-start(bf16[2,2,2,96,1152]{4,3,1,0,2:T(8,128)(2,1)} %copy_bitcast_fusion.1), channel_id=1, source_target_pairs={{0,2},{1,3},{2,0},{3,1},{4,6},{5,7},{6,4},{7,5},{8,10},{9,11},{10,... | collective-permute-start | bytes 5308424 | tf_op jit(solution)/shard_map/ppermute | solution.py:33
  808.8 40.6 %collective-permute-start.85 = (bf16[2,2,2,96,1152]{4,3,1,0,2:T(8,128)(2,1)}, bf16[2,2,2,96,1152]{4,3,1,0,2:T(8,128)(2,1)}, u32[]{:S(2)}, u32[]{:S(2)}) collective-permute-start(bf16[2,2,2,96,1152]{4,3,1,0,2:T(8,128)(2,1)} %copy_bitcast_fusion), channel_id=1, source_target_pairs={{0,4},{1,5},{2,6},{3,7},{4,0},{5,1},{6,2},{7,3},{8,12},{9,13},{10,... | collective-permute-start | bytes 5308424 | tf_op jit(solution)/shard_map/ppermute | solution.py:33
  856.8 40.7 %collective-permute-start.89 = (bf16[2,2,96,1152]{3,2,1,0:T(8,128)(2,1)}, bf16[2,2,96,1152]{3,2,1,0:T(8,128)(2,1)}, u32[]{:S(2)}, u32[]{:S(2)}) collective-permute-start(bf16[2,2,96,1152]{3,2,1,0:T(8,128)(2,1)} %get-tuple-element.535), channel_id=1, source_target_pairs={{0,4},{1,5},{2,6},{3,7},{4,0},{5,1},{6,2},{7,3},{8,12},{9,13},{10,... | collective-permute-start | bytes 2654216 | tf_op jit(solution)/shard_map/ppermute | solution.py:33
  857.3 40.1 %collective-permute-start.90 = (bf16[2,2,96,1152]{3,2,1,0:T(8,128)(2,1)}, bf16[2,2,96,1152]{3,2,1,0:T(8,128)(2,1)}, u32[]{:S(2)}, u32[]{:S(2)}) collective-permute-start(bf16[2,2,96,1152]{3,2,1,0:T(8,128)(2,1)} %get-tuple-element.536), channel_id=1, source_target_pairs={{0,2},{1,3},{2,0},{3,1},{4,6},{5,7},{6,4},{7,5},{8,10},{9,11},{10,... | collective-permute-start | bytes 2654216 | tf_op jit(solution)/shard_map/ppermute | solution.py:33
  860.3 37.1 %collective-permute-start.92 = (bf16[64,1536]{1,0:T(8,128)(2,1)}, bf16[64,1536]{1,0:T(8,128)(2,1)}, u32[]{:S(2)}, u32[]{:S(2)}) collective-permute-start(bf16[64,1536]{1,0:T(8,128)(2,1)} %fusion.68), channel_id=1, source_target_pairs={{0,16},{1,17},{2,18},{3,19},{4,20},{5,21},{6,22},{7,23},{8,24},{9,... | collective-permute-start | bytes 589832 | tf_op jit(solution)/shard_map/ppermute | solution.py:33
  860.3 37.1 %collective-permute-start.91 = (bf16[96,1024]{0,1:T(8,128)(2,1)}, bf16[96,1024]{0,1:T(8,128)(2,1)S(1)}, u32[]{:S(2)}, u32[]{:S(2)}) collective-permute-start(bf16[96,1024]{0,1:T(8,128)(2,1)} %fusion.54), channel_id=1, source_target_pairs={{0,16},{1,17},{2,18},{3,19},{4,20},{5,21},{6,22},{7,23},{8,24},{9,... | collective-permute-start | bytes 589832 | tf_op jit(solution)/shard_map/ppermute | solution.py:33
  913.0 54.3 %collective-permute-start.103 = (bf16[2,96,1152]{2,1,0:T(8,128)(2,1)}, bf16[2,96,1152]{2,1,0:T(8,128)(2,1)}, u32[]{:S(2)}, u32[]{:S(2)}) collective-permute-start(bf16[2,96,1152]{2,1,0:T(8,128)(2,1)} %get-tuple-element.559), channel_id=1, source_target_pairs={{0,8},{1,9},{2,10},{3,11},{4,12},{5,13},{6,14},{7,15},{8,0},{9,1},... | collective-permute-start | bytes 1327112 | tf_op jit(solution)/shard_map/ppermute | solution.py:33
  913.0 54.3 %collective-permute-start.104 = (bf16[2,96,1152]{2,1,0:T(8,128)(2,1)}, bf16[2,96,1152]{2,1,0:T(8,128)(2,1)}, u32[]{:S(2)}, u32[]{:S(2)}) collective-permute-start(bf16[2,96,1152]{2,1,0:T(8,128)(2,1)} %get-tuple-element.560), channel_id=1, source_target_pairs={{0,8},{1,9},{2,10},{3,11},{4,12},{5,13},{6,14},{7,15},{8,0},{9,1},... | collective-permute-start | bytes 1327112 | tf_op jit(solution)/shard_map/ppermute | solution.py:33
  915.0 52.3 %collective-permute-start.105 = (bf16[2,2,2,48,768]{4,3,1,0,2:T(8,128)(2,1)}, bf16[2,2,2,48,768]{4,3,1,0,2:T(8,128)(2,1)}, u32[]{:S(2)}, u32[]{:S(2)}) collective-permute-start(bf16[2,2,2,48,768]{4,3,1,0,2:T(8,128)(2,1)} %copy_bitcast_fusion.6), channel_id=1, source_target_pairs={{0,2},{1,3},{2,0},{3,1},{4,6},{5,7},{6,4},{7,5},{8,10},{9,11},{10,... | collective-permute-start | bytes 1769480 | tf_op jit(solution)/shard_map/ppermute | solution.py:33
  (204 other events, 2790.0 us)

commit v4 on v3

--- a/solution.py
+++ b/solution.py
@@ -60,6 +60,10 @@
 class Slots:
     def __init__(self, token):
         self.token = token
+
+    def after(self, *arrays):
+        arrays, self.token = lax.optimization_barrier((arrays, self.token))
+        return arrays
 
     def finish(self, flows):
         while any(flow.wanted is not None for flow in flows):
@@ -379,9 +383,6 @@
     up_ref,
     down_ref,
     kernel_ref,
-    up_held_ref,
-    down_held_ref,
-    kernel_held_ref,
     staying_ref,
     leaving_ref,
     up_grad_ref,
@@ -496,14 +497,14 @@
                     ref[index, plane] = acc[pl.ds(start, PLANE // 2), :].astype(low)
 
 
-def feed_forward(norm, norm_t, grad, up, down, kernel, core, first, count, held=None):
+def feed_forward(norm, norm_t, grad, up, down, kernel, core):
     tokens, model = norm.shape
     channels = up.shape[1]
     width = TILE
     whole = lambda j, words: (0, 0)
     half = lambda j, words: (0, 0, 0, 0)
-    across = lambda j, words: (0, first + j)
-    down_rows = lambda j, words: (first + j, 0)
+    across = lambda j, words: (0, j)
+    down_rows = lambda j, words: (j, 0)
     once = pl.Buffered(1)
     grads = [
         jax.ShapeDtypeStruct((model, channels), low),
@@ -511,18 +512,11 @@
         jax.ShapeDtypeStruct((16, channels), full),
     ]
     halves = jax.ShapeDtypeStruct((2, 4, PLANE // 2, model), low)
-    body = feed_body
-    if held is None:
-        held = ()
-
-        def body(*refs):
-            feed_body(*refs[:7], None, None, None, *refs[7:])
-
     return pl.pallas_call(
-        body,
+        feed_body,
         grid_spec=pltpu.PrefetchScalarGridSpec(
             num_scalar_prefetch=1,
-            grid=(count,),
+            grid=(channels // width,),
             in_specs=[
                 pl.BlockSpec((tokens, model), whole, pipeline_mode=once),
                 pl.BlockSpec((model, tokens), whole, pipeline_mode=once),
@@ -530,8 +524,7 @@
                 pl.BlockSpec((model, width), across),
                 pl.BlockSpec((width, model), down_rows),
                 pl.BlockSpec((16, width), across),
-            ]
-            + [pl.BlockSpec(memory_space=pl.ANY)] * len(held),
+            ],
             out_specs=[
                 pl.BlockSpec(halves.shape, half),
                 pl.BlockSpec(halves.shape, half),
@@ -550,15 +543,14 @@
             ],
         ),
         out_shape=[halves, halves] + grads,
-        input_output_aliases={7 + i: 2 + i for i in range(len(held))},
         compiler_params=pltpu.CompilerParams(vmem_limit_bytes=62 * 1024 * 1024),
         cost_estimate=pl.CostEstimate(
-            flops=12 * tokens * model * count * width,
-            bytes_accessed=8 * model * count * width + 10 * tokens * model,
-            transcendentals=tokens * count * width,
+            flops=12 * tokens * model * channels,
+            bytes_accessed=8 * model * channels + 10 * tokens * model,
+            transcendentals=tokens * channels,
         ),
         name="feed_forward",
-    )(core[None].astype(jnp.int32), norm, norm_t, grad, up, down, kernel, *held)
+    )(core[None].astype(jnp.int32), norm, norm_t, grad, up, down, kernel)
 
 
 def token_stats(x_ref, average, scale):
@@ -853,6 +845,27 @@
     qkv_split = qkv_weight.reshape(part, 3, 2, pairs, 128).transpose(0, 2, 3, 1, 4)
     qkv_rows = row_pair(qkv_split.reshape(part, 2, pairs * 384), 1)
     qkv_half = pairs * 384 // 2
+
+    picks = labels[:, None] == jnp.arange(class_count)[None, :]
+    angles_here = lax.dynamic_slice_in_dim(sinusoid(timesteps, model), rank * part, part, axis=1)
+    cond = angles_here + jnp.dot(picks.astype(low), class_table, preferred_element_type=full)
+    lift_value, lift_pull = jax.vjp(jax.nn.silu, cond)
+    lifted = lift_value.astype(low)
+    mods_part = jnp.dot(lifted, mod_weight, preferred_element_type=full)
+
+    slot = Slots(jnp.zeros((8, 128), full))
+    flow = lambda shard, colour: gather_flow(shard, colour, chip_bits)
+    sums = lambda parts, colour: scatter_flow(parts, colour, chip, chip_bits)
+    joined = lambda flows: [
+        gathered(f, colour, chip, chip_bits) for colour, f in enumerate(flows)
+    ]
+    mods_flow = scatter_flow(mods_part, 0, chip, chip_bits, sent=full)
+    qkv_flows = [flow(qkv_rows[:, :qkv_half], 0), flow(qkv_rows[:, qkv_half:], 1)]
+    slot(qkv_flows + [mods_flow])
+
+    tokens, cotangent, up_weight, proj_weight, ffn_kernel, attn_kernel = slot.after(
+        tokens, cotangent, up_weight, proj_weight, ffn_kernel, attn_kernel
+    )
     up_split = up_weight.reshape(part, chips, 2, CHUNKS, piece).transpose(0, 2, 3, 1, 4)
     up_rows = row_pair(up_split.reshape(part, 2, CHUNKS, chips * piece), 1)
     proj_there = [(r, r % chips * 2 + r // chips) for r in range(devices)]
@@ -860,17 +873,12 @@
     proj_rows = lax.ppermute(proj_weight, AXES, proj_there)
     mine = to_phases(tokens[0], half_rows)
     canvas = join_halves(mine, swap_core(mine), core)
-    grad_mine = to_phases(cotangent[0], half_rows)
-    grad_ph = join_halves(grad_mine, swap_core(grad_mine), core)
-
-    picks = labels[:, None] == jnp.arange(class_count)[None, :]
-    angles_here = lax.dynamic_slice_in_dim(sinusoid(timesteps, model), rank * part, part, axis=1)
-    cond = angles_here + jnp.dot(picks.astype(low), class_table, preferred_element_type=full)
-    lift_value, lift_pull = jax.vjp(jax.nn.silu, cond)
-    lifted = lift_value.astype(low)
-    mods_part = jnp.dot(lifted, mod_weight, preferred_element_type=full)
-    mods_half = scatter_sum(mods_part, 0, chip, chip_bits, sent=full)
-    mods = mods_half + swap_core(mods_half)
+
+    slot(qkv_flows + [mods_flow])
+    while mods_flow.wanted is not None:
+        array, bit = mods_flow.wanted
+        mods_flow.arrive(swap(array, bit + 1))
+    mods = mods_flow.result + swap_core(mods_flow.result)
     shift_a, scale_a, gate_a, shift_f, scale_f, gate_f = jnp.split(mods, 6)
 
     tap_count = 9 * (share + part)
@@ -893,25 +901,21 @@
     )
     mask = (segment[:, None] == segment[None, :]).astype(full)
 
-    slot = Slots(jnp.zeros((8, 128), full))
-    flow = lambda shard, colour: gather_flow(shard, colour, chip_bits)
-    sums = lambda parts, colour: scatter_flow(parts, colour, chip, chip_bits)
-    joined = lambda flows: [
-        gathered(f, colour, chip, chip_bits) for colour, f in enumerate(flows)
-    ]
-    qkv_flows = [flow(qkv_rows[:, :qkv_half], 0), flow(qkv_rows[:, qkv_half:], 1)]
     proj_flows = [flow(proj_rows[:, : model // 2], 0), flow(proj_rows[:, model // 2 :], 1)]
     feed_flows = [
         [flow(up_rows[:, t], 0), flow(down_weight[t * piece : (t + 1) * piece], 1)]
         for t in range(CHUNKS)
     ]
-
-    slot(qkv_flows)
-    slot(qkv_flows)
-
     mods_a = jnp.concatenate([shift_a[None], scale_a[None], jnp.zeros((6, model), full)], axis=0)
-    convolved = slot(qkv_flows + proj_flows, lambda: conv_in(canvas, attn_taps, mods_a))
-    slot(qkv_flows + proj_flows)
+
+    slot(qkv_flows + proj_flows + feed_flows[0])
+    convolved = slot(
+        qkv_flows + proj_flows + feed_flows[0], lambda: conv_in(canvas, attn_taps, mods_a)
+    )
+
+    (cotangent,) = slot.after(cotangent)
+    upstream = to_phases(cotangent[0], half_rows)
+    grad_ph = join_halves(upstream, swap_core(upstream), core)
 
     def project_in():
         weight = jnp.concatenate(
@@ -920,8 +924,10 @@
         return weight, jnp.dot(convolved, weight, preferred_element_type=full).astype(low)
 
     slot.finish(qkv_flows)
-    qkv_full, qkv = slot(proj_flows + feed_flows[0], project_in)
-    attended = slot(proj_flows + feed_flows[0], lambda: attend(mask, qkv))
+    qkv_full, qkv = slot(proj_flows + feed_flows[0] + feed_flows[1], project_in)
+    attended = slot(
+        proj_flows + feed_flows[1] + feed_flows[2], lambda: attend(mask, qkv)
+    )
 
     def project_out():
         weight = jnp.concatenate(
@@ -935,61 +941,47 @@
 
     source_ph = mine.astype(full)
     slot.finish(proj_flows)
-    proj_full, branch_a = slot(feed_flows[0] + feed_flows[1], project_out)
-
     def enter_feed():
+        proj_full, branch_a = project_out()
         middle = source_ph + gate_a * branch_a
         normed_low = modulate(middle, shift_f, scale_f).astype(low)
         norm = join_halves(normed_low, swap_core(normed_low), core)
-        return middle, norm, norm.T, (grad_ph.astype(full) * gate_f).astype(low)
-
-    middle, norm, norm_t, grad_branch_f = slot(feed_flows[0] + feed_flows[1], enter_feed)
+        grad_branch_f = (grad_ph.astype(full) * gate_f).astype(low)
+        return proj_full, branch_a, middle, norm, norm.T, grad_branch_f
+
+    proj_full, branch_a, middle, norm, norm_t, grad_branch_f = slot(
+        sum(feed_flows, []), enter_feed
+    )
 
     kept = []
     grads = [None] * CHUNKS
 
-    def feed(t, first, count):
+    def feed(t):
         def work():
-            if first == 0:
-                feed_weights[t] = [
-                    array.reshape(shape)
-                    for array, shape in zip(joined(feed_flows[t]), ((model, -1), (-1, model)))
-                ]
+            up, down = joined(feed_flows[t])
             staying, leaving, *grads_now = feed_forward(
-                norm, norm_t, grad_branch_f, *feed_weights[t], ffn_taps[t], core, first, count,
-                grads[t],
+                norm, norm_t, grad_branch_f, up.reshape(model, -1), down.reshape(-1, model),
+                ffn_taps[t], core,
             )
-            return feed_weights[t], staying, leaving, grads_now
+            return staying, leaving, grads_now
 
         return work
 
-    feed_weights = [None] * CHUNKS
-    back_flows = [None] * CHUNKS
-
-    def run_feed(flows, t, first, count):
+    back_flows = [[] for _ in range(CHUNKS)]
+
+    def run_feed(flows, t):
         slot.finish(feed_flows[t])
-        feed_weights[t], staying, leaving, grads[t] = slot(flows, feed(t, first, count))
+        staying, leaving, grads[t] = slot(flows, feed(t))
         kept.append((staying, leaving))
-
-    blocks = chips * piece // TILE
-    run_feed(feed_flows[1] + feed_flows[2], 0, 0, 1)
-    run_feed(feed_flows[1] + feed_flows[2], 0, 1, blocks - 1)
-    run_feed(feed_flows[2], 1, 0, 1)
-    run_feed(feed_flows[2], 1, 1, blocks - 1)
-
-    def begin_back(t):
         back_flows[t] = [
             sums(grads[t][0].reshape(chips, 2 * part, -1), 0),
             sums(grads[t][1].reshape(chips, piece, model), 1),
         ]
 
-    begin_back(0)
-    begin_back(1)
-    run_feed(back_flows[0], 2, 0, blocks - 1)
-    run_feed(back_flows[0], 2, blocks - 1, 1)
-    begin_back(2)
-
-    upstream = to_phases(cotangent[0], half_rows).astype(full)
+    run_feed(feed_flows[1] + feed_flows[2], 0)
+    run_feed(feed_flows[2] + back_flows[0], 1)
+    run_feed(back_flows[0] + back_flows[1], 2)
+    upstream = upstream.astype(full)
 
     def leave_feed():
         total = sum(
@@ -1011,7 +1003,7 @@
     (
         layer_out, grad_middle, grad_branch_mine,
         grad_gate_f, grad_shift_f, grad_scale_f, grad_gate_a,
-    ) = slot(back_flows[0] + back_flows[1], leave_feed)
+    ) = slot(sum(back_flows, []), leave_feed)
     layer_out = layer_out[None]
 
     def enter_attend():
@@ -1020,14 +1012,14 @@
         proj_grad = jnp.dot(attended.T, grad_branch_a, preferred_element_type=full)
         return grad_attended.astype(low), proj_grad.astype(low)
 
-    grad_attended, proj_grad = slot(back_flows[0] + back_flows[1], enter_attend)
+    grad_attended, proj_grad = slot(sum(back_flows, []), enter_attend)
     proj_grad = proj_grad.reshape(chips, -1, model)
     proj_flows = [sums(proj_grad[..., : model // 2], 0), sums(proj_grad[..., model // 2 :], 1)]
     grad_qkv = slot(
-        back_flows[1] + back_flows[2], lambda: attend_back(mask, qkv, grad_attended)
+        proj_flows + sum(back_flows, []), lambda: attend_back(mask, qkv, grad_attended)
     )
     qkv_grad = slot(
-        back_flows[1] + back_flows[2],
+        proj_flows + sum(back_flows, []),
         lambda: jnp.dot(convolved.T, grad_qkv, preferred_element_type=full).astype(low),
     )
     qkv_grad = qkv_grad.reshape(chips, 2 * part, -1)
@@ -1044,7 +1036,7 @@
         part_here = jnp.dot(grad_qkv, qkv_full.T, preferred_element_type=full).astype(low)
         return rows_near(part_here, core), swap_core(rows_near(part_here, 1 - core))
 
-    grad_conv = slot(qkv_flows + back_flows[2], leave_attend)
+    grad_conv = slot(qkv_flows + proj_flows + back_flows[2], leave_attend)
 
     def leave_block():
         input_grad, attn_tap_grad, mods_grad = conv_back(
@@ -1055,10 +1047,8 @@
         return attn_tap_grad[:9], input_grad, mods_grad[0], mods_grad[1]
 
     attn_tap_grad, input_grad, grad_shift_a, grad_scale_a = slot(
-        qkv_flows + back_flows[2], leave_block
-    )
-    slot(qkv_flows + proj_flows)
-    slot(qkv_flows + proj_flows)
+        qkv_flows + proj_flows + back_flows[2], leave_block
+    )
     slot.finish(sum(back_flows, proj_flows + qkv_flows))
     up_shares = [flows[0].result for flows in back_flows]
     down_shares = [flows[1].result for flows in back_flows]

time: 1040 us -> 1060 us (1.019)
  waiting for transfers between devices: 183 us -> 243 us
  Pallas kernels: 322 us -> 297 us
    ppermute x116 -> x113, waiting for transfers between devices: 183 us -> 243 us  [swap(): lax.ppermute(x, AXES, [(i, i ^ 1 << bit) for i in range(device_count())])]
    pallas_call x6 -> x3, Pallas kernels: 182 us -> 157 us  [feed_forward(): pl.pallas_call(feed_body, grid_spec=pltpu.PrefetchScalarGridSpec(num_scal...]
    ppermute x116 -> x113, starting transfers between devices: 112 us -> 101 us  [swap(): lax.ppermute(x, AXES, [(i, i ^ 1 << bit) for i in range(device_count())])]
    unnamed x247 -> x267, local copies, waits for them, and re-layouts: 25.2 us -> 24.5 us
  transfers between devices with their start and end apart: 118 -> 115, of which waited for: 41 -> 39; matrix products, arithmetic and copies ran while one was open for 32% -> 29% of each run, Pallas kernels for 31% -> 27%
where the time goes in v4:
time: 1060 us; the launch traced here: 1050 us
  Pallas kernels  297 us (28%)
  waiting for transfers between devices  243 us (23%)
  other arithmetic  189 us (18%)
  local copies, waits for them, and re-layouts  167 us (16%)
  starting transfers between devices  108 us (10%)
  matrix products  47.7 us (4%)
    ppermute x113, waiting for transfers between devices, swap(): lax.ppermute(x, AXES, [(i, i ^ 1 << bit) for i in range(device_count())])  243 us
    pallas_call x3, Pallas kernels, feed_forward(): pl.pallas_call(feed_body, grid_spec=pltpu.PrefetchScalarGridSpec(num_scal...  157 us
    ppermute x113, starting transfers between devices, swap(): lax.ppermute(x, AXES, [(i, i ^ 1 << bit) for i in range(device_count())])  101 us
    concatenate x28, other arithmetic, gather_steps(): held = jnp.concatenate([held, arriving], axis=0)  52.7 us
    pallas_call x10, Pallas kernels, assemble(): pl.pallas_call(functools.partial(assemble_body, steps), grid_spec=pltpu.P...  52.1 us
    convert_element_type x20, other arithmetic, scatter_steps(): sum((at_bit(h, axis, mine).astype(full) for h in held)).astype(sent)  44 us
    pallas_call x1, Pallas kernels, attend_back(): pl.pallas_call(attend_back_body, grid=(pairs,), in_specs=[pl.BlockSpec((P...  29.1 us
    unnamed x267, local copies, waits for them, and re-layouts  24.5 us
  transfers between devices with their start and end apart: 115, of which 39 were waited for; matrix products, arithmetic and copies ran while one was open for 29% of the time, Pallas kernels for 27%

profile of v4, /device:TPU:0, one launch (start us, length us, event | category | flops | bytes accessed | tf_op | source)
XLA Modules:
  0.0 1054.4 jit_solution(5897875500822461138)
XLA Ops:
  15.3 15.0 %collective-permute-done.1 = bf16[1,96,1152]{2,1,0:T(8,128)(2,1)S(1)} collective-permute-done((bf16[1,96,1152]{2,1,0:T(8,128)(2,1)S(1)}, bf16[1,96,1152]{2,1,0:T(8,128)(2,1)S(1)}, u32[]{:S(2)}, u32[]{:S(2)}) %collective-permute-start.1) | collective-permute-done | bytes 221216 | tf_op jit(solution)/shard_map/ppermute | solution.py:33
  142.9 22.8 %conv_in.1 = bf16[1024,1536]{1,0:T(8,128)(2,1)} custom-call(bf16[1024,1536]{1,0:T(8,128)(2,1)} %bitcast.601, f32[16,1536]{1,0:T(8,128)} %pad_convert_fusion.1.kernel_ref, f32[8,1536]{1,0:T(8,128)} %maximum_maximum_fusion.mods_ref), custom_call_target="tpu_custom_call" | custom-call | flops 47185920 | bytes 6291456 | tf_op jit(solution)/shard_map/conv_in/pallas_call | solution.py:617
  182.7 5.6 assemble.10
  188.3 5.7 assemble.11
  194.1 13.1 %convolution_convert_fusion.2.qkv_ref = bf16[1024,2304]{1,0:T(8,128)(2,1)} fusion(bf16[1024,1536]{1,0:T(8,128)(2,1)} %conv_in.1, bf16[1536,1152]{1,0:T(8,128)(2,1)} %bitcast.605, bf16[1536,1152]{1,0:T(8,128)(2,1)} %bitcast.603), kind=kOutput, calls=%fused_computation.6 | convolution fusion | flops 7264272384 | bytes 14942208 | tf_op jit(solution)/shard_map/dot_general | solution.py:924
  207.8 6.5 pad_maximum_fusion
  214.4 9.2 collective-permute-done.33
  247.0 15.4 %attend.1 = bf16[1024,768]{1,0:T(8,128)(2,1)} custom-call(f32[256,256]{1,0:T(8,128)} %compare_convert_fusion.mask_ref, bf16[1024,2304]{1,0:T(8,128)(2,1)} %convolution_convert_fusion.2.qkv_ref), custom_call_target="tpu_custom_call" | custom-call | flops 3221225472 | bytes 6291456 | tf_op jit(solution)/shard_map/attend/pallas_call | solution.py:312
  310.5 8.6 copy.320
  319.2 6.1 reshape.703
  325.3 24.2 %collective-permute-done.44 = bf16[4,96,1024]{2,1,0:T(8,128)(2,1)} collective-permute-done((bf16[4,96,1024]{2,1,0:T(8,128)(2,1)}, bf16[4,96,1024]{2,1,0:T(8,128)(2,1)}, u32[]{:S(2)}, u32[]{:S(2)}) %collective-permute-start.44) | collective-permute-done | bytes 786464 | tf_op jit(solution)/shard_map/ppermute | solution.py:33
  365.7 5.4 assemble.15
  378.0 52.3 %feed_forward.3 = (bf16[2,4,128,1536]{3,2,1,0:T(8,128)(2,1)}, bf16[2,4,128,1536]{3,2,1,0:T(8,128)(2,1)}, bf16[1536,1024]{1,0:T(8,128)(2,1)}, bf16[1024,1536]{1,0:T(8,128)(2,1)}, f32[16,1024]{1,0:T(8,128)}) custom-call(s32[1]{0:T(128)} %bitcast.45.core_ref, bf16[1024,1536]{1,0:T(8,128)(2,1)} %copy.326.norm_ref, bf16[1536,1024]{1,0:T(8,128)(2,1)} %bitcast.614, ...), custom_call_target="tpu_custom_call" | custom-call | flops 19327352832 | bytes 28311552 | tf_op jit(solution)/shard_map/feed_forward/pallas_call | solution.py:515
  439.3 5.4 assemble.16
  454.1 52.1 %feed_forward.4 = (bf16[2,4,128,1536]{3,2,1,0:T(8,128)(2,1)}, bf16[2,4,128,1536]{3,2,1,0:T(8,128)(2,1)}, bf16[1536,1024]{1,0:T(8,128)(2,1)}, bf16[1024,1536]{1,0:T(8,128)(2,1)}, f32[16,1024]{1,0:T(8,128)}) custom-call(s32[1]{0:T(128)} %bitcast.45.core_ref, bf16[1024,1536]{1,0:T(8,128)(2,1)} %copy.326.norm_ref, bf16[1536,1024]{1,0:T(8,128)(2,1)} %bitcast.615, ...), custom_call_target="tpu_custom_call" | custom-call | flops 19327352832 | bytes 28311552 | tf_op jit(solution)/shard_map/feed_forward/pallas_call | solution.py:515
  506.2 11.7 %collective-permute-done.57 = bf16[2,2,2,96,1024]{4,3,2,1,0:T(8,128)(2,1)} collective-permute-done((bf16[2,2,2,96,1024]{4,3,2,1,0:T(8,128)(2,1)}, bf16[2,2,2,96,1024]{4,3,2,1,0:T(8,128)(2,1)}, u32[]{:S(2)}, u32[]{:S(2)}) %collective-permute-start.57) | collective-permute-done | bytes 1572896 | tf_op jit(solution)/shard_map/ppermute | solution.py:33
  530.7 5.4 assemble.18
  536.1 5.4 assemble.19
  544.7 52.4 %feed_forward.5 = (bf16[2,4,128,1536]{3,2,1,0:T(8,128)(2,1)}, bf16[2,4,128,1536]{3,2,1,0:T(8,128)(2,1)}, bf16[1536,1024]{1,0:T(8,128)(2,1)}, bf16[1024,1536]{1,0:T(8,128)(2,1)}, f32[16,1024]{1,0:T(8,128)}) custom-call(s32[1]{0:T(128)} %bitcast.45.core_ref, bf16[1024,1536]{1,0:T(8,128)(2,1)} %copy.326.norm_ref, bf16[1536,1024]{1,0:T(8,128)(2,1)} %bitcast.616, ...), custom_call_target="tpu_custom_call" | custom-call | flops 19327352832 | bytes 28311552 | tf_op jit(solution)/shard_map/feed_forward/pallas_call | solution.py:515
  664.9 29.8 %collective-permute-done.66 = bf16[2,2,64,1536]{3,2,1,0:T(8,128)(2,1)} collective-permute-done((bf16[2,2,64,1536]{3,2,1,0:T(8,128)(2,1)}, bf16[2,2,64,1536]{3,2,1,0:T(8,128)(2,1)}, u32[]{:S(2)}, u32[]{:S(2)}) %collective-permute-start.66) | collective-permute-done | bytes 786464 | tf_op jit(solution)/shard_map/ppermute | solution.py:33
  738.3 11.1 %collective-permute-done.74 = bf16[2,96,1024]{1,2,0:T(8,128)(2,1)S(1)} collective-permute-done((bf16[2,96,1024]{1,2,0:T(8,128)(2,1)S(1)}, bf16[2,96,1024]{1,2,0:T(8,128)(2,1)S(1)}, u32[]{:S(2)}, u32[]{:S(2)}) %collective-permute-start.74) | collective-permute-done | bytes 393248 | tf_op jit(solution)/shard_map/ppermute | solution.py:33
  766.9 29.1 %attend_back.1 = bf16[1024,2304]{1,0:T(8,128)(2,1)} custom-call(f32[256,256]{1,0:T(8,128)} %compare_convert_fusion.mask_ref, bf16[1024,2304]{1,0:T(8,128)(2,1)} %convolution_convert_fusion.2.qkv_ref, bf16[1024,768]{1,0:T(8,128)(2,1)} %convolution_convert_fusion.6.grad_ref), custom_call_target="tpu_custom_call" | custom-call | flops 8053063680 | bytes 11010048 | tf_op jit(solution)/shard_map/attend_back/pallas_call | solution.py:333
  800.4 9.5 collective-permute-done.81
  809.9 10.7 %convolution_convert_fusion = bf16[1536,2304]{1,0:T(8,128)(2,1)S(1)} fusion(bf16[1024,1536]{1,0:T(8,128)(2,1)} %conv_in.1, bf16[1024,2304]{1,0:T(8,128)(2,1)} %attend_back.1), kind=kOutput, calls=%fused_computation | convolution fusion | flops 7251296256 | bytes 14942208 | tf_op jit(solution)/shard_map/dot_general | solution.py:1023
  820.6 7.7 convolution_convert_fusion.3
  840.9 7.6 collective-permute-done.88
  848.4 5.5 collective-permute-done.87
  873.7 27.5 %collective-permute-done.89 = bf16[2,2,2,96,1152]{4,3,1,0,2:T(8,128)(2,1)} collective-permute-done((bf16[2,2,2,96,1152]{4,3,1,0,2:T(8,128)(2,1)}, bf16[2,2,2,96,1152]{4,3,1,0,2:T(8,128)(2,1)}, u32[]{:S(2)}, u32[]{:S(2)}) %collective-permute-start.89) | collective-permute-done | bytes 1769504 | tf_op jit(solution)/shard_map/ppermute | solution.py:33
  916.6 20.9 %conv_back.1 = (f32[512,1536]{1,0:T(8,128)}, f32[16,1536]{1,0:T(8,128)}, f32[8,1536]{1,0:T(8,128)}) custom-call(s32[1]{0:T(128)} %bitcast.45.core_ref, bf16[576,1536]{1,0:T(8,128)(2,1)} %bitcast.622, bf16[576,1536]{1,0:T(8,128)(2,1)} %bitcast.623, bf16[576,1536]{1,0:T(8,128)(2,1)} %collective-permute-done.93.arriving_ref, ...), custom_call_target="tpu_custom_call" | custom-call | flops 55050240 | bytes 11010048 | tf_op jit(solution)/shard_map/conv_back/pallas_call | solution.py:766
  937.5 6.0 copy.368
  1008.2 9.5 collective-permute-done.107
  1026.5 13.7 %collective-permute-done.110 = bf16[96,1152]{1,0:T(8,128)(2,1)S(1)} collective-permute-done((bf16[96,1152]{1,0:T(8,128)(2,1)S(1)}, bf16[96,1152]{1,0:T(8,128)(2,1)S(1)}, u32[]{:S(2)}, u32[]{:S(2)}) %collective-permute-start.110) | collective-permute-done | bytes 221216 | tf_op jit(solution)/shard_map/ppermute | solution.py:33
  (749 shorter events, 541.0 us)
Async XLA Ops:
  77.2 43.0 %collective-permute-start.9 = (bf16[4,96,1152]{2,1,0:T(8,128)(2,1)}, bf16[4,96,1152]{2,1,0:T(8,128)(2,1)}, u32[]{:S(2)}, u32[]{:S(2)}) collective-permute-start(bf16[4,96,1152]{2,1,0:T(8,128)(2,1)} %pad_maximum_fusion.15), channel_id=1, source_target_pairs={{0,4},{1,5},{2,6},{3,7},{4,0},{5,1},{6,2},{7,3},{8,12},{9,13},{10,... | collective-permute-start | bytes 2654216 | tf_op jit(solution)/shard_map/ppermute | solution.py:33
  77.9 42.3 %collective-permute-start.10 = (bf16[4,96,1152]{2,1,0:T(8,128)(2,1)}, bf16[4,96,1152]{2,1,0:T(8,128)(2,1)}, u32[]{:S(2)}, u32[]{:S(2)}) collective-permute-start(bf16[4,96,1152]{2,1,0:T(8,128)(2,1)} %pad_maximum_fusion.16), channel_id=1, source_target_pairs={{0,2},{1,3},{2,0},{3,1},{4,6},{5,7},{6,4},{7,5},{8,10},{9,11},{10,... | collective-permute-start | bytes 2654216 | tf_op jit(solution)/shard_map/ppermute | solution.py:33
  214.3 62.3 %collective-permute-start.50 = (bf16[4,128,1536]{2,1,0:T(8,128)(2,1)S(1)}, bf16[4,128,1536]{2,1,0:T(8,128)(2,1)}, u32[]{:S(2)}, u32[]{:S(2)}) collective-permute-start(bf16[4,128,1536]{2,1,0:T(8,128)(2,1)S(1)} %bitcast.597), channel_id=1, source_target_pairs={{0,1},{1,0},{2,3},{3,2},{4,5},{5,4},{6,7},{7,6},{8,9},{9,8},{10,11... | collective-permute-start | bytes 4718600 | tf_op jit(solution)/shard_map/ppermute | solution.py:33
  296.1 53.4 %collective-permute-start.42 = (bf16[8,96,1024]{2,1,0:T(8,128)(2,1)S(1)}, bf16[8,96,1024]{2,1,0:T(8,128)(2,1)}, u32[]{:S(2)}, u32[]{:S(2)}) collective-permute-start(bf16[8,96,1024]{2,1,0:T(8,128)(2,1)S(1)} %pad_maximum_fusion.8.refs_0_), channel_id=1, source_target_pairs={{0,2},{1,3},{2,0},{3,1},{4,6},{5,7},{6,4},{7,5},{8,10},{9,11},{10,... | collective-permute-start | bytes 4718600 | tf_op jit(solution)/shard_map/ppermute | solution.py:33
  296.5 52.9 %collective-permute-start.43 = (bf16[8,64,1536]{2,1,0:T(8,128)(2,1)}, bf16[8,64,1536]{2,1,0:T(8,128)(2,1)}, u32[]{:S(2)}, u32[]{:S(2)}) collective-permute-start(bf16[8,64,1536]{2,1,0:T(8,128)(2,1)} %pad_maximum_fusion.9.refs_0_), channel_id=1, source_target_pairs={{0,4},{1,5},{2,6},{3,7},{4,0},{5,1},{6,2},{7,3},{8,12},{9,13},{10,... | collective-permute-start | bytes 4718600 | tf_op jit(solution)/shard_map/ppermute | solution.py:33
  306.7 42.8 %collective-permute-start.44 = (bf16[4,96,1024]{2,1,0:T(8,128)(2,1)}, bf16[4,96,1024]{2,1,0:T(8,128)(2,1)}, u32[]{:S(2)}, u32[]{:S(2)}) collective-permute-start(bf16[4,96,1024]{2,1,0:T(8,128)(2,1)} %pad_maximum_fusion.21), channel_id=1, source_target_pairs={{0,4},{1,5},{2,6},{3,7},{4,0},{5,1},{6,2},{7,3},{8,12},{9,13},{10,... | collective-permute-start | bytes 2359304 | tf_op jit(solution)/shard_map/ppermute | solution.py:33
  306.9 42.6 %collective-permute-start.45 = (bf16[4,64,1536]{2,1,0:T(8,128)(2,1)}, bf16[4,64,1536]{2,1,0:T(8,128)(2,1)}, u32[]{:S(2)}, u32[]{:S(2)}) collective-permute-start(bf16[4,64,1536]{2,1,0:T(8,128)(2,1)} %pad_maximum_fusion.22), channel_id=1, source_target_pairs={{0,2},{1,3},{2,0},{3,1},{4,6},{5,7},{6,4},{7,5},{8,10},{9,11},{10,... | collective-permute-start | bytes 2359304 | tf_op jit(solution)/shard_map/ppermute | solution.py:33
  358.6 71.7 %collective-permute-start.53 = (bf16[4,96,1024]{2,1,0:T(8,128)(2,1)}, bf16[4,96,1024]{2,1,0:T(8,128)(2,1)}, u32[]{:S(2)}, u32[]{:S(2)}) collective-permute-start(bf16[4,96,1024]{2,1,0:T(8,128)(2,1)} %pad_maximum_fusion.23), channel_id=1, source_target_pairs={{0,4},{1,5},{2,6},{3,7},{4,0},{5,1},{6,2},{7,3},{8,12},{9,13},{10,... | collective-permute-start | bytes 2359304 | tf_op jit(solution)/shard_map/ppermute | solution.py:33
  358.9 71.4 %collective-permute-start.54 = (bf16[4,64,1536]{2,1,0:T(8,128)(2,1)}, bf16[4,64,1536]{2,1,0:T(8,128)(2,1)}, u32[]{:S(2)}, u32[]{:S(2)}) collective-permute-start(bf16[4,64,1536]{2,1,0:T(8,128)(2,1)} %pad_maximum_fusion.24), channel_id=1, source_target_pairs={{0,2},{1,3},{2,0},{3,1},{4,6},{5,7},{6,4},{7,5},{8,10},{9,11},{10,... | collective-permute-start | bytes 2359304 | tf_op jit(solution)/shard_map/ppermute | solution.py:33
  371.1 59.2 %collective-permute-start.51 = (bf16[8,96,1024]{2,1,0:T(8,128)(2,1)}, bf16[8,96,1024]{2,1,0:T(8,128)(2,1)}, u32[]{:S(2)}, u32[]{:S(2)}) collective-permute-start(bf16[8,96,1024]{2,1,0:T(8,128)(2,1)} %pad_maximum_fusion.10.refs_0_), channel_id=1, source_target_pairs={{0,2},{1,3},{2,0},{3,1},{4,6},{5,7},{6,4},{7,5},{8,10},{9,11},{10,... | collective-permute-start | bytes 4718600 | tf_op jit(solution)/shard_map/ppermute | solution.py:33
  371.7 58.6 %collective-permute-start.52 = (bf16[8,64,1536]{2,1,0:T(8,128)(2,1)}, bf16[8,64,1536]{2,1,0:T(8,128)(2,1)}, u32[]{:S(2)}, u32[]{:S(2)}) collective-permute-start(bf16[8,64,1536]{2,1,0:T(8,128)(2,1)} %pad_maximum_fusion.11.refs_0_), channel_id=1, source_target_pairs={{0,4},{1,5},{2,6},{3,7},{4,0},{5,1},{6,2},{7,3},{8,12},{9,13},{10,... | collective-permute-start | bytes 4718600 | tf_op jit(solution)/shard_map/ppermute | solution.py:33
  450.0 56.1 %collective-permute-start.55 = (bf16[8,96,1024]{2,1,0:T(8,128)(2,1)}, bf16[8,96,1024]{2,1,0:T(8,128)(2,1)}, u32[]{:S(2)}, u32[]{:S(2)}) collective-permute-start(bf16[8,96,1024]{2,1,0:T(8,128)(2,1)} %pad_maximum_fusion.12.refs_0_), channel_id=1, source_target_pairs={{0,2},{1,3},{2,0},{3,1},{4,6},{5,7},{6,4},{7,5},{8,10},{9,11},{10,... | collective-permute-start | bytes 4718600 | tf_op jit(solution)/shard_map/ppermute | solution.py:33
  451.6 54.6 %collective-permute-start.56 = (bf16[8,64,1536]{2,1,0:T(8,128)(2,1)}, bf16[8,64,1536]{2,1,0:T(8,128)(2,1)}, u32[]{:S(2)}, u32[]{:S(2)}) collective-permute-start(bf16[8,64,1536]{2,1,0:T(8,128)(2,1)} %pad_maximum_fusion.13.refs_0_), channel_id=1, source_target_pairs={{0,4},{1,5},{2,6},{3,7},{4,0},{5,1},{6,2},{7,3},{8,12},{9,13},{10,... | collective-permute-start | bytes 4718600 | tf_op jit(solution)/shard_map/ppermute | solution.py:33
  451.8 66.0 %collective-permute-start.57 = (bf16[2,2,2,96,1024]{4,3,2,1,0:T(8,128)(2,1)}, bf16[2,2,2,96,1024]{4,3,2,1,0:T(8,128)(2,1)}, u32[]{:S(2)}, u32[]{:S(2)}) collective-permute-start(bf16[2,2,2,96,1024]{4,3,2,1,0:T(8,128)(2,1)} %dynamic-slice_bitcast_fusion.2), channel_id=1, source_target_pairs={{0,2},{1,3},{2,0},{3,1},{4,6},{5,7},{6,4},{7,5},{8,10},{9,11},{10,... | collective-permute-start | bytes 4718600 | tf_op jit(solution)/shard_map/ppermute | solution.py:33
  452.4 66.7 %collective-permute-start.58 = (bf16[2,2,2,64,1536]{4,3,1,0,2:T(8,128)(2,1)}, bf16[2,2,2,64,1536]{4,3,1,0,2:T(8,128)(2,1)}, u32[]{:S(2)}, u32[]{:S(2)}) collective-permute-start(bf16[2,2,2,64,1536]{4,3,1,0,2:T(8,128)(2,1)} %copy_bitcast_fusion.4), channel_id=1, source_target_pairs={{0,4},{1,5},{2,6},{3,7},{4,0},{5,1},{6,2},{7,3},{8,12},{9,13},{10,... | collective-permute-start | bytes 4718600 | tf_op jit(solution)/shard_map/ppermute | solution.py:33
  454.1 187.6 %collective-permute-start.69 = (bf16[2,4,128,1536]{3,2,1,0:T(8,128)(2,1)}, bf16[2,4,128,1536]{3,2,1,0:T(8,128)(2,1)}, u32[]{:S(2)}, u32[]{:S(2)}) collective-permute-start(bf16[2,4,128,1536]{3,2,1,0:T(8,128)(2,1)} %get-tuple-element.425), channel_id=1, source_target_pairs={{0,1},{1,0},{2,3},{3,2},{4,5},{5,4},{6,7},{7,6},{8,9},{9,8},{10,11... | collective-permute-start | bytes 9437192 | tf_op jit(solution)/shard_map/ppermute | solution.py:33
  529.9 67.2 %collective-permute-start.59 = (bf16[2,2,96,1024]{3,2,1,0:T(8,128)(2,1)}, bf16[2,2,96,1024]{3,2,1,0:T(8,128)(2,1)S(1)}, u32[]{:S(2)}, u32[]{:S(2)}) collective-permute-start(bf16[2,2,96,1024]{3,2,1,0:T(8,128)(2,1)} %fusion.19), channel_id=1, source_target_pairs={{0,4},{1,5},{2,6},{3,7},{4,0},{5,1},{6,2},{7,3},{8,12},{9,13},{10,... | collective-permute-start | bytes 2359304 | tf_op jit(solution)/shard_map/ppermute | solution.py:33
  530.2 66.9 %collective-permute-start.60 = (bf16[2,2,64,1536]{3,2,1,0:T(8,128)(2,1)}, bf16[2,2,64,1536]{3,2,1,0:T(8,128)(2,1)}, u32[]{:S(2)}, u32[]{:S(2)}) collective-permute-start(bf16[2,2,64,1536]{3,2,1,0:T(8,128)(2,1)} %get-tuple-element.399), channel_id=1, source_target_pairs={{0,2},{1,3},{2,0},{3,1},{4,6},{5,7},{6,4},{7,5},{8,10},{9,11},{10,... | collective-permute-start | bytes 2359304 | tf_op jit(solution)/shard_map/ppermute | solution.py:33
  541.5 55.7 %collective-permute-start.61 = (bf16[2,2,2,96,1024]{4,3,2,1,0:T(8,128)(2,1)}, bf16[2,2,2,96,1024]{4,3,2,1,0:T(8,128)(2,1)}, u32[]{:S(2)}, u32[]{:S(2)}) collective-permute-start(bf16[2,2,2,96,1024]{4,3,2,1,0:T(8,128)(2,1)} %dynamic-slice_bitcast_fusion.1), channel_id=1, source_target_pairs={{0,2},{1,3},{2,0},{3,1},{4,6},{5,7},{6,4},{7,5},{8,10},{9,11},{10,... | collective-permute-start | bytes 4718600 | tf_op jit(solution)/shard_map/ppermute | solution.py:33
  543.0 54.2 %collective-permute-start.62 = (bf16[2,2,2,64,1536]{4,3,1,0,2:T(8,128)(2,1)}, bf16[2,2,2,64,1536]{4,3,1,0,2:T(8,128)(2,1)}, u32[]{:S(2)}, u32[]{:S(2)}) collective-permute-start(bf16[2,2,2,64,1536]{4,3,1,0,2:T(8,128)(2,1)} %copy_bitcast_fusion.3), channel_id=1, source_target_pairs={{0,4},{1,5},{2,6},{3,7},{4,0},{5,1},{6,2},{7,3},{8,12},{9,13},{10,... | collective-permute-start | bytes 4718600 | tf_op jit(solution)/shard_map/ppermute | solution.py:33
  597.1 44.9 %collective-permute-start.70 = (bf16[2,4,128,1536]{3,2,1,0:T(8,128)(2,1)}, bf16[2,4,128,1536]{3,2,1,0:T(8,128)(2,1)}, u32[]{:S(2)}, u32[]{:S(2)}) collective-permute-start(bf16[2,4,128,1536]{3,2,1,0:T(8,128)(2,1)} %get-tuple-element.427), channel_id=1, source_target_pairs={{0,1},{1,0},{2,3},{3,2},{4,5},{5,4},{6,7},{7,6},{8,9},{9,8},{10,11... | collective-permute-start | bytes 9437192 | tf_op jit(solution)/shard_map/ppermute | solution.py:33
  597.2 45.3 %collective-permute-start.71 = (bf16[2,4,128,1536]{3,2,1,0:T(8,128)(2,1)}, bf16[2,4,128,1536]{3,2,1,0:T(8,128)(2,1)}, u32[]{:S(2)}, u32[]{:S(2)}) collective-permute-start(bf16[2,4,128,1536]{3,2,1,0:T(8,128)(2,1)} %get-tuple-element.429), channel_id=1, source_target_pairs={{0,1},{1,0},{2,3},{3,2},{4,5},{5,4},{6,7},{7,6},{8,9},{9,8},{10,11... | collective-permute-start | bytes 9437192 | tf_op jit(solution)/shard_map/ppermute | solution.py:33
  642.0 52.7 %collective-permute-start.67 = (bf16[2,2,2,96,1024]{4,3,2,1,0:T(8,128)(2,1)}, bf16[2,2,2,96,1024]{4,3,2,1,0:T(8,128)(2,1)}, u32[]{:S(2)}, u32[]{:S(2)}) collective-permute-start(bf16[2,2,2,96,1024]{4,3,2,1,0:T(8,128)(2,1)} %dynamic-slice_bitcast_fusion), channel_id=1, source_target_pairs={{0,2},{1,3},{2,0},{3,1},{4,6},{5,7},{6,4},{7,5},{8,10},{9,11},{10,... | collective-permute-start | bytes 4718600 | tf_op jit(solution)/shard_map/ppermute | solution.py:33
  642.5 52.2 %collective-permute-start.68 = (bf16[2,2,2,64,1536]{4,3,1,0,2:T(8,128)(2,1)}, bf16[2,2,2,64,1536]{4,3,1,0,2:T(8,128)(2,1)}, u32[]{:S(2)}, u32[]{:S(2)}) collective-permute-start(bf16[2,2,2,64,1536]{4,3,1,0,2:T(8,128)(2,1)} %copy_bitcast_fusion.2), channel_id=1, source_target_pairs={{0,4},{1,5},{2,6},{3,7},{4,0},{5,1},{6,2},{7,3},{8,12},{9,13},{10,... | collective-permute-start | bytes 4718600 | tf_op jit(solution)/shard_map/ppermute | solution.py:33
  762.3 47.5 %collective-permute-start.84 = (bf16[2,64,1536]{2,1,0:T(8,128)(2,1)}, bf16[2,64,1536]{2,1,0:T(8,128)(2,1)}, u32[]{:S(2)}, u32[]{:S(2)}) collective-permute-start(bf16[2,64,1536]{2,1,0:T(8,128)(2,1)} %get-tuple-element.457), channel_id=1, source_target_pairs={{0,8},{1,9},{2,10},{3,11},{4,12},{5,13},{6,14},{7,15},{8,0},{9,1},... | collective-permute-start | bytes 1179656 | tf_op jit(solution)/shard_map/ppermute | solution.py:33
  764.8 45.1 %collective-permute-start.83 = (bf16[2,96,1024]{1,2,0:T(8,128)(2,1)}, bf16[2,96,1024]{1,2,0:T(8,128)(2,1)}, u32[]{:S(2)}, u32[]{:S(2)}) collective-permute-start(bf16[2,96,1024]{1,2,0:T(8,128)(2,1)} %get-tuple-element.456), channel_id=1, source_target_pairs={{0,8},{1,9},{2,10},{3,11},{4,12},{5,13},{6,14},{7,15},{8,0},{9,1},... | collective-permute-start | bytes 1179656 | tf_op jit(solution)/shard_map/ppermute | solution.py:33
  764.8 45.1 %collective-permute-start.79 = (bf16[2,2,2,48,768]{4,3,0,1,2:T(8,128)(2,1)}, bf16[2,2,2,48,768]{4,3,0,1,2:T(8,128)(2,1)}, u32[]{:S(2)}, u32[]{:S(2)}) collective-permute-start(bf16[2,2,2,48,768]{4,3,0,1,2:T(8,128)(2,1)} %copy_bitcast_fusion.6), channel_id=1, source_target_pairs={{0,2},{1,3},{2,0},{3,1},{4,6},{5,7},{6,4},{7,5},{8,10},{9,11},{10,... | collective-permute-start | bytes 1769480 | tf_op jit(solution)/shard_map/ppermute | solution.py:33
  765.5 44.3 %collective-permute-start.80 = (bf16[2,2,2,48,768]{4,3,1,0,2:T(8,128)(2,1)}, bf16[2,2,2,48,768]{4,3,1,0,2:T(8,128)(2,1)}, u32[]{:S(2)}, u32[]{:S(2)}) collective-permute-start(bf16[2,2,2,48,768]{4,3,1,0,2:T(8,128)(2,1)} %copy_bitcast_fusion.5), channel_id=1, source_target_pairs={{0,4},{1,5},{2,6},{3,7},{4,0},{5,1},{6,2},{7,3},{8,12},{9,13},{10,... | collective-permute-start | bytes 1769480 | tf_op jit(solution)/shard_map/ppermute | solution.py:33
  860.4 40.8 %collective-permute-start.89 = (bf16[2,2,2,96,1152]{4,3,1,0,2:T(8,128)(2,1)}, bf16[2,2,2,96,1152]{4,3,1,0,2:T(8,128)(2,1)}, u32[]{:S(2)}, u32[]{:S(2)}) collective-permute-start(bf16[2,2,2,96,1152]{4,3,1,0,2:T(8,128)(2,1)} %copy_bitcast_fusion.1), channel_id=1, source_target_pairs={{0,2},{1,3},{2,0},{3,1},{4,6},{5,7},{6,4},{7,5},{8,10},{9,11},{10,... | collective-permute-start | bytes 5308424 | tf_op jit(solution)/shard_map/ppermute | solution.py:33
  872.0 43.0 %collective-permute-start.114 = (f32[48,16,3,64]{3,1,2,0:T(8,128)S(1)}, f32[48,16,3,64]{3,1,2,0:T(8,128)S(1)}, u32[]{:S(2)}, u32[]{:S(2)}) collective-permute-start(f32[48,16,3,64]{3,1,2,0:T(8,128)S(1)} %dynamic-slice_bitcast_fusion.3), channel_id=1, source_target_pairs={{0,1},{1,0},{2,3},{3,2},{4,5},{5,4},{6,7},{7,6},{8,9},{9,8},{10,11... | collective-permute-start | bytes 1769480 | tf_op jit(solution)/shard_map/ppermute | solution.py:33
  912.0 44.9 %collective-permute-start.94 = (bf16[2,2,96,1152]{3,2,1,0:T(8,128)(2,1)}, bf16[2,2,96,1152]{3,2,1,0:T(8,128)(2,1)}, u32[]{:S(2)}, u32[]{:S(2)}) collective-permute-start(bf16[2,2,96,1152]{3,2,1,0:T(8,128)(2,1)} %get-tuple-element.480), channel_id=1, source_target_pairs={{0,4},{1,5},{2,6},{3,7},{4,0},{5,1},{6,2},{7,3},{8,12},{9,13},{10,... | collective-permute-start | bytes 2654216 | tf_op jit(solution)/shard_map/ppermute | solution.py:33
  912.4 44.5 %collective-permute-start.95 = (bf16[2,2,96,1152]{3,2,1,0:T(8,128)(2,1)}, bf16[2,2,96,1152]{3,2,1,0:T(8,128)(2,1)}, u32[]{:S(2)}, u32[]{:S(2)}) collective-permute-start(bf16[2,2,96,1152]{3,2,1,0:T(8,128)(2,1)} %get-tuple-element.481), channel_id=1, source_target_pairs={{0,2},{1,3},{2,0},{3,1},{4,6},{5,7},{6,4},{7,5},{8,10},{9,11},{10,... | collective-permute-start | bytes 2654216 | tf_op jit(solution)/shard_map/ppermute | solution.py:33
  (210 other events, 3033.6 us)

commit v5 on v4

--- a/solution.py
+++ b/solution.py
@@ -162,6 +162,28 @@
         arriving = yield leaving, bit
         held = [staying, arriving]
     return held[0].astype(full) + held[1].astype(full)
+
+
+def halving_steps(leaving, staying, order):
+    arriving = yield leaving, order[0]
+    for bit in order[1:]:
+        half = staying.shape[0] // 2
+        leaving, staying = [
+            (staying[at].astype(full) + arriving[at].astype(full)).astype(low)
+            for at in (slice(half, None), slice(half))
+        ]
+        arriving = yield leaving, bit
+    return (staying.astype(full) + arriving.astype(full))[0]
+
+
+def owners(colour, chip, chip_bits):
+    order = gather_order(chip_bits, colour)
+    spots = jnp.arange(1 << chip_bits)
+    bits = list(enumerate(order))
+    owner = sum((jnp.bitwise_and(spots >> at, 1) << bit) for at, bit in bits)
+    apart = jnp.bitwise_xor(spots, chip)
+    place = sum((jnp.bitwise_and(apart >> bit, 1) << at) for at, bit in bits)
+    return jnp.bitwise_xor(owner, chip), place
 
 
 def scatter_flow(parts, colour, chip, chip_bits, sent=low):
@@ -376,29 +398,49 @@
 
 
 def feed_body(
-    core_ref,
+    spread,
+    words_ref,
     norm_ref,
     norm_t_ref,
     grad_ref,
-    up_ref,
-    down_ref,
-    kernel_ref,
-    staying_ref,
-    leaving_ref,
-    up_grad_ref,
-    down_grad_ref,
-    kernel_grad_ref,
-    branch_acc,
-    back_acc,
-    hidden,
-    widened_grad,
-    act_grad,
-    act,
-    hidden_grad,
+    *refs,
 ):
+    pieces = 2 if spread else 1
+    up_refs, refs = refs[:pieces], refs[pieces:]
+    down_refs, refs = refs[:pieces], refs[pieces:]
+    kernel_ref, staying_ref, leaving_ref, *refs = refs
+    up_grad_refs, refs = refs[:pieces], refs[pieces:]
+    down_grad_refs, refs = refs[:pieces], refs[pieces:]
+    kernel_grad_ref, branch_acc, back_acc, hidden, widened_grad, act_grad, act, hidden_grad = refs[
+        :8
+    ]
     step = pl.program_id(0)
+    core = words_ref[0]
     by_columns = (((1,), (1,)), ((), ()))
-    width = up_ref.shape[1]
+    width = kernel_ref.shape[1]
+    model = norm_t_ref.shape[0]
+    up_ref, down_ref = up_refs[0], down_refs[0]
+    if spread:
+        up_ref, down_all = refs[8:]
+        half, share, _ = up_refs[0].shape
+        piece = down_refs[0].shape[1]
+        chips = 2 * half
+        down_ref = down_all.at[pl.ds(pl.multiple_of(step * width, width), width), :]
+
+        for which in range(2):
+
+            @pl.loop(0, half)
+            def _(spot):
+                start = pl.multiple_of(words_ref[1 + which * half + spot] * share, share)
+                up_ref[pl.ds(start, share), :] = up_refs[which][spot]
+
+            @pl.when(step == 0)
+            def _():
+                @pl.loop(0, half)
+                def _(spot):
+                    owner = words_ref[1 + chips + which * half + spot]
+                    start = pl.multiple_of(owner * piece, piece)
+                    down_all[pl.ds(start, piece), :] = down_refs[which][spot]
 
     @pl.when(step == 0)
     def _():
@@ -475,45 +517,80 @@
             hidden_grad[rows, :], up_ref[...], by_columns, preferred_element_type=full
         )
 
-    model = norm_t_ref.shape[0]
-
-    @pl.loop(0, model // TILE)
-    def _(tile):
-        rows = pl.ds(pl.multiple_of(tile * TILE, TILE), TILE)
-        up_grad_ref[rows, :] = jnp.dot(
-            norm_t_ref[rows, :], hidden_grad[...], preferred_element_type=full
-        ).astype(low)
-
-    down_grad_ref[...] = lax.dot_general(
+    if spread:
+        for which in range(2):
+
+            @pl.loop(0, half // 4)
+            def _(group):
+                lhs = []
+                for k in range(4):
+                    owner = words_ref[1 + which * half + 4 * group + k]
+                    start = pl.multiple_of(owner * share, share)
+                    lhs.append(norm_t_ref[pl.ds(start, share), :])
+                result = jnp.dot(
+                    jnp.concatenate(lhs, axis=0), hidden_grad[...], preferred_element_type=full
+                ).astype(low)
+                for k in range(4):
+                    up_grad_refs[which][4 * group + k] = result[k * share : (k + 1) * share]
+
+    else:
+
+        @pl.loop(0, model // TILE)
+        def _(tile):
+            rows = pl.ds(pl.multiple_of(tile * TILE, TILE), TILE)
+            up_grad_refs[0][rows, :] = jnp.dot(
+                norm_t_ref[rows, :], hidden_grad[...], preferred_element_type=full
+            ).astype(low)
+
+    down_grad = lax.dot_general(
         act[...], grad_ref[...], (((0,), (0,)), ((), ())), preferred_element_type=full
     ).astype(low)
+    if spread:
+        for k in range(width // piece):
+            place = words_ref[1 + 2 * chips + step * (width // piece) + k]
+            for which in range(2):
+
+                @pl.when(place // half == which)
+                def _():
+                    down_grad_refs[which][place - which * half] = down_grad[
+                        k * piece : (k + 1) * piece
+                    ]
+
+    else:
+        down_grad_refs[0][...] = down_grad
 
     @pl.when(step == pl.num_programs(0) - 1)
     def _():
-        for ref, which in ((staying_ref, core_ref[0]), (leaving_ref, 1 - core_ref[0])):
+        for ref, which in ((staying_ref, core), (leaving_ref, 1 - core)):
             for index, acc in enumerate((branch_acc, back_acc)):
                 for plane in range(4):
                     start = plane * PLANE + pl.multiple_of(which * (PLANE // 2), PLANE // 2)
                     ref[index, plane] = acc[pl.ds(start, PLANE // 2), :].astype(low)
 
 
-def feed_forward(norm, norm_t, grad, up, down, kernel, core):
+def feed_forward(norm, norm_t, grad, up, down, kernel, words):
     tokens, model = norm.shape
-    channels = up.shape[1]
+    channels = kernel.shape[1]
     width = TILE
+    spread = len(up) == 2
     whole = lambda j, words: (0, 0)
     half = lambda j, words: (0, 0, 0, 0)
     across = lambda j, words: (0, j)
-    down_rows = lambda j, words: (j, 0)
     once = pl.Buffered(1)
-    grads = [
-        jax.ShapeDtypeStruct((model, channels), low),
-        jax.ShapeDtypeStruct((channels, model), low),
-        jax.ShapeDtypeStruct((16, channels), full),
-    ]
+    piece_scratch = []
+    if spread:
+        deep = lambda j, words: (0, 0, 0)
+        up_spec = pl.BlockSpec(up[0].shape[:2] + (width,), lambda j, words: (0, 0, j))
+        down_spec = pl.BlockSpec(down[0].shape, deep, pipeline_mode=once)
+        down_grad_spec = pl.BlockSpec(down[0].shape, deep)
+        piece_scratch = [pltpu.VMEM((model, width), low), pltpu.VMEM((channels, model), low)]
+    else:
+        up_spec = pl.BlockSpec((model, width), across)
+        down_spec = down_grad_spec = pl.BlockSpec((width, model), lambda j, words: (j, 0))
     halves = jax.ShapeDtypeStruct((2, 4, PLANE // 2, model), low)
-    return pl.pallas_call(
-        feed_body,
+    like = lambda arrays: [jax.ShapeDtypeStruct(array.shape, low) for array in arrays]
+    out = pl.pallas_call(
+        functools.partial(feed_body, spread),
         grid_spec=pltpu.PrefetchScalarGridSpec(
             num_scalar_prefetch=1,
             grid=(channels // width,),
@@ -521,15 +598,15 @@
                 pl.BlockSpec((tokens, model), whole, pipeline_mode=once),
                 pl.BlockSpec((model, tokens), whole, pipeline_mode=once),
                 pl.BlockSpec((tokens, model), whole, pipeline_mode=once),
-                pl.BlockSpec((model, width), across),
-                pl.BlockSpec((width, model), down_rows),
+                *[up_spec] * len(up),
+                *[down_spec] * len(down),
                 pl.BlockSpec((16, width), across),
             ],
             out_specs=[
                 pl.BlockSpec(halves.shape, half),
                 pl.BlockSpec(halves.shape, half),
-                pl.BlockSpec((model, width), across),
-                pl.BlockSpec((width, model), down_rows),
+                *[up_spec] * len(up),
+                *[down_grad_spec] * len(down),
                 pl.BlockSpec((16, width), across),
             ],
             scratch_shapes=[
@@ -540,17 +617,23 @@
                 pltpu.VMEM((tokens, width), full),
                 pltpu.VMEM((tokens, width), low),
                 pltpu.VMEM((tokens, width), low),
-            ],
+            ]
+            + piece_scratch,
         ),
-        out_shape=[halves, halves] + grads,
-        compiler_params=pltpu.CompilerParams(vmem_limit_bytes=62 * 1024 * 1024),
+        out_shape=[halves, halves]
+        + like(up)
+        + like(down)
+        + [jax.ShapeDtypeStruct((16, channels), full)],
+        compiler_params=pltpu.CompilerParams(vmem_limit_bytes=63 * 1024 * 1024),
         cost_estimate=pl.CostEstimate(
             flops=12 * tokens * model * channels,
             bytes_accessed=8 * model * channels + 10 * tokens * model,
             transcendentals=tokens * channels,
         ),
         name="feed_forward",
-    )(core[None].astype(jnp.int32), norm, norm_t, grad, up, down, kernel)
+    )(words, norm, norm_t, grad, *up, *down, kernel)
+    staying, leaving, *grads, kernel_grad = out
+    return staying, leaving, grads[: len(up)], grads[len(up) :], kernel_grad
 
 
 def token_stats(x_ref, average, scale):
@@ -861,17 +944,19 @@
     ]
     mods_flow = scatter_flow(mods_part, 0, chip, chip_bits, sent=full)
     qkv_flows = [flow(qkv_rows[:, :qkv_half], 0), flow(qkv_rows[:, qkv_half:], 1)]
-    slot(qkv_flows + [mods_flow])
-
-    tokens, cotangent, up_weight, proj_weight, ffn_kernel, attn_kernel = slot.after(
-        tokens, cotangent, up_weight, proj_weight, ffn_kernel, attn_kernel
+    mine, upstream = slot(
+        qkv_flows + [mods_flow],
+        lambda: (to_phases(tokens[0], half_rows), to_phases(cotangent[0], half_rows)),
+    )
+
+    up_weight, proj_weight, ffn_kernel, attn_kernel = slot.after(
+        up_weight, proj_weight, ffn_kernel, attn_kernel
     )
     up_split = up_weight.reshape(part, chips, 2, CHUNKS, piece).transpose(0, 2, 3, 1, 4)
     up_rows = row_pair(up_split.reshape(part, 2, CHUNKS, chips * piece), 1)
     proj_there = [(r, r % chips * 2 + r // chips) for r in range(devices)]
     proj_back = [(b, a) for a, b in proj_there]
     proj_rows = lax.ppermute(proj_weight, AXES, proj_there)
-    mine = to_phases(tokens[0], half_rows)
     canvas = join_halves(mine, swap_core(mine), core)
 
     slot(qkv_flows + [mods_flow])
@@ -913,8 +998,7 @@
         qkv_flows + proj_flows + feed_flows[0], lambda: conv_in(canvas, attn_taps, mods_a)
     )
 
-    (cotangent,) = slot.after(cotangent)
-    upstream = to_phases(cotangent[0], half_rows)
+    (upstream,) = slot.after(upstream)
     grad_ph = join_halves(upstream, swap_core(upstream), core)
 
     def project_in():
@@ -956,14 +1040,19 @@
     kept = []
     grads = [None] * CHUNKS
 
+    spread = 2 * part % STRIP == 0 and piece % STRIP == 0 and chips >= 8
+    up_owner, _ = owners(0, chip, chip_bits)
+    down_owner, down_place = owners(1, chip, chip_bits)
+    words = jnp.concatenate([core[None], up_owner, down_owner, down_place]).astype(jnp.int32)
+
     def feed(t):
         def work():
-            up, down = joined(feed_flows[t])
-            staying, leaving, *grads_now = feed_forward(
-                norm, norm_t, grad_branch_f, up.reshape(model, -1), down.reshape(-1, model),
-                ffn_taps[t], core,
-            )
-            return staying, leaving, grads_now
+            if spread:
+                up, down = [f.result for f in feed_flows[t]]
+            else:
+                up, down = joined(feed_flows[t])
+                up, down = [up.reshape(model, -1)], [down.reshape(-1, model)]
+            return feed_forward(norm, norm_t, grad_branch_f, up, down, ffn_taps[t], words)
 
         return work
 
@@ -971,12 +1060,19 @@
 
     def run_feed(flows, t):
         slot.finish(feed_flows[t])
-        staying, leaving, grads[t] = slot(flows, feed(t))
+        staying, leaving, up_grad, down_grad, tap_grad = slot(flows, feed(t))
         kept.append((staying, leaving))
-        back_flows[t] = [
-            sums(grads[t][0].reshape(chips, 2 * part, -1), 0),
-            sums(grads[t][1].reshape(chips, piece, model), 1),
-        ]
+        grads[t] = tap_grad
+        if spread:
+            back_flows[t] = [
+                Flow(halving_steps(*grad[::-1], gather_order(chip_bits, colour)[::-1]))
+                for colour, grad in enumerate((up_grad, down_grad))
+            ]
+        else:
+            back_flows[t] = [
+                sums(up_grad[0].reshape(chips, 2 * part, -1), 0),
+                sums(down_grad[0].reshape(chips, piece, model), 1),
+            ]
 
     run_feed(feed_flows[1] + feed_flows[2], 0)
     run_feed(feed_flows[2] + back_flows[0], 1)
@@ -1052,7 +1148,7 @@
     slot.finish(sum(back_flows, proj_flows + qkv_flows))
     up_shares = [flows[0].result for flows in back_flows]
     down_shares = [flows[1].result for flows in back_flows]
-    tap_grads = [g[2][:9].reshape(9, chips, piece) for g in grads]
+    tap_grads = [g[:9].reshape(9, chips, piece) for g in grads]
     qkv_share = jnp.concatenate([f.result for f in qkv_flows], axis=1)
     proj_share = jnp.concatenate([f.result for f in proj_flows], axis=1)
     proj_share = lax.ppermute(proj_share, AXES, proj_back)

time: 1060 us -> 970 us (0.915)
  waiting for transfers between devices: 243 us -> 197 us
  local copies, waits for them, and re-layouts: 167 us -> 137 us
  Pallas kernels: 297 us -> 272 us
    ppermute x113, waiting for transfers between devices: 243 us -> 197 us  [swap(): lax.ppermute(x, AXES, [(i, i ^ 1 << bit) for i in range(device_count())])]
    pallas_call x10 -> x4, Pallas kernels: 52.1 us -> 19.8 us  [assemble(): pl.pallas_call(functools.partial(assemble_body, steps), grid_spec=pltpu.P...]
    convert_element_type x0 -> x18, other arithmetic: none -> 30.7 us  [halving_steps(): (staying[at].astype(full) + arriving[at].astype(full)).astype(low)]
    convert_element_type x20 -> x8, other arithmetic: 44 us -> 15.4 us  [scatter_steps(): sum((at_bit(h, axis, mine).astype(full) for h in held)).astype(sent)]
    optimization_barrier x7 -> x1, local copies, waits for them, and re-layouts: 21.1 us -> 4.67 us  [__call__(): lax.optimization_barrier((arriving, work(), self.token))]
    convert_element_type x15 -> x6, other arithmetic: 19.8 us -> 6.17 us  [scatter_steps(): sum((at_bit(h, axis, 1 - mine).astype(full) for h in held)).astype(sent)]
    unnamed x267 -> x242, local copies, waits for them, and re-layouts: 24.5 us -> 17 us
  transfers between devices with their start and end apart: 115 -> 115, of which waited for: 39 -> 33; matrix products, arithmetic and copies ran while one was open for 29% -> 32% of each run, Pallas kernels for 27% -> 28%
where the time goes in v5:
time: 970 us; the launch traced here: 960 us
  Pallas kernels  272 us (28%)
  waiting for transfers between devices  197 us (20%)
  other arithmetic  187 us (19%)
  local copies, waits for them, and re-layouts  137 us (14%)
  starting transfers between devices  118 us (12%)
  matrix products  47.2 us (5%)
    ppermute x113, waiting for transfers between devices, swap(): lax.ppermute(x, AXES, [(i, i ^ 1 << bit) for i in range(device_count())])  197 us
    pallas_call x3, Pallas kernels, feed_forward(): pl.pallas_call(functools.partial(feed_body, spread), grid_spec=pltpu.Pref...  164 us
    ppermute x113, starting transfers between devices, swap(): lax.ppermute(x, AXES, [(i, i ^ 1 << bit) for i in range(device_count())])  110 us
    concatenate x28, other arithmetic, gather_steps(): held = jnp.concatenate([held, arriving], axis=0)  54.4 us
    convert_element_type x18, other arithmetic, halving_steps(): (staying[at].astype(full) + arriving[at].astype(full)).astype(low)  30.7 us
    pallas_call x1, Pallas kernels, attend_back(): pl.pallas_call(attend_back_body, grid=(pairs,), in_specs=[pl.BlockSpec((P...  28.9 us
    pallas_call x1, Pallas kernels, conv_in(): pl.pallas_call(conv_in_body, grid=(model // TILE,), in_specs=[pl.BlockSpe...  22.8 us
    pallas_call x1, Pallas kernels, conv_back(): pl.pallas_call(conv_back_body, grid_spec=pltpu.PrefetchScalarGridSpec(num...  21.2 us
  transfers between devices with their start and end apart: 115, of which 33 were waited for; matrix products, arithmetic and copies ran while one was open for 32% of the time, Pallas kernels for 28%

profile of v5, /device:TPU:0, one launch (start us, length us, event | category | flops | bytes accessed | tf_op | source)
XLA Modules:
  0.0 960.1 jit_solution(8121798506320093141)
XLA Ops:
  31.2 15.0 %collective-permute-done.1 = bf16[1,96,1152]{2,1,0:T(8,128)(2,1)S(1)} collective-permute-done((bf16[1,96,1152]{2,1,0:T(8,128)(2,1)S(1)}, bf16[1,96,1152]{2,1,0:T(8,128)(2,1)S(1)}, u32[]{:S(2)}, u32[]{:S(2)}) %collective-permute-start.1) | collective-permute-done | bytes 221216 | tf_op jit(solution)/shard_map/ppermute | solution.py:33
  118.2 4.8 collective-permute-done.12
  152.8 22.8 %conv_in.1 = bf16[1024,1536]{1,0:T(8,128)(2,1)} custom-call(bf16[1024,1536]{1,0:T(8,128)(2,1)} %bitcast.399, f32[16,1536]{1,0:T(8,128)} %pad_convert_fusion.1.kernel_ref, f32[8,1536]{1,0:T(8,128)} %maximum_maximum_fusion.mods_ref), custom_call_target="tpu_custom_call" | custom-call | flops 47185920 | bytes 6291456 | tf_op jit(solution)/shard_map/conv_in/pallas_call | solution.py:700
  175.7 5.2 collective-permute-done.15.refs_1_
  192.4 5.6 assemble.5
  198.0 5.6 assemble.4
  203.6 12.7 %convolution_convert_fusion.2.qkv_ref = bf16[1024,2304]{1,0:T(8,128)(2,1)} fusion(bf16[1024,1536]{1,0:T(8,128)(2,1)} %conv_in.1, bf16[1536,1152]{1,0:T(8,128)(2,1)} %bitcast.401, bf16[1536,1152]{1,0:T(8,128)(2,1)} %bitcast.403), kind=kOutput, calls=%fused_computation.6 | convolution fusion | flops 7264272384 | bytes 14942208 | tf_op jit(solution)/shard_map/dot_general | solution.py:1008
  219.4 6.4 pad_maximum_fusion
  252.1 15.4 %attend.1 = bf16[1024,768]{1,0:T(8,128)(2,1)} custom-call(f32[256,256]{1,0:T(8,128)} %compare_convert_fusion.mask_ref, bf16[1024,2304]{1,0:T(8,128)(2,1)} %convolution_convert_fusion.2.qkv_ref), custom_call_target="tpu_custom_call" | custom-call | flops 3221225472 | bytes 6291456 | tf_op jit(solution)/shard_map/attend/pallas_call | solution.py:334
  276.7 4.7 fusion.87
  317.2 8.6 copy.231
  325.8 6.3 reshape.488
  332.1 22.6 %collective-permute-done.44 = bf16[4,96,1024]{2,1,0:T(8,128)(2,1)} collective-permute-done((bf16[4,96,1024]{2,1,0:T(8,128)(2,1)}, bf16[4,96,1024]{2,1,0:T(8,128)(2,1)}, u32[]{:S(2)}, u32[]{:S(2)}) %collective-permute-start.44) | collective-permute-done | bytes 786464 | tf_op jit(solution)/shard_map/ppermute | solution.py:33
  367.6 4.7 copy.236.norm_ref
  372.3 54.5 %feed_forward.3 = (bf16[2,4,128,1536]{3,2,1,0:T(8,128)(2,1)}, bf16[2,4,128,1536]{3,2,1,0:T(8,128)(2,1)}, bf16[8,96,1024]{2,1,0:T(8,128)(2,1)}, bf16[8,96,1024]{2...) custom-call(s32[49]{0:T(128)} %pad_add_fusion.1.words_ref, ...), custom_call_target="tpu_custom_call" | custom-call | flops 19327352832 | bytes 28311552 | tf_op jit(solution)/shard_map/feed_forward/pallas_call | solution.py:592
  436.1 54.3 %feed_forward.4 = (bf16[2,4,128,1536]{3,2,1,0:T(8,128)(2,1)}, bf16[2,4,128,1536]{3,2,1,0:T(8,128)(2,1)}, bf16[8,96,1024]{2,1,0:T(8,128)(2,1)}, bf16[8,96,1024]{2...) custom-call(s32[49]{0:T(128)} %pad_add_fusion.1.words_ref, ...), custom_call_target="tpu_custom_call" | custom-call | flops 19327352832 | bytes 28311552 | tf_op jit(solution)/shard_map/feed_forward/pallas_call | solution.py:592
  490.4 9.7 %collective-permute-done.57 = bf16[8,96,1024]{2,1,0:T(8,128)(2,1)} collective-permute-done((bf16[8,96,1024]{2,1,0:T(8,128)(2,1)}, bf16[8,96,1024]{2,1,0:T(8,128)(2,1)}, u32[]{:S(2)}, u32[]{:S(2)}) %collective-permute-start.57) | collective-permute-done | bytes 1572896 | tf_op jit(solution)/shard_map/ppermute | solution.py:33
  511.2 54.7 %feed_forward.5 = (bf16[2,4,128,1536]{3,2,1,0:T(8,128)(2,1)}, bf16[2,4,128,1536]{3,2,1,0:T(8,128)(2,1)}, bf16[8,96,1024]{2,1,0:T(8,128)(2,1)}, bf16[8,96,1024]{2...) custom-call(s32[49]{0:T(128)} %pad_add_fusion.1.words_ref, ...), custom_call_target="tpu_custom_call" | custom-call | flops 19327352832 | bytes 28311552 | tf_op jit(solution)/shard_map/feed_forward/pallas_call | solution.py:592
  592.1 7.8 add_add_fusion
  614.6 27.1 %collective-permute-done.66 = bf16[4,64,1536]{2,1,0:T(8,128)(2,1)} collective-permute-done((bf16[4,64,1536]{2,1,0:T(8,128)(2,1)}, bf16[4,64,1536]{2,1,0:T(8,128)(2,1)}, u32[]{:S(2)}, u32[]{:S(2)}) %collective-permute-start.66) | collective-permute-done | bytes 786464 | tf_op jit(solution)/shard_map/ppermute | solution.py:33
  671.8 8.0 collective-permute-done.75
  691.0 28.9 %attend_back.1 = bf16[1024,2304]{1,0:T(8,128)(2,1)} custom-call(f32[256,256]{1,0:T(8,128)} %compare_convert_fusion.mask_ref, bf16[1024,2304]{1,0:T(8,128)(2,1)} %convolution_convert_fusion.2.qkv_ref, bf16[1024,768]{1,0:T(8,128)(2,1)} %convolution_convert_fusion.6.grad_ref), custom_call_target="tpu_custom_call" | custom-call | flops 8053063680 | bytes 11010048 | tf_op jit(solution)/shard_map/attend_back/pallas_call | solution.py:355
  725.8 4.8 collective-permute-done.82
  738.9 10.5 %convolution_convert_fusion = bf16[1536,2304]{1,0:T(8,128)(2,1)S(1)} fusion(bf16[1024,1536]{1,0:T(8,128)(2,1)S(1)} %copy-done.25, bf16[1024,2304]{1,0:T(8,128)(2,1)} %attend_back.1), kind=kOutput, calls=%fused_computation | convolution fusion | flops 7251296256 | bytes 14942208 | tf_op jit(solution)/shard_map/dot_general | solution.py:1119
  749.5 7.7 convolution_convert_fusion.3
  784.5 24.2 %collective-permute-done.89 = bf16[2,2,2,96,1152]{4,3,1,0,2:T(8,128)(2,1)} collective-permute-done((bf16[2,2,2,96,1152]{4,3,1,0,2:T(8,128)(2,1)}, bf16[2,2,2,96,1152]{4,3,1,0,2:T(8,128)(2,1)}, u32[]{:S(2)}, u32[]{:S(2)}) %collective-permute-start.89) | collective-permute-done | bytes 1769504 | tf_op jit(solution)/shard_map/ppermute | solution.py:33
  828.4 21.2 %conv_back.1 = (f32[512,1536]{1,0:T(8,128)}, f32[16,1536]{1,0:T(8,128)}, f32[8,1536]{1,0:T(8,128)}) custom-call(s32[1]{0:T(128)} %bitcast.43.core_ref, bf16[576,1536]{1,0:T(8,128)(2,1)} %bitcast.420, bf16[576,1536]{1,0:T(8,128)(2,1)} %bitcast.421, bf16[576,1536]{1,0:T(8,128)(2,1)} %collective-permute-done.93.arriving_ref, ...), custom_call_target="tpu_custom_call" | custom-call | flops 55050240 | bytes 11010048 | tf_op jit(solution)/shard_map/conv_back/pallas_call | solution.py:849
  849.6 6.0 copy.254
  855.6 5.3 reshape.504
  882.5 13.3 %collective-permute-done.99 = bf16[1,9216]{1,0:T(2,128)(2,1)S(1)} collective-permute-done((bf16[1,9216]{1,0:T(2,128)(2,1)S(1)}, bf16[1,9216]{1,0:T(2,128)(2,1)S(1)}, u32[]{:S(2)}, u32[]{:S(2)}) %collective-permute-start.99) | collective-permute-done | bytes 18464 | tf_op jit(solution)/shard_map/ppermute | solution.py:33
  919.5 4.8 reshape.513
  932.6 14.0 %collective-permute-done.110 = bf16[96,1152]{1,0:T(8,128)(2,1)S(1)} collective-permute-done((bf16[96,1152]{1,0:T(8,128)(2,1)S(1)}, bf16[96,1152]{1,0:T(8,128)(2,1)S(1)}, u32[]{:S(2)}, u32[]{:S(2)}) %collective-permute-start.110) | collective-permute-done | bytes 221216 | tf_op jit(solution)/shard_map/ppermute | solution.py:33
  (706 shorter events, 459.6 us)
Async XLA Ops:
  140.0 40.8 %collective-permute-start.15 = (bf16[8,96,1152]{2,1,0:T(8,128)(2,1)}, bf16[8,96,1152]{2,1,0:T(8,128)(2,1)}, u32[]{:S(2)}, u32[]{:S(2)}) collective-permute-start(bf16[8,96,1152]{2,1,0:T(8,128)(2,1)} %get-tuple-element.309.refs_0_), channel_id=1, source_target_pairs={{0,2},{1,3},{2,0},{3,1},{4,6},{5,7},{6,4},{7,5},{8,10},{9,11},{10,... | collective-permute-start | bytes 5308424 | tf_op jit(solution)/shard_map/ppermute | solution.py:33
  140.3 40.6 %collective-permute-start.16 = (bf16[8,96,1152]{2,1,0:T(8,128)(2,1)}, bf16[8,96,1152]{2,1,0:T(8,128)(2,1)}, u32[]{:S(2)}, u32[]{:S(2)}) collective-permute-start(bf16[8,96,1152]{2,1,0:T(8,128)(2,1)} %get-tuple-element.310.refs_0_), channel_id=1, source_target_pairs={{0,4},{1,5},{2,6},{3,7},{4,0},{5,1},{6,2},{7,3},{8,12},{9,13},{10,... | collective-permute-start | bytes 5308424 | tf_op jit(solution)/shard_map/ppermute | solution.py:33
  225.8 55.8 %collective-permute-start.50 = (bf16[4,128,1536]{2,1,0:T(8,128)(2,1)S(1)}, bf16[4,128,1536]{2,1,0:T(8,128)(2,1)}, u32[]{:S(2)}, u32[]{:S(2)}) collective-permute-start(bf16[4,128,1536]{2,1,0:T(8,128)(2,1)S(1)} %bitcast.395), channel_id=1, source_target_pairs={{0,1},{1,0},{2,3},{3,2},{4,5},{5,4},{6,7},{7,6},{8,9},{9,8},{10,11... | collective-permute-start | bytes 4718600 | tf_op jit(solution)/shard_map/ppermute | solution.py:33
  299.8 54.9 %collective-permute-start.42 = (bf16[8,96,1024]{2,1,0:T(8,128)(2,1)}, bf16[8,96,1024]{2,1,0:T(8,128)(2,1)}, u32[]{:S(2)}, u32[]{:S(2)}) collective-permute-start(bf16[8,96,1024]{2,1,0:T(8,128)(2,1)} %pad_maximum_fusion.8.refs_0_), channel_id=1, source_target_pairs={{0,2},{1,3},{2,0},{3,1},{4,6},{5,7},{6,4},{7,5},{8,10},{9,11},{10,... | collective-permute-start | bytes 4718600 | tf_op jit(solution)/shard_map/ppermute | solution.py:33
  301.5 53.2 %collective-permute-start.43 = (bf16[8,64,1536]{2,1,0:T(8,128)(2,1)}, bf16[8,64,1536]{2,1,0:T(8,128)(2,1)}, u32[]{:S(2)}, u32[]{:S(2)}) collective-permute-start(bf16[8,64,1536]{2,1,0:T(8,128)(2,1)} %pad_maximum_fusion.9.refs_2_), channel_id=1, source_target_pairs={{0,4},{1,5},{2,6},{3,7},{4,0},{5,1},{6,2},{7,3},{8,12},{9,13},{10,... | collective-permute-start | bytes 4718600 | tf_op jit(solution)/shard_map/ppermute | solution.py:33
  305.7 49.0 %collective-permute-start.44 = (bf16[4,96,1024]{2,1,0:T(8,128)(2,1)}, bf16[4,96,1024]{2,1,0:T(8,128)(2,1)}, u32[]{:S(2)}, u32[]{:S(2)}) collective-permute-start(bf16[4,96,1024]{2,1,0:T(8,128)(2,1)} %pad_maximum_fusion.21), channel_id=1, source_target_pairs={{0,4},{1,5},{2,6},{3,7},{4,0},{5,1},{6,2},{7,3},{8,12},{9,13},{10,... | collective-permute-start | bytes 2359304 | tf_op jit(solution)/shard_map/ppermute | solution.py:33
  312.3 42.4 %collective-permute-start.45 = (bf16[4,64,1536]{2,1,0:T(8,128)(2,1)}, bf16[4,64,1536]{2,1,0:T(8,128)(2,1)}, u32[]{:S(2)}, u32[]{:S(2)}) collective-permute-start(bf16[4,64,1536]{2,1,0:T(8,128)(2,1)} %pad_maximum_fusion.22), channel_id=1, source_target_pairs={{0,2},{1,3},{2,0},{3,1},{4,6},{5,7},{6,4},{7,5},{8,10},{9,11},{10,... | collective-permute-start | bytes 2359304 | tf_op jit(solution)/shard_map/ppermute | solution.py:33
  363.6 63.3 %collective-permute-start.51 = (bf16[8,96,1024]{2,1,0:T(8,128)(2,1)}, bf16[8,96,1024]{2,1,0:T(8,128)(2,1)}, u32[]{:S(2)}, u32[]{:S(2)}) collective-permute-start(bf16[8,96,1024]{2,1,0:T(8,128)(2,1)} %pad_maximum_fusion.10.refs_0_), channel_id=1, source_target_pairs={{0,2},{1,3},{2,0},{3,1},{4,6},{5,7},{6,4},{7,5},{8,10},{9,11},{10,... | collective-permute-start | bytes 4718600 | tf_op jit(solution)/shard_map/ppermute | solution.py:33
  363.9 62.9 %collective-permute-start.52 = (bf16[8,64,1536]{2,1,0:T(8,128)(2,1)}, bf16[8,64,1536]{2,1,0:T(8,128)(2,1)}, u32[]{:S(2)}, u32[]{:S(2)}) collective-permute-start(bf16[8,64,1536]{2,1,0:T(8,128)(2,1)} %pad_maximum_fusion.11.refs_2_), channel_id=1, source_target_pairs={{0,4},{1,5},{2,6},{3,7},{4,0},{5,1},{6,2},{7,3},{8,12},{9,13},{10,... | collective-permute-start | bytes 4718600 | tf_op jit(solution)/shard_map/ppermute | solution.py:33
  364.4 62.4 %collective-permute-start.53 = (bf16[4,96,1024]{2,1,0:T(8,128)(2,1)}, bf16[4,96,1024]{2,1,0:T(8,128)(2,1)}, u32[]{:S(2)}, u32[]{:S(2)}) collective-permute-start(bf16[4,96,1024]{2,1,0:T(8,128)(2,1)} %pad_maximum_fusion.23), channel_id=1, source_target_pairs={{0,4},{1,5},{2,6},{3,7},{4,0},{5,1},{6,2},{7,3},{8,12},{9,13},{10,... | collective-permute-start | bytes 2359304 | tf_op jit(solution)/shard_map/ppermute | solution.py:33
  366.0 60.8 %collective-permute-start.54 = (bf16[4,64,1536]{2,1,0:T(8,128)(2,1)}, bf16[4,64,1536]{2,1,0:T(8,128)(2,1)}, u32[]{:S(2)}, u32[]{:S(2)}) collective-permute-start(bf16[4,64,1536]{2,1,0:T(8,128)(2,1)} %pad_maximum_fusion.24), channel_id=1, source_target_pairs={{0,2},{1,3},{2,0},{3,1},{4,6},{5,7},{6,4},{7,5},{8,10},{9,11},{10,... | collective-permute-start | bytes 2359304 | tf_op jit(solution)/shard_map/ppermute | solution.py:33
  432.0 58.4 %collective-permute-start.55 = (bf16[8,96,1024]{2,1,0:T(8,128)(2,1)}, bf16[8,96,1024]{2,1,0:T(8,128)(2,1)}, u32[]{:S(2)}, u32[]{:S(2)}) collective-permute-start(bf16[8,96,1024]{2,1,0:T(8,128)(2,1)} %pad_maximum_fusion.12.refs_0_), channel_id=1, source_target_pairs={{0,2},{1,3},{2,0},{3,1},{4,6},{5,7},{6,4},{7,5},{8,10},{9,11},{10,... | collective-permute-start | bytes 4718600 | tf_op jit(solution)/shard_map/ppermute | solution.py:33
  432.4 58.0 %collective-permute-start.56 = (bf16[8,64,1536]{2,1,0:T(8,128)(2,1)}, bf16[8,64,1536]{2,1,0:T(8,128)(2,1)}, u32[]{:S(2)}, u32[]{:S(2)}) collective-permute-start(bf16[8,64,1536]{2,1,0:T(8,128)(2,1)} %pad_maximum_fusion.13.refs_2_), channel_id=1, source_target_pairs={{0,4},{1,5},{2,6},{3,7},{4,0},{5,1},{6,2},{7,3},{8,12},{9,13},{10,... | collective-permute-start | bytes 4718600 | tf_op jit(solution)/shard_map/ppermute | solution.py:33
  432.8 67.3 %collective-permute-start.57 = (bf16[8,96,1024]{2,1,0:T(8,128)(2,1)}, bf16[8,96,1024]{2,1,0:T(8,128)(2,1)}, u32[]{:S(2)}, u32[]{:S(2)}) collective-permute-start(bf16[8,96,1024]{2,1,0:T(8,128)(2,1)} %get-tuple-element.398), channel_id=1, source_target_pairs={{0,2},{1,3},{2,0},{3,1},{4,6},{5,7},{6,4},{7,5},{8,10},{9,11},{10,... | collective-permute-start | bytes 4718600 | tf_op jit(solution)/shard_map/ppermute | solution.py:33
  434.3 66.0 %collective-permute-start.58 = (bf16[8,64,1536]{2,1,0:T(8,128)(2,1)}, bf16[8,64,1536]{2,1,0:T(8,128)(2,1)}, u32[]{:S(2)}, u32[]{:S(2)}) collective-permute-start(bf16[8,64,1536]{2,1,0:T(8,128)(2,1)} %get-tuple-element.399), channel_id=1, source_target_pairs={{0,4},{1,5},{2,6},{3,7},{4,0},{5,1},{6,2},{7,3},{8,12},{9,13},{10,... | collective-permute-start | bytes 4718600 | tf_op jit(solution)/shard_map/ppermute | solution.py:33
  436.1 152.5 %collective-permute-start.69 = (bf16[2,4,128,1536]{3,2,1,0:T(8,128)(2,1)}, bf16[2,4,128,1536]{3,2,1,0:T(8,128)(2,1)}, u32[]{:S(2)}, u32[]{:S(2)}) collective-permute-start(bf16[2,4,128,1536]{3,2,1,0:T(8,128)(2,1)} %get-tuple-element.447), channel_id=1, source_target_pairs={{0,1},{1,0},{2,3},{3,2},{4,5},{5,4},{6,7},{7,6},{8,9},{9,8},{10,11... | collective-permute-start | bytes 9437192 | tf_op jit(solution)/shard_map/ppermute | solution.py:33
  507.2 58.8 %collective-permute-start.59 = (bf16[4,96,1024]{2,1,0:T(8,128)(2,1)}, bf16[4,96,1024]{2,1,0:T(8,128)(2,1)}, u32[]{:S(2)}, u32[]{:S(2)}) collective-permute-start(bf16[4,96,1024]{2,1,0:T(8,128)(2,1)} %get-tuple-element.416), channel_id=1, source_target_pairs={{0,4},{1,5},{2,6},{3,7},{4,0},{5,1},{6,2},{7,3},{8,12},{9,13},{10,... | collective-permute-start | bytes 2359304 | tf_op jit(solution)/shard_map/ppermute | solution.py:33
  507.5 58.6 %collective-permute-start.60 = (bf16[4,64,1536]{2,1,0:T(8,128)(2,1)}, bf16[4,64,1536]{2,1,0:T(8,128)(2,1)}, u32[]{:S(2)}, u32[]{:S(2)}) collective-permute-start(bf16[4,64,1536]{2,1,0:T(8,128)(2,1)} %get-tuple-element.417), channel_id=1, source_target_pairs={{0,2},{1,3},{2,0},{3,1},{4,6},{5,7},{6,4},{7,5},{8,10},{9,11},{10,... | collective-permute-start | bytes 2359304 | tf_op jit(solution)/shard_map/ppermute | solution.py:33
  509.0 57.1 %collective-permute-start.61 = (bf16[8,96,1024]{2,1,0:T(8,128)(2,1)}, bf16[8,96,1024]{2,1,0:T(8,128)(2,1)}, u32[]{:S(2)}, u32[]{:S(2)}) collective-permute-start(bf16[8,96,1024]{2,1,0:T(8,128)(2,1)} %get-tuple-element.418), channel_id=1, source_target_pairs={{0,2},{1,3},{2,0},{3,1},{4,6},{5,7},{6,4},{7,5},{8,10},{9,11},{10,... | collective-permute-start | bytes 4718600 | tf_op jit(solution)/shard_map/ppermute | solution.py:33
  509.5 56.6 %collective-permute-start.62 = (bf16[8,64,1536]{2,1,0:T(8,128)(2,1)}, bf16[8,64,1536]{2,1,0:T(8,128)(2,1)}, u32[]{:S(2)}, u32[]{:S(2)}) collective-permute-start(bf16[8,64,1536]{2,1,0:T(8,128)(2,1)} %get-tuple-element.419), channel_id=1, source_target_pairs={{0,4},{1,5},{2,6},{3,7},{4,0},{5,1},{6,2},{7,3},{8,12},{9,13},{10,... | collective-permute-start | bytes 4718600 | tf_op jit(solution)/shard_map/ppermute | solution.py:33
  588.9 52.7 %collective-permute-start.67 = (bf16[8,96,1024]{2,1,0:T(8,128)(2,1)}, bf16[8,96,1024]{2,1,0:T(8,128)(2,1)}, u32[]{:S(2)}, u32[]{:S(2)}) collective-permute-start(bf16[8,96,1024]{2,1,0:T(8,128)(2,1)} %get-tuple-element.443), channel_id=1, source_target_pairs={{0,2},{1,3},{2,0},{3,1},{4,6},{5,7},{6,4},{7,5},{8,10},{9,11},{10,... | collective-permute-start | bytes 4718600 | tf_op jit(solution)/shard_map/ppermute | solution.py:33
  590.4 51.3 %collective-permute-start.68 = (bf16[8,64,1536]{2,1,0:T(8,128)(2,1)}, bf16[8,64,1536]{2,1,0:T(8,128)(2,1)}, u32[]{:S(2)}, u32[]{:S(2)}) collective-permute-start(bf16[8,64,1536]{2,1,0:T(8,128)(2,1)} %get-tuple-element.444), channel_id=1, source_target_pairs={{0,4},{1,5},{2,6},{3,7},{4,0},{5,1},{6,2},{7,3},{8,12},{9,13},{10,... | collective-permute-start | bytes 4718600 | tf_op jit(solution)/shard_map/ppermute | solution.py:33
  684.8 45.8 %collective-permute-start.79 = (bf16[2,2,2,48,768]{4,3,0,1,2:T(8,128)(2,1)}, bf16[2,2,2,48,768]{4,3,0,1,2:T(8,128)(2,1)}, u32[]{:S(2)}, u32[]{:S(2)}) collective-permute-start(bf16[2,2,2,48,768]{4,3,0,1,2:T(8,128)(2,1)} %copy_bitcast_fusion.3), channel_id=1, source_target_pairs={{0,2},{1,3},{2,0},{3,1},{4,6},{5,7},{6,4},{7,5},{8,10},{9,11},{10,... | collective-permute-start | bytes 1769480 | tf_op jit(solution)/shard_map/ppermute | solution.py:33
  686.3 44.3 %collective-permute-start.80 = (bf16[2,2,2,48,768]{4,3,1,0,2:T(8,128)(2,1)}, bf16[2,2,2,48,768]{4,3,1,0,2:T(8,128)(2,1)}, u32[]{:S(2)}, u32[]{:S(2)}) collective-permute-start(bf16[2,2,2,48,768]{4,3,1,0,2:T(8,128)(2,1)} %copy_bitcast_fusion.2), channel_id=1, source_target_pairs={{0,4},{1,5},{2,6},{3,7},{4,0},{5,1},{6,2},{7,3},{8,12},{9,13},{10,... | collective-permute-start | bytes 1769480 | tf_op jit(solution)/shard_map/ppermute | solution.py:33
  688.8 41.8 %collective-permute-start.83 = (bf16[2,96,1024]{2,1,0:T(8,128)(2,1)}, bf16[2,96,1024]{2,1,0:T(8,128)(2,1)}, u32[]{:S(2)}, u32[]{:S(2)}) collective-permute-start(bf16[2,96,1024]{2,1,0:T(8,128)(2,1)} %get-tuple-element.480), channel_id=1, source_target_pairs={{0,8},{1,9},{2,10},{3,11},{4,12},{5,13},{6,14},{7,15},{8,0},{9,1},... | collective-permute-start | bytes 1179656 | tf_op jit(solution)/shard_map/ppermute | solution.py:33
  767.4 41.3 %collective-permute-start.89 = (bf16[2,2,2,96,1152]{4,3,1,0,2:T(8,128)(2,1)}, bf16[2,2,2,96,1152]{4,3,1,0,2:T(8,128)(2,1)}, u32[]{:S(2)}, u32[]{:S(2)}) collective-permute-start(bf16[2,2,2,96,1152]{4,3,1,0,2:T(8,128)(2,1)} %copy_bitcast_fusion.1), channel_id=1, source_target_pairs={{0,2},{1,3},{2,0},{3,1},{4,6},{5,7},{6,4},{7,5},{8,10},{9,11},{10,... | collective-permute-start | bytes 5308424 | tf_op jit(solution)/shard_map/ppermute | solution.py:33
  768.8 41.1 %collective-permute-start.90 = (bf16[2,2,2,96,1152]{4,3,1,0,2:T(8,128)(2,1)}, bf16[2,2,2,96,1152]{4,3,1,0,2:T(8,128)(2,1)}, u32[]{:S(2)}, u32[]{:S(2)}) collective-permute-start(bf16[2,2,2,96,1152]{4,3,1,0,2:T(8,128)(2,1)} %copy_bitcast_fusion), channel_id=1, source_target_pairs={{0,4},{1,5},{2,6},{3,7},{4,0},{5,1},{6,2},{7,3},{8,12},{9,13},{10,... | collective-permute-start | bytes 5308424 | tf_op jit(solution)/shard_map/ppermute | solution.py:33
  782.7 41.1 %collective-permute-start.114 = (f32[48,16,3,64]{3,1,2,0:T(8,128)S(1)}, f32[48,16,3,64]{3,1,2,0:T(8,128)S(1)}, u32[]{:S(2)}, u32[]{:S(2)}) collective-permute-start(f32[48,16,3,64]{3,1,2,0:T(8,128)S(1)} %dynamic-slice_bitcast_fusion), channel_id=1, source_target_pairs={{0,1},{1,0},{2,3},{3,2},{4,5},{5,4},{6,7},{7,6},{8,9},{9,8},{10,11... | collective-permute-start | bytes 1769480 | tf_op jit(solution)/shard_map/ppermute | solution.py:33
  819.4 42.5 %collective-permute-start.94 = (bf16[2,2,96,1152]{3,2,1,0:T(8,128)(2,1)}, bf16[2,2,96,1152]{3,2,1,0:T(8,128)(2,1)}, u32[]{:S(2)}, u32[]{:S(2)}) collective-permute-start(bf16[2,2,96,1152]{3,2,1,0:T(8,128)(2,1)} %get-tuple-element.504), channel_id=1, source_target_pairs={{0,4},{1,5},{2,6},{3,7},{4,0},{5,1},{6,2},{7,3},{8,12},{9,13},{10,... | collective-permute-start | bytes 2654216 | tf_op jit(solution)/shard_map/ppermute | solution.py:33
  821.1 40.8 %collective-permute-start.95 = (bf16[2,2,96,1152]{3,2,1,0:T(8,128)(2,1)}, bf16[2,2,96,1152]{3,2,1,0:T(8,128)(2,1)}, u32[]{:S(2)}, u32[]{:S(2)}) collective-permute-start(bf16[2,2,96,1152]{3,2,1,0:T(8,128)(2,1)} %get-tuple-element.505), channel_id=1, source_target_pairs={{0,2},{1,3},{2,0},{3,1},{4,6},{5,7},{6,4},{7,5},{8,10},{9,11},{10,... | collective-permute-start | bytes 2654216 | tf_op jit(solution)/shard_map/ppermute | solution.py:33
  875.5 51.8 %collective-permute-start.108 = (bf16[2,96,1152]{2,1,0:T(8,128)(2,1)}, bf16[2,96,1152]{2,1,0:T(8,128)(2,1)}, u32[]{:S(2)}, u32[]{:S(2)}) collective-permute-start(bf16[2,96,1152]{2,1,0:T(8,128)(2,1)} %get-tuple-element.527), channel_id=1, source_target_pairs={{0,8},{1,9},{2,10},{3,11},{4,12},{5,13},{6,14},{7,15},{8,0},{9,1},... | collective-permute-start | bytes 1327112 | tf_op jit(solution)/shard_map/ppermute | solution.py:33
  875.5 51.8 %collective-permute-start.109 = (bf16[2,96,1152]{2,1,0:T(8,128)(2,1)}, bf16[2,96,1152]{2,1,0:T(8,128)(2,1)}, u32[]{:S(2)}, u32[]{:S(2)}) collective-permute-start(bf16[2,96,1152]{2,1,0:T(8,128)(2,1)} %get-tuple-element.528), channel_id=1, source_target_pairs={{0,8},{1,9},{2,10},{3,11},{4,12},{5,13},{6,14},{7,15},{8,0},{9,1},... | collective-permute-start | bytes 1327112 | tf_op jit(solution)/shard_map/ppermute | solution.py:33
  (199 other events, 3263.6 us)

commit v6 on v5

--- a/solution.py
+++ b/solution.py
@@ -888,6 +888,108 @@
     )(core[None].astype(jnp.int32), x_near, kept, arriving, kernel, mods, grad_middle)
 
 
+def row_stats(values):
+    mean = jnp.mean(values, axis=-1, keepdims=True)
+    centred = values - mean
+    scale = lax.rsqrt(jnp.mean(centred * centred, axis=-1, keepdims=True) + ln_epsilon)
+    return centred * scale, scale
+
+
+def enter_feed_body(x_ref, part_ref, other_ref, grad_ref, mods_ref, norm_ref, norm_t_ref, out_ref):
+    @pl.loop(0, x_ref.shape[0] // STRIP)
+    def _(strip):
+        rows = pl.ds(pl.multiple_of(strip * STRIP, STRIP), STRIP)
+        branch = part_ref[rows, :].astype(full) + other_ref[rows, :].astype(full)
+        plain, _ = row_stats(x_ref[rows, :].astype(full) + mods_ref[0:1, :] * branch)
+        normed = plain * (1.0 + mods_ref[2:3, :]) + mods_ref[1:2, :]
+        norm_ref[rows, :] = normed.astype(low)
+        out_ref[rows, :] = (grad_ref[rows, :].astype(full) * mods_ref[3:4, :]).astype(low)
+
+    norm_t_ref[...] = norm_ref[...].T
+
+
+def enter_feed(canvas, part, other, grad, mods):
+    tokens, model = canvas.shape
+    rows = PLANE // 2
+    along = pl.BlockSpec((rows, model), lambda j: (j, 0))
+    return pl.pallas_call(
+        enter_feed_body,
+        grid=(tokens // rows,),
+        in_specs=[along] * 4 + [pl.BlockSpec((8, model), lambda j: (0, 0))],
+        out_specs=[along, pl.BlockSpec((model, rows), lambda j: (0, j)), along],
+        out_shape=[
+            jax.ShapeDtypeStruct((tokens, model), low),
+            jax.ShapeDtypeStruct((model, tokens), low),
+            jax.ShapeDtypeStruct((tokens, model), low),
+        ],
+        cost_estimate=pl.CostEstimate(flops=1000, bytes_accessed=1000, transcendentals=0),
+        name="enter_feed",
+    )(canvas, part, other, grad, mods)
+
+
+def leave_feed_body(words_ref, x_ref, part_ref, other_ref, grad_ref, mods_ref, *refs):
+    *kept_refs, out_ref, middle_grad_ref, branch_grad_ref, sums_ref, totals = refs
+    plane = pl.program_id(0)
+
+    @pl.when(plane == 0)
+    def _():
+        totals[...] = jnp.zeros_like(totals)
+
+    @pl.loop(0, x_ref.shape[0] // STRIP)
+    def _(strip):
+        rows = pl.ds(pl.multiple_of(strip * STRIP, STRIP), STRIP)
+        gate_a, gate_f = mods_ref[0:1, :], mods_ref[3:4, :]
+        branch_a = part_ref[rows, :].astype(full) + other_ref[rows, :].astype(full)
+        middle = x_ref[rows, :].astype(full) + gate_a * branch_a
+        plain, scale = row_stats(middle)
+        branch_f = sum(ref[0, 0, rows, :].astype(full) for ref in kept_refs)
+        back = sum(ref[1, 0, rows, :].astype(full) for ref in kept_refs)
+        grad = grad_ref[rows, :].astype(full)
+        out_ref[rows, :] = (middle + gate_f * branch_f).astype(low)
+        scaled = back * (1.0 + mods_ref[2:3, :])
+        mean_plain = jnp.mean(scaled, axis=-1, keepdims=True)
+        mean_normed = jnp.mean(scaled * plain, axis=-1, keepdims=True)
+        grad_middle = grad + scale * (scaled - mean_plain - plain * mean_normed)
+        middle_grad_ref[rows, :] = grad_middle
+        branch_grad_ref[rows, :] = (grad_middle * gate_a).astype(low)
+        products = (grad * branch_f, back, back * plain, grad_middle * branch_a)
+        for index, product in enumerate(products):
+            totals[index] += product[:8] + product[8:]
+
+    @pl.when(plane == pl.num_programs(0) - 1)
+    def _():
+        lines = [jnp.sum(totals[k], axis=0, keepdims=True) for k in range(4)]
+        sums_ref[...] = jnp.concatenate(lines + [jnp.zeros_like(sums_ref[:4])], axis=0)
+
+
+def leave_feed(words, canvas, part, other, grad, mods, kept):
+    model = canvas.shape[1]
+    rows = PLANE // 2
+    own = pl.BlockSpec((rows, model), lambda j, words: (2 * j + words[0], 0))
+    half = pl.BlockSpec((rows, model), lambda j, words: (j, 0))
+    whole = pl.BlockSpec((8, model), lambda j, words: (0, 0))
+    return pl.pallas_call(
+        leave_feed_body,
+        grid_spec=pltpu.PrefetchScalarGridSpec(
+            num_scalar_prefetch=1,
+            grid=(4,),
+            in_specs=[own] * 4
+            + [whole]
+            + [pl.BlockSpec((2, 1, rows, model), lambda j, words: (0, j, 0, 0))] * len(kept),
+            out_specs=[half, half, half, whole],
+            scratch_shapes=[pltpu.VMEM((4, 8, model), full)],
+        ),
+        out_shape=[
+            jax.ShapeDtypeStruct((4 * rows, model), low),
+            jax.ShapeDtypeStruct((4 * rows, model), full),
+            jax.ShapeDtypeStruct((4 * rows, model), low),
+            jax.ShapeDtypeStruct((8, model), full),
+        ],
+        cost_estimate=pl.CostEstimate(flops=1000, bytes_accessed=1000, transcendentals=0),
+        name="leave_feed",
+    )(words, canvas, part, other, grad, mods, *kept)
+
+
 def on_device(
     tokens,
     seg_ids,
@@ -995,7 +1097,7 @@
 
     slot(qkv_flows + proj_flows + feed_flows[0])
     convolved = slot(
-        qkv_flows + proj_flows + feed_flows[0], lambda: conv_in(canvas, attn_taps, mods_a)
+        qkv_flows + proj_flows + feed_flows[0] + feed_flows[1], lambda: conv_in(canvas, attn_taps, mods_a)
     )
 
     (upstream,) = slot.after(upstream)
@@ -1013,28 +1115,21 @@
         proj_flows + feed_flows[1] + feed_flows[2], lambda: attend(mask, qkv)
     )
 
+    mods_f = jnp.concatenate(
+        [gate_a[None], shift_f[None], scale_f[None], gate_f[None], jnp.zeros((4, model), full)]
+    )
+
     def project_out():
         weight = jnp.concatenate(
             [array.reshape(-1, model // 2) for array in joined(proj_flows)], axis=1
         )
-        branch_part = jnp.dot(attended, weight, preferred_element_type=full)
-        branch = half_of(branch_part, core) + swap_core(
-            half_of(branch_part, 1 - core).astype(low)
-        ).astype(full)
-        return weight, branch
-
-    source_ph = mine.astype(full)
+        branch_part = jnp.dot(attended, weight, preferred_element_type=full).astype(low)
+        other = swap_core(branch_part)
+        return weight, branch_part, other, *enter_feed(canvas, branch_part, other, grad_ph, mods_f)
+
     slot.finish(proj_flows)
-    def enter_feed():
-        proj_full, branch_a = project_out()
-        middle = source_ph + gate_a * branch_a
-        normed_low = modulate(middle, shift_f, scale_f).astype(low)
-        norm = join_halves(normed_low, swap_core(normed_low), core)
-        grad_branch_f = (grad_ph.astype(full) * gate_f).astype(low)
-        return proj_full, branch_a, middle, norm, norm.T, grad_branch_f
-
-    proj_full, branch_a, middle, norm, norm_t, grad_branch_f = slot(
-        sum(feed_flows, []), enter_feed
+    proj_full, branch_part, branch_other, norm, norm_t, grad_branch_f = slot(
+        feed_flows[0] + feed_flows[2], project_out
     )
 
     kept = []
@@ -1077,30 +1172,17 @@
     run_feed(feed_flows[1] + feed_flows[2], 0)
     run_feed(feed_flows[2] + back_flows[0], 1)
     run_feed(back_flows[0] + back_flows[1], 2)
-    upstream = upstream.astype(full)
-
-    def leave_feed():
-        total = sum(
-            staying.astype(full) + swap_core(leaving).astype(full) for staying, leaving in kept
-        )
-        branch_sum, back_sum = total[0], total[1]
-        layer_out = from_phases((middle + gate_f * branch_sum).astype(low), half_rows)
-        grad_gate_f = jnp.sum(upstream * branch_sum, axis=(0, 1))
-        _, norm_pull_f = jax.vjp(modulate, middle, shift_f, scale_f)
-        grad_middle, grad_shift_f, grad_scale_f = norm_pull_f(back_sum)
-        grad_middle = grad_middle + upstream
-        grad_gate_a = jnp.sum(grad_middle * branch_a, axis=(0, 1))
-        grad_branch_mine = (grad_middle * gate_a).astype(low)
-        return (
-            layer_out, grad_middle, grad_branch_mine,
-            grad_gate_f, grad_shift_f, grad_scale_f, grad_gate_a,
-        )
-
-    (
-        layer_out, grad_middle, grad_branch_mine,
-        grad_gate_f, grad_shift_f, grad_scale_f, grad_gate_a,
-    ) = slot(sum(back_flows, []), leave_feed)
-    layer_out = layer_out[None]
+
+    def after_feed():
+        parts = [array for staying, leaving in kept for array in (staying, swap_core(leaving))]
+        return leave_feed(words[:1], canvas, branch_part, branch_other, grad_ph, mods_f, parts)
+
+    layer_out, grad_middle, grad_branch_mine, feed_sums = slot(
+        back_flows[0] + back_flows[2], after_feed
+    )
+    grad_gate_f, grad_shift_f, grad_scale_f, grad_gate_a = feed_sums[:4]
+    grad_branch_mine = grad_branch_mine.reshape(4, -1, model)
+    layer_out = from_phases(layer_out.reshape(4, -1, model), half_rows)[None]
 
     def enter_attend():
         grad_branch_a = join_halves(grad_branch_mine, swap_core(grad_branch_mine), core)
@@ -1108,7 +1190,7 @@
         proj_grad = jnp.dot(attended.T, grad_branch_a, preferred_element_type=full)
         return grad_attended.astype(low), proj_grad.astype(low)
 
-    grad_attended, proj_grad = slot(sum(back_flows, []), enter_attend)
+    grad_attended, proj_grad = slot(back_flows[0] + back_flows[1], enter_attend)
     proj_grad = proj_grad.reshape(chips, -1, model)
     proj_flows = [sums(proj_grad[..., : model // 2], 0), sums(proj_grad[..., model // 2 :], 1)]
     grad_qkv = slot(
@@ -1137,7 +1219,7 @@
     def leave_block():
         input_grad, attn_tap_grad, mods_grad = conv_back(
             core, rows_near(canvas, core), *grad_conv, attn_taps, mods_a,
-            grad_middle.reshape(half_tokens, model),
+            grad_middle,
         )
         input_grad = from_phases(input_grad.reshape(4, -1, model), half_rows)
         return attn_tap_grad[:9], input_grad, mods_grad[0], mods_grad[1]

time: 970 us -> 908 us (0.936)
  other arithmetic: 187 us -> 143 us
  local copies, waits for them, and re-layouts: 137 us -> 99.1 us
  Pallas kernels: 272 us -> 305 us
  waiting for transfers between devices: 197 us -> 182 us
    pallas_call x0 -> x2, Pallas kernels: none -> 33.1 us  [the longest x1 17.6 us: enter_feed(): pl.pallas_call(enter_feed_body, grid=(tokens // rows,), in_specs=[along]...]
    ppermute x113 -> x112, waiting for transfers between devices: 197 us -> 182 us  [swap(): lax.ppermute(x, AXES, [(i, i ^ 1 << bit) for i in range(device_count())])]
    reduce_sum x7 -> x0, other arithmetic: 12.4 us -> none  [the longest x2 4.55 us: layer_norm(): average = jnp.mean(values, axis=-1, keepdims=True)]
    concatenate x28, other arithmetic: 54.4 us -> 44.2 us  [gather_steps(): held = jnp.concatenate([held, arriving], axis=0)]
    ppermute x113 -> x112, starting transfers between devices: 110 us -> 112 us  [swap(): lax.ppermute(x, AXES, [(i, i ^ 1 << bit) for i in range(device_count())])]
  transfers between devices with their start and end apart: 115 -> 114, of which waited for: 33 -> 39; matrix products, arithmetic and copies ran while one was open for 32% -> 23% of each run, Pallas kernels for 28% -> 33%
where the time goes in v6:
time: 908 us; the launch traced here: 899 us
  Pallas kernels  305 us (34%)
  waiting for transfers between devices  182 us (20%)
  other arithmetic  143 us (16%)
  starting transfers between devices  119 us (13%)
  local copies, waits for them, and re-layouts  99.1 us (11%)
  matrix products  47.9 us (5%)
    ppermute x112, waiting for transfers between devices, swap(): lax.ppermute(x, AXES, [(i, i ^ 1 << bit) for i in range(device_count())])  182 us
    pallas_call x3, Pallas kernels, feed_forward(): pl.pallas_call(functools.partial(feed_body, spread), grid_spec=pltpu.Pref...  164 us
    ppermute x112, starting transfers between devices, swap(): lax.ppermute(x, AXES, [(i, i ^ 1 << bit) for i in range(device_count())])  112 us
    concatenate x28, other arithmetic, gather_steps(): held = jnp.concatenate([held, arriving], axis=0)  44.2 us
    convert_element_type x18, other arithmetic, halving_steps(): (staying[at].astype(full) + arriving[at].astype(full)).astype(low)  33.1 us
    pallas_call x1, Pallas kernels, attend_back(): pl.pallas_call(attend_back_body, grid=(pairs,), in_specs=[pl.BlockSpec((P...  28.9 us
    pallas_call x1, Pallas kernels, conv_in(): pl.pallas_call(conv_in_body, grid=(model // TILE,), in_specs=[pl.BlockSpe...  22.8 us
    pallas_call x1, Pallas kernels, conv_back(): pl.pallas_call(conv_back_body, grid_spec=pltpu.PrefetchScalarGridSpec(num...  21.1 us
  transfers between devices with their start and end apart: 114, of which 39 were waited for; matrix products, arithmetic and copies ran while one was open for 23% of the time, Pallas kernels for 33%

profile of v6, /device:TPU:0, one launch (start us, length us, event | category | flops | bytes accessed | tf_op | source)
XLA Modules:
  0.0 899.0 jit_solution(9567192581601500588)
XLA Ops:
  27.1 4.5 collective-permute-done.2
  91.4 5.2 collective-permute-done.12
  100.9 8.0 collective-permute-done.14
  115.7 5.2 collective-permute-done.17
  132.7 13.3 %collective-permute-done.21 = bf16[1,96,1024]{2,1,0:T(8,128)(2,1)S(1)} collective-permute-done((bf16[1,96,1024]{2,1,0:T(8,128)(2,1)S(1)}, bf16[1,96,1024]{2,1,0:T(8,128)(2,1)S(1)}, u32[]{:S(2)}, u32[]{:S(2)}) %collective-permute-start.21) | collective-permute-done | bytes 196640 | tf_op jit(solution)/shard_map/ppermute | solution.py:33
  151.7 22.8 %conv_in.1 = bf16[1024,1536]{1,0:T(8,128)(2,1)} custom-call(bf16[1024,1536]{1,0:T(8,128)(2,1)} %bitcast.355, f32[16,1536]{1,0:T(8,128)} %pad_convert_fusion.1.kernel_ref, f32[8,1536]{1,0:T(8,128)} %maximum_maximum_fusion.mods_ref), custom_call_target="tpu_custom_call" | custom-call | flops 47185920 | bytes 6291456 | tf_op jit(solution)/shard_map/conv_in/pallas_call | solution.py:700
  187.3 5.6 assemble.5
  192.9 5.6 assemble.4
  198.5 12.9 %convolution_convert_fusion.2.qkv_ref = bf16[1024,2304]{1,0:T(8,128)(2,1)} fusion(bf16[1024,1536]{1,0:T(8,128)(2,1)} %conv_in.1, bf16[1536,1152]{1,0:T(8,128)(2,1)} %bitcast.361, bf16[1536,1152]{1,0:T(8,128)(2,1)} %bitcast.363), kind=kOutput, calls=%fused_computation.3 | convolution fusion | flops 7264272384 | bytes 14942208 | tf_op jit(solution)/shard_map/dot_general | solution.py:1110
  213.6 5.4 pad_maximum_fusion
  232.4 9.0 %collective-permute-done.42 = bf16[1,96,1024]{2,1,0:T(8,128)(2,1)S(1)} collective-permute-done((bf16[1,96,1024]{2,1,0:T(8,128)(2,1)S(1)}, bf16[1,96,1024]{2,1,0:T(8,128)(2,1)S(1)}, u32[]{:S(2)}, u32[]{:S(2)}) %collective-permute-start.42) | collective-permute-done | bytes 196640 | tf_op jit(solution)/shard_map/ppermute | solution.py:33
  241.4 15.5 %attend.1 = bf16[1024,768]{1,0:T(8,128)(2,1)} custom-call(f32[256,256]{1,0:T(8,128)} %compare_convert_fusion.mask_ref, bf16[1024,2304]{1,0:T(8,128)(2,1)} %convolution_convert_fusion.2.qkv_ref), custom_call_target="tpu_custom_call" | custom-call | flops 3221225472 | bytes 6291456 | tf_op jit(solution)/shard_map/attend/pallas_call | solution.py:334
  265.7 6.1 convolution_convert_fusion.4.part_ref
  302.0 17.6 %enter_feed.1 = (bf16[1024,1536]{1,0:T(8,128)(2,1)}, bf16[1536,1024]{1,0:T(8,128)(2,1)}, bf16[1024,1536]{1,0:T(8,128)(2,1)}) custom-call(bf16[1024,1536]{1,0:T(8,128)(2,1)} %bitcast.356, bf16[1024,1536]{1,0:T(8,128)(2,1)} %convolution_convert_fusion.4.part_ref, bf16[1024,1536]{1,0:T(8,128)(2,1)} %collective-permute-done.48.other_ref, ...), custom_call_target="tpu_custom_call" | custom-call | flops 1000 | bytes 1000 | tf_op jit(solution)/shard_map/enter_feed/pallas_call | solution.py:915
  325.6 54.8 %feed_forward.3 = (bf16[2,4,128,1536]{3,2,1,0:T(8,128)(2,1)}, bf16[2,4,128,1536]{3,2,1,0:T(8,128)(2,1)}, bf16[8,96,1024]{2,1,0:T(8,128)(2,1)}, bf16[8,96,1024]{2...) custom-call(s32[49]{0:T(128)} %pad_add_fusion.1.words_ref, ...), custom_call_target="tpu_custom_call" | custom-call | flops 19327352832 | bytes 28311552 | tf_op jit(solution)/shard_map/feed_forward/pallas_call | solution.py:592
  389.8 54.3 %feed_forward.4 = (bf16[2,4,128,1536]{3,2,1,0:T(8,128)(2,1)}, bf16[2,4,128,1536]{3,2,1,0:T(8,128)(2,1)}, bf16[8,96,1024]{2,1,0:T(8,128)(2,1)}, bf16[8,96,1024]{2...) custom-call(s32[49]{0:T(128)} %pad_add_fusion.1.words_ref, ...), custom_call_target="tpu_custom_call" | custom-call | flops 19327352832 | bytes 28311552 | tf_op jit(solution)/shard_map/feed_forward/pallas_call | solution.py:592
  444.1 10.5 %collective-permute-done.56 = bf16[8,96,1024]{2,1,0:T(8,128)(2,1)} collective-permute-done((bf16[8,96,1024]{2,1,0:T(8,128)(2,1)}, bf16[8,96,1024]{2,1,0:T(8,128)(2,1)}, u32[]{:S(2)}, u32[]{:S(2)}) %collective-permute-start.56) | collective-permute-done | bytes 1572896 | tf_op jit(solution)/shard_map/ppermute | solution.py:33
  466.5 16.4 %collective-permute-done.58 = bf16[4,96,1024]{2,1,0:T(8,128)(2,1)S(1)} collective-permute-done((bf16[4,96,1024]{2,1,0:T(8,128)(2,1)S(1)}, bf16[4,96,1024]{2,1,0:T(8,128)(2,1)S(1)}, u32[]{:S(2)}, u32[]{:S(2)}) %collective-permute-start.58) | collective-permute-done | bytes 786464 | tf_op jit(solution)/shard_map/ppermute | solution.py:33
  483.7 54.4 %feed_forward.5 = (bf16[2,4,128,1536]{3,2,1,0:T(8,128)(2,1)}, bf16[2,4,128,1536]{3,2,1,0:T(8,128)(2,1)}, bf16[8,96,1024]{2,1,0:T(8,128)(2,1)}, bf16[8,96,1024]{2...) custom-call(s32[49]{0:T(128)} %pad_add_fusion.1.words_ref, ...), custom_call_target="tpu_custom_call" | custom-call | flops 19327352832 | bytes 28311552 | tf_op jit(solution)/shard_map/feed_forward/pallas_call | solution.py:592
  549.3 15.6 %leave_feed.1 = (bf16[512,1536]{1,0:T(8,128)(2,1)}, f32[512,1536]{1,0:T(8,128)}, bf16[512,1536]{1,0:T(8,128)(2,1)}, f32[8,1536]{1,0:T(8,128)}) custom-call(s32[1]{0:T(128)} %bitcast.37.words_ref.core_ref, bf16[1024,1536]{1,0:T(8,128)(2,1)} %bitcast.357, bf16[1024,1536]{1,0:T(8,128)(2,1)} %convolution_convert_fusion.4.part_ref, ...), custom_call_target="tpu_custom_call" | custom-call | flops 1000 | bytes 1000 | tf_op jit(solution)/shard_map/leave_feed/pallas_call | solution.py:971
  564.8 15.2 %collective-permute-done.64 = bf16[8,96,1024]{2,1,0:T(8,128)(2,1)} collective-permute-done((bf16[8,96,1024]{2,1,0:T(8,128)(2,1)}, bf16[8,96,1024]{2,1,0:T(8,128)(2,1)}, u32[]{:S(2)}, u32[]{:S(2)}) %collective-permute-start.64) | collective-permute-done | bytes 1572896 | tf_op jit(solution)/shard_map/ppermute | solution.py:33
  625.4 28.9 %attend_back.1 = bf16[1024,2304]{1,0:T(8,128)(2,1)} custom-call(f32[256,256]{1,0:T(8,128)} %compare_convert_fusion.mask_ref, bf16[1024,2304]{1,0:T(8,128)(2,1)} %convolution_convert_fusion.2.qkv_ref, bf16[1024,768]{1,0:T(8,128)(2,1)} %convolution_convert_fusion.7.grad_ref), custom_call_target="tpu_custom_call" | custom-call | flops 8053063680 | bytes 11010048 | tf_op jit(solution)/shard_map/attend_back/pallas_call | solution.py:355
  669.6 10.5 %convolution_convert_fusion = bf16[1536,2304]{1,0:T(8,128)(2,1)S(1)} fusion(bf16[1024,1536]{1,0:T(8,128)(2,1)S(1)} %copy-done.27, bf16[1024,2304]{1,0:T(8,128)(2,1)} %attend_back.1), kind=kOutput, calls=%fused_computation | convolution fusion | flops 7251296256 | bytes 14942208 | tf_op jit(solution)/shard_map/dot_general | solution.py:1201
  680.2 7.7 convolution_convert_fusion.3
  721.3 7.7 collective-permute-done.90
  731.2 10.9 %collective-permute-done.86 = bf16[2,2,2,96,1152]{4,3,1,0,2:T(8,128)(2,1)} collective-permute-done((bf16[2,2,2,96,1152]{4,3,1,0,2:T(8,128)(2,1)}, bf16[2,2,2,96,1152]{4,3,1,0,2:T(8,128)(2,1)}, u32[]{:S(2)}, u32[]{:S(2)}) %collective-permute-start.86) | collective-permute-done | bytes 1769504 | tf_op jit(solution)/shard_map/ppermute | solution.py:33
  755.8 21.1 %conv_back.1 = (f32[512,1536]{1,0:T(8,128)}, f32[16,1536]{1,0:T(8,128)}, f32[8,1536]{1,0:T(8,128)}) custom-call(s32[1]{0:T(128)} %bitcast.37.words_ref.core_ref, bf16[576,1536]{1,0:T(8,128)(2,1)} %bitcast.374, bf16[576,1536]{1,0:T(8,128)(2,1)} %bitcast.375, bf16[576,1536]{1,0:T(8,128)(2,1)} %collective-permute-done.92.arriving_ref, ...), custom_call_target="tpu_custom_call" | custom-call | flops 55050240 | bytes 11010048 | tf_op jit(solution)/shard_map/conv_back/pallas_call | solution.py:849
  776.9 6.0 copy.226
  782.9 5.3 reshape.440
  820.7 13.5 %collective-permute-done.98 = bf16[1,9216]{1,0:T(2,128)(2,1)S(1)} collective-permute-done((bf16[1,9216]{1,0:T(2,128)(2,1)S(1)}, bf16[1,9216]{1,0:T(2,128)(2,1)S(1)}, u32[]{:S(2)}, u32[]{:S(2)}) %collective-permute-start.98) | collective-permute-done | bytes 18464 | tf_op jit(solution)/shard_map/ppermute | solution.py:33
  857.1 4.8 reshape.449
  870.2 14.6 %collective-permute-done.109 = bf16[96,1152]{1,0:T(8,128)(2,1)S(1)} collective-permute-done((bf16[96,1152]{1,0:T(8,128)(2,1)S(1)}, bf16[96,1152]{1,0:T(8,128)(2,1)S(1)}, u32[]{:S(2)}, u32[]{:S(2)}) %collective-permute-start.109) | collective-permute-done | bytes 221216 | tf_op jit(solution)/shard_map/ppermute | solution.py:33
  (763 shorter events, 406.5 us)
Async XLA Ops:
  113.5 61.0 %collective-permute-start.15 = (bf16[8,96,1152]{2,1,0:T(8,128)(2,1)S(1)}, bf16[8,96,1152]{2,1,0:T(8,128)(2,1)}, u32[]{:S(2)}, u32[]{:S(2)}) collective-permute-start(bf16[8,96,1152]{2,1,0:T(8,128)(2,1)S(1)} %get-tuple-element.313.refs_0_), channel_id=1, source_target_pairs={{0,2},{1,3},{2,0},{3,1},{4,6},{5,7},{6,4},{7,5},{8,10},{9,11},{10,... | collective-permute-start | bytes 5308424 | tf_op jit(solution)/shard_map/ppermute | solution.py:33
  115.0 59.5 %collective-permute-start.16 = (bf16[8,96,1152]{2,1,0:T(8,128)(2,1)}, bf16[8,96,1152]{2,1,0:T(8,128)(2,1)}, u32[]{:S(2)}, u32[]{:S(2)}) collective-permute-start(bf16[8,96,1152]{2,1,0:T(8,128)(2,1)} %get-tuple-element.314.refs_0_), channel_id=1, source_target_pairs={{0,4},{1,5},{2,6},{3,7},{4,0},{5,1},{6,2},{7,3},{8,12},{9,13},{10,... | collective-permute-start | bytes 5308424 | tf_op jit(solution)/shard_map/ppermute | solution.py:33
  126.0 48.5 %collective-permute-start.19 = (bf16[2,96,1024]{2,1,0:T(8,128)(2,1)}, bf16[2,96,1024]{2,1,0:T(8,128)(2,1)}, u32[]{:S(2)}, u32[]{:S(2)}) collective-permute-start(bf16[2,96,1024]{2,1,0:T(8,128)(2,1)} %pad_maximum_fusion.29), channel_id=1, source_target_pairs={{0,8},{1,9},{2,10},{3,11},{4,12},{5,13},{6,14},{7,15},{8,0},{9,1},... | collective-permute-start | bytes 1179656 | tf_op jit(solution)/shard_map/ppermute | solution.py:33
  126.3 48.2 %collective-permute-start.20 = (bf16[2,64,1536]{2,1,0:T(8,128)(2,1)}, bf16[2,64,1536]{2,1,0:T(8,128)(2,1)}, u32[]{:S(2)}, u32[]{:S(2)}) collective-permute-start(bf16[2,64,1536]{2,1,0:T(8,128)(2,1)} %pad_maximum_fusion.30), channel_id=1, source_target_pairs={{0,8},{1,9},{2,10},{3,11},{4,12},{5,13},{6,14},{7,15},{8,0},{9,1},... | collective-permute-start | bytes 1179656 | tf_op jit(solution)/shard_map/ppermute | solution.py:33
  278.6 41.0 %collective-permute-start.44 = (bf16[8,96,1024]{2,1,0:T(8,128)(2,1)}, bf16[8,96,1024]{2,1,0:T(8,128)(2,1)}, u32[]{:S(2)}, u32[]{:S(2)}) collective-permute-start(bf16[8,96,1024]{2,1,0:T(8,128)(2,1)} %pad_maximum_fusion.10.refs_0_), channel_id=1, source_target_pairs={{0,2},{1,3},{2,0},{3,1},{4,6},{5,7},{6,4},{7,5},{8,10},{9,11},{10,... | collective-permute-start | bytes 4718600 | tf_op jit(solution)/shard_map/ppermute | solution.py:33
  278.9 40.7 %collective-permute-start.45 = (bf16[8,64,1536]{2,1,0:T(8,128)(2,1)}, bf16[8,64,1536]{2,1,0:T(8,128)(2,1)}, u32[]{:S(2)}, u32[]{:S(2)}) collective-permute-start(bf16[8,64,1536]{2,1,0:T(8,128)(2,1)} %pad_maximum_fusion.11.refs_2_), channel_id=1, source_target_pairs={{0,4},{1,5},{2,6},{3,7},{4,0},{5,1},{6,2},{7,3},{8,12},{9,13},{10,... | collective-permute-start | bytes 4718600 | tf_op jit(solution)/shard_map/ppermute | solution.py:33
  321.6 58.9 %collective-permute-start.50 = (bf16[8,96,1024]{2,1,0:T(8,128)(2,1)}, bf16[8,96,1024]{2,1,0:T(8,128)(2,1)}, u32[]{:S(2)}, u32[]{:S(2)}) collective-permute-start(bf16[8,96,1024]{2,1,0:T(8,128)(2,1)} %pad_maximum_fusion.8.refs_0_), channel_id=1, source_target_pairs={{0,2},{1,3},{2,0},{3,1},{4,6},{5,7},{6,4},{7,5},{8,10},{9,11},{10,... | collective-permute-start | bytes 4718600 | tf_op jit(solution)/shard_map/ppermute | solution.py:33
  323.3 57.3 %collective-permute-start.51 = (bf16[8,64,1536]{2,1,0:T(8,128)(2,1)}, bf16[8,64,1536]{2,1,0:T(8,128)(2,1)}, u32[]{:S(2)}, u32[]{:S(2)}) collective-permute-start(bf16[8,64,1536]{2,1,0:T(8,128)(2,1)} %pad_maximum_fusion.9.refs_2_), channel_id=1, source_target_pairs={{0,4},{1,5},{2,6},{3,7},{4,0},{5,1},{6,2},{7,3},{8,12},{9,13},{10,... | collective-permute-start | bytes 4718600 | tf_op jit(solution)/shard_map/ppermute | solution.py:33
  323.9 56.5 %collective-permute-start.52 = (bf16[4,96,1024]{2,1,0:T(8,128)(2,1)}, bf16[4,96,1024]{2,1,0:T(8,128)(2,1)}, u32[]{:S(2)}, u32[]{:S(2)}) collective-permute-start(bf16[4,96,1024]{2,1,0:T(8,128)(2,1)} %pad_maximum_fusion.23), channel_id=1, source_target_pairs={{0,4},{1,5},{2,6},{3,7},{4,0},{5,1},{6,2},{7,3},{8,12},{9,13},{10,... | collective-permute-start | bytes 2359304 | tf_op jit(solution)/shard_map/ppermute | solution.py:33
  325.3 55.2 %collective-permute-start.53 = (bf16[4,64,1536]{2,1,0:T(8,128)(2,1)}, bf16[4,64,1536]{2,1,0:T(8,128)(2,1)}, u32[]{:S(2)}, u32[]{:S(2)}) collective-permute-start(bf16[4,64,1536]{2,1,0:T(8,128)(2,1)} %pad_maximum_fusion.24), channel_id=1, source_target_pairs={{0,2},{1,3},{2,0},{3,1},{4,6},{5,7},{6,4},{7,5},{8,10},{9,11},{10,... | collective-permute-start | bytes 2359304 | tf_op jit(solution)/shard_map/ppermute | solution.py:33
  385.7 58.4 %collective-permute-start.54 = (bf16[8,96,1024]{2,1,0:T(8,128)(2,1)}, bf16[8,96,1024]{2,1,0:T(8,128)(2,1)}, u32[]{:S(2)}, u32[]{:S(2)}) collective-permute-start(bf16[8,96,1024]{2,1,0:T(8,128)(2,1)} %pad_maximum_fusion.12.refs_0_), channel_id=1, source_target_pairs={{0,2},{1,3},{2,0},{3,1},{4,6},{5,7},{6,4},{7,5},{8,10},{9,11},{10,... | collective-permute-start | bytes 4718600 | tf_op jit(solution)/shard_map/ppermute | solution.py:33
  387.4 56.7 %collective-permute-start.55 = (bf16[8,64,1536]{2,1,0:T(8,128)(2,1)}, bf16[8,64,1536]{2,1,0:T(8,128)(2,1)}, u32[]{:S(2)}, u32[]{:S(2)}) collective-permute-start(bf16[8,64,1536]{2,1,0:T(8,128)(2,1)} %pad_maximum_fusion.13.refs_2_), channel_id=1, source_target_pairs={{0,4},{1,5},{2,6},{3,7},{4,0},{5,1},{6,2},{7,3},{8,12},{9,13},{10,... | collective-permute-start | bytes 4718600 | tf_op jit(solution)/shard_map/ppermute | solution.py:33
  388.1 66.5 %collective-permute-start.56 = (bf16[8,96,1024]{2,1,0:T(8,128)(2,1)}, bf16[8,96,1024]{2,1,0:T(8,128)(2,1)}, u32[]{:S(2)}, u32[]{:S(2)}) collective-permute-start(bf16[8,96,1024]{2,1,0:T(8,128)(2,1)} %get-tuple-element.405), channel_id=1, source_target_pairs={{0,2},{1,3},{2,0},{3,1},{4,6},{5,7},{6,4},{7,5},{8,10},{9,11},{10,... | collective-permute-start | bytes 4718600 | tf_op jit(solution)/shard_map/ppermute | solution.py:33
  388.4 67.5 %collective-permute-start.57 = (bf16[8,64,1536]{2,1,0:T(8,128)(2,1)}, bf16[8,64,1536]{2,1,0:T(8,128)(2,1)}, u32[]{:S(2)}, u32[]{:S(2)}) collective-permute-start(bf16[8,64,1536]{2,1,0:T(8,128)(2,1)} %get-tuple-element.406), channel_id=1, source_target_pairs={{0,4},{1,5},{2,6},{3,7},{4,0},{5,1},{6,2},{7,3},{8,12},{9,13},{10,... | collective-permute-start | bytes 4718600 | tf_op jit(solution)/shard_map/ppermute | solution.py:33
  463.1 81.8 %collective-permute-start.66 = (bf16[2,4,128,1536]{3,2,1,0:T(8,128)(2,1)}, bf16[2,4,128,1536]{3,2,1,0:T(8,128)(2,1)}, u32[]{:S(2)}, u32[]{:S(2)}) collective-permute-start(bf16[2,4,128,1536]{3,2,1,0:T(8,128)(2,1)} %get-tuple-element.449), channel_id=1, source_target_pairs={{0,1},{1,0},{2,3},{3,2},{4,5},{5,4},{6,7},{7,6},{8,9},{9,8},{10,11... | collective-permute-start | bytes 9437192 | tf_op jit(solution)/shard_map/ppermute | solution.py:33
  463.1 75.0 %collective-permute-start.59 = (bf16[4,64,1536]{2,1,0:T(8,128)(2,1)}, bf16[4,64,1536]{2,1,0:T(8,128)(2,1)}, u32[]{:S(2)}, u32[]{:S(2)}) collective-permute-start(bf16[4,64,1536]{2,1,0:T(8,128)(2,1)} %get-tuple-element.424), channel_id=1, source_target_pairs={{0,2},{1,3},{2,0},{3,1},{4,6},{5,7},{6,4},{7,5},{8,10},{9,11},{10,... | collective-permute-start | bytes 2359304 | tf_op jit(solution)/shard_map/ppermute | solution.py:33
  463.5 74.7 %collective-permute-start.60 = (bf16[8,96,1024]{2,1,0:T(8,128)(2,1)}, bf16[8,96,1024]{2,1,0:T(8,128)(2,1)}, u32[]{:S(2)}, u32[]{:S(2)}) collective-permute-start(bf16[8,96,1024]{2,1,0:T(8,128)(2,1)} %get-tuple-element.425), channel_id=1, source_target_pairs={{0,2},{1,3},{2,0},{3,1},{4,6},{5,7},{6,4},{7,5},{8,10},{9,11},{10,... | collective-permute-start | bytes 4718600 | tf_op jit(solution)/shard_map/ppermute | solution.py:33
  465.2 73.0 %collective-permute-start.61 = (bf16[8,64,1536]{2,1,0:T(8,128)(2,1)}, bf16[8,64,1536]{2,1,0:T(8,128)(2,1)}, u32[]{:S(2)}, u32[]{:S(2)}) collective-permute-start(bf16[8,64,1536]{2,1,0:T(8,128)(2,1)} %get-tuple-element.426), channel_id=1, source_target_pairs={{0,4},{1,5},{2,6},{3,7},{4,0},{5,1},{6,2},{7,3},{8,12},{9,13},{10,... | collective-permute-start | bytes 4718600 | tf_op jit(solution)/shard_map/ppermute | solution.py:33
  483.7 62.9 %collective-permute-start.67 = (bf16[2,4,128,1536]{3,2,1,0:T(8,128)(2,1)}, bf16[2,4,128,1536]{3,2,1,0:T(8,128)(2,1)}, u32[]{:S(2)}, u32[]{:S(2)}) collective-permute-start(bf16[2,4,128,1536]{3,2,1,0:T(8,128)(2,1)} %get-tuple-element.451), channel_id=1, source_target_pairs={{0,1},{1,0},{2,3},{3,2},{4,5},{5,4},{6,7},{7,6},{8,9},{9,8},{10,11... | collective-permute-start | bytes 9437192 | tf_op jit(solution)/shard_map/ppermute | solution.py:33
  543.4 36.7 %collective-permute-start.64 = (bf16[8,96,1024]{2,1,0:T(8,128)(2,1)}, bf16[8,96,1024]{2,1,0:T(8,128)(2,1)}, u32[]{:S(2)}, u32[]{:S(2)}) collective-permute-start(bf16[8,96,1024]{2,1,0:T(8,128)(2,1)} %get-tuple-element.444), channel_id=1, source_target_pairs={{0,2},{1,3},{2,0},{3,1},{4,6},{5,7},{6,4},{7,5},{8,10},{9,11},{10,... | collective-permute-start | bytes 4718600 | tf_op jit(solution)/shard_map/ppermute | solution.py:33
  543.7 36.4 %collective-permute-start.65 = (bf16[8,64,1536]{2,1,0:T(8,128)(2,1)}, bf16[8,64,1536]{2,1,0:T(8,128)(2,1)}, u32[]{:S(2)}, u32[]{:S(2)}) collective-permute-start(bf16[8,64,1536]{2,1,0:T(8,128)(2,1)} %get-tuple-element.445), channel_id=1, source_target_pairs={{0,4},{1,5},{2,6},{3,7},{4,0},{5,1},{6,2},{7,3},{8,12},{9,13},{10,... | collective-permute-start | bytes 4718600 | tf_op jit(solution)/shard_map/ppermute | solution.py:33
  615.4 38.9 %collective-permute-start.78 = (bf16[4,96,1024]{2,1,0:T(8,128)(2,1)}, bf16[4,96,1024]{2,1,0:T(8,128)(2,1)}, u32[]{:S(2)}, u32[]{:S(2)}) collective-permute-start(bf16[4,96,1024]{2,1,0:T(8,128)(2,1)} %get-tuple-element.483), channel_id=1, source_target_pairs={{0,4},{1,5},{2,6},{3,7},{4,0},{5,1},{6,2},{7,3},{8,12},{9,13},{10,... | collective-permute-start | bytes 2359304 | tf_op jit(solution)/shard_map/ppermute | solution.py:33
  616.9 37.5 %collective-permute-start.79 = (bf16[4,64,1536]{2,1,0:T(8,128)(2,1)}, bf16[4,64,1536]{2,1,0:T(8,128)(2,1)}, u32[]{:S(2)}, u32[]{:S(2)}) collective-permute-start(bf16[4,64,1536]{2,1,0:T(8,128)(2,1)} %get-tuple-element.484), channel_id=1, source_target_pairs={{0,2},{1,3},{2,0},{3,1},{4,6},{5,7},{6,4},{7,5},{8,10},{9,11},{10,... | collective-permute-start | bytes 2359304 | tf_op jit(solution)/shard_map/ppermute | solution.py:33
  691.6 39.5 %collective-permute-start.92 = (bf16[576,1536]{1,0:T(8,128)(2,1)}, bf16[576,1536]{1,0:T(8,128)(2,1)}, u32[]{:S(2)}, u32[]{:S(2)}) collective-permute-start(bf16[576,1536]{1,0:T(8,128)(2,1)} %bitcast.72), channel_id=1, source_target_pairs={{0,1},{1,0},{2,3},{3,2},{4,5},{5,4},{6,7},{7,6},{8,9},{9,8},{10,11... | collective-permute-start | bytes 5308424 | tf_op jit(solution)/shard_map/ppermute | solution.py:33
  704.0 38.1 %collective-permute-start.86 = (bf16[2,2,2,96,1152]{4,3,1,0,2:T(8,128)(2,1)}, bf16[2,2,2,96,1152]{4,3,1,0,2:T(8,128)(2,1)}, u32[]{:S(2)}, u32[]{:S(2)}) collective-permute-start(bf16[2,2,2,96,1152]{4,3,1,0,2:T(8,128)(2,1)} %copy_bitcast_fusion.1), channel_id=1, source_target_pairs={{0,2},{1,3},{2,0},{3,1},{4,6},{5,7},{6,4},{7,5},{8,10},{9,11},{10,... | collective-permute-start | bytes 5308424 | tf_op jit(solution)/shard_map/ppermute | solution.py:33
  704.3 37.9 %collective-permute-start.87 = (bf16[2,2,2,96,1152]{4,3,1,0,2:T(8,128)(2,1)}, bf16[2,2,2,96,1152]{4,3,1,0,2:T(8,128)(2,1)}, u32[]{:S(2)}, u32[]{:S(2)}) collective-permute-start(bf16[2,2,2,96,1152]{4,3,1,0,2:T(8,128)(2,1)} %copy_bitcast_fusion), channel_id=1, source_target_pairs={{0,4},{1,5},{2,6},{3,7},{4,0},{5,1},{6,2},{7,3},{8,12},{9,13},{10,... | collective-permute-start | bytes 5308424 | tf_op jit(solution)/shard_map/ppermute | solution.py:33
  750.5 47.8 %collective-permute-start.93 = (bf16[2,2,96,1152]{3,2,1,0:T(8,128)(2,1)}, bf16[2,2,96,1152]{3,2,1,0:T(8,128)(2,1)}, u32[]{:S(2)}, u32[]{:S(2)}) collective-permute-start(bf16[2,2,96,1152]{3,2,1,0:T(8,128)(2,1)} %get-tuple-element.515), channel_id=1, source_target_pairs={{0,4},{1,5},{2,6},{3,7},{4,0},{5,1},{6,2},{7,3},{8,12},{9,13},{10,... | collective-permute-start | bytes 2654216 | tf_op jit(solution)/shard_map/ppermute | solution.py:33
  751.2 47.1 %collective-permute-start.94 = (bf16[2,2,96,1152]{3,2,1,0:T(8,128)(2,1)}, bf16[2,2,96,1152]{3,2,1,0:T(8,128)(2,1)}, u32[]{:S(2)}, u32[]{:S(2)}) collective-permute-start(bf16[2,2,96,1152]{3,2,1,0:T(8,128)(2,1)} %get-tuple-element.516), channel_id=1, source_target_pairs={{0,2},{1,3},{2,0},{3,1},{4,6},{5,7},{6,4},{7,5},{8,10},{9,11},{10,... | collective-permute-start | bytes 2654216 | tf_op jit(solution)/shard_map/ppermute | solution.py:33
  752.9 45.4 %collective-permute-start.95 = (bf16[48,768]{1,0:T(8,128)(2,1)}, bf16[48,768]{1,0:T(8,128)(2,1)}, u32[]{:S(2)}, u32[]{:S(2)}) collective-permute-start(bf16[48,768]{1,0:T(8,128)(2,1)} %fusion.38), channel_id=1, source_target_pairs={{0,16},{1,17},{2,18},{3,19},{4,20},{5,21},{6,22},{7,23},{8,24},{9,... | collective-permute-start | bytes 221192 | tf_op jit(solution)/shard_map/ppermute | solution.py:33
  754.8 43.5 %collective-permute-start.96 = (bf16[48,768]{1,0:T(8,128)(2,1)}, bf16[48,768]{1,0:T(8,128)(2,1)}, u32[]{:S(2)}, u32[]{:S(2)}) collective-permute-start(bf16[48,768]{1,0:T(8,128)(2,1)} %fusion.39), channel_id=1, source_target_pairs={{0,16},{1,17},{2,18},{3,19},{4,20},{5,21},{6,22},{7,23},{8,24},{9,... | collective-permute-start | bytes 221192 | tf_op jit(solution)/shard_map/ppermute | solution.py:33
  812.3 52.6 %collective-permute-start.107 = (bf16[2,96,1152]{2,1,0:T(8,128)(2,1)}, bf16[2,96,1152]{2,1,0:T(8,128)(2,1)}, u32[]{:S(2)}, u32[]{:S(2)}) collective-permute-start(bf16[2,96,1152]{2,1,0:T(8,128)(2,1)} %get-tuple-element.535), channel_id=1, source_target_pairs={{0,8},{1,9},{2,10},{3,11},{4,12},{5,13},{6,14},{7,15},{8,0},{9,1},... | collective-permute-start | bytes 1327112 | tf_op jit(solution)/shard_map/ppermute | solution.py:33
  813.9 50.9 %collective-permute-start.108 = (bf16[2,96,1152]{2,1,0:T(8,128)(2,1)}, bf16[2,96,1152]{2,1,0:T(8,128)(2,1)}, u32[]{:S(2)}, u32[]{:S(2)}) collective-permute-start(bf16[2,96,1152]{2,1,0:T(8,128)(2,1)} %get-tuple-element.536), channel_id=1, source_target_pairs={{0,8},{1,9},{2,10},{3,11},{4,12},{5,13},{6,14},{7,15},{8,0},{9,1},... | collective-permute-start | bytes 1327112 | tf_op jit(solution)/shard_map/ppermute | solution.py:33
  (236 other events, 3079.9 us)

commit v7 on v6

--- a/solution.py
+++ b/solution.py
@@ -191,26 +191,25 @@
     return Flow(scatter_steps(parts, order, chip, chip_bits, sent))
 
 
-def scatter_sum(parts, colour, chip, chip_bits, sent=low):
-    flow = scatter_flow(parts, colour, chip, chip_bits, sent)
+def row_steps(row, chip, chip_bits, first_bit):
+    held = row[None]
+    for bit in range(chip_bits):
+        arriving = yield held, bit + first_bit - 1
+        held = jnp.concatenate([held, arriving], axis=0)
+    places = jnp.arange(1 << chip_bits)
+    pick = jnp.bitwise_xor(places, chip)[:, None] == places[None, :]
+    return jnp.dot(pick.astype(held.dtype), held, preferred_element_type=full).astype(held.dtype)
+
+
+def row_flow(row, chip, chip_bits, first_bit=1):
+    return Flow(row_steps(row, chip, chip_bits, first_bit))
+
+
+def run(flow):
     while flow.wanted is not None:
         array, bit = flow.wanted
         flow.arrive(swap(array, bit + 1))
     return flow.result
-
-
-def gather_rows(row, chip, chip_bits, first_bit=1):
-    order = gather_order(chip_bits, 0)
-    held = row[None]
-    for bit in order:
-        held = jnp.concatenate([held, swap(held, bit + first_bit)], axis=0)
-    places = jnp.arange(1 << chip_bits)
-    position = jnp.zeros_like(places)
-    apart = jnp.bitwise_xor(places, chip)
-    for step, bit in enumerate(order):
-        position = position + (jnp.bitwise_and(apart >> bit, 1) << step)
-    pick = position[:, None] == places[None, :]
-    return jnp.dot(pick.astype(held.dtype), held, preferred_element_type=full).astype(held.dtype)
 
 
 def to_phases(block_in, row_count):
@@ -737,6 +736,7 @@
     held,
     sum_plain,
     sum_normed,
+    woven,
 ):
     step = pl.program_id(0)
     core = core_ref[0]
@@ -834,9 +834,17 @@
                     at = pl.ds(block * width, width)
                     plain = normed_strip(x_ref, average, scale, near, at)
                     spread = jnp.concatenate([scale[near, :]] * (width // 128), axis=1)
-                    out_ref[rows, at] = middle_ref[rows, at] + spread * (
+                    result = middle_ref[rows, at] + spread * (
                         held[block, rows, :] - mean_plain - plain * mean_normed
                     )
+                    for lane in range(0, width, 128):
+                        woven[(block * width + lane) // 128, pl.ds(plane % 2, STRIP, stride=2), :] = (
+                            result[:, lane : lane + 128]
+                        )
+                if plane % 2 == 1:
+                    start = pl.multiple_of((2 * row + plane // 2) * SIDE, SIDE)
+                    for lane in range(model // 128):
+                        out_ref[pl.ds(start, SIDE), lane * 128 : lane * 128 + 128] = woven[lane]
 
 
 def conv_back(core, x_near, kept, arriving, kernel, mods, grad_middle):
@@ -872,6 +880,7 @@
                 pltpu.VMEM((model // TILE, own_tokens, TILE), full),
                 pltpu.VMEM((own_tokens, 128), full),
                 pltpu.VMEM((own_tokens, 128), full),
+                pltpu.VMEM((model // 128, SIDE, 128), full),
             ],
         ),
         out_shape=[
@@ -952,7 +961,7 @@
         grad_middle = grad + scale * (scaled - mean_plain - plain * mean_normed)
         middle_grad_ref[rows, :] = grad_middle
         branch_grad_ref[rows, :] = (grad_middle * gate_a).astype(low)
-        products = (grad * branch_f, back, back * plain, grad_middle * branch_a)
+        products = (grad_middle * branch_a, back, back * plain, grad * branch_f)
         for index, product in enumerate(products):
             totals[index] += product[:8] + product[8:]
 
@@ -1062,16 +1071,14 @@
     canvas = join_halves(mine, swap_core(mine), core)
 
     slot(qkv_flows + [mods_flow])
-    while mods_flow.wanted is not None:
-        array, bit = mods_flow.wanted
-        mods_flow.arrive(swap(array, bit + 1))
-    mods = mods_flow.result + swap_core(mods_flow.result)
+    mods_half = run(mods_flow)
+    mods = mods_half + swap_core(mods_half)
     shift_a, scale_a, gate_a, shift_f, scale_f, gate_f = jnp.split(mods, 6)
 
     tap_count = 9 * (share + part)
     tap_words = jnp.concatenate([ffn_kernel.reshape(-1), attn_kernel.reshape(-1)])
     tap_words = jnp.pad(tap_words, (0, -tap_count % 128))
-    taps = gather_rows(tap_words, rank, chip_bits + 1, 0)
+    taps = run(row_flow(tap_words, rank, chip_bits + 1, 0))
     ffn_taps = taps[:, : 9 * share].reshape(chips, 2, 9, share)
     ffn_taps = at_bit(ffn_taps, 1, core).reshape(chips, 9, CHUNKS, piece)
     ffn_taps = ffn_taps.transpose(2, 1, 0, 3).reshape(CHUNKS, 9, chips * piece).astype(full)
@@ -1180,7 +1187,6 @@
     layer_out, grad_middle, grad_branch_mine, feed_sums = slot(
         back_flows[0] + back_flows[2], after_feed
     )
-    grad_gate_f, grad_shift_f, grad_scale_f, grad_gate_a = feed_sums[:4]
     grad_branch_mine = grad_branch_mine.reshape(4, -1, model)
     layer_out = from_phases(layer_out.reshape(4, -1, model), half_rows)[None]
 
@@ -1221,51 +1227,63 @@
             core, rows_near(canvas, core), *grad_conv, attn_taps, mods_a,
             grad_middle,
         )
-        input_grad = from_phases(input_grad.reshape(4, -1, model), half_rows)
-        return attn_tap_grad[:9], input_grad, mods_grad[0], mods_grad[1]
-
-    attn_tap_grad, input_grad, grad_shift_a, grad_scale_a = slot(
+        return attn_tap_grad[:9], input_grad, mods_grad[:2]
+
+    attn_tap_grad, input_grad, attn_sums = slot(
         qkv_flows + proj_flows + back_flows[2], leave_block
     )
-    slot.finish(sum(back_flows, proj_flows + qkv_flows))
-    up_shares = [flows[0].result for flows in back_flows]
-    down_shares = [flows[1].result for flows in back_flows]
-    tap_grads = [g[:9].reshape(9, chips, piece) for g in grads]
-    qkv_share = jnp.concatenate([f.result for f in qkv_flows], axis=1)
-    proj_share = jnp.concatenate([f.result for f in proj_flows], axis=1)
-    proj_share = lax.ppermute(proj_share, AXES, proj_back)
-
-    grad_mods = jnp.concatenate(
-        [grad_shift_a, grad_scale_a, grad_gate_a, grad_shift_f, grad_scale_f, grad_gate_f]
-    )
-    grad_mods = (grad_mods + swap_core(grad_mods)).astype(low)
-    grad_mods_all = gather_rows(grad_mods, chip, chip_bits)
-    mod_grad = jnp.dot(lifted.T, grad_mods_all, preferred_element_type=full)
-    (cond_grad,) = lift_pull(jnp.dot(grad_mods_all, mod_weight.T, preferred_element_type=full))
-    table_grad = jnp.dot(picks.astype(full).T, cond_grad, precision=highest)
-
-    ffn_tap_grad = jnp.concatenate(tap_grads, axis=2).transpose(1, 0, 2)
-    attn_split = attn_tap_grad.reshape(9, chips, 2, part)
-    attn_kept, attn_leaving = halves_of(attn_split, 2)
-    attn_tap_grad = (attn_kept + swap_core(attn_leaving)).transpose(1, 0, 2)
-    tap_parts = jnp.concatenate(
-        [ffn_tap_grad.reshape(chips, -1), attn_tap_grad.reshape(chips, -1)], axis=1
-    )
-    tap_share = scatter_sum(tap_parts, 0, chip, chip_bits, sent=full)
-    ffn_share = tap_share[: 9 * share].reshape(9, share)
-    kernel_share = tap_share[9 * share :].reshape(9, part)
-
     def row_split(array, axis):
         pair = array.reshape((2, part) + array.shape[1:])
         kept, leaving = halves_of(pair, 0)
         arriving = swap_core(leaving)
         return jnp.stack(in_core_order(kept, arriving, core), axis=axis)
 
-    up_all = jnp.stack(up_shares, axis=1).reshape(2 * part, CHUNKS, chips, piece)
-    up_share = row_split(up_all.transpose(0, 2, 1, 3), 2).reshape(part, -1)
+    slot.finish(sum(back_flows, []))
+    grad_mods = jnp.concatenate([attn_sums, feed_sums[:4]], axis=0)
+    tap_grads = [g[:9].reshape(9, chips, piece) for g in grads]
+    ffn_tap_grad = jnp.concatenate(tap_grads, axis=2).transpose(1, 0, 2)
+    attn_kept, attn_leaving = halves_of(attn_tap_grad.reshape(9, chips, 2, part), 2)
+
+    def between_cores():
+        both = (grad_mods + swap_core(grad_mods)).astype(low)
+        return both, attn_kept + swap_core(attn_leaving)
+
+    grad_mods, attn_tap_grad = slot(qkv_flows + proj_flows, between_cores)
+    mods_flow = row_flow(grad_mods.reshape(-1), chip, chip_bits)
+    tap_parts = jnp.concatenate(
+        [ffn_tap_grad.reshape(chips, -1), attn_tap_grad.transpose(1, 0, 2).reshape(chips, -1)],
+        axis=1,
+    )
+    tap_flow = scatter_flow(tap_parts, 0, chip, chip_bits, sent=full)
+    up_shares = [flows[0].result for flows in back_flows]
+    down_shares = [flows[1].result for flows in back_flows]
+
+    def split_up():
+        up_all = jnp.stack(up_shares, axis=1).reshape(2 * part, CHUNKS, chips, piece)
+        return row_split(up_all.transpose(0, 2, 1, 3), 2).reshape(part, -1)
+
+    slot.finish(proj_flows)
+    proj_share = jnp.concatenate([f.result for f in proj_flows], axis=1)
+    up_share = slot(qkv_flows + [mods_flow, tap_flow], split_up)
+    slot.finish(qkv_flows)
+    qkv_share = jnp.concatenate([f.result for f in qkv_flows], axis=1)
+
+    def split_qkv():
+        qkv_all = qkv_share.reshape(2 * part, pairs, 3, 128).transpose(0, 2, 1, 3)
+        qkv_out = row_split(qkv_all, 2).reshape(part, -1)
+        return qkv_out, lax.ppermute(proj_share, AXES, proj_back)
+
+    qkv_out, proj_share = slot([mods_flow, tap_flow], split_qkv)
+    slot.finish([mods_flow, tap_flow])
     down_share = jnp.concatenate(down_shares, axis=0)
-    qkv_all = qkv_share.reshape(2 * part, pairs, 3, 128).transpose(0, 2, 1, 3)
-    qkv_out = row_split(qkv_all, 2).reshape(part, -1)
+
+    grad_mods_all = mods_flow.result
+    mod_grad = jnp.dot(lifted.T, grad_mods_all, preferred_element_type=full)
+    (cond_grad,) = lift_pull(jnp.dot(grad_mods_all, mod_weight.T, preferred_element_type=full))
+    table_grad = jnp.dot(picks.astype(full).T, cond_grad, precision=highest)
+    tap_share = tap_flow.result
+    ffn_share = tap_share[: 9 * share].reshape(9, share)
+    kernel_share = tap_share[9 * share :].reshape(9, part)
 
     return (
         layer_out,
@@ -1278,7 +1296,7 @@
         up_share,
         ffn_share,
         down_share,
-        grad_shift_f[None],
+        feed_sums[1:2],
     )
 
 

time: 908 us -> 894 us (0.985)
  local copies, waits for them, and re-layouts: 99.1 us -> 81.3 us
  transfers between devices with their start and end apart: 114 -> 114, of which waited for: 39 -> 40; matrix products, arithmetic and copies ran while one was open for 23% -> 23% of each run, Pallas kernels for 33% -> 34%
where the time goes in v7:
time: 894 us; the launch traced here: 885 us
  Pallas kernels  305 us (34%)
  waiting for transfers between devices  178 us (20%)
  other arithmetic  144 us (16%)
  starting transfers between devices  125 us (14%)
  local copies, waits for them, and re-layouts  81.3 us (9%)
  matrix products  48.2 us (5%)
    ppermute x112, waiting for transfers between devices, swap(): lax.ppermute(x, AXES, [(i, i ^ 1 << bit) for i in range(device_count())])  178 us
    pallas_call x3, Pallas kernels, feed_forward(): pl.pallas_call(functools.partial(feed_body, spread), grid_spec=pltpu.Pref...  163 us
    ppermute x112, starting transfers between devices, swap(): lax.ppermute(x, AXES, [(i, i ^ 1 << bit) for i in range(device_count())])  119 us
    concatenate x28, other arithmetic, gather_steps(): held = jnp.concatenate([held, arriving], axis=0)  49 us
    convert_element_type x18, other arithmetic, halving_steps(): (staying[at].astype(full) + arriving[at].astype(full)).astype(low)  33.2 us
    pallas_call x1, Pallas kernels, attend_back(): pl.pallas_call(attend_back_body, grid=(pairs,), in_specs=[pl.BlockSpec((P...  28.9 us
    pallas_call x1, Pallas kernels, conv_in(): pl.pallas_call(conv_in_body, grid=(model // TILE,), in_specs=[pl.BlockSpe...  22.8 us
    pallas_call x1, Pallas kernels, conv_back(): pl.pallas_call(conv_back_body, grid_spec=pltpu.PrefetchScalarGridSpec(num...  21.4 us
  transfers between devices with their start and end apart: 114, of which 40 were waited for; matrix products, arithmetic and copies ran while one was open for 23% of the time, Pallas kernels for 34%

profile of v7, /device:TPU:0, one launch (start us, length us, event | category | flops | bytes accessed | tf_op | source)
XLA Modules:
  0.0 884.9 jit_solution(3772599772975767580)
XLA Ops:
  27.1 4.5 collective-permute-done.2
  58.7 8.1 collective-permute-done.27
  88.5 10.5 %collective-permute-done.11 = bf16[1,48,768]{2,1,0:T(8,128)(2,1)S(1)} collective-permute-done((bf16[1,48,768]{2,1,0:T(8,128)(2,1)S(1)}, bf16[1,48,768]{2,1,0:T(8,128)(2,1)S(1)}, u32[]{:S(2)}, u32[]{:S(2)}) %collective-permute-start.11) | collective-permute-done | bytes 73760 | tf_op jit(solution)/shard_map/ppermute | solution.py:33
  123.4 5.0 collective-permute-done.18
  132.1 11.3 %collective-permute-done.21 = bf16[1,96,1024]{2,1,0:T(8,128)(2,1)S(1)} collective-permute-done((bf16[1,96,1024]{2,1,0:T(8,128)(2,1)S(1)}, bf16[1,96,1024]{2,1,0:T(8,128)(2,1)S(1)}, u32[]{:S(2)}, u32[]{:S(2)}) %collective-permute-start.21) | collective-permute-done | bytes 196640 | tf_op jit(solution)/shard_map/ppermute | solution.py:33
  149.1 22.8 %conv_in.1 = bf16[1024,1536]{1,0:T(8,128)(2,1)} custom-call(bf16[1024,1536]{1,0:T(8,128)(2,1)} %bitcast.356, f32[16,1536]{1,0:T(8,128)} %pad_convert_fusion.1.kernel_ref, f32[8,1536]{1,0:T(8,128)} %maximum_maximum_fusion.mods_ref), custom_call_target="tpu_custom_call" | custom-call | flops 47185920 | bytes 6291456 | tf_op jit(solution)/shard_map/conv_in/pallas_call | solution.py:699
  184.7 5.6 assemble.5
  190.3 5.6 assemble.4
  195.9 12.9 %convolution_convert_fusion.2.qkv_ref = bf16[1024,2304]{1,0:T(8,128)(2,1)} fusion(bf16[1024,1536]{1,0:T(8,128)(2,1)} %conv_in.1, bf16[1536,1152]{1,0:T(8,128)(2,1)} %bitcast.362, bf16[1536,1152]{1,0:T(8,128)(2,1)} %bitcast.364), kind=kOutput, calls=%fused_computation.3 | convolution fusion | flops 7264272384 | bytes 14942208 | tf_op jit(solution)/shard_map/dot_general | solution.py:1117
  211.0 5.4 pad_maximum_fusion
  229.8 10.2 %collective-permute-done.42 = bf16[1,96,1024]{2,1,0:T(8,128)(2,1)S(1)} collective-permute-done((bf16[1,96,1024]{2,1,0:T(8,128)(2,1)S(1)}, bf16[1,96,1024]{2,1,0:T(8,128)(2,1)S(1)}, u32[]{:S(2)}, u32[]{:S(2)}) %collective-permute-start.42) | collective-permute-done | bytes 196640 | tf_op jit(solution)/shard_map/ppermute | solution.py:33
  240.6 15.4 %attend.1 = bf16[1024,768]{1,0:T(8,128)(2,1)} custom-call(f32[256,256]{1,0:T(8,128)} %compare_convert_fusion.mask_ref, bf16[1024,2304]{1,0:T(8,128)(2,1)} %convolution_convert_fusion.2.qkv_ref), custom_call_target="tpu_custom_call" | custom-call | flops 3221225472 | bytes 6291456 | tf_op jit(solution)/shard_map/attend/pallas_call | solution.py:333
  264.7 6.4 convolution_convert_fusion.4.part_ref
  305.8 17.6 %enter_feed.1 = (bf16[1024,1536]{1,0:T(8,128)(2,1)}, bf16[1536,1024]{1,0:T(8,128)(2,1)}, bf16[1024,1536]{1,0:T(8,128)(2,1)}) custom-call(bf16[1024,1536]{1,0:T(8,128)(2,1)} %bitcast.357, bf16[1024,1536]{1,0:T(8,128)(2,1)} %convolution_convert_fusion.4.part_ref, bf16[1024,1536]{1,0:T(8,128)(2,1)} %collective-permute-done.48.other_ref, ...), custom_call_target="tpu_custom_call" | custom-call | flops 1000 | bytes 1000 | tf_op jit(solution)/shard_map/enter_feed/pallas_call | solution.py:924
  336.1 54.8 %feed_forward.3 = (bf16[2,4,128,1536]{3,2,1,0:T(8,128)(2,1)}, bf16[2,4,128,1536]{3,2,1,0:T(8,128)(2,1)}, bf16[8,96,1024]{2,1,0:T(8,128)(2,1)}, bf16[8,96,1024]{2...) custom-call(s32[49]{0:T(128)} %pad_add_fusion.1.words_ref, ...), custom_call_target="tpu_custom_call" | custom-call | flops 19327352832 | bytes 28311552 | tf_op jit(solution)/shard_map/feed_forward/pallas_call | solution.py:591
  400.3 54.4 %feed_forward.4 = (bf16[2,4,128,1536]{3,2,1,0:T(8,128)(2,1)}, bf16[2,4,128,1536]{3,2,1,0:T(8,128)(2,1)}, bf16[8,96,1024]{2,1,0:T(8,128)(2,1)}, bf16[8,96,1024]{2...) custom-call(s32[49]{0:T(128)} %pad_add_fusion.1.words_ref, ...), custom_call_target="tpu_custom_call" | custom-call | flops 19327352832 | bytes 28311552 | tf_op jit(solution)/shard_map/feed_forward/pallas_call | solution.py:591
  454.7 9.7 %collective-permute-done.56 = bf16[8,96,1024]{2,1,0:T(8,128)(2,1)} collective-permute-done((bf16[8,96,1024]{2,1,0:T(8,128)(2,1)}, bf16[8,96,1024]{2,1,0:T(8,128)(2,1)}, u32[]{:S(2)}, u32[]{:S(2)}) %collective-permute-start.56) | collective-permute-done | bytes 1572896 | tf_op jit(solution)/shard_map/ppermute | solution.py:33
  476.1 16.4 %collective-permute-done.58 = bf16[4,96,1024]{2,1,0:T(8,128)(2,1)S(1)} collective-permute-done((bf16[4,96,1024]{2,1,0:T(8,128)(2,1)S(1)}, bf16[4,96,1024]{2,1,0:T(8,128)(2,1)S(1)}, u32[]{:S(2)}, u32[]{:S(2)}) %collective-permute-start.58) | collective-permute-done | bytes 786464 | tf_op jit(solution)/shard_map/ppermute | solution.py:33
  493.3 54.3 %feed_forward.5 = (bf16[2,4,128,1536]{3,2,1,0:T(8,128)(2,1)}, bf16[2,4,128,1536]{3,2,1,0:T(8,128)(2,1)}, bf16[8,96,1024]{2,1,0:T(8,128)(2,1)}, bf16[8,96,1024]{2...) custom-call(s32[49]{0:T(128)} %pad_add_fusion.1.words_ref, ...), custom_call_target="tpu_custom_call" | custom-call | flops 19327352832 | bytes 28311552 | tf_op jit(solution)/shard_map/feed_forward/pallas_call | solution.py:591
  560.0 15.6 %leave_feed.1 = (bf16[512,1536]{1,0:T(8,128)(2,1)}, f32[512,1536]{1,0:T(8,128)}, bf16[512,1536]{1,0:T(8,128)(2,1)}, f32[8,1536]{1,0:T(8,128)}) custom-call(s32[1]{0:T(128)} %bitcast.37.words_ref.core_ref, bf16[1024,1536]{1,0:T(8,128)(2,1)} %bitcast.358, bf16[1024,1536]{1,0:T(8,128)(2,1)} %convolution_convert_fusion.4.part_ref, ...), custom_call_target="tpu_custom_call" | custom-call | flops 1000 | bytes 1000 | tf_op jit(solution)/shard_map/leave_feed/pallas_call | solution.py:980
  575.7 13.9 %collective-permute-done.64 = bf16[8,96,1024]{2,1,0:T(8,128)(2,1)} collective-permute-done((bf16[8,96,1024]{2,1,0:T(8,128)(2,1)}, bf16[8,96,1024]{2,1,0:T(8,128)(2,1)}, u32[]{:S(2)}, u32[]{:S(2)}) %collective-permute-start.64) | collective-permute-done | bytes 1572896 | tf_op jit(solution)/shard_map/ppermute | solution.py:33
  634.0 28.9 %attend_back.1 = bf16[1024,2304]{1,0:T(8,128)(2,1)} custom-call(f32[256,256]{1,0:T(8,128)} %compare_convert_fusion.mask_ref, bf16[1024,2304]{1,0:T(8,128)(2,1)} %convolution_convert_fusion.2.qkv_ref, bf16[1024,768]{1,0:T(8,128)(2,1)} %convolution_convert_fusion.7.grad_ref), custom_call_target="tpu_custom_call" | custom-call | flops 8053063680 | bytes 11010048 | tf_op jit(solution)/shard_map/attend_back/pallas_call | solution.py:354
  676.1 10.3 %convolution_convert_fusion = bf16[1536,2304]{1,0:T(8,128)(2,1)S(1)} fusion(bf16[1024,1536]{1,0:T(8,128)(2,1)S(1)} %copy-done.19, bf16[1024,2304]{1,0:T(8,128)(2,1)} %attend_back.1), kind=kOutput, calls=%fused_computation | convolution fusion | flops 7251296256 | bytes 14942208 | tf_op jit(solution)/shard_map/dot_general | solution.py:1207
  686.5 8.0 convolution_convert_fusion.3
  734.8 7.5 collective-permute-done.90
  744.7 5.0 collective-permute-done.86
  771.1 21.4 %conv_back.1 = (f32[512,1536]{1,0:T(8,128)}, f32[16,1536]{1,0:T(8,128)}, f32[8,1536]{1,0:T(8,128)}) custom-call(s32[1]{0:T(128)} %bitcast.37.words_ref.core_ref, bf16[576,1536]{1,0:T(8,128)(2,1)} %bitcast.376, bf16[576,1536]{1,0:T(8,128)(2,1)} %bitcast.377, bf16[576,1536]{1,0:T(8,128)(2,1)} %collective-permute-done.92.arriving_ref, ...), custom_call_target="tpu_custom_call" | custom-call | flops 55050240 | bytes 11010048 | tf_op jit(solution)/shard_map/conv_back/pallas_call | solution.py:857
  800.4 4.6 reshape.408
  822.1 8.4 collective-permute-done.98
  840.7 8.7 collective-permute-done.101
  849.5 4.6 collective-permute-done.102
  872.1 5.6 collective-permute-done.113
  (694 shorter events, 408.2 us)
Async XLA Ops:
  114.0 57.9 %collective-permute-start.15 = (bf16[8,96,1152]{2,1,0:T(8,128)(2,1)S(1)}, bf16[8,96,1152]{2,1,0:T(8,128)(2,1)}, u32[]{:S(2)}, u32[]{:S(2)}) collective-permute-start(bf16[8,96,1152]{2,1,0:T(8,128)(2,1)S(1)} %get-tuple-element.339.refs_0_), channel_id=1, source_target_pairs={{0,2},{1,3},{2,0},{3,1},{4,6},{5,7},{6,4},{7,5},{8,10},{9,11},{10,... | collective-permute-start | bytes 5308424 | tf_op jit(solution)/shard_map/ppermute | solution.py:33
  115.6 56.4 %collective-permute-start.16 = (bf16[8,96,1152]{2,1,0:T(8,128)(2,1)}, bf16[8,96,1152]{2,1,0:T(8,128)(2,1)}, u32[]{:S(2)}, u32[]{:S(2)}) collective-permute-start(bf16[8,96,1152]{2,1,0:T(8,128)(2,1)} %get-tuple-element.340.refs_0_), channel_id=1, source_target_pairs={{0,4},{1,5},{2,6},{3,7},{4,0},{5,1},{6,2},{7,3},{8,12},{9,13},{10,... | collective-permute-start | bytes 5308424 | tf_op jit(solution)/shard_map/ppermute | solution.py:33
  123.1 48.8 %collective-permute-start.19 = (bf16[2,96,1024]{2,1,0:T(8,128)(2,1)}, bf16[2,96,1024]{2,1,0:T(8,128)(2,1)}, u32[]{:S(2)}, u32[]{:S(2)}) collective-permute-start(bf16[2,96,1024]{2,1,0:T(8,128)(2,1)} %pad_maximum_fusion.29), channel_id=1, source_target_pairs={{0,8},{1,9},{2,10},{3,11},{4,12},{5,13},{6,14},{7,15},{8,0},{9,1},... | collective-permute-start | bytes 1179656 | tf_op jit(solution)/shard_map/ppermute | solution.py:33
  128.4 43.5 %collective-permute-start.20 = (bf16[2,64,1536]{2,1,0:T(8,128)(2,1)}, bf16[2,64,1536]{2,1,0:T(8,128)(2,1)}, u32[]{:S(2)}, u32[]{:S(2)}) collective-permute-start(bf16[2,64,1536]{2,1,0:T(8,128)(2,1)} %pad_maximum_fusion.30), channel_id=1, source_target_pairs={{0,8},{1,9},{2,10},{3,11},{4,12},{5,13},{6,14},{7,15},{8,0},{9,1},... | collective-permute-start | bytes 1179656 | tf_op jit(solution)/shard_map/ppermute | solution.py:33
  256.0 39.3 %collective-permute-start.49 = (bf16[4,128,1536]{2,1,0:T(8,128)(2,1)S(1)}, bf16[4,128,1536]{2,1,0:T(8,128)(2,1)}, u32[]{:S(2)}, u32[]{:S(2)}) collective-permute-start(bf16[4,128,1536]{2,1,0:T(8,128)(2,1)S(1)} %bitcast.378), channel_id=1, source_target_pairs={{0,1},{1,0},{2,3},{3,2},{4,5},{5,4},{6,7},{7,6},{8,9},{9,8},{10,11... | collective-permute-start | bytes 4718600 | tf_op jit(solution)/shard_map/ppermute | solution.py:33
  291.2 36.6 %collective-permute-start.44 = (bf16[8,96,1024]{2,1,0:T(8,128)(2,1)}, bf16[8,96,1024]{2,1,0:T(8,128)(2,1)}, u32[]{:S(2)}, u32[]{:S(2)}) collective-permute-start(bf16[8,96,1024]{2,1,0:T(8,128)(2,1)} %pad_maximum_fusion.10.refs_0_), channel_id=1, source_target_pairs={{0,2},{1,3},{2,0},{3,1},{4,6},{5,7},{6,4},{7,5},{8,10},{9,11},{10,... | collective-permute-start | bytes 4718600 | tf_op jit(solution)/shard_map/ppermute | solution.py:33
  332.0 58.9 %collective-permute-start.50 = (bf16[8,96,1024]{2,1,0:T(8,128)(2,1)}, bf16[8,96,1024]{2,1,0:T(8,128)(2,1)}, u32[]{:S(2)}, u32[]{:S(2)}) collective-permute-start(bf16[8,96,1024]{2,1,0:T(8,128)(2,1)} %pad_maximum_fusion.8.refs_0_), channel_id=1, source_target_pairs={{0,2},{1,3},{2,0},{3,1},{4,6},{5,7},{6,4},{7,5},{8,10},{9,11},{10,... | collective-permute-start | bytes 4718600 | tf_op jit(solution)/shard_map/ppermute | solution.py:33
  333.6 57.3 %collective-permute-start.51 = (bf16[8,64,1536]{2,1,0:T(8,128)(2,1)}, bf16[8,64,1536]{2,1,0:T(8,128)(2,1)}, u32[]{:S(2)}, u32[]{:S(2)}) collective-permute-start(bf16[8,64,1536]{2,1,0:T(8,128)(2,1)} %pad_maximum_fusion.9.refs_2_), channel_id=1, source_target_pairs={{0,4},{1,5},{2,6},{3,7},{4,0},{5,1},{6,2},{7,3},{8,12},{9,13},{10,... | collective-permute-start | bytes 4718600 | tf_op jit(solution)/shard_map/ppermute | solution.py:33
  334.1 56.7 %collective-permute-start.52 = (bf16[4,96,1024]{2,1,0:T(8,128)(2,1)}, bf16[4,96,1024]{2,1,0:T(8,128)(2,1)}, u32[]{:S(2)}, u32[]{:S(2)}) collective-permute-start(bf16[4,96,1024]{2,1,0:T(8,128)(2,1)} %pad_maximum_fusion.23), channel_id=1, source_target_pairs={{0,4},{1,5},{2,6},{3,7},{4,0},{5,1},{6,2},{7,3},{8,12},{9,13},{10,... | collective-permute-start | bytes 2359304 | tf_op jit(solution)/shard_map/ppermute | solution.py:33
  335.6 55.3 %collective-permute-start.53 = (bf16[4,64,1536]{2,1,0:T(8,128)(2,1)}, bf16[4,64,1536]{2,1,0:T(8,128)(2,1)}, u32[]{:S(2)}, u32[]{:S(2)}) collective-permute-start(bf16[4,64,1536]{2,1,0:T(8,128)(2,1)} %pad_maximum_fusion.24), channel_id=1, source_target_pairs={{0,2},{1,3},{2,0},{3,1},{4,6},{5,7},{6,4},{7,5},{8,10},{9,11},{10,... | collective-permute-start | bytes 2359304 | tf_op jit(solution)/shard_map/ppermute | solution.py:33
  396.2 58.5 %collective-permute-start.54 = (bf16[8,96,1024]{2,1,0:T(8,128)(2,1)}, bf16[8,96,1024]{2,1,0:T(8,128)(2,1)}, u32[]{:S(2)}, u32[]{:S(2)}) collective-permute-start(bf16[8,96,1024]{2,1,0:T(8,128)(2,1)} %pad_maximum_fusion.12.refs_0_), channel_id=1, source_target_pairs={{0,2},{1,3},{2,0},{3,1},{4,6},{5,7},{6,4},{7,5},{8,10},{9,11},{10,... | collective-permute-start | bytes 4718600 | tf_op jit(solution)/shard_map/ppermute | solution.py:33
  397.8 56.9 %collective-permute-start.55 = (bf16[8,64,1536]{2,1,0:T(8,128)(2,1)}, bf16[8,64,1536]{2,1,0:T(8,128)(2,1)}, u32[]{:S(2)}, u32[]{:S(2)}) collective-permute-start(bf16[8,64,1536]{2,1,0:T(8,128)(2,1)} %pad_maximum_fusion.13.refs_2_), channel_id=1, source_target_pairs={{0,4},{1,5},{2,6},{3,7},{4,0},{5,1},{6,2},{7,3},{8,12},{9,13},{10,... | collective-permute-start | bytes 4718600 | tf_op jit(solution)/shard_map/ppermute | solution.py:33
  398.3 66.1 %collective-permute-start.56 = (bf16[8,96,1024]{2,1,0:T(8,128)(2,1)}, bf16[8,96,1024]{2,1,0:T(8,128)(2,1)}, u32[]{:S(2)}, u32[]{:S(2)}) collective-permute-start(bf16[8,96,1024]{2,1,0:T(8,128)(2,1)} %get-tuple-element.431), channel_id=1, source_target_pairs={{0,2},{1,3},{2,0},{3,1},{4,6},{5,7},{6,4},{7,5},{8,10},{9,11},{10,... | collective-permute-start | bytes 4718600 | tf_op jit(solution)/shard_map/ppermute | solution.py:33
  398.9 66.7 %collective-permute-start.57 = (bf16[8,64,1536]{2,1,0:T(8,128)(2,1)}, bf16[8,64,1536]{2,1,0:T(8,128)(2,1)}, u32[]{:S(2)}, u32[]{:S(2)}) collective-permute-start(bf16[8,64,1536]{2,1,0:T(8,128)(2,1)} %get-tuple-element.432), channel_id=1, source_target_pairs={{0,4},{1,5},{2,6},{3,7},{4,0},{5,1},{6,2},{7,3},{8,12},{9,13},{10,... | collective-permute-start | bytes 4718600 | tf_op jit(solution)/shard_map/ppermute | solution.py:33
  472.6 81.5 %collective-permute-start.66 = (bf16[2,4,128,1536]{3,2,1,0:T(8,128)(2,1)}, bf16[2,4,128,1536]{3,2,1,0:T(8,128)(2,1)}, u32[]{:S(2)}, u32[]{:S(2)}) collective-permute-start(bf16[2,4,128,1536]{3,2,1,0:T(8,128)(2,1)} %get-tuple-element.475), channel_id=1, source_target_pairs={{0,1},{1,0},{2,3},{3,2},{4,5},{5,4},{6,7},{7,6},{8,9},{9,8},{10,11... | collective-permute-start | bytes 9437192 | tf_op jit(solution)/shard_map/ppermute | solution.py:33
  472.6 75.0 %collective-permute-start.59 = (bf16[4,64,1536]{2,1,0:T(8,128)(2,1)}, bf16[4,64,1536]{2,1,0:T(8,128)(2,1)}, u32[]{:S(2)}, u32[]{:S(2)}) collective-permute-start(bf16[4,64,1536]{2,1,0:T(8,128)(2,1)} %get-tuple-element.450), channel_id=1, source_target_pairs={{0,2},{1,3},{2,0},{3,1},{4,6},{5,7},{6,4},{7,5},{8,10},{9,11},{10,... | collective-permute-start | bytes 2359304 | tf_op jit(solution)/shard_map/ppermute | solution.py:33
  473.2 74.5 %collective-permute-start.60 = (bf16[8,96,1024]{2,1,0:T(8,128)(2,1)}, bf16[8,96,1024]{2,1,0:T(8,128)(2,1)}, u32[]{:S(2)}, u32[]{:S(2)}) collective-permute-start(bf16[8,96,1024]{2,1,0:T(8,128)(2,1)} %get-tuple-element.451), channel_id=1, source_target_pairs={{0,2},{1,3},{2,0},{3,1},{4,6},{5,7},{6,4},{7,5},{8,10},{9,11},{10,... | collective-permute-start | bytes 4718600 | tf_op jit(solution)/shard_map/ppermute | solution.py:33
  474.6 73.0 %collective-permute-start.61 = (bf16[8,64,1536]{2,1,0:T(8,128)(2,1)}, bf16[8,64,1536]{2,1,0:T(8,128)(2,1)}, u32[]{:S(2)}, u32[]{:S(2)}) collective-permute-start(bf16[8,64,1536]{2,1,0:T(8,128)(2,1)} %get-tuple-element.452), channel_id=1, source_target_pairs={{0,4},{1,5},{2,6},{3,7},{4,0},{5,1},{6,2},{7,3},{8,12},{9,13},{10,... | collective-permute-start | bytes 4718600 | tf_op jit(solution)/shard_map/ppermute | solution.py:33
  493.3 63.7 %collective-permute-start.67 = (bf16[2,4,128,1536]{3,2,1,0:T(8,128)(2,1)}, bf16[2,4,128,1536]{3,2,1,0:T(8,128)(2,1)}, u32[]{:S(2)}, u32[]{:S(2)}) collective-permute-start(bf16[2,4,128,1536]{3,2,1,0:T(8,128)(2,1)} %get-tuple-element.477), channel_id=1, source_target_pairs={{0,1},{1,0},{2,3},{3,2},{4,5},{5,4},{6,7},{7,6},{8,9},{9,8},{10,11... | collective-permute-start | bytes 9437192 | tf_op jit(solution)/shard_map/ppermute | solution.py:33
  552.9 36.7 %collective-permute-start.64 = (bf16[8,96,1024]{2,1,0:T(8,128)(2,1)}, bf16[8,96,1024]{2,1,0:T(8,128)(2,1)}, u32[]{:S(2)}, u32[]{:S(2)}) collective-permute-start(bf16[8,96,1024]{2,1,0:T(8,128)(2,1)} %get-tuple-element.470), channel_id=1, source_target_pairs={{0,2},{1,3},{2,0},{3,1},{4,6},{5,7},{6,4},{7,5},{8,10},{9,11},{10,... | collective-permute-start | bytes 4718600 | tf_op jit(solution)/shard_map/ppermute | solution.py:33
  553.5 36.4 %collective-permute-start.65 = (bf16[8,64,1536]{2,1,0:T(8,128)(2,1)}, bf16[8,64,1536]{2,1,0:T(8,128)(2,1)}, u32[]{:S(2)}, u32[]{:S(2)}) collective-permute-start(bf16[8,64,1536]{2,1,0:T(8,128)(2,1)} %get-tuple-element.471), channel_id=1, source_target_pairs={{0,4},{1,5},{2,6},{3,7},{4,0},{5,1},{6,2},{7,3},{8,12},{9,13},{10,... | collective-permute-start | bytes 4718600 | tf_op jit(solution)/shard_map/ppermute | solution.py:33
  623.9 39.1 %collective-permute-start.78 = (bf16[4,96,1024]{2,1,0:T(8,128)(2,1)}, bf16[4,96,1024]{2,1,0:T(8,128)(2,1)}, u32[]{:S(2)}, u32[]{:S(2)}) collective-permute-start(bf16[4,96,1024]{2,1,0:T(8,128)(2,1)} %get-tuple-element.512), channel_id=1, source_target_pairs={{0,4},{1,5},{2,6},{3,7},{4,0},{5,1},{6,2},{7,3},{8,12},{9,13},{10,... | collective-permute-start | bytes 2359304 | tf_op jit(solution)/shard_map/ppermute | solution.py:33
  624.3 38.6 %collective-permute-start.79 = (bf16[4,64,1536]{2,1,0:T(8,128)(2,1)}, bf16[4,64,1536]{2,1,0:T(8,128)(2,1)}, u32[]{:S(2)}, u32[]{:S(2)}) collective-permute-start(bf16[4,64,1536]{2,1,0:T(8,128)(2,1)} %get-tuple-element.513), channel_id=1, source_target_pairs={{0,2},{1,3},{2,0},{3,1},{4,6},{5,7},{6,4},{7,5},{8,10},{9,11},{10,... | collective-permute-start | bytes 2359304 | tf_op jit(solution)/shard_map/ppermute | solution.py:33
  625.8 37.1 %collective-permute-start.74 = (bf16[2,2,2,48,768]{4,3,0,1,2:T(8,128)(2,1)}, bf16[2,2,2,48,768]{4,3,0,1,2:T(8,128)(2,1)}, u32[]{:S(2)}, u32[]{:S(2)}) collective-permute-start(bf16[2,2,2,48,768]{4,3,0,1,2:T(8,128)(2,1)} %copy_bitcast_fusion.4), channel_id=1, source_target_pairs={{0,2},{1,3},{2,0},{3,1},{4,6},{5,7},{6,4},{7,5},{8,10},{9,11},{10,... | collective-permute-start | bytes 1769480 | tf_op jit(solution)/shard_map/ppermute | solution.py:33
  626.4 36.5 %collective-permute-start.75 = (bf16[2,2,2,48,768]{4,3,1,0,2:T(8,128)(2,1)}, bf16[2,2,2,48,768]{4,3,1,0,2:T(8,128)(2,1)}, u32[]{:S(2)}, u32[]{:S(2)}) collective-permute-start(bf16[2,2,2,48,768]{4,3,1,0,2:T(8,128)(2,1)} %copy_bitcast_fusion.3), channel_id=1, source_target_pairs={{0,4},{1,5},{2,6},{3,7},{4,0},{5,1},{6,2},{7,3},{8,12},{9,13},{10,... | collective-permute-start | bytes 1769480 | tf_op jit(solution)/shard_map/ppermute | solution.py:33
  699.3 45.5 %collective-permute-start.92 = (bf16[576,1536]{1,0:T(8,128)(2,1)}, bf16[576,1536]{1,0:T(8,128)(2,1)}, u32[]{:S(2)}, u32[]{:S(2)}) collective-permute-start(bf16[576,1536]{1,0:T(8,128)(2,1)} %bitcast.72), channel_id=1, source_target_pairs={{0,1},{1,0},{2,3},{3,2},{4,5},{5,4},{6,7},{7,6},{8,9},{9,8},{10,11... | collective-permute-start | bytes 5308424 | tf_op jit(solution)/shard_map/ppermute | solution.py:33
  710.5 39.3 %collective-permute-start.86 = (bf16[2,2,2,96,1152]{4,3,0,1,2:T(8,128)(2,1)}, bf16[2,2,2,96,1152]{4,3,0,1,2:T(8,128)(2,1)}, u32[]{:S(2)}, u32[]{:S(2)}) collective-permute-start(bf16[2,2,2,96,1152]{4,3,0,1,2:T(8,128)(2,1)} %copy_bitcast_fusion.1), channel_id=1, source_target_pairs={{0,2},{1,3},{2,0},{3,1},{4,6},{5,7},{6,4},{7,5},{8,10},{9,11},{10,... | collective-permute-start | bytes 5308424 | tf_op jit(solution)/shard_map/ppermute | solution.py:33
  711.0 39.0 %collective-permute-start.87 = (bf16[2,2,2,96,1152]{4,3,1,0,2:T(8,128)(2,1)}, bf16[2,2,2,96,1152]{4,3,1,0,2:T(8,128)(2,1)}, u32[]{:S(2)}, u32[]{:S(2)}) collective-permute-start(bf16[2,2,2,96,1152]{4,3,1,0,2:T(8,128)(2,1)} %copy_bitcast_fusion), channel_id=1, source_target_pairs={{0,4},{1,5},{2,6},{3,7},{4,0},{5,1},{6,2},{7,3},{8,12},{9,13},{10,... | collective-permute-start | bytes 5308424 | tf_op jit(solution)/shard_map/ppermute | solution.py:33
  757.7 47.3 %collective-permute-start.93 = (bf16[2,2,96,1152]{3,2,0,1:T(8,128)(2,1)}, bf16[2,2,96,1152]{3,2,0,1:T(8,128)(2,1)}, u32[]{:S(2)}, u32[]{:S(2)}) collective-permute-start(bf16[2,2,96,1152]{3,2,0,1:T(8,128)(2,1)} %fusion.3), channel_id=1, source_target_pairs={{0,4},{1,5},{2,6},{3,7},{4,0},{5,1},{6,2},{7,3},{8,12},{9,13},{10,... | collective-permute-start | bytes 2654216 | tf_op jit(solution)/shard_map/ppermute | solution.py:33
  759.2 45.9 %collective-permute-start.94 = (bf16[2,2,96,1152]{3,2,1,0:T(8,128)(2,1)}, bf16[2,2,96,1152]{3,2,1,0:T(8,128)(2,1)}, u32[]{:S(2)}, u32[]{:S(2)}) collective-permute-start(bf16[2,2,96,1152]{3,2,1,0:T(8,128)(2,1)} %get-tuple-element.548), channel_id=1, source_target_pairs={{0,2},{1,3},{2,0},{3,1},{4,6},{5,7},{6,4},{7,5},{8,10},{9,11},{10,... | collective-permute-start | bytes 2654216 | tf_op jit(solution)/shard_map/ppermute | solution.py:33
  768.2 36.9 %collective-permute-start.95 = (bf16[48,768]{1,0:T(8,128)(2,1)}, bf16[48,768]{1,0:T(8,128)(2,1)}, u32[]{:S(2)}, u32[]{:S(2)}) collective-permute-start(bf16[48,768]{1,0:T(8,128)(2,1)} %fusion.38), channel_id=1, source_target_pairs={{0,16},{1,17},{2,18},{3,19},{4,20},{5,21},{6,22},{7,23},{8,24},{9,... | collective-permute-start | bytes 221192 | tf_op jit(solution)/shard_map/ppermute | solution.py:33
  815.3 47.4 %collective-permute-start.109 = (f32[48,1536]{1,0:T(8,128)}, f32[48,1536]{1,0:T(8,128)}, u32[]{:S(2)}, u32[]{:S(2)}) collective-permute-start(f32[48,1536]{1,0:T(8,128)} %pad_maximum_fusion.37), channel_id=1, source_target_pairs={{0,0},{2,1},{4,2},{6,3},{8,4},{10,5},{12,6},{14,7},{16,8},{18,9},{... | collective-permute-start | bytes 884744 | tf_op jit(solution)/shard_map/ppermute | solution.py:1274
  (203 other events, 2885.6 us)

commit v8 on v7

--- a/solution.py
+++ b/solution.py
@@ -72,21 +72,36 @@
     def __call__(self, flows, work=lambda: ()):
         flows = [flow for flow in flows if flow.wanted is not None]
         wanted = [flow.wanted for flow in flows]
-        leaving, self.token = lax.optimization_barrier(([w[0] for w in wanted], self.token))
-        arriving = [swap(array, bit + 1) for array, (_, bit) in zip(leaving, wanted)]
+        leaving, self.token = lax.optimization_barrier(
+            ([[array for array, _ in pairs] for pairs in wanted], self.token)
+        )
+        arriving = [
+            [swap(array, bit + 1) for array, (_, bit) in zip(arrays, pairs)]
+            for arrays, pairs in zip(leaving, wanted)
+        ]
         arriving, result, self.token = lax.optimization_barrier((arriving, work(), self.token))
-        for flow, array in zip(flows, arriving):
-            flow.arrive(array)
+        for flow, arrays in zip(flows, arriving):
+            flow.arrive(arrays)
         return result
 
 
-def gather_steps(shard, order):
-    held = shard[None]
-    for bit in order[:-1]:
-        arriving = yield held, bit
-        held = jnp.concatenate([held, arriving], axis=0)
-    arriving = yield held, order[-1]
-    return held, arriving
+def join(held, arriving):
+    return [jnp.concatenate(pair, axis=0) for pair in zip(held, arriving)]
+
+
+def near_steps(shards, chip_bits):
+    held = [shard[None] for shard in shards]
+    for bit in range(chip_bits - 1, 1, -1):
+        arriving = yield [(array, bit) for array in held]
+        held = join(held, arriving)
+    return held
+
+
+def far_steps(held):
+    arriving = yield [(held[0], 1), (held[1], 0)]
+    held = join(held, arriving)
+    arriving = yield [(held[0], 0), (held[1], 1)]
+    return list(zip(held, arriving))
 
 
 def assemble_body(steps, chip_ref, *refs):
@@ -138,41 +153,46 @@
     return out.reshape(chips, rows, columns)
 
 
-def gather_flow(shard, colour, chip_bits):
-    return Flow(gather_steps(shard, gather_order(chip_bits, colour)))
-
-
-def gathered(flow, colour, chip, chip_bits):
-    return assemble(flow.result, gather_order(chip_bits, colour), chip)
-
-
 def at_bit(array, axis, bit):
     return lax.dynamic_index_in_dim(array, bit, axis, keepdims=False)
 
 
-def scatter_steps(parts, order, chip, chip_bits, sent):
-    left = list(range(chip_bits - 1, -1, -1))
-    held = [parts.reshape((2,) * chip_bits + parts.shape[1:])]
-    for bit in order:
-        axis = left.index(bit)
-        left.remove(bit)
-        mine = jnp.bitwise_and(chip >> bit, 1)
-        leaving = sum(at_bit(h, axis, 1 - mine).astype(full) for h in held).astype(sent)
-        staying = sum(at_bit(h, axis, mine).astype(full) for h in held).astype(sent)
-        arriving = yield leaving, bit
-        held = [staying, arriving]
-    return held[0].astype(full) + held[1].astype(full)
+def halves_at(held, axis, mine, sent):
+    leaving = sum(at_bit(h, axis, 1 - mine).astype(full) for h in held).astype(sent)
+    staying = sum(at_bit(h, axis, mine).astype(full) for h in held).astype(sent)
+    return leaving, staying
+
+
+def scatter_steps(parts, chip, chip_bits, sent):
+    orders = [gather_order(chip_bits, colour)[::-1] for colour in range(len(parts))]
+    lefts = [list(range(chip_bits - 1, -1, -1)) for _ in parts]
+    held = [[array.reshape((2,) * chip_bits + array.shape[1:])] for array in parts]
+    for step in range(chip_bits):
+        if step == 2 and len(held) == 2:
+            held = [[jnp.concatenate(pair, axis=-1) for pair in zip(*held)]]
+        leaving, staying = [], []
+        for order, left, arrays in zip(orders, lefts, held):
+            bit = order[step]
+            axis = left.index(bit)
+            left.remove(bit)
+            going, kept = halves_at(arrays, axis, jnp.bitwise_and(chip >> bit, 1), sent)
+            leaving.append((going, bit))
+            staying.append(kept)
+        arriving = yield leaving
+        held = [list(pair) for pair in zip(staying, arriving)]
+    ((kept, arrived),) = held
+    return kept.astype(full) + arrived.astype(full)
 
 
 def halving_steps(leaving, staying, order):
-    arriving = yield leaving, order[0]
+    (arriving,) = yield [(leaving, order[0])]
     for bit in order[1:]:
         half = staying.shape[0] // 2
         leaving, staying = [
             (staying[at].astype(full) + arriving[at].astype(full)).astype(low)
             for at in (slice(half, None), slice(half))
         ]
-        arriving = yield leaving, bit
+        (arriving,) = yield [(leaving, bit)]
     return (staying.astype(full) + arriving.astype(full))[0]
 
 
@@ -186,15 +206,14 @@
     return jnp.bitwise_xor(owner, chip), place
 
 
-def scatter_flow(parts, colour, chip, chip_bits, sent=low):
-    order = gather_order(chip_bits, colour)[::-1]
-    return Flow(scatter_steps(parts, order, chip, chip_bits, sent))
+def scatter_flow(parts, chip, chip_bits, sent=low):
+    return Flow(scatter_steps(parts, chip, chip_bits, sent))
 
 
 def row_steps(row, chip, chip_bits, first_bit):
     held = row[None]
     for bit in range(chip_bits):
-        arriving = yield held, bit + first_bit - 1
+        (arriving,) = yield [(held, bit + first_bit - 1)]
         held = jnp.concatenate([held, arriving], axis=0)
     places = jnp.arange(1 << chip_bits)
     pick = jnp.bitwise_xor(places, chip)[:, None] == places[None, :]
@@ -207,8 +226,7 @@
 
 def run(flow):
     while flow.wanted is not None:
-        array, bit = flow.wanted
-        flow.arrive(swap(array, bit + 1))
+        flow.arrive([swap(array, bit + 1) for array, bit in flow.wanted])
     return flow.result
 
 
@@ -1048,15 +1066,16 @@
     mods_part = jnp.dot(lifted, mod_weight, preferred_element_type=full)
 
     slot = Slots(jnp.zeros((8, 128), full))
-    flow = lambda shard, colour: gather_flow(shard, colour, chip_bits)
-    sums = lambda parts, colour: scatter_flow(parts, colour, chip, chip_bits)
-    joined = lambda flows: [
-        gathered(f, colour, chip, chip_bits) for colour, f in enumerate(flows)
+    near = lambda *shards: Flow(near_steps(shards, chip_bits))
+    sums = lambda *parts: scatter_flow(parts, chip, chip_bits)
+    joined = lambda flow: [
+        assemble(pieces, gather_order(chip_bits, colour), chip)
+        for colour, pieces in enumerate(flow.result)
     ]
-    mods_flow = scatter_flow(mods_part, 0, chip, chip_bits, sent=full)
-    qkv_flows = [flow(qkv_rows[:, :qkv_half], 0), flow(qkv_rows[:, qkv_half:], 1)]
+    mods_flow = scatter_flow([mods_part], chip, chip_bits, sent=full)
+    qkv_near = near(qkv_rows)
     mine, upstream = slot(
-        qkv_flows + [mods_flow],
+        [qkv_near, mods_flow],
         lambda: (to_phases(tokens[0], half_rows), to_phases(cotangent[0], half_rows)),
     )
 
@@ -1068,13 +1087,8 @@
     proj_there = [(r, r % chips * 2 + r // chips) for r in range(devices)]
     proj_back = [(b, a) for a, b in proj_there]
     proj_rows = lax.ppermute(proj_weight, AXES, proj_there)
-    canvas = join_halves(mine, swap_core(mine), core)
-
-    slot(qkv_flows + [mods_flow])
-    mods_half = run(mods_flow)
-    mods = mods_half + swap_core(mods_half)
-    shift_a, scale_a, gate_a, shift_f, scale_f, gate_f = jnp.split(mods, 6)
-
+    canvas = slot([qkv_near, mods_flow], lambda: join_halves(mine, swap_core(mine), core))
+    slot.finish([qkv_near])
     tap_count = 9 * (share + part)
     tap_words = jnp.concatenate([ffn_kernel.reshape(-1), attn_kernel.reshape(-1)])
     tap_words = jnp.pad(tap_words, (0, -tap_count % 128))
@@ -1095,32 +1109,47 @@
     )
     mask = (segment[:, None] == segment[None, :]).astype(full)
 
-    proj_flows = [flow(proj_rows[:, : model // 2], 0), flow(proj_rows[:, model // 2 :], 1)]
-    feed_flows = [
-        [flow(up_rows[:, t], 0), flow(down_weight[t * piece : (t + 1) * piece], 1)]
-        for t in range(CHUNKS)
+    def far(arrays, where):
+        return Flow(far_steps([array[at] for array, at in zip(arrays, where)]))
+
+    wide = chips * piece
+    later = range(CHUNKS - 1)
+    proj_near = near(proj_rows)
+    feed_near = [
+        near(up_rows[:, 0], down_weight[:piece]),
+        near(up_rows[:, 1:].reshape(2 * part, -1), down_weight[piece:]),
     ]
+    left, right = (Ellipsis, slice(qkv_half)), (Ellipsis, slice(qkv_half, None))
+    qkv_flow = far(qkv_near.result * 2, (left, right))
+    slot([qkv_flow, mods_flow, proj_near, feed_near[0]])
+    mods_half = run(mods_flow)
+    mods = mods_half + swap_core(mods_half)
+    shift_a, scale_a, gate_a, shift_f, scale_f, gate_f = jnp.split(mods, 6)
+
     mods_a = jnp.concatenate([shift_a[None], scale_a[None], jnp.zeros((6, model), full)], axis=0)
 
-    slot(qkv_flows + proj_flows + feed_flows[0])
     convolved = slot(
-        qkv_flows + proj_flows + feed_flows[0] + feed_flows[1], lambda: conv_in(canvas, attn_taps, mods_a)
-    )
-
+        [qkv_flow, proj_near, feed_near[0]], lambda: conv_in(canvas, attn_taps, mods_a)
+    )
+    slot.finish([qkv_flow, proj_near, feed_near[0]])
+    left, right = (Ellipsis, slice(model // 2)), (Ellipsis, slice(model // 2, None))
+    proj_flow = far(proj_near.result * 2, (left, right))
+    feed_flows = [far(feed_near[0].result, (Ellipsis, Ellipsis))]
+
+    def project_in():
+        weight = jnp.concatenate(
+            [array.reshape(model, qkv_half) for array in joined(qkv_flow)], axis=1
+        )
+        return weight, jnp.dot(convolved, weight, preferred_element_type=full).astype(low)
+
+    qkv_full, qkv = slot([proj_flow, feed_flows[0], feed_near[1]], project_in)
     (upstream,) = slot.after(upstream)
     grad_ph = join_halves(upstream, swap_core(upstream), core)
-
-    def project_in():
-        weight = jnp.concatenate(
-            [array.reshape(model, qkv_half) for array in joined(qkv_flows)], axis=1
-        )
-        return weight, jnp.dot(convolved, weight, preferred_element_type=full).astype(low)
-
-    slot.finish(qkv_flows)
-    qkv_full, qkv = slot(proj_flows + feed_flows[0] + feed_flows[1], project_in)
-    attended = slot(
-        proj_flows + feed_flows[1] + feed_flows[2], lambda: attend(mask, qkv)
-    )
+    attended = slot([proj_flow, feed_near[1]], lambda: attend(mask, qkv))
+    slot.finish([proj_flow, feed_near[1]])
+    for t in later:
+        columns, rows = slice(t * wide, t * wide + wide), slice(t * piece, t * piece + piece)
+        feed_flows.append(far(feed_near[1].result, ((Ellipsis, columns), (slice(None), rows))))
 
     mods_f = jnp.concatenate(
         [gate_a[None], shift_f[None], scale_f[None], gate_f[None], jnp.zeros((4, model), full)]
@@ -1128,15 +1157,14 @@
 
     def project_out():
         weight = jnp.concatenate(
-            [array.reshape(-1, model // 2) for array in joined(proj_flows)], axis=1
+            [array.reshape(-1, model // 2) for array in joined(proj_flow)], axis=1
         )
         branch_part = jnp.dot(attended, weight, preferred_element_type=full).astype(low)
         other = swap_core(branch_part)
         return weight, branch_part, other, *enter_feed(canvas, branch_part, other, grad_ph, mods_f)
 
-    slot.finish(proj_flows)
     proj_full, branch_part, branch_other, norm, norm_t, grad_branch_f = slot(
-        feed_flows[0] + feed_flows[2], project_out
+        feed_flows[:2], project_out
     )
 
     kept = []
@@ -1150,7 +1178,7 @@
     def feed(t):
         def work():
             if spread:
-                up, down = [f.result for f in feed_flows[t]]
+                up, down = feed_flows[t].result
             else:
                 up, down = joined(feed_flows[t])
                 up, down = [up.reshape(model, -1)], [down.reshape(-1, model)]
@@ -1161,7 +1189,7 @@
     back_flows = [[] for _ in range(CHUNKS)]
 
     def run_feed(flows, t):
-        slot.finish(feed_flows[t])
+        slot.finish(feed_flows[t : t + 1])
         staying, leaving, up_grad, down_grad, tap_grad = slot(flows, feed(t))
         kept.append((staying, leaving))
         grads[t] = tap_grad
@@ -1172,12 +1200,12 @@
             ]
         else:
             back_flows[t] = [
-                sums(up_grad[0].reshape(chips, 2 * part, -1), 0),
-                sums(down_grad[0].reshape(chips, piece, model), 1),
+                sums(up_grad[0].reshape(chips, 2 * part, -1)),
+                sums(down_grad[0].reshape(chips, piece, model)),
             ]
 
-    run_feed(feed_flows[1] + feed_flows[2], 0)
-    run_feed(feed_flows[2] + back_flows[0], 1)
+    run_feed(feed_flows[1:], 0)
+    run_feed(feed_flows[2:] + back_flows[0], 1)
     run_feed(back_flows[0] + back_flows[1], 2)
 
     def after_feed():
@@ -1198,16 +1226,16 @@
 
     grad_attended, proj_grad = slot(back_flows[0] + back_flows[1], enter_attend)
     proj_grad = proj_grad.reshape(chips, -1, model)
-    proj_flows = [sums(proj_grad[..., : model // 2], 0), sums(proj_grad[..., model // 2 :], 1)]
+    proj_flow = sums(proj_grad[..., : model // 2], proj_grad[..., model // 2 :])
     grad_qkv = slot(
-        proj_flows + sum(back_flows, []), lambda: attend_back(mask, qkv, grad_attended)
+        [proj_flow] + sum(back_flows, []), lambda: attend_back(mask, qkv, grad_attended)
     )
     qkv_grad = slot(
-        proj_flows + sum(back_flows, []),
+        [proj_flow] + sum(back_flows, []),
         lambda: jnp.dot(convolved.T, grad_qkv, preferred_element_type=full).astype(low),
     )
     qkv_grad = qkv_grad.reshape(chips, 2 * part, -1)
-    qkv_flows = [sums(qkv_grad[..., :qkv_half], 0), sums(qkv_grad[..., qkv_half:], 1)]
+    qkv_flow = sums(qkv_grad[..., :qkv_half], qkv_grad[..., qkv_half:])
 
     def rows_near(array, which):
         size = PLANE // 2 + STRIP
@@ -1220,7 +1248,7 @@
         part_here = jnp.dot(grad_qkv, qkv_full.T, preferred_element_type=full).astype(low)
         return rows_near(part_here, core), swap_core(rows_near(part_here, 1 - core))
 
-    grad_conv = slot(qkv_flows + proj_flows + back_flows[2], leave_attend)
+    grad_conv = slot([qkv_flow, proj_flow] + back_flows[2], leave_attend)
 
     def leave_block():
         input_grad, attn_tap_grad, mods_grad = conv_back(
@@ -1230,7 +1258,7 @@
         return attn_tap_grad[:9], input_grad, mods_grad[:2]
 
     attn_tap_grad, input_grad, attn_sums = slot(
-        qkv_flows + proj_flows + back_flows[2], leave_block
+        [qkv_flow, proj_flow] + back_flows[2], leave_block
     )
     def row_split(array, axis):
         pair = array.reshape((2, part) + array.shape[1:])
@@ -1248,13 +1276,13 @@
         both = (grad_mods + swap_core(grad_mods)).astype(low)
         return both, attn_kept + swap_core(attn_leaving)
 
-    grad_mods, attn_tap_grad = slot(qkv_flows + proj_flows, between_cores)
+    grad_mods, attn_tap_grad = slot([qkv_flow, proj_flow], between_cores)
     mods_flow = row_flow(grad_mods.reshape(-1), chip, chip_bits)
     tap_parts = jnp.concatenate(
         [ffn_tap_grad.reshape(chips, -1), attn_tap_grad.transpose(1, 0, 2).reshape(chips, -1)],
         axis=1,
     )
-    tap_flow = scatter_flow(tap_parts, 0, chip, chip_bits, sent=full)
+    tap_flow = scatter_flow([tap_parts], chip, chip_bits, sent=full)
     up_shares = [flows[0].result for flows in back_flows]
     down_shares = [flows[1].result for flows in back_flows]
 
@@ -1262,11 +1290,11 @@
         up_all = jnp.stack(up_shares, axis=1).reshape(2 * part, CHUNKS, chips, piece)
         return row_split(up_all.transpose(0, 2, 1, 3), 2).reshape(part, -1)
 
-    slot.finish(proj_flows)
-    proj_share = jnp.concatenate([f.result for f in proj_flows], axis=1)
-    up_share = slot(qkv_flows + [mods_flow, tap_flow], split_up)
-    slot.finish(qkv_flows)
-    qkv_share = jnp.concatenate([f.result for f in qkv_flows], axis=1)
+    slot.finish([proj_flow])
+    proj_share = proj_flow.result
+    up_share = slot([qkv_flow, mods_flow, tap_flow], split_up)
+    slot.finish([qkv_flow])
+    qkv_share = qkv_flow.result
 
     def split_qkv():
         qkv_all = qkv_share.reshape(2 * part, pairs, 3, 128).transpose(0, 2, 1, 3)

time: 894 us -> 921 us (1.030)
  waiting for transfers between devices: 178 us -> 213 us
  local copies, waits for them, and re-layouts: 81.3 us -> 99.1 us
  starting transfers between devices: 125 us -> 111 us
  other arithmetic: 144 us -> 131 us
    ppermute x112 -> x100, waiting for transfers between devices: 178 us -> 213 us  [swap(): lax.ppermute(x, AXES, [(i, i ^ 1 << bit) for i in range(device_count())])]
    ppermute x112 -> x100, starting transfers between devices: 119 us -> 105 us  [swap(): lax.ppermute(x, AXES, [(i, i ^ 1 << bit) for i in range(device_count())])]
    concatenate x30 -> x22, other arithmetic: 49.7 us -> 38.5 us  [the longest x21 38.5 us: join(): return [jnp.concatenate(pair, axis=0) for pair in zip(held, arriving)]]
    convert_element_type x16 -> x12, other arithmetic: 21.8 us -> 15.7 us  [the longest x6 8.36 us: halves_at(): sum((at_bit(h, axis, mine).astype(full) for h in held)).astype(sent)]
  transfers between devices with their start and end apart: 114 -> 102, of which waited for: 40 -> 38; matrix products, arithmetic and copies ran while one was open for 23% -> 21% of each run, Pallas kernels for 34% -> 32%
where the time goes in v8:
time: 921 us; the launch traced here: 911 us
  Pallas kernels  304 us (33%)
  waiting for transfers between devices  213 us (23%)
  other arithmetic  131 us (14%)
  starting transfers between devices  111 us (12%)
  local copies, waits for them, and re-layouts  99.1 us (11%)
  matrix products  48.9 us (5%)
    ppermute x100, waiting for transfers between devices, swap(): lax.ppermute(x, AXES, [(i, i ^ 1 << bit) for i in range(device_count())])  213 us
    pallas_call x3, Pallas kernels, feed_forward(): pl.pallas_call(functools.partial(feed_body, spread), grid_spec=pltpu.Pref...  163 us
    ppermute x100, starting transfers between devices, swap(): lax.ppermute(x, AXES, [(i, i ^ 1 << bit) for i in range(device_count())])  105 us
    concatenate x21, other arithmetic, join(): return [jnp.concatenate(pair, axis=0) for pair in zip(held, arriving)]  38.5 us
    convert_element_type x18, other arithmetic, halving_steps(): (staying[at].astype(full) + arriving[at].astype(full)).astype(low)  33.1 us
    pallas_call x1, Pallas kernels, attend_back(): pl.pallas_call(attend_back_body, grid=(pairs,), in_specs=[pl.BlockSpec((P...  28.9 us
    pallas_call x1, Pallas kernels, conv_in(): pl.pallas_call(conv_in_body, grid=(model // TILE,), in_specs=[pl.BlockSpe...  22.8 us
    pallas_call x1, Pallas kernels, conv_back(): pl.pallas_call(conv_back_body, grid_spec=pltpu.PrefetchScalarGridSpec(num...  21.1 us
  transfers between devices with their start and end apart: 102, of which 38 were waited for; matrix products, arithmetic and copies ran while one was open for 21% of the time, Pallas kernels for 32%

profile of v8, /device:TPU:0, one launch (start us, length us, event | category | flops | bytes accessed | tf_op | source)
XLA Modules:
  0.0 910.6 jit_solution(2945690877609340036)
XLA Ops:
  12.6 4.5 reshape_squeeze.7
  30.8 6.0 collective-permute-done.2
  36.8 11.2 %collective-permute-done.1 = bf16[1,96,2304]{2,1,0:T(8,128)(2,1)S(1)} collective-permute-done((bf16[1,96,2304]{2,1,0:T(8,128)(2,1)S(1)}, bf16[1,96,2304]{2,1,0:T(8,128)(2,1)S(1)}, u32[]{:S(2)}, u32[]{:S(2)}) %collective-permute-start.1) | collective-permute-done | bytes 442400 | tf_op jit(solution)/shard_map/ppermute | solution.py:33
  111.4 8.6 collective-permute-done.11
  148.2 22.8 %conv_in.1 = bf16[1024,1536]{1,0:T(8,128)(2,1)} custom-call(bf16[1024,1536]{1,0:T(8,128)(2,1)} %bitcast.319, f32[16,1536]{1,0:T(8,128)} %pad_convert_fusion.1.kernel_ref, f32[8,1536]{1,0:T(8,128)} %maximum_maximum_fusion.mods_ref), custom_call_target="tpu_custom_call" | custom-call | flops 47185920 | bytes 6291456 | tf_op jit(solution)/shard_map/conv_in/pallas_call | solution.py:717
  187.0 5.6 assemble.5
  192.5 5.6 assemble.4
  198.2 12.8 %convolution_convert_fusion.2.qkv_ref = bf16[1024,2304]{1,0:T(8,128)(2,1)} fusion(bf16[1024,1536]{1,0:T(8,128)(2,1)} %conv_in.1, bf16[1536,1152]{1,0:T(8,128)(2,1)} %bitcast.325, bf16[1536,1152]{1,0:T(8,128)(2,1)} %bitcast.327), kind=kOutput, calls=%fused_computation.3 | convolution fusion | flops 7264272384 | bytes 14942208 | tf_op jit(solution)/shard_map/dot_general | solution.py:1143
  213.9 5.4 pad_maximum_fusion
  219.4 8.6 collective-permute-done.31
  240.9 15.4 %attend.1 = bf16[1024,768]{1,0:T(8,128)(2,1)} custom-call(f32[256,256]{1,0:T(8,128)} %compare_convert_fusion.mask_ref, bf16[1024,2304]{1,0:T(8,128)(2,1)} %convolution_convert_fusion.2.qkv_ref), custom_call_target="tpu_custom_call" | custom-call | flops 3221225472 | bytes 6291456 | tf_op jit(solution)/shard_map/attend/pallas_call | solution.py:351
  256.3 14.4 %collective-permute-done.35 = bf16[2,128,1536]{2,1,0:T(8,128)(2,1)} collective-permute-done((bf16[2,128,1536]{2,1,0:T(8,128)(2,1)}, bf16[2,128,1536]{2,1,0:T(8,128)(2,1)}, u32[]{:S(2)}, u32[]{:S(2)}) %collective-permute-start.35) | collective-permute-done | bytes 786464 | tf_op jit(solution)/shard_map/ppermute | solution.py:33
  279.5 6.0 convolution_convert_fusion.4.part_ref
  305.4 17.6 %enter_feed.1 = (bf16[1024,1536]{1,0:T(8,128)(2,1)}, bf16[1536,1024]{1,0:T(8,128)(2,1)}, bf16[1024,1536]{1,0:T(8,128)(2,1)}) custom-call(bf16[1024,1536]{1,0:T(8,128)(2,1)} %bitcast.320, bf16[1024,1536]{1,0:T(8,128)(2,1)} %convolution_convert_fusion.4.part_ref, bf16[1024,1536]{1,0:T(8,128)(2,1)} %collective-permute-done.40.other_ref, ...), custom_call_target="tpu_custom_call" | custom-call | flops 1000 | bytes 1000 | tf_op jit(solution)/shard_map/enter_feed/pallas_call | solution.py:942
  323.0 25.7 %collective-permute-done.38 = bf16[4,96,1024]{2,1,0:T(8,128)(2,1)} collective-permute-done((bf16[4,96,1024]{2,1,0:T(8,128)(2,1)}, bf16[4,96,1024]{2,1,0:T(8,128)(2,1)}, u32[]{:S(2)}, u32[]{:S(2)}) %collective-permute-start.38) | collective-permute-done | bytes 786464 | tf_op jit(solution)/shard_map/ppermute | solution.py:33
  358.0 54.5 %feed_forward.3 = (bf16[2,4,128,1536]{3,2,1,0:T(8,128)(2,1)}, bf16[2,4,128,1536]{3,2,1,0:T(8,128)(2,1)}, bf16[8,96,1024]{2,1,0:T(8,128)(2,1)}, bf16[8,96,1024]{2...) custom-call(s32[49]{0:T(128)} %pad_add_fusion.1.words_ref, ...), custom_call_target="tpu_custom_call" | custom-call | flops 19327352832 | bytes 28311552 | tf_op jit(solution)/shard_map/feed_forward/pallas_call | solution.py:609
  422.1 54.3 %feed_forward.4 = (bf16[2,4,128,1536]{3,2,1,0:T(8,128)(2,1)}, bf16[2,4,128,1536]{3,2,1,0:T(8,128)(2,1)}, bf16[8,96,1024]{2,1,0:T(8,128)(2,1)}, bf16[8,96,1024]{2...) custom-call(s32[49]{0:T(128)} %pad_add_fusion.1.words_ref, ...), custom_call_target="tpu_custom_call" | custom-call | flops 19327352832 | bytes 28311552 | tf_op jit(solution)/shard_map/feed_forward/pallas_call | solution.py:609
  476.4 10.1 %collective-permute-done.48 = bf16[8,96,1024]{2,1,0:T(8,128)(2,1)} collective-permute-done((bf16[8,96,1024]{2,1,0:T(8,128)(2,1)}, bf16[8,96,1024]{2,1,0:T(8,128)(2,1)}, u32[]{:S(2)}, u32[]{:S(2)}) %collective-permute-start.48) | collective-permute-done | bytes 1572896 | tf_op jit(solution)/shard_map/ppermute | solution.py:33
  497.2 16.4 %collective-permute-done.50 = bf16[4,96,1024]{2,1,0:T(8,128)(2,1)S(1)} collective-permute-done((bf16[4,96,1024]{2,1,0:T(8,128)(2,1)S(1)}, bf16[4,96,1024]{2,1,0:T(8,128)(2,1)S(1)}, u32[]{:S(2)}, u32[]{:S(2)}) %collective-permute-start.50) | collective-permute-done | bytes 786464 | tf_op jit(solution)/shard_map/ppermute | solution.py:33
  514.5 54.6 %feed_forward.5 = (bf16[2,4,128,1536]{3,2,1,0:T(8,128)(2,1)}, bf16[2,4,128,1536]{3,2,1,0:T(8,128)(2,1)}, bf16[8,96,1024]{2,1,0:T(8,128)(2,1)}, bf16[8,96,1024]{2...) custom-call(s32[49]{0:T(128)} %pad_add_fusion.1.words_ref, ...), custom_call_target="tpu_custom_call" | custom-call | flops 19327352832 | bytes 28311552 | tf_op jit(solution)/shard_map/feed_forward/pallas_call | solution.py:609
  581.7 15.4 %leave_feed.1 = (bf16[512,1536]{1,0:T(8,128)(2,1)}, f32[512,1536]{1,0:T(8,128)}, bf16[512,1536]{1,0:T(8,128)(2,1)}, f32[8,1536]{1,0:T(8,128)}) custom-call(s32[1]{0:T(128)} %bitcast.32.words_ref.core_ref, bf16[1024,1536]{1,0:T(8,128)(2,1)} %bitcast.321, bf16[1024,1536]{1,0:T(8,128)(2,1)} %convolution_convert_fusion.4.part_ref, ...), custom_call_target="tpu_custom_call" | custom-call | flops 1000 | bytes 1000 | tf_op jit(solution)/shard_map/leave_feed/pallas_call | solution.py:998
  597.2 13.9 %collective-permute-done.56 = bf16[8,96,1024]{2,1,0:T(8,128)(2,1)} collective-permute-done((bf16[8,96,1024]{2,1,0:T(8,128)(2,1)}, bf16[8,96,1024]{2,1,0:T(8,128)(2,1)}, u32[]{:S(2)}, u32[]{:S(2)}) %collective-permute-start.56) | collective-permute-done | bytes 1572896 | tf_op jit(solution)/shard_map/ppermute | solution.py:33
  657.2 28.9 %attend_back.1 = bf16[1024,2304]{1,0:T(8,128)(2,1)} custom-call(f32[256,256]{1,0:T(8,128)} %compare_convert_fusion.mask_ref, bf16[1024,2304]{1,0:T(8,128)(2,1)} %convolution_convert_fusion.2.qkv_ref, bf16[1024,768]{1,0:T(8,128)(2,1)} %convolution_convert_fusion.7.grad_ref), custom_call_target="tpu_custom_call" | custom-call | flops 8053063680 | bytes 11010048 | tf_op jit(solution)/shard_map/attend_back/pallas_call | solution.py:372
  701.3 10.3 %convolution_convert_fusion = bf16[1536,2304]{1,0:T(8,128)(2,1)S(1)} fusion(bf16[1024,1536]{1,0:T(8,128)(2,1)S(1)} %copy-done.14, bf16[1024,2304]{1,0:T(8,128)(2,1)} %attend_back.1), kind=kOutput, calls=%fused_computation | convolution fusion | flops 7251296256 | bytes 14942208 | tf_op jit(solution)/shard_map/dot_general | solution.py:1235
  711.6 7.9 convolution_convert_fusion.3
  751.2 5.3 collective-permute-done.81
  765.4 8.0 collective-permute-done.78
  793.6 21.1 %conv_back.1 = (f32[512,1536]{1,0:T(8,128)}, f32[16,1536]{1,0:T(8,128)}, f32[8,1536]{1,0:T(8,128)}) custom-call(s32[1]{0:T(128)} %bitcast.32.words_ref.core_ref, bf16[576,1536]{1,0:T(8,128)(2,1)} %bitcast.339, bf16[576,1536]{1,0:T(8,128)(2,1)} %bitcast.340, bf16[576,1536]{1,0:T(8,128)(2,1)} %collective-permute-done.83.arriving_ref, ...), custom_call_target="tpu_custom_call" | custom-call | flops 55050240 | bytes 11010048 | tf_op jit(solution)/shard_map/conv_back/pallas_call | solution.py:875
  822.7 4.7 reshape.364
  835.4 18.2 %collective-permute-done.87 = bf16[2,96,2304]{2,1,0:T(8,128)(2,1)S(1)} collective-permute-done((bf16[2,96,2304]{2,1,0:T(8,128)(2,1)}, bf16[2,96,2304]{2,1,0:T(8,128)(2,1)S(1)}, u32[]{:S(2)}, u32[]{:S(2)}) %collective-permute-start.87) | collective-permute-done | bytes 884768 | tf_op jit(solution)/shard_map/ppermute | solution.py:33
  866.3 12.7 %collective-permute-done.90 = bf16[96,2304]{1,0:T(8,128)(2,1)S(1)} collective-permute-done((bf16[96,2304]{1,0:T(8,128)(2,1)S(1)}, bf16[96,2304]{1,0:T(8,128)(2,1)S(1)}, u32[]{:S(2)}, u32[]{:S(2)}) %collective-permute-start.90) | collective-permute-done | bytes 442400 | tf_op jit(solution)/shard_map/ppermute | solution.py:33
  898.0 5.6 collective-permute-done.101
  (682 shorter events, 395.7 us)
Async XLA Ops:
  85.6 41.5 %collective-permute-start.8 = (bf16[4,96,1152]{2,1,0:T(8,128)(2,1)S(1)}, bf16[4,96,1152]{2,1,0:T(8,128)(2,1)}, u32[]{:S(2)}, u32[]{:S(2)}) collective-permute-start(bf16[4,96,1152]{2,1,0:T(8,128)(2,1)S(1)} %get-tuple-element.301), channel_id=1, source_target_pairs={{0,4},{1,5},{2,6},{3,7},{4,0},{5,1},{6,2},{7,3},{8,12},{9,13},{10,... | collective-permute-start | bytes 2654216 | tf_op jit(solution)/shard_map/ppermute | solution.py:33
  85.8 42.1 %collective-permute-start.9 = (bf16[4,96,1152]{2,1,0:T(8,128)(2,1)S(1)}, bf16[4,96,1152]{2,1,0:T(8,128)(2,1)}, u32[]{:S(2)}, u32[]{:S(2)}) collective-permute-start(bf16[4,96,1152]{2,1,0:T(8,128)(2,1)S(1)} %get-tuple-element.302), channel_id=1, source_target_pairs={{0,2},{1,3},{2,0},{3,1},{4,6},{5,7},{6,4},{7,5},{8,10},{9,11},{10,... | collective-permute-start | bytes 2654216 | tf_op jit(solution)/shard_map/ppermute | solution.py:33
  136.1 39.5 %collective-permute-start.14 = (bf16[8,96,1152]{2,1,0:T(8,128)(2,1)S(1)}, bf16[8,96,1152]{2,1,0:T(8,128)(2,1)}, u32[]{:S(2)}, u32[]{:S(2)}) collective-permute-start(bf16[8,96,1152]{2,1,0:T(8,128)(2,1)S(1)} %pad_maximum_fusion.7.refs_0_), channel_id=1, source_target_pairs={{0,2},{1,3},{2,0},{3,1},{4,6},{5,7},{6,4},{7,5},{8,10},{9,11},{10,... | collective-permute-start | bytes 5308424 | tf_op jit(solution)/shard_map/ppermute | solution.py:33
  137.6 39.4 %collective-permute-start.15 = (bf16[8,96,1152]{2,1,0:T(8,128)(2,1)}, bf16[8,96,1152]{2,1,0:T(8,128)(2,1)}, u32[]{:S(2)}, u32[]{:S(2)}) collective-permute-start(bf16[8,96,1152]{2,1,0:T(8,128)(2,1)} %pad_maximum_fusion.8.refs_0_), channel_id=1, source_target_pairs={{0,4},{1,5},{2,6},{3,7},{4,0},{5,1},{6,2},{7,3},{8,12},{9,13},{10,... | collective-permute-start | bytes 5308424 | tf_op jit(solution)/shard_map/ppermute | solution.py:33
  184.2 43.8 %collective-permute-start.28 = (bf16[4,96,1024]{2,1,0:T(8,128)(2,1)}, bf16[4,96,1024]{2,1,0:T(8,128)(2,1)}, u32[]{:S(2)}, u32[]{:S(2)}) collective-permute-start(bf16[4,96,1024]{2,1,0:T(8,128)(2,1)} %pad_maximum_fusion.19), channel_id=1, source_target_pairs={{0,4},{1,5},{2,6},{3,7},{4,0},{5,1},{6,2},{7,3},{8,12},{9,13},{10,... | collective-permute-start | bytes 2359304 | tf_op jit(solution)/shard_map/ppermute | solution.py:33
  185.5 43.1 %collective-permute-start.29 = (bf16[4,64,1536]{2,1,0:T(8,128)(2,1)}, bf16[4,64,1536]{2,1,0:T(8,128)(2,1)}, u32[]{:S(2)}, u32[]{:S(2)}) collective-permute-start(bf16[4,64,1536]{2,1,0:T(8,128)(2,1)} %pad_maximum_fusion.20), channel_id=1, source_target_pairs={{0,2},{1,3},{2,0},{3,1},{4,6},{5,7},{6,4},{7,5},{8,10},{9,11},{10,... | collective-permute-start | bytes 2359304 | tf_op jit(solution)/shard_map/ppermute | solution.py:33
  293.4 55.2 %collective-permute-start.36 = (bf16[8,96,1024]{2,1,0:T(8,128)(2,1)}, bf16[8,96,1024]{2,1,0:T(8,128)(2,1)}, u32[]{:S(2)}, u32[]{:S(2)}) collective-permute-start(bf16[8,96,1024]{2,1,0:T(8,128)(2,1)} %pad_maximum_fusion.9.refs_0_), channel_id=1, source_target_pairs={{0,2},{1,3},{2,0},{3,1},{4,6},{5,7},{6,4},{7,5},{8,10},{9,11},{10,... | collective-permute-start | bytes 4718600 | tf_op jit(solution)/shard_map/ppermute | solution.py:33
  295.1 53.6 %collective-permute-start.37 = (bf16[8,64,1536]{2,1,0:T(8,128)(2,1)}, bf16[8,64,1536]{2,1,0:T(8,128)(2,1)}, u32[]{:S(2)}, u32[]{:S(2)}) collective-permute-start(bf16[8,64,1536]{2,1,0:T(8,128)(2,1)} %pad_maximum_fusion.10.refs_2_), channel_id=1, source_target_pairs={{0,4},{1,5},{2,6},{3,7},{4,0},{5,1},{6,2},{7,3},{8,12},{9,13},{10,... | collective-permute-start | bytes 4718600 | tf_op jit(solution)/shard_map/ppermute | solution.py:33
  297.2 51.4 %collective-permute-start.38 = (bf16[4,96,1024]{2,1,0:T(8,128)(2,1)}, bf16[4,96,1024]{2,1,0:T(8,128)(2,1)}, u32[]{:S(2)}, u32[]{:S(2)}) collective-permute-start(bf16[4,96,1024]{2,1,0:T(8,128)(2,1)} %get-tuple-element.358), channel_id=1, source_target_pairs={{0,4},{1,5},{2,6},{3,7},{4,0},{5,1},{6,2},{7,3},{8,12},{9,13},{10,... | collective-permute-start | bytes 2359304 | tf_op jit(solution)/shard_map/ppermute | solution.py:33
  298.3 50.3 %collective-permute-start.39 = (bf16[4,64,1536]{2,1,0:T(8,128)(2,1)}, bf16[4,64,1536]{2,1,0:T(8,128)(2,1)}, u32[]{:S(2)}, u32[]{:S(2)}) collective-permute-start(bf16[4,64,1536]{2,1,0:T(8,128)(2,1)} %get-tuple-element.359), channel_id=1, source_target_pairs={{0,2},{1,3},{2,0},{3,1},{4,6},{5,7},{6,4},{7,5},{8,10},{9,11},{10,... | collective-permute-start | bytes 2359304 | tf_op jit(solution)/shard_map/ppermute | solution.py:33
  354.0 58.6 %collective-permute-start.42 = (bf16[8,96,1024]{2,1,0:T(8,128)(2,1)}, bf16[8,96,1024]{2,1,0:T(8,128)(2,1)}, u32[]{:S(2)}, u32[]{:S(2)}) collective-permute-start(bf16[8,96,1024]{2,1,0:T(8,128)(2,1)} %pad_maximum_fusion.12.refs_0_), channel_id=1, source_target_pairs={{0,2},{1,3},{2,0},{3,1},{4,6},{5,7},{6,4},{7,5},{8,10},{9,11},{10,... | collective-permute-start | bytes 4718600 | tf_op jit(solution)/shard_map/ppermute | solution.py:33
  354.3 58.3 %collective-permute-start.43 = (bf16[8,64,1536]{2,1,0:T(8,128)(2,1)}, bf16[8,64,1536]{2,1,0:T(8,128)(2,1)}, u32[]{:S(2)}, u32[]{:S(2)}) collective-permute-start(bf16[8,64,1536]{2,1,0:T(8,128)(2,1)} %pad_maximum_fusion.13.refs_2_), channel_id=1, source_target_pairs={{0,4},{1,5},{2,6},{3,7},{4,0},{5,1},{6,2},{7,3},{8,12},{9,13},{10,... | collective-permute-start | bytes 4718600 | tf_op jit(solution)/shard_map/ppermute | solution.py:33
  355.7 56.9 %collective-permute-start.44 = (bf16[4,96,1024]{2,1,0:T(8,128)(2,1)}, bf16[4,96,1024]{2,1,0:T(8,128)(2,1)}, u32[]{:S(2)}, u32[]{:S(2)}) collective-permute-start(bf16[4,96,1024]{2,1,0:T(8,128)(2,1)} %get-tuple-element.373), channel_id=1, source_target_pairs={{0,4},{1,5},{2,6},{3,7},{4,0},{5,1},{6,2},{7,3},{8,12},{9,13},{10,... | collective-permute-start | bytes 2359304 | tf_op jit(solution)/shard_map/ppermute | solution.py:33
  356.4 56.2 %collective-permute-start.45 = (bf16[4,64,1536]{2,1,0:T(8,128)(2,1)}, bf16[4,64,1536]{2,1,0:T(8,128)(2,1)}, u32[]{:S(2)}, u32[]{:S(2)}) collective-permute-start(bf16[4,64,1536]{2,1,0:T(8,128)(2,1)} %get-tuple-element.374), channel_id=1, source_target_pairs={{0,2},{1,3},{2,0},{3,1},{4,6},{5,7},{6,4},{7,5},{8,10},{9,11},{10,... | collective-permute-start | bytes 2359304 | tf_op jit(solution)/shard_map/ppermute | solution.py:33
  418.0 58.3 %collective-permute-start.46 = (bf16[8,96,1024]{2,1,0:T(8,128)(2,1)}, bf16[8,96,1024]{2,1,0:T(8,128)(2,1)}, u32[]{:S(2)}, u32[]{:S(2)}) collective-permute-start(bf16[8,96,1024]{2,1,0:T(8,128)(2,1)} %pad_maximum_fusion.14.refs_0_), channel_id=1, source_target_pairs={{0,2},{1,3},{2,0},{3,1},{4,6},{5,7},{6,4},{7,5},{8,10},{9,11},{10,... | collective-permute-start | bytes 4718600 | tf_op jit(solution)/shard_map/ppermute | solution.py:33
  418.4 58.0 %collective-permute-start.47 = (bf16[8,64,1536]{2,1,0:T(8,128)(2,1)}, bf16[8,64,1536]{2,1,0:T(8,128)(2,1)}, u32[]{:S(2)}, u32[]{:S(2)}) collective-permute-start(bf16[8,64,1536]{2,1,0:T(8,128)(2,1)} %pad_maximum_fusion.15.refs_2_), channel_id=1, source_target_pairs={{0,4},{1,5},{2,6},{3,7},{4,0},{5,1},{6,2},{7,3},{8,12},{9,13},{10,... | collective-permute-start | bytes 4718600 | tf_op jit(solution)/shard_map/ppermute | solution.py:33
  419.7 66.7 %collective-permute-start.48 = (bf16[8,96,1024]{2,1,0:T(8,128)(2,1)}, bf16[8,96,1024]{2,1,0:T(8,128)(2,1)}, u32[]{:S(2)}, u32[]{:S(2)}) collective-permute-start(bf16[8,96,1024]{2,1,0:T(8,128)(2,1)} %get-tuple-element.396), channel_id=1, source_target_pairs={{0,2},{1,3},{2,0},{3,1},{4,6},{5,7},{6,4},{7,5},{8,10},{9,11},{10,... | collective-permute-start | bytes 4718600 | tf_op jit(solution)/shard_map/ppermute | solution.py:33
  421.0 65.7 %collective-permute-start.49 = (bf16[8,64,1536]{2,1,0:T(8,128)(2,1)}, bf16[8,64,1536]{2,1,0:T(8,128)(2,1)}, u32[]{:S(2)}, u32[]{:S(2)}) collective-permute-start(bf16[8,64,1536]{2,1,0:T(8,128)(2,1)} %get-tuple-element.397), channel_id=1, source_target_pairs={{0,4},{1,5},{2,6},{3,7},{4,0},{5,1},{6,2},{7,3},{8,12},{9,13},{10,... | collective-permute-start | bytes 4718600 | tf_op jit(solution)/shard_map/ppermute | solution.py:33
  494.3 82.4 %collective-permute-start.58 = (bf16[2,4,128,1536]{3,2,1,0:T(8,128)(2,1)}, bf16[2,4,128,1536]{3,2,1,0:T(8,128)(2,1)}, u32[]{:S(2)}, u32[]{:S(2)}) collective-permute-start(bf16[2,4,128,1536]{3,2,1,0:T(8,128)(2,1)} %get-tuple-element.440), channel_id=1, source_target_pairs={{0,1},{1,0},{2,3},{3,2},{4,5},{5,4},{6,7},{7,6},{8,9},{9,8},{10,11... | collective-permute-start | bytes 9437192 | tf_op jit(solution)/shard_map/ppermute | solution.py:33
  494.3 74.7 %collective-permute-start.51 = (bf16[4,64,1536]{2,1,0:T(8,128)(2,1)}, bf16[4,64,1536]{2,1,0:T(8,128)(2,1)}, u32[]{:S(2)}, u32[]{:S(2)}) collective-permute-start(bf16[4,64,1536]{2,1,0:T(8,128)(2,1)} %get-tuple-element.415), channel_id=1, source_target_pairs={{0,2},{1,3},{2,0},{3,1},{4,6},{5,7},{6,4},{7,5},{8,10},{9,11},{10,... | collective-permute-start | bytes 2359304 | tf_op jit(solution)/shard_map/ppermute | solution.py:33
  495.6 73.5 %collective-permute-start.52 = (bf16[8,96,1024]{2,1,0:T(8,128)(2,1)}, bf16[8,96,1024]{2,1,0:T(8,128)(2,1)}, u32[]{:S(2)}, u32[]{:S(2)}) collective-permute-start(bf16[8,96,1024]{2,1,0:T(8,128)(2,1)} %get-tuple-element.416), channel_id=1, source_target_pairs={{0,2},{1,3},{2,0},{3,1},{4,6},{5,7},{6,4},{7,5},{8,10},{9,11},{10,... | collective-permute-start | bytes 4718600 | tf_op jit(solution)/shard_map/ppermute | solution.py:33
  496.4 72.7 %collective-permute-start.53 = (bf16[8,64,1536]{2,1,0:T(8,128)(2,1)}, bf16[8,64,1536]{2,1,0:T(8,128)(2,1)}, u32[]{:S(2)}, u32[]{:S(2)}) collective-permute-start(bf16[8,64,1536]{2,1,0:T(8,128)(2,1)} %get-tuple-element.417), channel_id=1, source_target_pairs={{0,4},{1,5},{2,6},{3,7},{4,0},{5,1},{6,2},{7,3},{8,12},{9,13},{10,... | collective-permute-start | bytes 4718600 | tf_op jit(solution)/shard_map/ppermute | solution.py:33
  514.5 64.0 %collective-permute-start.59 = (bf16[2,4,128,1536]{3,2,1,0:T(8,128)(2,1)}, bf16[2,4,128,1536]{3,2,1,0:T(8,128)(2,1)}, u32[]{:S(2)}, u32[]{:S(2)}) collective-permute-start(bf16[2,4,128,1536]{3,2,1,0:T(8,128)(2,1)} %get-tuple-element.442), channel_id=1, source_target_pairs={{0,1},{1,0},{2,3},{3,2},{4,5},{5,4},{6,7},{7,6},{8,9},{9,8},{10,11... | collective-permute-start | bytes 9437192 | tf_op jit(solution)/shard_map/ppermute | solution.py:33
  574.3 36.7 %collective-permute-start.56 = (bf16[8,96,1024]{2,1,0:T(8,128)(2,1)}, bf16[8,96,1024]{2,1,0:T(8,128)(2,1)}, u32[]{:S(2)}, u32[]{:S(2)}) collective-permute-start(bf16[8,96,1024]{2,1,0:T(8,128)(2,1)} %get-tuple-element.435), channel_id=1, source_target_pairs={{0,2},{1,3},{2,0},{3,1},{4,6},{5,7},{6,4},{7,5},{8,10},{9,11},{10,... | collective-permute-start | bytes 4718600 | tf_op jit(solution)/shard_map/ppermute | solution.py:33
  575.8 36.4 %collective-permute-start.57 = (bf16[8,64,1536]{2,1,0:T(8,128)(2,1)}, bf16[8,64,1536]{2,1,0:T(8,128)(2,1)}, u32[]{:S(2)}, u32[]{:S(2)}) collective-permute-start(bf16[8,64,1536]{2,1,0:T(8,128)(2,1)} %get-tuple-element.436), channel_id=1, source_target_pairs={{0,4},{1,5},{2,6},{3,7},{4,0},{5,1},{6,2},{7,3},{8,12},{9,13},{10,... | collective-permute-start | bytes 4718600 | tf_op jit(solution)/shard_map/ppermute | solution.py:33
  649.9 36.2 %collective-permute-start.66 = (bf16[2,2,2,48,768]{4,3,0,1,2:T(8,128)(2,1)}, bf16[2,2,2,48,768]{4,3,0,1,2:T(8,128)(2,1)}, u32[]{:S(2)}, u32[]{:S(2)}) collective-permute-start(bf16[2,2,2,48,768]{4,3,0,1,2:T(8,128)(2,1)} %copy_bitcast_fusion.6), channel_id=1, source_target_pairs={{0,2},{1,3},{2,0},{3,1},{4,6},{5,7},{6,4},{7,5},{8,10},{9,11},{10,... | collective-permute-start | bytes 1769480 | tf_op jit(solution)/shard_map/ppermute | solution.py:33
  723.1 42.3 %collective-permute-start.83 = (bf16[576,1536]{1,0:T(8,128)(2,1)}, bf16[576,1536]{1,0:T(8,128)(2,1)}, u32[]{:S(2)}, u32[]{:S(2)}) collective-permute-start(bf16[576,1536]{1,0:T(8,128)(2,1)} %bitcast.66), channel_id=1, source_target_pairs={{0,1},{1,0},{2,3},{3,2},{4,5},{5,4},{6,7},{7,6},{8,9},{9,8},{10,11... | collective-permute-start | bytes 5308424 | tf_op jit(solution)/shard_map/ppermute | solution.py:33
  735.4 38.1 %collective-permute-start.78 = (bf16[2,2,2,96,1152]{4,3,0,1,2:T(8,128)(2,1)}, bf16[2,2,2,96,1152]{4,3,0,1,2:T(8,128)(2,1)}, u32[]{:S(2)}, u32[]{:S(2)}) collective-permute-start(bf16[2,2,2,96,1152]{4,3,0,1,2:T(8,128)(2,1)} %copy_bitcast_fusion.1), channel_id=1, source_target_pairs={{0,2},{1,3},{2,0},{3,1},{4,6},{5,7},{6,4},{7,5},{8,10},{9,11},{10,... | collective-permute-start | bytes 5308424 | tf_op jit(solution)/shard_map/ppermute | solution.py:33
  736.0 37.5 %collective-permute-start.79 = (bf16[2,2,2,96,1152]{4,3,0,1,2:T(8,128)(2,1)}, bf16[2,2,2,96,1152]{4,3,0,1,2:T(8,128)(2,1)}, u32[]{:S(2)}, u32[]{:S(2)}) collective-permute-start(bf16[2,2,2,96,1152]{4,3,0,1,2:T(8,128)(2,1)} %copy_bitcast_fusion), channel_id=1, source_target_pairs={{0,4},{1,5},{2,6},{3,7},{4,0},{5,1},{6,2},{7,3},{8,12},{9,13},{10,... | collective-permute-start | bytes 5308424 | tf_op jit(solution)/shard_map/ppermute | solution.py:33
  780.8 46.6 %collective-permute-start.84 = (bf16[2,2,96,1152]{3,2,0,1:T(8,128)(2,1)}, bf16[2,2,96,1152]{3,2,0,1:T(8,128)(2,1)}, u32[]{:S(2)}, u32[]{:S(2)}) collective-permute-start(bf16[2,2,96,1152]{3,2,0,1:T(8,128)(2,1)} %fusion.4), channel_id=1, source_target_pairs={{0,4},{1,5},{2,6},{3,7},{4,0},{5,1},{6,2},{7,3},{8,12},{9,13},{10,... | collective-permute-start | bytes 2654216 | tf_op jit(solution)/shard_map/ppermute | solution.py:33
  782.0 45.4 %collective-permute-start.85 = (bf16[2,2,96,1152]{3,2,0,1:T(8,128)(2,1)}, bf16[2,2,96,1152]{3,2,0,1:T(8,128)(2,1)}, u32[]{:S(2)}, u32[]{:S(2)}) collective-permute-start(bf16[2,2,96,1152]{3,2,0,1:T(8,128)(2,1)} %get-tuple-element.511), channel_id=1, source_target_pairs={{0,2},{1,3},{2,0},{3,1},{4,6},{5,7},{6,4},{7,5},{8,10},{9,11},{10,... | collective-permute-start | bytes 2654216 | tf_op jit(solution)/shard_map/ppermute | solution.py:33
  791.1 36.4 %collective-permute-start.86 = (bf16[48,1536]{1,0:T(8,128)(2,1)}, bf16[48,1536]{1,0:T(8,128)(2,1)}, u32[]{:S(2)}, u32[]{:S(2)}) collective-permute-start(bf16[48,1536]{1,0:T(8,128)(2,1)} %fusion.30), channel_id=1, source_target_pairs={{0,16},{1,17},{2,18},{3,19},{4,20},{5,21},{6,22},{7,23},{8,24},{9,... | collective-permute-start | bytes 442376 | tf_op jit(solution)/shard_map/ppermute | solution.py:33
  (198 other events, 2284.8 us)

commit v9 on v8

--- a/solution.py
+++ b/solution.py
@@ -95,6 +95,11 @@
         arriving = yield [(array, bit) for array in held]
         held = join(held, arriving)
     return held
+
+
+def core_steps(array):
+    (arriving,) = yield [(array, -1)]
+    return arriving
 
 
 def far_steps(held):
@@ -1087,7 +1092,10 @@
     proj_there = [(r, r % chips * 2 + r // chips) for r in range(devices)]
     proj_back = [(b, a) for a, b in proj_there]
     proj_rows = lax.ppermute(proj_weight, AXES, proj_there)
-    canvas = slot([qkv_near, mods_flow], lambda: join_halves(mine, swap_core(mine), core))
+    proj_near = near(proj_rows)
+    canvas = slot(
+        [qkv_near, mods_flow, proj_near], lambda: join_halves(mine, swap_core(mine), core)
+    )
     slot.finish([qkv_near])
     tap_count = 9 * (share + part)
     tap_words = jnp.concatenate([ffn_kernel.reshape(-1), attn_kernel.reshape(-1)])
@@ -1114,7 +1122,6 @@
 
     wide = chips * piece
     later = range(CHUNKS - 1)
-    proj_near = near(proj_rows)
     feed_near = [
         near(up_rows[:, 0], down_weight[:piece]),
         near(up_rows[:, 1:].reshape(2 * part, -1), down_weight[piece:]),
@@ -1128,12 +1135,13 @@
 
     mods_a = jnp.concatenate([shift_a[None], scale_a[None], jnp.zeros((6, model), full)], axis=0)
 
-    convolved = slot(
-        [qkv_flow, proj_near, feed_near[0]], lambda: conv_in(canvas, attn_taps, mods_a)
-    )
-    slot.finish([qkv_flow, proj_near, feed_near[0]])
+    slot.finish([proj_near])
     left, right = (Ellipsis, slice(model // 2)), (Ellipsis, slice(model // 2, None))
     proj_flow = far(proj_near.result * 2, (left, right))
+    convolved = slot(
+        [qkv_flow, proj_flow, feed_near[0]], lambda: conv_in(canvas, attn_taps, mods_a)
+    )
+    slot.finish([qkv_flow, feed_near[0]])
     feed_flows = [far(feed_near[0].result, (Ellipsis, Ellipsis))]
 
     def project_in():
@@ -1145,8 +1153,16 @@
     qkv_full, qkv = slot([proj_flow, feed_flows[0], feed_near[1]], project_in)
     (upstream,) = slot.after(upstream)
     grad_ph = join_halves(upstream, swap_core(upstream), core)
-    attended = slot([proj_flow, feed_near[1]], lambda: attend(mask, qkv))
-    slot.finish([proj_flow, feed_near[1]])
+    slot.finish([proj_flow])
+
+    def attend_and_assemble():
+        weight = jnp.concatenate(
+            [array.reshape(-1, model // 2) for array in joined(proj_flow)], axis=1
+        )
+        return attend(mask, qkv), weight
+
+    attended, proj_full = slot([feed_flows[0], feed_near[1]], attend_and_assemble)
+    slot.finish([feed_near[1]])
     for t in later:
         columns, rows = slice(t * wide, t * wide + wide), slice(t * piece, t * piece + piece)
         feed_flows.append(far(feed_near[1].result, ((Ellipsis, columns), (slice(None), rows))))
@@ -1156,16 +1172,11 @@
     )
 
     def project_out():
-        weight = jnp.concatenate(
-            [array.reshape(-1, model // 2) for array in joined(proj_flow)], axis=1
-        )
-        branch_part = jnp.dot(attended, weight, preferred_element_type=full).astype(low)
+        branch_part = jnp.dot(attended, proj_full, preferred_element_type=full).astype(low)
         other = swap_core(branch_part)
-        return weight, branch_part, other, *enter_feed(canvas, branch_part, other, grad_ph, mods_f)
-
-    proj_full, branch_part, branch_other, norm, norm_t, grad_branch_f = slot(
-        feed_flows[:2], project_out
-    )
+        return branch_part, other, *enter_feed(canvas, branch_part, other, grad_ph, mods_f)
+
+    branch_part, branch_other, norm, norm_t, grad_branch_f = slot(feed_flows[:2], project_out)
 
     kept = []
     grads = [None] * CHUNKS
@@ -1191,7 +1202,7 @@
     def run_feed(flows, t):
         slot.finish(feed_flows[t : t + 1])
         staying, leaving, up_grad, down_grad, tap_grad = slot(flows, feed(t))
-        kept.append((staying, leaving))
+        kept.append((staying, Flow(core_steps(leaving))))
         grads[t] = tap_grad
         if spread:
             back_flows[t] = [
@@ -1205,11 +1216,11 @@
             ]
 
     run_feed(feed_flows[1:], 0)
-    run_feed(feed_flows[2:] + back_flows[0], 1)
-    run_feed(back_flows[0] + back_flows[1], 2)
+    run_feed(feed_flows[2:] + back_flows[0] + [kept[0][1]], 1)
+    run_feed(back_flows[0] + back_flows[1] + [kept[1][1]], 2)
 
     def after_feed():
-        parts = [array for staying, leaving in kept for array in (staying, swap_core(leaving))]
+        parts = [array for staying, exchange in kept for array in (staying, run(exchange))]
         return leave_feed(words[:1], canvas, branch_part, branch_other, grad_ph, mods_f, parts)
 
     layer_out, grad_middle, grad_branch_mine, feed_sums = slot(
@@ -1228,10 +1239,10 @@
     proj_grad = proj_grad.reshape(chips, -1, model)
     proj_flow = sums(proj_grad[..., : model // 2], proj_grad[..., model // 2 :])
     grad_qkv = slot(
-        [proj_flow] + sum(back_flows, []), lambda: attend_back(mask, qkv, grad_attended)
+        [proj_flow] + back_flows[1] + back_flows[2], lambda: attend_back(mask, qkv, grad_attended)
     )
     qkv_grad = slot(
-        [proj_flow] + sum(back_flows, []),
+        [proj_flow] + back_flows[1],
         lambda: jnp.dot(convolved.T, grad_qkv, preferred_element_type=full).astype(low),
     )
     qkv_grad = qkv_grad.reshape(chips, 2 * part, -1)
@@ -1248,7 +1259,7 @@
         part_here = jnp.dot(grad_qkv, qkv_full.T, preferred_element_type=full).astype(low)
         return rows_near(part_here, core), swap_core(rows_near(part_here, 1 - core))
 
-    grad_conv = slot([qkv_flow, proj_flow] + back_flows[2], leave_attend)
+    grad_conv = slot([qkv_flow] + back_flows[2], leave_attend)
 
     def leave_block():
         input_grad, attn_tap_grad, mods_grad = conv_back(

time: 921 us -> 890 us (0.966)
  waiting for transfers between devices: 213 us -> 182 us
    ppermute x100, waiting for transfers between devices: 213 us -> 182 us  [swap(): lax.ppermute(x, AXES, [(i, i ^ 1 << bit) for i in range(device_count())])]
  transfers between devices with their start and end apart: 102 -> 102, of which waited for: 38 -> 27; matrix products, arithmetic and copies ran while one was open for 21% -> 22% of each run, Pallas kernels for 32% -> 35%
where the time goes in v9:
time: 890 us; the launch traced here: 880 us
  Pallas kernels  305 us (34%)
  waiting for transfers between devices  182 us (20%)
  other arithmetic  134 us (15%)
  local copies, waits for them, and re-layouts  106 us (12%)
  starting transfers between devices  104 us (12%)
  matrix products  47 us (5%)
    ppermute x100, waiting for transfers between devices, swap(): lax.ppermute(x, AXES, [(i, i ^ 1 << bit) for i in range(device_count())])  182 us
    pallas_call x3, Pallas kernels, feed_forward(): pl.pallas_call(functools.partial(feed_body, spread), grid_spec=pltpu.Pref...  164 us
    ppermute x100, starting transfers between devices, swap(): lax.ppermute(x, AXES, [(i, i ^ 1 << bit) for i in range(device_count())])  96.7 us
    concatenate x21, other arithmetic, join(): return [jnp.concatenate(pair, axis=0) for pair in zip(held, arriving)]  38.5 us
    convert_element_type x18, other arithmetic, halving_steps(): (staying[at].astype(full) + arriving[at].astype(full)).astype(low)  35.5 us
    pallas_call x1, Pallas kernels, attend_back(): pl.pallas_call(attend_back_body, grid=(pairs,), in_specs=[pl.BlockSpec((P...  28.9 us
    pallas_call x1, Pallas kernels, conv_in(): pl.pallas_call(conv_in_body, grid=(model // TILE,), in_specs=[pl.BlockSpe...  23 us
    pallas_call x1, Pallas kernels, conv_back(): pl.pallas_call(conv_back_body, grid_spec=pltpu.PrefetchScalarGridSpec(num...  21.1 us
  transfers between devices with their start and end apart: 102, of which 27 were waited for; matrix products, arithmetic and copies ran while one was open for 22% of the time, Pallas kernels for 35%

profile of v9, /device:TPU:0, one launch (start us, length us, event | category | flops | bytes accessed | tf_op | source)
XLA Modules:
  0.0 880.3 jit_solution(12607672384335197834)
XLA Ops:
  13.6 4.5 reshape_squeeze.7
  28.8 6.0 collective-permute-done.2
  34.8 11.2 %collective-permute-done.1 = bf16[1,96,2304]{2,1,0:T(8,128)(2,1)S(1)} collective-permute-done((bf16[1,96,2304]{2,1,0:T(8,128)(2,1)S(1)}, bf16[1,96,2304]{2,1,0:T(8,128)(2,1)S(1)}, u32[]{:S(2)}, u32[]{:S(2)}) %collective-permute-start.1) | collective-permute-done | bytes 442400 | tf_op jit(solution)/shard_map/ppermute | solution.py:33
  83.7 12.6 %collective-permute-done.7 = bf16[1,48,1536]{2,1,0:T(8,128)(2,1)S(1)} collective-permute-done((bf16[1,48,1536]{2,1,0:T(8,128)(2,1)}, bf16[1,48,1536]{2,1,0:T(8,128)(2,1)S(1)}, u32[]{:S(2)}, u32[]{:S(2)}) %collective-permute-start.7) | collective-permute-done | bytes 147488 | tf_op jit(solution)/shard_map/ppermute | solution.py:33
  122.7 6.8 collective-permute-done.13
  152.6 33.7 %collective-permute-done.17 = bf16[4,48,768]{2,1,0:T(8,128)(2,1)} collective-permute-done((bf16[4,48,768]{2,1,0:T(8,128)(2,1)}, bf16[4,48,768]{2,1,0:T(8,128)(2,1)}, u32[]{:S(2)}, u32[]{:S(2)}) %collective-permute-start.17) | collective-permute-done | bytes 294944 | tf_op jit(solution)/shard_map/ppermute | solution.py:33
  187.0 23.0 %conv_in.1 = bf16[1024,1536]{1,0:T(8,128)(2,1)} custom-call(bf16[1024,1536]{1,0:T(8,128)(2,1)} %bitcast.320, f32[16,1536]{1,0:T(8,128)} %pad_convert_fusion.1.kernel_ref, f32[8,1536]{1,0:T(8,128)} %maximum_maximum_fusion.mods_ref), custom_call_target="tpu_custom_call" | custom-call | flops 47185920 | bytes 6291456 | tf_op jit(solution)/shard_map/conv_in/pallas_call | solution.py:722
  223.8 5.6 assemble.5
  229.4 5.6 assemble.4
  235.1 12.7 %convolution_convert_fusion.2.qkv_ref = bf16[1024,2304]{1,0:T(8,128)(2,1)} fusion(bf16[1024,1536]{1,0:T(8,128)(2,1)} %conv_in.1, bf16[1536,1152]{1,0:T(8,128)(2,1)} %bitcast.326, bf16[1536,1152]{1,0:T(8,128)(2,1)} %bitcast.328), kind=kOutput, calls=%fused_computation.3 | convolution fusion | flops 7264272384 | bytes 14942208 | tf_op jit(solution)/shard_map/dot_general | solution.py:1151
  248.4 5.4 pad_maximum_fusion
  253.8 9.4 %collective-permute-done.33 = bf16[1,128,1536]{2,1,0:T(8,128)(2,1)} collective-permute-done((bf16[1,128,1536]{2,1,0:T(8,128)(2,1)S(1)}, bf16[1,128,1536]{2,1,0:T(8,128)(2,1)}, u32[]{:S(2)}, u32[]{:S(2)}) %collective-permute-start.33) | collective-permute-done | bytes 393248 | tf_op jit(solution)/shard_map/ppermute | solution.py:33
  286.0 15.6 %attend.1 = bf16[1024,768]{1,0:T(8,128)(2,1)} custom-call(f32[256,256]{1,0:T(8,128)} %compare_convert_fusion.mask_ref, bf16[1024,2304]{1,0:T(8,128)(2,1)} %convolution_convert_fusion.2.qkv_ref), custom_call_target="tpu_custom_call" | custom-call | flops 3221225472 | bytes 6291456 | tf_op jit(solution)/shard_map/attend/pallas_call | solution.py:356
  301.8 7.6 collective-permute-done.37
  327.7 17.5 %enter_feed.1 = (bf16[1024,1536]{1,0:T(8,128)(2,1)}, bf16[1536,1024]{1,0:T(8,128)(2,1)}, bf16[1024,1536]{1,0:T(8,128)(2,1)}) custom-call(bf16[1024,1536]{1,0:T(8,128)(2,1)} %bitcast.321, bf16[1024,1536]{1,0:T(8,128)(2,1)} %convolution_convert_fusion.4.part_ref, bf16[1024,1536]{1,0:T(8,128)(2,1)} %collective-permute-done.40.other_ref, ...), custom_call_target="tpu_custom_call" | custom-call | flops 1000 | bytes 1000 | tf_op jit(solution)/shard_map/enter_feed/pallas_call | solution.py:947
  354.4 54.8 %feed_forward.3 = (bf16[2,4,128,1536]{3,2,1,0:T(8,128)(2,1)}, bf16[2,4,128,1536]{3,2,1,0:T(8,128)(2,1)}, bf16[8,96,1024]{2,1,0:T(8,128)(2,1)}, bf16[8,96,1024]{2...) custom-call(s32[49]{0:T(128)} %pad_add_fusion.1.words_ref, ...), custom_call_target="tpu_custom_call" | custom-call | flops 19327352832 | bytes 28311552 | tf_op jit(solution)/shard_map/feed_forward/pallas_call | solution.py:614
  418.6 54.4 %feed_forward.4 = (bf16[2,4,128,1536]{3,2,1,0:T(8,128)(2,1)}, bf16[2,4,128,1536]{3,2,1,0:T(8,128)(2,1)}, bf16[8,96,1024]{2,1,0:T(8,128)(2,1)}, bf16[8,96,1024]{2...) custom-call(s32[49]{0:T(128)} %pad_add_fusion.1.words_ref, ...), custom_call_target="tpu_custom_call" | custom-call | flops 19327352832 | bytes 28311552 | tf_op jit(solution)/shard_map/feed_forward/pallas_call | solution.py:614
  473.1 12.3 %collective-permute-done.48 = bf16[8,96,1024]{2,1,0:T(8,128)(2,1)} collective-permute-done((bf16[8,96,1024]{2,1,0:T(8,128)(2,1)}, bf16[8,96,1024]{2,1,0:T(8,128)(2,1)}, u32[]{:S(2)}, u32[]{:S(2)}) %collective-permute-start.48) | collective-permute-done | bytes 1572896 | tf_op jit(solution)/shard_map/ppermute | solution.py:33
  497.7 54.6 %feed_forward.5 = (bf16[2,4,128,1536]{3,2,1,0:T(8,128)(2,1)}, bf16[2,4,128,1536]{3,2,1,0:T(8,128)(2,1)}, bf16[8,96,1024]{2,1,0:T(8,128)(2,1)}, bf16[8,96,1024]{2...) custom-call(s32[49]{0:T(128)} %pad_add_fusion.1.words_ref, ...), custom_call_target="tpu_custom_call" | custom-call | flops 19327352832 | bytes 28311552 | tf_op jit(solution)/shard_map/feed_forward/pallas_call | solution.py:614
  572.7 15.4 %leave_feed.1 = (bf16[512,1536]{1,0:T(8,128)(2,1)}, f32[512,1536]{1,0:T(8,128)}, bf16[512,1536]{1,0:T(8,128)(2,1)}, f32[8,1536]{1,0:T(8,128)}) custom-call(s32[1]{0:T(128)} %bitcast.32.words_ref.core_ref, bf16[1024,1536]{1,0:T(8,128)(2,1)} %bitcast.323, bf16[1024,1536]{1,0:T(8,128)(2,1)} %convolution_convert_fusion.4.part_ref, ...), custom_call_target="tpu_custom_call" | custom-call | flops 1000 | bytes 1000 | tf_op jit(solution)/shard_map/leave_feed/pallas_call | solution.py:1003
  588.1 6.1 collective-permute-done.58
  635.7 28.9 %attend_back.1 = bf16[1024,2304]{1,0:T(8,128)(2,1)} custom-call(f32[256,256]{1,0:T(8,128)} %compare_convert_fusion.mask_ref, bf16[1024,2304]{1,0:T(8,128)(2,1)} %convolution_convert_fusion.2.qkv_ref, bf16[1024,768]{1,0:T(8,128)(2,1)} %convolution_convert_fusion.7.grad_ref), custom_call_target="tpu_custom_call" | custom-call | flops 8053063680 | bytes 11010048 | tf_op jit(solution)/shard_map/attend_back/pallas_call | solution.py:377
  668.2 5.5 collective-permute-done.69
  683.2 10.3 %convolution_convert_fusion = bf16[1536,2304]{1,0:T(8,128)(2,1)S(1)} fusion(bf16[1024,1536]{1,0:T(8,128)(2,1)S(1)} %copy-done.15, bf16[1024,2304]{1,0:T(8,128)(2,1)} %attend_back.1), kind=kOutput, calls=%fused_computation | convolution fusion | flops 7251296256 | bytes 14942208 | tf_op jit(solution)/shard_map/dot_general | solution.py:1246
  693.6 8.2 convolution_convert_fusion.3
  725.2 5.8 collective-permute-done.78
  731.0 7.3 collective-permute-done.79
  738.3 17.6 %collective-permute-done.76 = bf16[2,2,2,96,1152]{4,3,0,1,2:T(8,128)(2,1)} collective-permute-done((bf16[2,2,2,96,1152]{4,3,0,1,2:T(8,128)(2,1)}, bf16[2,2,2,96,1152]{4,3,0,1,2:T(8,128)(2,1)}, u32[]{:S(2)}, u32[]{:S(2)}) %collective-permute-start.76) | collective-permute-done | bytes 1769504 | tf_op jit(solution)/shard_map/ppermute | solution.py:33
  770.6 21.1 %conv_back.1 = (f32[512,1536]{1,0:T(8,128)}, f32[16,1536]{1,0:T(8,128)}, f32[8,1536]{1,0:T(8,128)}) custom-call(s32[1]{0:T(128)} %bitcast.32.words_ref.core_ref, bf16[576,1536]{1,0:T(8,128)(2,1)} %bitcast.340, bf16[576,1536]{1,0:T(8,128)(2,1)} %bitcast.341, bf16[576,1536]{1,0:T(8,128)(2,1)} %collective-permute-done.80.arriving_ref, ...), custom_call_target="tpu_custom_call" | custom-call | flops 55050240 | bytes 11010048 | tf_op jit(solution)/shard_map/conv_back/pallas_call | solution.py:880
  816.4 4.7 reshape.364
  833.5 15.1 %collective-permute-done.90 = bf16[96,2304]{1,0:T(8,128)(2,1)S(1)} collective-permute-done((bf16[96,2304]{1,0:T(8,128)(2,1)S(1)}, bf16[96,2304]{1,0:T(8,128)(2,1)S(1)}, u32[]{:S(2)}, u32[]{:S(2)}) %collective-permute-start.90) | collective-permute-done | bytes 442400 | tf_op jit(solution)/shard_map/ppermute | solution.py:33
  867.7 5.6 collective-permute-done.101
  (661 shorter events, 372.3 us)
Async XLA Ops:
  140.7 69.3 %collective-permute-start.15 = (bf16[8,96,1152]{2,1,0:T(8,128)(2,1)S(1)}, bf16[8,96,1152]{2,1,0:T(8,128)(2,1)}, u32[]{:S(2)}, u32[]{:S(2)}) collective-permute-start(bf16[8,96,1152]{2,1,0:T(8,128)(2,1)S(1)} %pad_maximum_fusion.7.refs_0_), channel_id=1, source_target_pairs={{0,2},{1,3},{2,0},{3,1},{4,6},{5,7},{6,4},{7,5},{8,10},{9,11},{10,... | collective-permute-start | bytes 5308424 | tf_op jit(solution)/shard_map/ppermute | solution.py:33
  141.9 68.2 %collective-permute-start.16 = (bf16[8,96,1152]{2,1,0:T(8,128)(2,1)}, bf16[8,96,1152]{2,1,0:T(8,128)(2,1)}, u32[]{:S(2)}, u32[]{:S(2)}) collective-permute-start(bf16[8,96,1152]{2,1,0:T(8,128)(2,1)} %pad_maximum_fusion.8.refs_0_), channel_id=1, source_target_pairs={{0,4},{1,5},{2,6},{3,7},{4,0},{5,1},{6,2},{7,3},{8,12},{9,13},{10,... | collective-permute-start | bytes 5308424 | tf_op jit(solution)/shard_map/ppermute | solution.py:33
  145.5 40.8 %collective-permute-start.17 = (bf16[4,48,768]{2,1,0:T(8,128)(2,1)}, bf16[4,48,768]{2,1,0:T(8,128)(2,1)}, u32[]{:S(2)}, u32[]{:S(2)}) collective-permute-start(bf16[4,48,768]{2,1,0:T(8,128)(2,1)} %get-tuple-element.323), channel_id=1, source_target_pairs={{0,4},{1,5},{2,6},{3,7},{4,0},{5,1},{6,2},{7,3},{8,12},{9,13},{10,... | collective-permute-start | bytes 884744 | tf_op jit(solution)/shard_map/ppermute | solution.py:33
  152.2 57.9 %collective-permute-start.18 = (bf16[4,48,768]{2,1,0:T(8,128)(2,1)}, bf16[4,48,768]{2,1,0:T(8,128)(2,1)}, u32[]{:S(2)}, u32[]{:S(2)}) collective-permute-start(bf16[4,48,768]{2,1,0:T(8,128)(2,1)} %get-tuple-element.324), channel_id=1, source_target_pairs={{0,2},{1,3},{2,0},{3,1},{4,6},{5,7},{6,4},{7,5},{8,10},{9,11},{10,... | collective-permute-start | bytes 884744 | tf_op jit(solution)/shard_map/ppermute | solution.py:33
  152.5 57.5 %collective-permute-start.19 = (bf16[2,96,1024]{2,1,0:T(8,128)(2,1)}, bf16[2,96,1024]{2,1,0:T(8,128)(2,1)}, u32[]{:S(2)}, u32[]{:S(2)}) collective-permute-start(bf16[2,96,1024]{2,1,0:T(8,128)(2,1)} %pad_maximum_fusion.26), channel_id=1, source_target_pairs={{0,8},{1,9},{2,10},{3,11},{4,12},{5,13},{6,14},{7,15},{8,0},{9,1},... | collective-permute-start | bytes 1179656 | tf_op jit(solution)/shard_map/ppermute | solution.py:33
  217.3 45.9 %collective-permute-start.28 = (bf16[8,48,768]{2,1,0:T(8,128)(2,1)S(1)}, bf16[8,48,768]{2,1,0:T(8,128)(2,1)}, u32[]{:S(2)}, u32[]{:S(2)}) collective-permute-start(bf16[8,48,768]{2,1,0:T(8,128)(2,1)S(1)} %pad_maximum_fusion.24.refs_0_), channel_id=1, source_target_pairs={{0,2},{1,3},{2,0},{3,1},{4,6},{5,7},{6,4},{7,5},{8,10},{9,11},{10,... | collective-permute-start | bytes 1769480 | tf_op jit(solution)/shard_map/ppermute | solution.py:33
  218.1 45.1 %collective-permute-start.29 = (bf16[8,48,768]{2,1,0:T(8,128)(2,1)}, bf16[8,48,768]{2,1,0:T(8,128)(2,1)}, u32[]{:S(2)}, u32[]{:S(2)}) collective-permute-start(bf16[8,48,768]{2,1,0:T(8,128)(2,1)} %pad_maximum_fusion.25.refs_0_), channel_id=1, source_target_pairs={{0,4},{1,5},{2,6},{3,7},{4,0},{5,1},{6,2},{7,3},{8,12},{9,13},{10,... | collective-permute-start | bytes 1769480 | tf_op jit(solution)/shard_map/ppermute | solution.py:33
  219.3 43.9 %collective-permute-start.30 = (bf16[4,96,1024]{2,1,0:T(8,128)(2,1)}, bf16[4,96,1024]{2,1,0:T(8,128)(2,1)}, u32[]{:S(2)}, u32[]{:S(2)}) collective-permute-start(bf16[4,96,1024]{2,1,0:T(8,128)(2,1)} %pad_maximum_fusion.19), channel_id=1, source_target_pairs={{0,4},{1,5},{2,6},{3,7},{4,0},{5,1},{6,2},{7,3},{8,12},{9,13},{10,... | collective-permute-start | bytes 2359304 | tf_op jit(solution)/shard_map/ppermute | solution.py:33
  220.1 43.1 %collective-permute-start.31 = (bf16[4,64,1536]{2,1,0:T(8,128)(2,1)}, bf16[4,64,1536]{2,1,0:T(8,128)(2,1)}, u32[]{:S(2)}, u32[]{:S(2)}) collective-permute-start(bf16[4,64,1536]{2,1,0:T(8,128)(2,1)} %pad_maximum_fusion.20), channel_id=1, source_target_pairs={{0,2},{1,3},{2,0},{3,1},{4,6},{5,7},{6,4},{7,5},{8,10},{9,11},{10,... | collective-permute-start | bytes 2359304 | tf_op jit(solution)/shard_map/ppermute | solution.py:33
  272.3 37.1 %collective-permute-start.34 = (bf16[8,96,1024]{2,1,0:T(8,128)(2,1)}, bf16[8,96,1024]{2,1,0:T(8,128)(2,1)}, u32[]{:S(2)}, u32[]{:S(2)}) collective-permute-start(bf16[8,96,1024]{2,1,0:T(8,128)(2,1)} %pad_maximum_fusion.9.refs_0_), channel_id=1, source_target_pairs={{0,2},{1,3},{2,0},{3,1},{4,6},{5,7},{6,4},{7,5},{8,10},{9,11},{10,... | collective-permute-start | bytes 4718600 | tf_op jit(solution)/shard_map/ppermute | solution.py:33
  350.3 58.9 %collective-permute-start.42 = (bf16[8,96,1024]{2,1,0:T(8,128)(2,1)}, bf16[8,96,1024]{2,1,0:T(8,128)(2,1)}, u32[]{:S(2)}, u32[]{:S(2)}) collective-permute-start(bf16[8,96,1024]{2,1,0:T(8,128)(2,1)} %pad_maximum_fusion.12.refs_0_), channel_id=1, source_target_pairs={{0,2},{1,3},{2,0},{3,1},{4,6},{5,7},{6,4},{7,5},{8,10},{9,11},{10,... | collective-permute-start | bytes 4718600 | tf_op jit(solution)/shard_map/ppermute | solution.py:33
  352.1 57.1 %collective-permute-start.43 = (bf16[8,64,1536]{2,1,0:T(8,128)(2,1)}, bf16[8,64,1536]{2,1,0:T(8,128)(2,1)}, u32[]{:S(2)}, u32[]{:S(2)}) collective-permute-start(bf16[8,64,1536]{2,1,0:T(8,128)(2,1)} %pad_maximum_fusion.13.refs_2_), channel_id=1, source_target_pairs={{0,4},{1,5},{2,6},{3,7},{4,0},{5,1},{6,2},{7,3},{8,12},{9,13},{10,... | collective-permute-start | bytes 4718600 | tf_op jit(solution)/shard_map/ppermute | solution.py:33
  352.4 56.8 %collective-permute-start.44 = (bf16[4,96,1024]{2,1,0:T(8,128)(2,1)}, bf16[4,96,1024]{2,1,0:T(8,128)(2,1)}, u32[]{:S(2)}, u32[]{:S(2)}) collective-permute-start(bf16[4,96,1024]{2,1,0:T(8,128)(2,1)} %get-tuple-element.379), channel_id=1, source_target_pairs={{0,4},{1,5},{2,6},{3,7},{4,0},{5,1},{6,2},{7,3},{8,12},{9,13},{10,... | collective-permute-start | bytes 2359304 | tf_op jit(solution)/shard_map/ppermute | solution.py:33
  354.1 55.1 %collective-permute-start.45 = (bf16[4,64,1536]{2,1,0:T(8,128)(2,1)}, bf16[4,64,1536]{2,1,0:T(8,128)(2,1)}, u32[]{:S(2)}, u32[]{:S(2)}) collective-permute-start(bf16[4,64,1536]{2,1,0:T(8,128)(2,1)} %get-tuple-element.380), channel_id=1, source_target_pairs={{0,2},{1,3},{2,0},{3,1},{4,6},{5,7},{6,4},{7,5},{8,10},{9,11},{10,... | collective-permute-start | bytes 2359304 | tf_op jit(solution)/shard_map/ppermute | solution.py:33
  414.6 72.3 %collective-permute-start.50 = (bf16[2,4,128,1536]{3,2,1,0:T(8,128)(2,1)}, bf16[2,4,128,1536]{3,2,1,0:T(8,128)(2,1)}, u32[]{:S(2)}, u32[]{:S(2)}) collective-permute-start(bf16[2,4,128,1536]{3,2,1,0:T(8,128)(2,1)} %get-tuple-element.405), channel_id=1, source_target_pairs={{0,1},{1,0},{2,3},{3,2},{4,5},{5,4},{6,7},{7,6},{8,9},{9,8},{10,11... | collective-permute-start | bytes 9437192 | tf_op jit(solution)/shard_map/ppermute | solution.py:33
  414.6 58.5 %collective-permute-start.46 = (bf16[8,96,1024]{2,1,0:T(8,128)(2,1)}, bf16[8,96,1024]{2,1,0:T(8,128)(2,1)}, u32[]{:S(2)}, u32[]{:S(2)}) collective-permute-start(bf16[8,96,1024]{2,1,0:T(8,128)(2,1)} %pad_maximum_fusion.14.refs_0_), channel_id=1, source_target_pairs={{0,2},{1,3},{2,0},{3,1},{4,6},{5,7},{6,4},{7,5},{8,10},{9,11},{10,... | collective-permute-start | bytes 4718600 | tf_op jit(solution)/shard_map/ppermute | solution.py:33
  416.3 56.8 %collective-permute-start.47 = (bf16[8,64,1536]{2,1,0:T(8,128)(2,1)}, bf16[8,64,1536]{2,1,0:T(8,128)(2,1)}, u32[]{:S(2)}, u32[]{:S(2)}) collective-permute-start(bf16[8,64,1536]{2,1,0:T(8,128)(2,1)} %pad_maximum_fusion.15.refs_2_), channel_id=1, source_target_pairs={{0,4},{1,5},{2,6},{3,7},{4,0},{5,1},{6,2},{7,3},{8,12},{9,13},{10,... | collective-permute-start | bytes 4718600 | tf_op jit(solution)/shard_map/ppermute | solution.py:33
  416.6 68.8 %collective-permute-start.48 = (bf16[8,96,1024]{2,1,0:T(8,128)(2,1)}, bf16[8,96,1024]{2,1,0:T(8,128)(2,1)}, u32[]{:S(2)}, u32[]{:S(2)}) collective-permute-start(bf16[8,96,1024]{2,1,0:T(8,128)(2,1)} %get-tuple-element.403), channel_id=1, source_target_pairs={{0,2},{1,3},{2,0},{3,1},{4,6},{5,7},{6,4},{7,5},{8,10},{9,11},{10,... | collective-permute-start | bytes 4718600 | tf_op jit(solution)/shard_map/ppermute | solution.py:33
  416.9 70.0 %collective-permute-start.49 = (bf16[8,64,1536]{2,1,0:T(8,128)(2,1)}, bf16[8,64,1536]{2,1,0:T(8,128)(2,1)}, u32[]{:S(2)}, u32[]{:S(2)}) collective-permute-start(bf16[8,64,1536]{2,1,0:T(8,128)(2,1)} %get-tuple-element.404), channel_id=1, source_target_pairs={{0,4},{1,5},{2,6},{3,7},{4,0},{5,1},{6,2},{7,3},{8,12},{9,13},{10,... | collective-permute-start | bytes 4718600 | tf_op jit(solution)/shard_map/ppermute | solution.py:33
  493.7 58.7 %collective-permute-start.55 = (bf16[2,4,128,1536]{3,2,1,0:T(8,128)(2,1)}, bf16[2,4,128,1536]{3,2,1,0:T(8,128)(2,1)}, u32[]{:S(2)}, u32[]{:S(2)}) collective-permute-start(bf16[2,4,128,1536]{3,2,1,0:T(8,128)(2,1)} %get-tuple-element.427), channel_id=1, source_target_pairs={{0,1},{1,0},{2,3},{3,2},{4,5},{5,4},{6,7},{7,6},{8,9},{9,8},{10,11... | collective-permute-start | bytes 9437192 | tf_op jit(solution)/shard_map/ppermute | solution.py:33
  493.7 58.6 %collective-permute-start.51 = (bf16[4,96,1024]{2,1,0:T(8,128)(2,1)}, bf16[4,96,1024]{2,1,0:T(8,128)(2,1)}, u32[]{:S(2)}, u32[]{:S(2)}) collective-permute-start(bf16[4,96,1024]{2,1,0:T(8,128)(2,1)} %get-tuple-element.423), channel_id=1, source_target_pairs={{0,4},{1,5},{2,6},{3,7},{4,0},{5,1},{6,2},{7,3},{8,12},{9,13},{10,... | collective-permute-start | bytes 2359304 | tf_op jit(solution)/shard_map/ppermute | solution.py:33
  494.0 58.4 %collective-permute-start.52 = (bf16[4,64,1536]{2,1,0:T(8,128)(2,1)}, bf16[4,64,1536]{2,1,0:T(8,128)(2,1)}, u32[]{:S(2)}, u32[]{:S(2)}) collective-permute-start(bf16[4,64,1536]{2,1,0:T(8,128)(2,1)} %get-tuple-element.424), channel_id=1, source_target_pairs={{0,2},{1,3},{2,0},{3,1},{4,6},{5,7},{6,4},{7,5},{8,10},{9,11},{10,... | collective-permute-start | bytes 2359304 | tf_op jit(solution)/shard_map/ppermute | solution.py:33
  494.3 58.1 %collective-permute-start.53 = (bf16[8,96,1024]{2,1,0:T(8,128)(2,1)}, bf16[8,96,1024]{2,1,0:T(8,128)(2,1)}, u32[]{:S(2)}, u32[]{:S(2)}) collective-permute-start(bf16[8,96,1024]{2,1,0:T(8,128)(2,1)} %get-tuple-element.425), channel_id=1, source_target_pairs={{0,2},{1,3},{2,0},{3,1},{4,6},{5,7},{6,4},{7,5},{8,10},{9,11},{10,... | collective-permute-start | bytes 4718600 | tf_op jit(solution)/shard_map/ppermute | solution.py:33
  496.0 56.4 %collective-permute-start.54 = (bf16[8,64,1536]{2,1,0:T(8,128)(2,1)}, bf16[8,64,1536]{2,1,0:T(8,128)(2,1)}, u32[]{:S(2)}, u32[]{:S(2)}) collective-permute-start(bf16[8,64,1536]{2,1,0:T(8,128)(2,1)} %get-tuple-element.426), channel_id=1, source_target_pairs={{0,4},{1,5},{2,6},{3,7},{4,0},{5,1},{6,2},{7,3},{8,12},{9,13},{10,... | collective-permute-start | bytes 4718600 | tf_op jit(solution)/shard_map/ppermute | solution.py:33
  557.1 37.0 %collective-permute-start.58 = (bf16[8,96,1024]{2,1,0:T(8,128)(2,1)}, bf16[8,96,1024]{2,1,0:T(8,128)(2,1)}, u32[]{:S(2)}, u32[]{:S(2)}) collective-permute-start(bf16[8,96,1024]{2,1,0:T(8,128)(2,1)} %get-tuple-element.445), channel_id=1, source_target_pairs={{0,2},{1,3},{2,0},{3,1},{4,6},{5,7},{6,4},{7,5},{8,10},{9,11},{10,... | collective-permute-start | bytes 4718600 | tf_op jit(solution)/shard_map/ppermute | solution.py:33
  557.4 36.7 %collective-permute-start.59 = (bf16[8,64,1536]{2,1,0:T(8,128)(2,1)}, bf16[8,64,1536]{2,1,0:T(8,128)(2,1)}, u32[]{:S(2)}, u32[]{:S(2)}) collective-permute-start(bf16[8,64,1536]{2,1,0:T(8,128)(2,1)} %get-tuple-element.446), channel_id=1, source_target_pairs={{0,4},{1,5},{2,6},{3,7},{4,0},{5,1},{6,2},{7,3},{8,12},{9,13},{10,... | collective-permute-start | bytes 4718600 | tf_op jit(solution)/shard_map/ppermute | solution.py:33
  631.2 42.5 %collective-permute-start.66 = (bf16[2,2,2,48,768]{4,3,0,1,2:T(8,128)(2,1)}, bf16[2,2,2,48,768]{4,3,0,1,2:T(8,128)(2,1)}, u32[]{:S(2)}, u32[]{:S(2)}) collective-permute-start(bf16[2,2,2,48,768]{4,3,0,1,2:T(8,128)(2,1)} %copy_bitcast_fusion.6), channel_id=1, source_target_pairs={{0,2},{1,3},{2,0},{3,1},{4,6},{5,7},{6,4},{7,5},{8,10},{9,11},{10,... | collective-permute-start | bytes 1769480 | tf_op jit(solution)/shard_map/ppermute | solution.py:33
  632.9 40.8 %collective-permute-start.67 = (bf16[2,2,2,48,768]{4,3,0,1,2:T(8,128)(2,1)}, bf16[2,2,2,48,768]{4,3,0,1,2:T(8,128)(2,1)}, u32[]{:S(2)}, u32[]{:S(2)}) collective-permute-start(bf16[2,2,2,48,768]{4,3,0,1,2:T(8,128)(2,1)} %copy_bitcast_fusion.5), channel_id=1, source_target_pairs={{0,4},{1,5},{2,6},{3,7},{4,0},{5,1},{6,2},{7,3},{8,12},{9,13},{10,... | collective-permute-start | bytes 1769480 | tf_op jit(solution)/shard_map/ppermute | solution.py:33
  634.9 38.7 %collective-permute-start.70 = (bf16[4,96,1024]{2,1,0:T(8,128)(2,1)}, bf16[4,96,1024]{2,1,0:T(8,128)(2,1)}, u32[]{:S(2)}, u32[]{:S(2)}) collective-permute-start(bf16[4,96,1024]{2,1,0:T(8,128)(2,1)} %get-tuple-element.486), channel_id=1, source_target_pairs={{0,4},{1,5},{2,6},{3,7},{4,0},{5,1},{6,2},{7,3},{8,12},{9,13},{10,... | collective-permute-start | bytes 2359304 | tf_op jit(solution)/shard_map/ppermute | solution.py:33
  635.2 38.5 %collective-permute-start.71 = (bf16[4,64,1536]{2,1,0:T(8,128)(2,1)}, bf16[4,64,1536]{2,1,0:T(8,128)(2,1)}, u32[]{:S(2)}, u32[]{:S(2)}) collective-permute-start(bf16[4,64,1536]{2,1,0:T(8,128)(2,1)} %get-tuple-element.487), channel_id=1, source_target_pairs={{0,2},{1,3},{2,0},{3,1},{4,6},{5,7},{6,4},{7,5},{8,10},{9,11},{10,... | collective-permute-start | bytes 2359304 | tf_op jit(solution)/shard_map/ppermute | solution.py:33
  714.7 41.3 %collective-permute-start.76 = (bf16[2,2,2,96,1152]{4,3,0,1,2:T(8,128)(2,1)}, bf16[2,2,2,96,1152]{4,3,0,1,2:T(8,128)(2,1)}, u32[]{:S(2)}, u32[]{:S(2)}) collective-permute-start(bf16[2,2,2,96,1152]{4,3,0,1,2:T(8,128)(2,1)} %copy_bitcast_fusion.1), channel_id=1, source_target_pairs={{0,2},{1,3},{2,0},{3,1},{4,6},{5,7},{6,4},{7,5},{8,10},{9,11},{10,... | collective-permute-start | bytes 5308424 | tf_op jit(solution)/shard_map/ppermute | solution.py:33
  715.4 41.0 %collective-permute-start.77 = (bf16[2,2,2,96,1152]{4,3,0,1,2:T(8,128)(2,1)}, bf16[2,2,2,96,1152]{4,3,0,1,2:T(8,128)(2,1)}, u32[]{:S(2)}, u32[]{:S(2)}) collective-permute-start(bf16[2,2,2,96,1152]{4,3,0,1,2:T(8,128)(2,1)} %copy_bitcast_fusion), channel_id=1, source_target_pairs={{0,4},{1,5},{2,6},{3,7},{4,0},{5,1},{6,2},{7,3},{8,12},{9,13},{10,... | collective-permute-start | bytes 5308424 | tf_op jit(solution)/shard_map/ppermute | solution.py:33
  (187 other events, 2387.8 us)

commit v10 on v9

--- a/solution.py
+++ b/solution.py
@@ -95,6 +95,15 @@
         arriving = yield [(array, bit) for array in held]
         held = join(held, arriving)
     return held
+
+
+def one_colour_steps(shard, chip_bits):
+    held = shard[None]
+    for bit in range(chip_bits - 1, 0, -1):
+        (arriving,) = yield [(held, bit)]
+        held = jnp.concatenate([held, arriving], axis=0)
+    (arriving,) = yield [(held, 0)]
+    return held, arriving
 
 
 def core_steps(array):
@@ -1092,9 +1101,9 @@
     proj_there = [(r, r % chips * 2 + r // chips) for r in range(devices)]
     proj_back = [(b, a) for a, b in proj_there]
     proj_rows = lax.ppermute(proj_weight, AXES, proj_there)
-    proj_near = near(proj_rows)
+    proj_flow = Flow(one_colour_steps(proj_rows, chip_bits))
     canvas = slot(
-        [qkv_near, mods_flow, proj_near], lambda: join_halves(mine, swap_core(mine), core)
+        [qkv_near, mods_flow, proj_flow], lambda: join_halves(mine, swap_core(mine), core)
     )
     slot.finish([qkv_near])
     tap_count = 9 * (share + part)
@@ -1128,16 +1137,13 @@
     ]
     left, right = (Ellipsis, slice(qkv_half)), (Ellipsis, slice(qkv_half, None))
     qkv_flow = far(qkv_near.result * 2, (left, right))
-    slot([qkv_flow, mods_flow, proj_near, feed_near[0]])
+    slot([qkv_flow, mods_flow, proj_flow, feed_near[0]])
     mods_half = run(mods_flow)
     mods = mods_half + swap_core(mods_half)
     shift_a, scale_a, gate_a, shift_f, scale_f, gate_f = jnp.split(mods, 6)
 
     mods_a = jnp.concatenate([shift_a[None], scale_a[None], jnp.zeros((6, model), full)], axis=0)
 
-    slot.finish([proj_near])
-    left, right = (Ellipsis, slice(model // 2)), (Ellipsis, slice(model // 2, None))
-    proj_flow = far(proj_near.result * 2, (left, right))
     convolved = slot(
         [qkv_flow, proj_flow, feed_near[0]], lambda: conv_in(canvas, attn_taps, mods_a)
     )
@@ -1156,10 +1162,8 @@
     slot.finish([proj_flow])
 
     def attend_and_assemble():
-        weight = jnp.concatenate(
-            [array.reshape(-1, model // 2) for array in joined(proj_flow)], axis=1
-        )
-        return attend(mask, qkv), weight
+        weight = assemble(proj_flow.result, gather_order(chip_bits, 0), chip)
+        return attend(mask, qkv), weight.reshape(-1, model)
 
     attended, proj_full = slot([feed_flows[0], feed_near[1]], attend_and_assemble)
     slot.finish([feed_near[1]])
@@ -1237,7 +1241,7 @@
 
     grad_attended, proj_grad = slot(back_flows[0] + back_flows[1], enter_attend)
     proj_grad = proj_grad.reshape(chips, -1, model)
-    proj_flow = sums(proj_grad[..., : model // 2], proj_grad[..., model // 2 :])
+    proj_flow = sums(proj_grad)
     grad_qkv = slot(
         [proj_flow] + back_flows[1] + back_flows[2], lambda: attend_back(mask, qkv, grad_attended)
     )

time: 890 us -> 856 us (0.962)
  waiting for transfers between devices: 182 us -> 165 us
  local copies, waits for them, and re-layouts: 106 us -> 93.8 us
    ppermute x100 -> x96, waiting for transfers between devices: 182 us -> 165 us  [swap(): lax.ppermute(x, AXES, [(i, i ^ 1 << bit) for i in range(device_count())])]
    concatenate x21 -> x17, other arithmetic: 38.5 us -> 32.9 us  [join(): return [jnp.concatenate(pair, axis=0) for pair in zip(held, arriving)]]
    pallas_call x4 -> x3, Pallas kernels: 19.8 us -> 16.1 us  [assemble(): pl.pallas_call(functools.partial(assemble_body, steps), grid_spec=pltpu.P...]
    ppermute x100 -> x96, starting transfers between devices: 96.7 us -> 98.8 us  [swap(): lax.ppermute(x, AXES, [(i, i ^ 1 << bit) for i in range(device_count())])]
  transfers between devices with their start and end apart: 102 -> 98, of which waited for: 27 -> 31; matrix products, arithmetic and copies ran while one was open for 22% -> 21% of each run, Pallas kernels for 35% -> 36%
where the time goes in v10:
time: 856 us; the launch traced here: 846 us
  Pallas kernels  301 us (35%)
  waiting for transfers between devices  165 us (19%)
  other arithmetic  129 us (15%)
  starting transfers between devices  106 us (12%)
  local copies, waits for them, and re-layouts  93.8 us (11%)
  matrix products  48.9 us (6%)
    ppermute x96, waiting for transfers between devices, swap(): lax.ppermute(x, AXES, [(i, i ^ 1 << bit) for i in range(device_count())])  165 us
    pallas_call x3, Pallas kernels, feed_forward(): pl.pallas_call(functools.partial(feed_body, spread), grid_spec=pltpu.Pref...  164 us
    ppermute x96, starting transfers between devices, swap(): lax.ppermute(x, AXES, [(i, i ^ 1 << bit) for i in range(device_count())])  98.8 us
    concatenate x17, other arithmetic, join(): return [jnp.concatenate(pair, axis=0) for pair in zip(held, arriving)]  32.9 us
    convert_element_type x18, other arithmetic, halving_steps(): (staying[at].astype(full) + arriving[at].astype(full)).astype(low)  32.1 us
    pallas_call x1, Pallas kernels, attend_back(): pl.pallas_call(attend_back_body, grid=(pairs,), in_specs=[pl.BlockSpec((P...  28.9 us
    pallas_call x1, Pallas kernels, conv_in(): pl.pallas_call(conv_in_body, grid=(model // TILE,), in_specs=[pl.BlockSpe...  23 us
    pallas_call x1, Pallas kernels, conv_back(): pl.pallas_call(conv_back_body, grid_spec=pltpu.PrefetchScalarGridSpec(num...  21.1 us
  transfers between devices with their start and end apart: 98, of which 31 were waited for; matrix products, arithmetic and copies ran while one was open for 21% of the time, Pallas kernels for 36%

profile of v10, /device:TPU:0, one launch (start us, length us, event | category | flops | bytes accessed | tf_op | source)
XLA Modules:
  0.0 846.4 jit_solution(4910687940753317126)
XLA Ops:
  28.8 6.0 collective-permute-done.2
  34.8 11.2 %collective-permute-done.1 = bf16[1,96,2304]{2,1,0:T(8,128)(2,1)S(1)} collective-permute-done((bf16[1,96,2304]{2,1,0:T(8,128)(2,1)S(1)}, bf16[1,96,2304]{2,1,0:T(8,128)(2,1)S(1)}, u32[]{:S(2)}, u32[]{:S(2)}) %collective-permute-start.1) | collective-permute-done | bytes 442400 | tf_op jit(solution)/shard_map/ppermute | solution.py:33
  83.6 12.7 %collective-permute-done.7 = bf16[1,48,1536]{2,1,0:T(8,128)(2,1)S(1)} collective-permute-done((bf16[1,48,1536]{2,1,0:T(8,128)(2,1)}, bf16[1,48,1536]{2,1,0:T(8,128)(2,1)S(1)}, u32[]{:S(2)}, u32[]{:S(2)}) %collective-permute-start.7) | collective-permute-done | bytes 147488 | tf_op jit(solution)/shard_map/ppermute | solution.py:33
  122.7 6.8 collective-permute-done.13
  155.2 23.0 %conv_in.1 = bf16[1024,1536]{1,0:T(8,128)(2,1)} custom-call(bf16[1024,1536]{1,0:T(8,128)(2,1)} %bitcast.291, f32[16,1536]{1,0:T(8,128)} %pad_convert_fusion.1.kernel_ref, f32[8,1536]{1,0:T(8,128)} %maximum_maximum_fusion.mods_ref), custom_call_target="tpu_custom_call" | custom-call | flops 47185920 | bytes 6291456 | tf_op jit(solution)/shard_map/conv_in/pallas_call | solution.py:731
  178.3 14.4 %collective-permute-done.17 = bf16[4,48,1536]{2,1,0:T(8,128)(2,1)} collective-permute-done((bf16[4,48,1536]{2,1,0:T(8,128)(2,1)}, bf16[4,48,1536]{2,1,0:T(8,128)(2,1)}, u32[]{:S(2)}, u32[]{:S(2)}) %collective-permute-start.17) | collective-permute-done | bytes 589856 | tf_op jit(solution)/shard_map/ppermute | solution.py:33
  205.0 5.6 assemble.4
  210.6 5.6 assemble.3
  216.2 12.7 %convolution_convert_fusion.2.qkv_ref = bf16[1024,2304]{1,0:T(8,128)(2,1)} fusion(bf16[1024,1536]{1,0:T(8,128)(2,1)} %conv_in.1, bf16[1536,1152]{1,0:T(8,128)(2,1)} %bitcast.297, bf16[1536,1152]{1,0:T(8,128)(2,1)} %bitcast.299), kind=kOutput, calls=%fused_computation.3 | convolution fusion | flops 7264272384 | bytes 14942208 | tf_op jit(solution)/shard_map/dot_general | solution.py:1157
  228.9 5.4 pad_maximum_fusion
  234.4 5.2 collective-permute-done.29
  253.8 4.9 assemble.5
  258.8 15.4 %attend.1 = bf16[1024,768]{1,0:T(8,128)(2,1)} custom-call(f32[256,256]{1,0:T(8,128)} %compare_convert_fusion.mask_ref, bf16[1024,2304]{1,0:T(8,128)(2,1)} %convolution_convert_fusion.2.qkv_ref), custom_call_target="tpu_custom_call" | custom-call | flops 3221225472 | bytes 6291456 | tf_op jit(solution)/shard_map/attend/pallas_call | solution.py:365
  274.1 8.2 collective-permute-done.35
  282.3 6.4 convolution_convert_fusion.4.part_ref
  301.9 17.6 %enter_feed.1 = (bf16[1024,1536]{1,0:T(8,128)(2,1)}, bf16[1536,1024]{1,0:T(8,128)(2,1)}, bf16[1024,1536]{1,0:T(8,128)(2,1)}) custom-call(bf16[1024,1536]{1,0:T(8,128)(2,1)} %bitcast.292, bf16[1024,1536]{1,0:T(8,128)(2,1)} %convolution_convert_fusion.4.part_ref, bf16[1024,1536]{1,0:T(8,128)(2,1)} %collective-permute-done.38.other_ref, ...), custom_call_target="tpu_custom_call" | custom-call | flops 1000 | bytes 1000 | tf_op jit(solution)/shard_map/enter_feed/pallas_call | solution.py:956
  328.7 54.8 %feed_forward.3 = (bf16[2,4,128,1536]{3,2,1,0:T(8,128)(2,1)}, bf16[2,4,128,1536]{3,2,1,0:T(8,128)(2,1)}, bf16[8,96,1024]{2,1,0:T(8,128)(2,1)}, bf16[8,96,1024]{2...) custom-call(s32[49]{0:T(128)} %pad_add_fusion.1.words_ref, ...), custom_call_target="tpu_custom_call" | custom-call | flops 19327352832 | bytes 28311552 | tf_op jit(solution)/shard_map/feed_forward/pallas_call | solution.py:623
  392.9 54.4 %feed_forward.4 = (bf16[2,4,128,1536]{3,2,1,0:T(8,128)(2,1)}, bf16[2,4,128,1536]{3,2,1,0:T(8,128)(2,1)}, bf16[8,96,1024]{2,1,0:T(8,128)(2,1)}, bf16[8,96,1024]{2...) custom-call(s32[49]{0:T(128)} %pad_add_fusion.1.words_ref, ...), custom_call_target="tpu_custom_call" | custom-call | flops 19327352832 | bytes 28311552 | tf_op jit(solution)/shard_map/feed_forward/pallas_call | solution.py:623
  447.3 12.4 %collective-permute-done.46 = bf16[8,96,1024]{2,1,0:T(8,128)(2,1)} collective-permute-done((bf16[8,96,1024]{2,1,0:T(8,128)(2,1)}, bf16[8,96,1024]{2,1,0:T(8,128)(2,1)}, u32[]{:S(2)}, u32[]{:S(2)}) %collective-permute-start.46) | collective-permute-done | bytes 1572896 | tf_op jit(solution)/shard_map/ppermute | solution.py:33
  470.8 54.5 %feed_forward.5 = (bf16[2,4,128,1536]{3,2,1,0:T(8,128)(2,1)}, bf16[2,4,128,1536]{3,2,1,0:T(8,128)(2,1)}, bf16[8,96,1024]{2,1,0:T(8,128)(2,1)}, bf16[8,96,1024]{2...) custom-call(s32[49]{0:T(128)} %pad_add_fusion.1.words_ref, ...), custom_call_target="tpu_custom_call" | custom-call | flops 19327352832 | bytes 28311552 | tf_op jit(solution)/shard_map/feed_forward/pallas_call | solution.py:623
  536.6 15.4 %leave_feed.1 = (bf16[512,1536]{1,0:T(8,128)(2,1)}, f32[512,1536]{1,0:T(8,128)}, bf16[512,1536]{1,0:T(8,128)(2,1)}, f32[8,1536]{1,0:T(8,128)}) custom-call(s32[1]{0:T(128)} %bitcast.31.words_ref.core_ref, bf16[1024,1536]{1,0:T(8,128)(2,1)} %bitcast.293, bf16[1024,1536]{1,0:T(8,128)(2,1)} %convolution_convert_fusion.4.part_ref, ...), custom_call_target="tpu_custom_call" | custom-call | flops 1000 | bytes 1000 | tf_op jit(solution)/shard_map/leave_feed/pallas_call | solution.py:1012
  552.0 13.9 %collective-permute-done.56 = bf16[8,96,1024]{2,1,0:T(8,128)(2,1)} collective-permute-done((bf16[8,96,1024]{2,1,0:T(8,128)(2,1)}, bf16[8,96,1024]{2,1,0:T(8,128)(2,1)}, u32[]{:S(2)}, u32[]{:S(2)}) %collective-permute-start.56) | collective-permute-done | bytes 1572896 | tf_op jit(solution)/shard_map/ppermute | solution.py:33
  603.5 28.9 %attend_back.1 = bf16[1024,2304]{1,0:T(8,128)(2,1)} custom-call(f32[256,256]{1,0:T(8,128)} %compare_convert_fusion.mask_ref, bf16[1024,2304]{1,0:T(8,128)(2,1)} %convolution_convert_fusion.2.qkv_ref, bf16[1024,768]{1,0:T(8,128)(2,1)} %convolution_convert_fusion.7.grad_ref), custom_call_target="tpu_custom_call" | custom-call | flops 8053063680 | bytes 11010048 | tf_op jit(solution)/shard_map/attend_back/pallas_call | solution.py:386
  632.5 10.4 %collective-permute-done.68 = bf16[4,64,1536]{2,1,0:T(8,128)(2,1)} collective-permute-done((bf16[4,64,1536]{2,1,0:T(8,128)(2,1)}, bf16[4,64,1536]{2,1,0:T(8,128)(2,1)}, u32[]{:S(2)}, u32[]{:S(2)}) %collective-permute-start.68) | collective-permute-done | bytes 786464 | tf_op jit(solution)/shard_map/ppermute | solution.py:33
  650.2 10.3 %convolution_convert_fusion = bf16[1536,2304]{1,0:T(8,128)(2,1)S(1)} fusion(bf16[1024,1536]{1,0:T(8,128)(2,1)S(1)} %copy-done.12, bf16[1024,2304]{1,0:T(8,128)(2,1)} %attend_back.1), kind=kOutput, calls=%fused_computation | convolution fusion | flops 7251296256 | bytes 14942208 | tf_op jit(solution)/shard_map/dot_general | solution.py:1250
  660.6 7.7 convolution_convert_fusion.3
  698.1 6.6 collective-permute-done.74
  704.7 7.5 collective-permute-done.75
  712.2 7.6 collective-permute-done.72
  736.3 21.1 %conv_back.1 = (f32[512,1536]{1,0:T(8,128)}, f32[16,1536]{1,0:T(8,128)}, f32[8,1536]{1,0:T(8,128)}) custom-call(s32[1]{0:T(128)} %bitcast.31.words_ref.core_ref, bf16[576,1536]{1,0:T(8,128)(2,1)} %bitcast.311, bf16[576,1536]{1,0:T(8,128)(2,1)} %bitcast.312, bf16[576,1536]{1,0:T(8,128)(2,1)} %collective-permute-done.76.arriving_ref, ...), custom_call_target="tpu_custom_call" | custom-call | flops 55050240 | bytes 11010048 | tf_op jit(solution)/shard_map/conv_back/pallas_call | solution.py:889
  801.0 13.5 %collective-permute-done.86 = bf16[96,2304]{1,0:T(8,128)(2,1)S(1)} collective-permute-done((bf16[96,2304]{1,0:T(8,128)(2,1)S(1)}, bf16[96,2304]{1,0:T(8,128)(2,1)S(1)}, u32[]{:S(2)}, u32[]{:S(2)}) %collective-permute-start.86) | collective-permute-done | bytes 442400 | tf_op jit(solution)/shard_map/ppermute | solution.py:33
  833.9 5.6 collective-permute-done.97
  (631 shorter events, 358.0 us)
Async XLA Ops:
  140.8 51.9 %collective-permute-start.15 = (bf16[8,96,1152]{2,1,0:T(8,128)(2,1)S(1)}, bf16[8,96,1152]{2,1,0:T(8,128)(2,1)}, u32[]{:S(2)}, u32[]{:S(2)}) collective-permute-start(bf16[8,96,1152]{2,1,0:T(8,128)(2,1)S(1)} %pad_maximum_fusion.6.refs_0_), channel_id=1, source_target_pairs={{0,2},{1,3},{2,0},{3,1},{4,6},{5,7},{6,4},{7,5},{8,10},{9,11},{10,... | collective-permute-start | bytes 5308424 | tf_op jit(solution)/shard_map/ppermute | solution.py:33
  141.9 50.8 %collective-permute-start.16 = (bf16[8,96,1152]{2,1,0:T(8,128)(2,1)}, bf16[8,96,1152]{2,1,0:T(8,128)(2,1)}, u32[]{:S(2)}, u32[]{:S(2)}) collective-permute-start(bf16[8,96,1152]{2,1,0:T(8,128)(2,1)} %pad_maximum_fusion.7.refs_0_), channel_id=1, source_target_pairs={{0,4},{1,5},{2,6},{3,7},{4,0},{5,1},{6,2},{7,3},{8,12},{9,13},{10,... | collective-permute-start | bytes 5308424 | tf_op jit(solution)/shard_map/ppermute | solution.py:33
  152.2 40.5 %collective-permute-start.17 = (bf16[4,48,1536]{2,1,0:T(8,128)(2,1)}, bf16[4,48,1536]{2,1,0:T(8,128)(2,1)}, u32[]{:S(2)}, u32[]{:S(2)}) collective-permute-start(bf16[4,48,1536]{2,1,0:T(8,128)(2,1)} %pad_maximum_fusion.23), channel_id=1, source_target_pairs={{0,4},{1,5},{2,6},{3,7},{4,0},{5,1},{6,2},{7,3},{8,12},{9,13},{10,... | collective-permute-start | bytes 1769480 | tf_op jit(solution)/shard_map/ppermute | solution.py:33
  198.3 41.3 %collective-permute-start.27 = (bf16[8,48,1536]{2,1,0:T(8,128)(2,1)S(1)}, bf16[8,48,1536]{2,1,0:T(8,128)(2,1)}, u32[]{:S(2)}, u32[]{:S(2)}) collective-permute-start(bf16[8,48,1536]{2,1,0:T(8,128)(2,1)S(1)} %pad_maximum_fusion.15.refs_0_), channel_id=1, source_target_pairs={{0,2},{1,3},{2,0},{3,1},{4,6},{5,7},{6,4},{7,5},{8,10},{9,11},{10,... | collective-permute-start | bytes 3538952 | tf_op jit(solution)/shard_map/ppermute | solution.py:33
  199.1 35.3 %collective-permute-start.28 = (bf16[4,96,1024]{2,1,0:T(8,128)(2,1)}, bf16[4,96,1024]{2,1,0:T(8,128)(2,1)}, u32[]{:S(2)}, u32[]{:S(2)}) collective-permute-start(bf16[4,96,1024]{2,1,0:T(8,128)(2,1)} %pad_maximum_fusion.19), channel_id=1, source_target_pairs={{0,4},{1,5},{2,6},{3,7},{4,0},{5,1},{6,2},{7,3},{8,12},{9,13},{10,... | collective-permute-start | bytes 2359304 | tf_op jit(solution)/shard_map/ppermute | solution.py:33
  200.3 39.3 %collective-permute-start.29 = (bf16[4,64,1536]{2,1,0:T(8,128)(2,1)}, bf16[4,64,1536]{2,1,0:T(8,128)(2,1)}, u32[]{:S(2)}, u32[]{:S(2)}) collective-permute-start(bf16[4,64,1536]{2,1,0:T(8,128)(2,1)} %pad_maximum_fusion.20), channel_id=1, source_target_pairs={{0,2},{1,3},{2,0},{3,1},{4,6},{5,7},{6,4},{7,5},{8,10},{9,11},{10,... | collective-permute-start | bytes 2359304 | tf_op jit(solution)/shard_map/ppermute | solution.py:33
  202.1 32.3 %collective-permute-start.30 = (bf16[1,96,2048]{2,1,0:T(8,128)(2,1)S(1)}, bf16[1,96,2048]{2,1,0:T(8,128)(2,1)}, u32[]{:S(2)}, u32[]{:S(2)}) collective-permute-start(bf16[1,96,2048]{2,1,0:T(8,128)(2,1)S(1)} %broadcast_in_dim_reshape.9), channel_id=1, source_target_pairs={{0,16},{1,17},{2,18},{3,19},{4,20},{5,21},{6,22},{7,23},{8,24},{9,... | collective-permute-start | bytes 1179656 | tf_op jit(solution)/shard_map/ppermute | solution.py:33
  248.8 33.5 %collective-permute-start.32 = (bf16[8,96,1024]{2,1,0:T(8,128)(2,1)}, bf16[8,96,1024]{2,1,0:T(8,128)(2,1)}, u32[]{:S(2)}, u32[]{:S(2)}) collective-permute-start(bf16[8,96,1024]{2,1,0:T(8,128)(2,1)} %pad_maximum_fusion.8.refs_0_), channel_id=1, source_target_pairs={{0,2},{1,3},{2,0},{3,1},{4,6},{5,7},{6,4},{7,5},{8,10},{9,11},{10,... | collective-permute-start | bytes 4718600 | tf_op jit(solution)/shard_map/ppermute | solution.py:33
  249.4 32.9 %collective-permute-start.33 = (bf16[8,64,1536]{2,1,0:T(8,128)(2,1)}, bf16[8,64,1536]{2,1,0:T(8,128)(2,1)}, u32[]{:S(2)}, u32[]{:S(2)}) collective-permute-start(bf16[8,64,1536]{2,1,0:T(8,128)(2,1)} %pad_maximum_fusion.9.refs_2_), channel_id=1, source_target_pairs={{0,4},{1,5},{2,6},{3,7},{4,0},{5,1},{6,2},{7,3},{8,12},{9,13},{10,... | collective-permute-start | bytes 4718600 | tf_op jit(solution)/shard_map/ppermute | solution.py:33
  324.6 58.9 %collective-permute-start.40 = (bf16[8,96,1024]{2,1,0:T(8,128)(2,1)}, bf16[8,96,1024]{2,1,0:T(8,128)(2,1)}, u32[]{:S(2)}, u32[]{:S(2)}) collective-permute-start(bf16[8,96,1024]{2,1,0:T(8,128)(2,1)} %pad_maximum_fusion.11.refs_0_), channel_id=1, source_target_pairs={{0,2},{1,3},{2,0},{3,1},{4,6},{5,7},{6,4},{7,5},{8,10},{9,11},{10,... | collective-permute-start | bytes 4718600 | tf_op jit(solution)/shard_map/ppermute | solution.py:33
  325.2 58.3 %collective-permute-start.41 = (bf16[8,64,1536]{2,1,0:T(8,128)(2,1)}, bf16[8,64,1536]{2,1,0:T(8,128)(2,1)}, u32[]{:S(2)}, u32[]{:S(2)}) collective-permute-start(bf16[8,64,1536]{2,1,0:T(8,128)(2,1)} %pad_maximum_fusion.12.refs_2_), channel_id=1, source_target_pairs={{0,4},{1,5},{2,6},{3,7},{4,0},{5,1},{6,2},{7,3},{8,12},{9,13},{10,... | collective-permute-start | bytes 4718600 | tf_op jit(solution)/shard_map/ppermute | solution.py:33
  326.5 57.0 %collective-permute-start.42 = (bf16[4,96,1024]{2,1,0:T(8,128)(2,1)}, bf16[4,96,1024]{2,1,0:T(8,128)(2,1)}, u32[]{:S(2)}, u32[]{:S(2)}) collective-permute-start(bf16[4,96,1024]{2,1,0:T(8,128)(2,1)} %get-tuple-element.367), channel_id=1, source_target_pairs={{0,4},{1,5},{2,6},{3,7},{4,0},{5,1},{6,2},{7,3},{8,12},{9,13},{10,... | collective-permute-start | bytes 2359304 | tf_op jit(solution)/shard_map/ppermute | solution.py:33
  327.2 56.3 %collective-permute-start.43 = (bf16[4,64,1536]{2,1,0:T(8,128)(2,1)}, bf16[4,64,1536]{2,1,0:T(8,128)(2,1)}, u32[]{:S(2)}, u32[]{:S(2)}) collective-permute-start(bf16[4,64,1536]{2,1,0:T(8,128)(2,1)} %get-tuple-element.368), channel_id=1, source_target_pairs={{0,2},{1,3},{2,0},{3,1},{4,6},{5,7},{6,4},{7,5},{8,10},{9,11},{10,... | collective-permute-start | bytes 2359304 | tf_op jit(solution)/shard_map/ppermute | solution.py:33
  388.8 71.1 %collective-permute-start.48 = (bf16[2,4,128,1536]{3,2,1,0:T(8,128)(2,1)}, bf16[2,4,128,1536]{3,2,1,0:T(8,128)(2,1)}, u32[]{:S(2)}, u32[]{:S(2)}) collective-permute-start(bf16[2,4,128,1536]{3,2,1,0:T(8,128)(2,1)} %get-tuple-element.393), channel_id=1, source_target_pairs={{0,1},{1,0},{2,3},{3,2},{4,5},{5,4},{6,7},{7,6},{8,9},{9,8},{10,11... | collective-permute-start | bytes 9437192 | tf_op jit(solution)/shard_map/ppermute | solution.py:33
  388.8 58.5 %collective-permute-start.44 = (bf16[8,96,1024]{2,1,0:T(8,128)(2,1)}, bf16[8,96,1024]{2,1,0:T(8,128)(2,1)}, u32[]{:S(2)}, u32[]{:S(2)}) collective-permute-start(bf16[8,96,1024]{2,1,0:T(8,128)(2,1)} %pad_maximum_fusion.13.refs_0_), channel_id=1, source_target_pairs={{0,2},{1,3},{2,0},{3,1},{4,6},{5,7},{6,4},{7,5},{8,10},{9,11},{10,... | collective-permute-start | bytes 4718600 | tf_op jit(solution)/shard_map/ppermute | solution.py:33
  389.4 57.9 %collective-permute-start.45 = (bf16[8,64,1536]{2,1,0:T(8,128)(2,1)}, bf16[8,64,1536]{2,1,0:T(8,128)(2,1)}, u32[]{:S(2)}, u32[]{:S(2)}) collective-permute-start(bf16[8,64,1536]{2,1,0:T(8,128)(2,1)} %pad_maximum_fusion.14.refs_2_), channel_id=1, source_target_pairs={{0,4},{1,5},{2,6},{3,7},{4,0},{5,1},{6,2},{7,3},{8,12},{9,13},{10,... | collective-permute-start | bytes 4718600 | tf_op jit(solution)/shard_map/ppermute | solution.py:33
  390.7 68.9 %collective-permute-start.46 = (bf16[8,96,1024]{2,1,0:T(8,128)(2,1)}, bf16[8,96,1024]{2,1,0:T(8,128)(2,1)}, u32[]{:S(2)}, u32[]{:S(2)}) collective-permute-start(bf16[8,96,1024]{2,1,0:T(8,128)(2,1)} %get-tuple-element.391), channel_id=1, source_target_pairs={{0,2},{1,3},{2,0},{3,1},{4,6},{5,7},{6,4},{7,5},{8,10},{9,11},{10,... | collective-permute-start | bytes 4718600 | tf_op jit(solution)/shard_map/ppermute | solution.py:33
  392.5 67.5 %collective-permute-start.47 = (bf16[8,64,1536]{2,1,0:T(8,128)(2,1)}, bf16[8,64,1536]{2,1,0:T(8,128)(2,1)}, u32[]{:S(2)}, u32[]{:S(2)}) collective-permute-start(bf16[8,64,1536]{2,1,0:T(8,128)(2,1)} %get-tuple-element.392), channel_id=1, source_target_pairs={{0,4},{1,5},{2,6},{3,7},{4,0},{5,1},{6,2},{7,3},{8,12},{9,13},{10,... | collective-permute-start | bytes 4718600 | tf_op jit(solution)/shard_map/ppermute | solution.py:33
  466.7 58.7 %collective-permute-start.53 = (bf16[2,4,128,1536]{3,2,1,0:T(8,128)(2,1)}, bf16[2,4,128,1536]{3,2,1,0:T(8,128)(2,1)}, u32[]{:S(2)}, u32[]{:S(2)}) collective-permute-start(bf16[2,4,128,1536]{3,2,1,0:T(8,128)(2,1)} %get-tuple-element.415), channel_id=1, source_target_pairs={{0,1},{1,0},{2,3},{3,2},{4,5},{5,4},{6,7},{7,6},{8,9},{9,8},{10,11... | collective-permute-start | bytes 9437192 | tf_op jit(solution)/shard_map/ppermute | solution.py:33
  466.7 58.6 %collective-permute-start.49 = (bf16[4,96,1024]{2,1,0:T(8,128)(2,1)}, bf16[4,96,1024]{2,1,0:T(8,128)(2,1)}, u32[]{:S(2)}, u32[]{:S(2)}) collective-permute-start(bf16[4,96,1024]{2,1,0:T(8,128)(2,1)} %get-tuple-element.411), channel_id=1, source_target_pairs={{0,4},{1,5},{2,6},{3,7},{4,0},{5,1},{6,2},{7,3},{8,12},{9,13},{10,... | collective-permute-start | bytes 2359304 | tf_op jit(solution)/shard_map/ppermute | solution.py:33
  468.1 57.3 %collective-permute-start.50 = (bf16[4,64,1536]{2,1,0:T(8,128)(2,1)}, bf16[4,64,1536]{2,1,0:T(8,128)(2,1)}, u32[]{:S(2)}, u32[]{:S(2)}) collective-permute-start(bf16[4,64,1536]{2,1,0:T(8,128)(2,1)} %get-tuple-element.412), channel_id=1, source_target_pairs={{0,2},{1,3},{2,0},{3,1},{4,6},{5,7},{6,4},{7,5},{8,10},{9,11},{10,... | collective-permute-start | bytes 2359304 | tf_op jit(solution)/shard_map/ppermute | solution.py:33
  469.8 55.6 %collective-permute-start.51 = (bf16[8,96,1024]{2,1,0:T(8,128)(2,1)}, bf16[8,96,1024]{2,1,0:T(8,128)(2,1)}, u32[]{:S(2)}, u32[]{:S(2)}) collective-permute-start(bf16[8,96,1024]{2,1,0:T(8,128)(2,1)} %get-tuple-element.413), channel_id=1, source_target_pairs={{0,2},{1,3},{2,0},{3,1},{4,6},{5,7},{6,4},{7,5},{8,10},{9,11},{10,... | collective-permute-start | bytes 4718600 | tf_op jit(solution)/shard_map/ppermute | solution.py:33
  470.1 55.3 %collective-permute-start.52 = (bf16[8,64,1536]{2,1,0:T(8,128)(2,1)}, bf16[8,64,1536]{2,1,0:T(8,128)(2,1)}, u32[]{:S(2)}, u32[]{:S(2)}) collective-permute-start(bf16[8,64,1536]{2,1,0:T(8,128)(2,1)} %get-tuple-element.414), channel_id=1, source_target_pairs={{0,4},{1,5},{2,6},{3,7},{4,0},{5,1},{6,2},{7,3},{8,12},{9,13},{10,... | collective-permute-start | bytes 4718600 | tf_op jit(solution)/shard_map/ppermute | solution.py:33
  528.7 37.1 %collective-permute-start.56 = (bf16[8,96,1024]{2,1,0:T(8,128)(2,1)}, bf16[8,96,1024]{2,1,0:T(8,128)(2,1)}, u32[]{:S(2)}, u32[]{:S(2)}) collective-permute-start(bf16[8,96,1024]{2,1,0:T(8,128)(2,1)} %get-tuple-element.433), channel_id=1, source_target_pairs={{0,2},{1,3},{2,0},{3,1},{4,6},{5,7},{6,4},{7,5},{8,10},{9,11},{10,... | collective-permute-start | bytes 4718600 | tf_op jit(solution)/shard_map/ppermute | solution.py:33
  530.3 36.7 %collective-permute-start.57 = (bf16[8,64,1536]{2,1,0:T(8,128)(2,1)}, bf16[8,64,1536]{2,1,0:T(8,128)(2,1)}, u32[]{:S(2)}, u32[]{:S(2)}) collective-permute-start(bf16[8,64,1536]{2,1,0:T(8,128)(2,1)} %get-tuple-element.434), channel_id=1, source_target_pairs={{0,4},{1,5},{2,6},{3,7},{4,0},{5,1},{6,2},{7,3},{8,12},{9,13},{10,... | collective-permute-start | bytes 4718600 | tf_op jit(solution)/shard_map/ppermute | solution.py:33
  599.0 43.9 %collective-permute-start.64 = (bf16[2,2,2,48,1536]{4,3,1,0,2:T(8,128)(2,1)}, bf16[2,2,2,48,1536]{4,3,1,0,2:T(8,128)(2,1)}, u32[]{:S(2)}, u32[]{:S(2)}) collective-permute-start(bf16[2,2,2,48,1536]{4,3,1,0,2:T(8,128)(2,1)} %copy_bitcast_fusion.2), channel_id=1, source_target_pairs={{0,2},{1,3},{2,0},{3,1},{4,6},{5,7},{6,4},{7,5},{8,10},{9,11},{10,... | collective-permute-start | bytes 3538952 | tf_op jit(solution)/shard_map/ppermute | solution.py:33
  599.4 33.1 %collective-permute-start.67 = (bf16[4,96,1024]{2,1,0:T(8,128)(2,1)}, bf16[4,96,1024]{2,1,0:T(8,128)(2,1)S(1)}, u32[]{:S(2)}, u32[]{:S(2)}) collective-permute-start(bf16[4,96,1024]{2,1,0:T(8,128)(2,1)} %get-tuple-element.473), channel_id=1, source_target_pairs={{0,4},{1,5},{2,6},{3,7},{4,0},{5,1},{6,2},{7,3},{8,12},{9,13},{10,... | collective-permute-start | bytes 2359304 | tf_op jit(solution)/shard_map/ppermute | solution.py:33
  600.1 42.7 %collective-permute-start.68 = (bf16[4,64,1536]{2,1,0:T(8,128)(2,1)}, bf16[4,64,1536]{2,1,0:T(8,128)(2,1)}, u32[]{:S(2)}, u32[]{:S(2)}) collective-permute-start(bf16[4,64,1536]{2,1,0:T(8,128)(2,1)} %get-tuple-element.474), channel_id=1, source_target_pairs={{0,2},{1,3},{2,0},{3,1},{4,6},{5,7},{6,4},{7,5},{8,10},{9,11},{10,... | collective-permute-start | bytes 2359304 | tf_op jit(solution)/shard_map/ppermute | solution.py:33
  670.5 41.8 %collective-permute-start.76 = (bf16[576,1536]{1,0:T(8,128)(2,1)}, bf16[576,1536]{1,0:T(8,128)(2,1)}, u32[]{:S(2)}, u32[]{:S(2)}) collective-permute-start(bf16[576,1536]{1,0:T(8,128)(2,1)} %bitcast.55), channel_id=1, source_target_pairs={{0,1},{1,0},{2,3},{3,2},{4,5},{5,4},{6,7},{7,6},{8,9},{9,8},{10,11... | collective-permute-start | bytes 5308424 | tf_op jit(solution)/shard_map/ppermute | solution.py:33
  678.6 41.3 %collective-permute-start.72 = (bf16[2,2,2,96,1152]{4,3,0,1,2:T(8,128)(2,1)}, bf16[2,2,2,96,1152]{4,3,0,1,2:T(8,128)(2,1)}, u32[]{:S(2)}, u32[]{:S(2)}) collective-permute-start(bf16[2,2,2,96,1152]{4,3,0,1,2:T(8,128)(2,1)} %copy_bitcast_fusion.1), channel_id=1, source_target_pairs={{0,2},{1,3},{2,0},{3,1},{4,6},{5,7},{6,4},{7,5},{8,10},{9,11},{10,... | collective-permute-start | bytes 5308424 | tf_op jit(solution)/shard_map/ppermute | solution.py:33
  679.4 41.0 %collective-permute-start.73 = (bf16[2,2,2,96,1152]{4,3,0,1,2:T(8,128)(2,1)}, bf16[2,2,2,96,1152]{4,3,0,1,2:T(8,128)(2,1)}, u32[]{:S(2)}, u32[]{:S(2)}) collective-permute-start(bf16[2,2,2,96,1152]{4,3,0,1,2:T(8,128)(2,1)} %copy_bitcast_fusion), channel_id=1, source_target_pairs={{0,4},{1,5},{2,6},{3,7},{4,0},{5,1},{6,2},{7,3},{8,12},{9,13},{10,... | collective-permute-start | bytes 5308424 | tf_op jit(solution)/shard_map/ppermute | solution.py:33
  727.2 32.7 %collective-permute-start.77 = (bf16[2,2,96,1152]{3,2,0,1:T(8,128)(2,1)}, bf16[2,2,96,1152]{3,2,0,1:T(8,128)(2,1)}, u32[]{:S(2)}, u32[]{:S(2)}) collective-permute-start(bf16[2,2,96,1152]{3,2,0,1:T(8,128)(2,1)} %fusion.4), channel_id=1, source_target_pairs={{0,4},{1,5},{2,6},{3,7},{4,0},{5,1},{6,2},{7,3},{8,12},{9,13},{10,... | collective-permute-start | bytes 2654216 | tf_op jit(solution)/shard_map/ppermute | solution.py:33
  (178 other events, 2146.6 us)

commit v11 on v10

--- a/solution.py
+++ b/solution.py
@@ -1088,19 +1088,18 @@
     ]
     mods_flow = scatter_flow([mods_part], chip, chip_bits, sent=full)
     qkv_near = near(qkv_rows)
-    mine, upstream = slot(
-        [qkv_near, mods_flow],
-        lambda: (to_phases(tokens[0], half_rows), to_phases(cotangent[0], half_rows)),
-    )
-
-    up_weight, proj_weight, ffn_kernel, attn_kernel = slot.after(
-        up_weight, proj_weight, ffn_kernel, attn_kernel
-    )
+    proj_there = [(r, r % chips * 2 + r // chips) for r in range(devices)]
+    proj_back = [(b, a) for a, b in proj_there]
+
+    def first_work():
+        phases = [to_phases(array[0], half_rows) for array in (tokens, cotangent)]
+        return *phases, lax.ppermute(proj_weight, AXES, proj_there)
+
+    mine, upstream, proj_rows = slot([qkv_near, mods_flow], first_work)
+
+    up_weight, ffn_kernel, attn_kernel = slot.after(up_weight, ffn_kernel, attn_kernel)
     up_split = up_weight.reshape(part, chips, 2, CHUNKS, piece).transpose(0, 2, 3, 1, 4)
     up_rows = row_pair(up_split.reshape(part, 2, CHUNKS, chips * piece), 1)
-    proj_there = [(r, r % chips * 2 + r // chips) for r in range(devices)]
-    proj_back = [(b, a) for a, b in proj_there]
-    proj_rows = lax.ppermute(proj_weight, AXES, proj_there)
     proj_flow = Flow(one_colour_steps(proj_rows, chip_bits))
     canvas = slot(
         [qkv_near, mods_flow, proj_flow], lambda: join_halves(mine, swap_core(mine), core)
@@ -1298,7 +1297,7 @@
         axis=1,
     )
     tap_flow = scatter_flow([tap_parts], chip, chip_bits, sent=full)
-    up_shares = [flows[0].result for flows in back_flows]
+    up_shares = slot.after(*[flows[0].result for flows in back_flows])
     down_shares = [flows[1].result for flows in back_flows]
 
     def split_up():

time: 856 us -> 837 us (0.978)
  waiting for transfers between devices: 165 us -> 155 us
    ppermute x96, waiting for transfers between devices: 165 us -> 155 us  [swap(): lax.ppermute(x, AXES, [(i, i ^ 1 << bit) for i in range(device_count())])]
  transfers between devices with their start and end apart: 98 -> 98, of which waited for: 31 -> 30; matrix products, arithmetic and copies ran while one was open for 21% -> 21% of each run, Pallas kernels for 36% -> 36%
where the time goes in v11:
time: 837 us; the launch traced here: 830 us
  Pallas kernels  301 us (36%)
  waiting for transfers between devices  155 us (19%)
  other arithmetic  123 us (15%)
  starting transfers between devices  108 us (13%)
  local copies, waits for them, and re-layouts  91.3 us (11%)
  matrix products  48.9 us (6%)
    pallas_call x3, Pallas kernels, feed_forward(): pl.pallas_call(functools.partial(feed_body, spread), grid_spec=pltpu.Pref...  164 us
    ppermute x96, waiting for transfers between devices, swap(): lax.ppermute(x, AXES, [(i, i ^ 1 << bit) for i in range(device_count())])  155 us
    ppermute x96, starting transfers between devices, swap(): lax.ppermute(x, AXES, [(i, i ^ 1 << bit) for i in range(device_count())])  102 us
    concatenate x17, other arithmetic, join(): return [jnp.concatenate(pair, axis=0) for pair in zip(held, arriving)]  32.4 us
    convert_element_type x18, other arithmetic, halving_steps(): (staying[at].astype(full) + arriving[at].astype(full)).astype(low)  32.2 us
    pallas_call x1, Pallas kernels, attend_back(): pl.pallas_call(attend_back_body, grid=(pairs,), in_specs=[pl.BlockSpec((P...  28.9 us
    pallas_call x1, Pallas kernels, conv_in(): pl.pallas_call(conv_in_body, grid=(model // TILE,), in_specs=[pl.BlockSpe...  23.1 us
    pallas_call x1, Pallas kernels, conv_back(): pl.pallas_call(conv_back_body, grid_spec=pltpu.PrefetchScalarGridSpec(num...  21.1 us
  transfers between devices with their start and end apart: 98, of which 30 were waited for; matrix products, arithmetic and copies ran while one was open for 21% of the time, Pallas kernels for 36%

profile of v11, /device:TPU:0, one launch (start us, length us, event | category | flops | bytes accessed | tf_op | source)
XLA Modules:
  0.0 830.4 jit_solution(13796405282089558406)
XLA Ops:
  27.0 5.1 collective-permute-done.1
  61.9 11.1 %collective-permute-done.7 = bf16[1,48,1536]{2,1,0:T(8,128)(2,1)S(1)} collective-permute-done((bf16[1,48,1536]{2,1,0:T(8,128)(2,1)S(1)}, bf16[1,48,1536]{2,1,0:T(8,128)(2,1)S(1)}, u32[]{:S(2)}, u32[]{:S(2)}) %collective-permute-start.7) | collective-permute-done | bytes 147488 | tf_op jit(solution)/shard_map/ppermute | solution.py:33
  100.9 7.7 collective-permute-done.13
  124.0 4.6 collective-permute-done.25
  134.3 23.1 %conv_in.1 = bf16[1024,1536]{1,0:T(8,128)(2,1)} custom-call(bf16[1024,1536]{1,0:T(8,128)(2,1)} %bitcast.297, f32[16,1536]{1,0:T(8,128)} %pad_convert_fusion.1.kernel_ref, f32[8,1536]{1,0:T(8,128)} %maximum_maximum_fusion.mods_ref), custom_call_target="tpu_custom_call" | custom-call | flops 47185920 | bytes 6291456 | tf_op jit(solution)/shard_map/conv_in/pallas_call | solution.py:731
  157.5 13.8 %collective-permute-done.17 = bf16[4,48,1536]{2,1,0:T(8,128)(2,1)} collective-permute-done((bf16[4,48,1536]{2,1,0:T(8,128)(2,1)}, bf16[4,48,1536]{2,1,0:T(8,128)(2,1)}, u32[]{:S(2)}, u32[]{:S(2)}) %collective-permute-start.17) | collective-permute-done | bytes 589856 | tf_op jit(solution)/shard_map/ppermute | solution.py:33
  183.6 5.6 assemble.4
  189.2 5.7 assemble.3
  194.9 12.7 %convolution_convert_fusion.2.qkv_ref = bf16[1024,2304]{1,0:T(8,128)(2,1)} fusion(bf16[1024,1536]{1,0:T(8,128)(2,1)} %conv_in.1, bf16[1536,1152]{1,0:T(8,128)(2,1)} %bitcast.303, bf16[1536,1152]{1,0:T(8,128)(2,1)} %bitcast.305), kind=kOutput, calls=%fused_computation.3 | convolution fusion | flops 7264272384 | bytes 14942208 | tf_op jit(solution)/shard_map/dot_general | solution.py:1156
  207.6 5.4 pad_maximum_fusion
  233.9 4.9 assemble.5
  238.8 15.4 %attend.1 = bf16[1024,768]{1,0:T(8,128)(2,1)} custom-call(f32[256,256]{1,0:T(8,128)} %compare_convert_fusion.mask_ref, bf16[1024,2304]{1,0:T(8,128)(2,1)} %convolution_convert_fusion.2.qkv_ref), custom_call_target="tpu_custom_call" | custom-call | flops 3221225472 | bytes 6291456 | tf_op jit(solution)/shard_map/attend/pallas_call | solution.py:365
  254.2 6.8 collective-permute-done.35
  261.0 6.4 convolution_convert_fusion.4.part_ref
  284.1 17.6 %enter_feed.1 = (bf16[1024,1536]{1,0:T(8,128)(2,1)}, bf16[1536,1024]{1,0:T(8,128)(2,1)}, bf16[1024,1536]{1,0:T(8,128)(2,1)}) custom-call(bf16[1024,1536]{1,0:T(8,128)(2,1)} %bitcast.298, bf16[1024,1536]{1,0:T(8,128)(2,1)} %convolution_convert_fusion.4.part_ref, bf16[1024,1536]{1,0:T(8,128)(2,1)} %collective-permute-done.38.other_ref, ...), custom_call_target="tpu_custom_call" | custom-call | flops 1000 | bytes 1000 | tf_op jit(solution)/shard_map/enter_feed/pallas_call | solution.py:956
  310.8 54.7 %feed_forward.3 = (bf16[2,4,128,1536]{3,2,1,0:T(8,128)(2,1)}, bf16[2,4,128,1536]{3,2,1,0:T(8,128)(2,1)}, bf16[8,96,1024]{2,1,0:T(8,128)(2,1)}, bf16[8,96,1024]{2...) custom-call(s32[49]{0:T(128)} %pad_add_fusion.1.words_ref, ...), custom_call_target="tpu_custom_call" | custom-call | flops 19327352832 | bytes 28311552 | tf_op jit(solution)/shard_map/feed_forward/pallas_call | solution.py:623
  374.9 54.5 %feed_forward.4 = (bf16[2,4,128,1536]{3,2,1,0:T(8,128)(2,1)}, bf16[2,4,128,1536]{3,2,1,0:T(8,128)(2,1)}, bf16[8,96,1024]{2,1,0:T(8,128)(2,1)}, bf16[8,96,1024]{2...) custom-call(s32[49]{0:T(128)} %pad_add_fusion.1.words_ref, ...), custom_call_target="tpu_custom_call" | custom-call | flops 19327352832 | bytes 28311552 | tf_op jit(solution)/shard_map/feed_forward/pallas_call | solution.py:623
  429.4 12.3 %collective-permute-done.46 = bf16[8,96,1024]{2,1,0:T(8,128)(2,1)} collective-permute-done((bf16[8,96,1024]{2,1,0:T(8,128)(2,1)}, bf16[8,96,1024]{2,1,0:T(8,128)(2,1)}, u32[]{:S(2)}, u32[]{:S(2)}) %collective-permute-start.46) | collective-permute-done | bytes 1572896 | tf_op jit(solution)/shard_map/ppermute | solution.py:33
  453.3 54.5 %feed_forward.5 = (bf16[2,4,128,1536]{3,2,1,0:T(8,128)(2,1)}, bf16[2,4,128,1536]{3,2,1,0:T(8,128)(2,1)}, bf16[8,96,1024]{2,1,0:T(8,128)(2,1)}, bf16[8,96,1024]{2...) custom-call(s32[49]{0:T(128)} %pad_add_fusion.1.words_ref, ...), custom_call_target="tpu_custom_call" | custom-call | flops 19327352832 | bytes 28311552 | tf_op jit(solution)/shard_map/feed_forward/pallas_call | solution.py:623
  518.7 15.4 %leave_feed.1 = (bf16[512,1536]{1,0:T(8,128)(2,1)}, f32[512,1536]{1,0:T(8,128)}, bf16[512,1536]{1,0:T(8,128)(2,1)}, f32[8,1536]{1,0:T(8,128)}) custom-call(s32[1]{0:T(128)} %bitcast.31.words_ref.core_ref, bf16[1024,1536]{1,0:T(8,128)(2,1)} %bitcast.299, bf16[1024,1536]{1,0:T(8,128)(2,1)} %convolution_convert_fusion.4.part_ref, ...), custom_call_target="tpu_custom_call" | custom-call | flops 1000 | bytes 1000 | tf_op jit(solution)/shard_map/leave_feed/pallas_call | solution.py:1012
  534.2 14.2 %collective-permute-done.56 = bf16[8,96,1024]{2,1,0:T(8,128)(2,1)} collective-permute-done((bf16[8,96,1024]{2,1,0:T(8,128)(2,1)}, bf16[8,96,1024]{2,1,0:T(8,128)(2,1)}, u32[]{:S(2)}, u32[]{:S(2)}) %collective-permute-start.56) | collective-permute-done | bytes 1572896 | tf_op jit(solution)/shard_map/ppermute | solution.py:33
  586.3 28.9 %attend_back.1 = bf16[1024,2304]{1,0:T(8,128)(2,1)} custom-call(f32[256,256]{1,0:T(8,128)} %compare_convert_fusion.mask_ref, bf16[1024,2304]{1,0:T(8,128)(2,1)} %convolution_convert_fusion.2.qkv_ref, bf16[1024,768]{1,0:T(8,128)(2,1)} %convolution_convert_fusion.7.grad_ref), custom_call_target="tpu_custom_call" | custom-call | flops 8053063680 | bytes 11010048 | tf_op jit(solution)/shard_map/attend_back/pallas_call | solution.py:386
  615.3 10.4 %collective-permute-done.68 = bf16[4,64,1536]{2,1,0:T(8,128)(2,1)} collective-permute-done((bf16[4,64,1536]{2,1,0:T(8,128)(2,1)}, bf16[4,64,1536]{2,1,0:T(8,128)(2,1)}, u32[]{:S(2)}, u32[]{:S(2)}) %collective-permute-start.68) | collective-permute-done | bytes 786464 | tf_op jit(solution)/shard_map/ppermute | solution.py:33
  633.3 10.3 %convolution_convert_fusion = bf16[1536,2304]{1,0:T(8,128)(2,1)S(1)} fusion(bf16[1024,1536]{1,0:T(8,128)(2,1)S(1)} %copy-done.13, bf16[1024,2304]{1,0:T(8,128)(2,1)} %attend_back.1), kind=kOutput, calls=%fused_computation | convolution fusion | flops 7251296256 | bytes 14942208 | tf_op jit(solution)/shard_map/dot_general | solution.py:1249
  643.7 7.7 convolution_convert_fusion.3
  679.9 8.0 collective-permute-done.74
  687.9 7.3 collective-permute-done.75
  695.2 7.7 collective-permute-done.72
  720.5 21.1 %conv_back.1 = (f32[512,1536]{1,0:T(8,128)}, f32[16,1536]{1,0:T(8,128)}, f32[8,1536]{1,0:T(8,128)}) custom-call(s32[1]{0:T(128)} %bitcast.31.words_ref.core_ref, bf16[576,1536]{1,0:T(8,128)(2,1)} %bitcast.317, bf16[576,1536]{1,0:T(8,128)(2,1)} %bitcast.318, bf16[576,1536]{1,0:T(8,128)(2,1)} %collective-permute-done.76.arriving_ref, ...), custom_call_target="tpu_custom_call" | custom-call | flops 55050240 | bytes 11010048 | tf_op jit(solution)/shard_map/conv_back/pallas_call | solution.py:889
  767.0 4.6 reshape.340
  783.7 15.1 %collective-permute-done.86 = bf16[96,2304]{1,0:T(8,128)(2,1)S(1)} collective-permute-done((bf16[96,2304]{1,0:T(8,128)(2,1)S(1)}, bf16[96,2304]{1,0:T(8,128)(2,1)S(1)}, u32[]{:S(2)}, u32[]{:S(2)}) %collective-permute-start.86) | collective-permute-done | bytes 442400 | tf_op jit(solution)/shard_map/ppermute | solution.py:33
  817.9 5.6 collective-permute-done.97
  (635 shorter events, 349.2 us)
Async XLA Ops:
  76.5 34.3 %collective-permute-start.9 = (bf16[4,96,1152]{2,1,0:T(8,128)(2,1)S(1)}, bf16[4,96,1152]{2,1,0:T(8,128)(2,1)}, u32[]{:S(2)}, u32[]{:S(2)}) collective-permute-start(bf16[4,96,1152]{2,1,0:T(8,128)(2,1)S(1)} %get-tuple-element.304), channel_id=1, source_target_pairs={{0,4},{1,5},{2,6},{3,7},{4,0},{5,1},{6,2},{7,3},{8,12},{9,13},{10,... | collective-permute-start | bytes 2654216 | tf_op jit(solution)/shard_map/ppermute | solution.py:33
  78.0 33.4 %collective-permute-start.10 = (bf16[4,96,1152]{2,1,0:T(8,128)(2,1)S(1)}, bf16[4,96,1152]{2,1,0:T(8,128)(2,1)}, u32[]{:S(2)}, u32[]{:S(2)}) collective-permute-start(bf16[4,96,1152]{2,1,0:T(8,128)(2,1)S(1)} %get-tuple-element.305), channel_id=1, source_target_pairs={{0,2},{1,3},{2,0},{3,1},{4,6},{5,7},{6,4},{7,5},{8,10},{9,11},{10,... | collective-permute-start | bytes 2654216 | tf_op jit(solution)/shard_map/ppermute | solution.py:33
  119.9 51.4 %collective-permute-start.15 = (bf16[8,96,1152]{2,1,0:T(8,128)(2,1)S(1)}, bf16[8,96,1152]{2,1,0:T(8,128)(2,1)}, u32[]{:S(2)}, u32[]{:S(2)}) collective-permute-start(bf16[8,96,1152]{2,1,0:T(8,128)(2,1)S(1)} %pad_maximum_fusion.6.refs_0_), channel_id=1, source_target_pairs={{0,2},{1,3},{2,0},{3,1},{4,6},{5,7},{6,4},{7,5},{8,10},{9,11},{10,... | collective-permute-start | bytes 5308424 | tf_op jit(solution)/shard_map/ppermute | solution.py:33
  120.6 50.7 %collective-permute-start.16 = (bf16[8,96,1152]{2,1,0:T(8,128)(2,1)}, bf16[8,96,1152]{2,1,0:T(8,128)(2,1)}, u32[]{:S(2)}, u32[]{:S(2)}) collective-permute-start(bf16[8,96,1152]{2,1,0:T(8,128)(2,1)} %pad_maximum_fusion.7.refs_0_), channel_id=1, source_target_pairs={{0,4},{1,5},{2,6},{3,7},{4,0},{5,1},{6,2},{7,3},{8,12},{9,13},{10,... | collective-permute-start | bytes 5308424 | tf_op jit(solution)/shard_map/ppermute | solution.py:33
  131.1 40.2 %collective-permute-start.17 = (bf16[4,48,1536]{2,1,0:T(8,128)(2,1)}, bf16[4,48,1536]{2,1,0:T(8,128)(2,1)}, u32[]{:S(2)}, u32[]{:S(2)}) collective-permute-start(bf16[4,48,1536]{2,1,0:T(8,128)(2,1)} %pad_maximum_fusion.23), channel_id=1, source_target_pairs={{0,4},{1,5},{2,6},{3,7},{4,0},{5,1},{6,2},{7,3},{8,12},{9,13},{10,... | collective-permute-start | bytes 1769480 | tf_op jit(solution)/shard_map/ppermute | solution.py:33
  176.9 41.2 %collective-permute-start.27 = (bf16[8,48,1536]{2,1,0:T(8,128)(2,1)S(1)}, bf16[8,48,1536]{2,1,0:T(8,128)(2,1)}, u32[]{:S(2)}, u32[]{:S(2)}) collective-permute-start(bf16[8,48,1536]{2,1,0:T(8,128)(2,1)S(1)} %pad_maximum_fusion.15.refs_0_), channel_id=1, source_target_pairs={{0,2},{1,3},{2,0},{3,1},{4,6},{5,7},{6,4},{7,5},{8,10},{9,11},{10,... | collective-permute-start | bytes 3538952 | tf_op jit(solution)/shard_map/ppermute | solution.py:33
  178.1 35.5 %collective-permute-start.28 = (bf16[4,96,1024]{2,1,0:T(8,128)(2,1)}, bf16[4,96,1024]{2,1,0:T(8,128)(2,1)}, u32[]{:S(2)}, u32[]{:S(2)}) collective-permute-start(bf16[4,96,1024]{2,1,0:T(8,128)(2,1)} %pad_maximum_fusion.19), channel_id=1, source_target_pairs={{0,4},{1,5},{2,6},{3,7},{4,0},{5,1},{6,2},{7,3},{8,12},{9,13},{10,... | collective-permute-start | bytes 2359304 | tf_op jit(solution)/shard_map/ppermute | solution.py:33
  179.2 38.9 %collective-permute-start.29 = (bf16[4,64,1536]{2,1,0:T(8,128)(2,1)}, bf16[4,64,1536]{2,1,0:T(8,128)(2,1)}, u32[]{:S(2)}, u32[]{:S(2)}) collective-permute-start(bf16[4,64,1536]{2,1,0:T(8,128)(2,1)} %pad_maximum_fusion.20), channel_id=1, source_target_pairs={{0,2},{1,3},{2,0},{3,1},{4,6},{5,7},{6,4},{7,5},{8,10},{9,11},{10,... | collective-permute-start | bytes 2359304 | tf_op jit(solution)/shard_map/ppermute | solution.py:33
  226.7 34.3 %collective-permute-start.32 = (bf16[8,96,1024]{2,1,0:T(8,128)(2,1)S(1)}, bf16[8,96,1024]{2,1,0:T(8,128)(2,1)}, u32[]{:S(2)}, u32[]{:S(2)}) collective-permute-start(bf16[8,96,1024]{2,1,0:T(8,128)(2,1)S(1)} %pad_maximum_fusion.8.refs_0_), channel_id=1, source_target_pairs={{0,2},{1,3},{2,0},{3,1},{4,6},{5,7},{6,4},{7,5},{8,10},{9,11},{10,... | collective-permute-start | bytes 4718600 | tf_op jit(solution)/shard_map/ppermute | solution.py:33
  227.9 33.2 %collective-permute-start.33 = (bf16[8,64,1536]{2,1,0:T(8,128)(2,1)}, bf16[8,64,1536]{2,1,0:T(8,128)(2,1)}, u32[]{:S(2)}, u32[]{:S(2)}) collective-permute-start(bf16[8,64,1536]{2,1,0:T(8,128)(2,1)} %pad_maximum_fusion.9.refs_2_), channel_id=1, source_target_pairs={{0,4},{1,5},{2,6},{3,7},{4,0},{5,1},{6,2},{7,3},{8,12},{9,13},{10,... | collective-permute-start | bytes 4718600 | tf_op jit(solution)/shard_map/ppermute | solution.py:33
  306.8 58.8 %collective-permute-start.40 = (bf16[8,96,1024]{2,1,0:T(8,128)(2,1)}, bf16[8,96,1024]{2,1,0:T(8,128)(2,1)}, u32[]{:S(2)}, u32[]{:S(2)}) collective-permute-start(bf16[8,96,1024]{2,1,0:T(8,128)(2,1)} %pad_maximum_fusion.11.refs_0_), channel_id=1, source_target_pairs={{0,2},{1,3},{2,0},{3,1},{4,6},{5,7},{6,4},{7,5},{8,10},{9,11},{10,... | collective-permute-start | bytes 4718600 | tf_op jit(solution)/shard_map/ppermute | solution.py:33
  307.8 57.7 %collective-permute-start.41 = (bf16[8,64,1536]{2,1,0:T(8,128)(2,1)}, bf16[8,64,1536]{2,1,0:T(8,128)(2,1)}, u32[]{:S(2)}, u32[]{:S(2)}) collective-permute-start(bf16[8,64,1536]{2,1,0:T(8,128)(2,1)} %pad_maximum_fusion.12.refs_2_), channel_id=1, source_target_pairs={{0,4},{1,5},{2,6},{3,7},{4,0},{5,1},{6,2},{7,3},{8,12},{9,13},{10,... | collective-permute-start | bytes 4718600 | tf_op jit(solution)/shard_map/ppermute | solution.py:33
  309.1 56.4 %collective-permute-start.42 = (bf16[4,96,1024]{2,1,0:T(8,128)(2,1)}, bf16[4,96,1024]{2,1,0:T(8,128)(2,1)}, u32[]{:S(2)}, u32[]{:S(2)}) collective-permute-start(bf16[4,96,1024]{2,1,0:T(8,128)(2,1)} %get-tuple-element.371), channel_id=1, source_target_pairs={{0,4},{1,5},{2,6},{3,7},{4,0},{5,1},{6,2},{7,3},{8,12},{9,13},{10,... | collective-permute-start | bytes 2359304 | tf_op jit(solution)/shard_map/ppermute | solution.py:33
  309.8 55.7 %collective-permute-start.43 = (bf16[4,64,1536]{2,1,0:T(8,128)(2,1)}, bf16[4,64,1536]{2,1,0:T(8,128)(2,1)}, u32[]{:S(2)}, u32[]{:S(2)}) collective-permute-start(bf16[4,64,1536]{2,1,0:T(8,128)(2,1)} %get-tuple-element.372), channel_id=1, source_target_pairs={{0,2},{1,3},{2,0},{3,1},{4,6},{5,7},{6,4},{7,5},{8,10},{9,11},{10,... | collective-permute-start | bytes 2359304 | tf_op jit(solution)/shard_map/ppermute | solution.py:33
  370.9 71.6 %collective-permute-start.48 = (bf16[2,4,128,1536]{3,2,1,0:T(8,128)(2,1)}, bf16[2,4,128,1536]{3,2,1,0:T(8,128)(2,1)}, u32[]{:S(2)}, u32[]{:S(2)}) collective-permute-start(bf16[2,4,128,1536]{3,2,1,0:T(8,128)(2,1)} %get-tuple-element.397), channel_id=1, source_target_pairs={{0,1},{1,0},{2,3},{3,2},{4,5},{5,4},{6,7},{7,6},{8,9},{9,8},{10,11... | collective-permute-start | bytes 9437192 | tf_op jit(solution)/shard_map/ppermute | solution.py:33
  370.9 58.5 %collective-permute-start.44 = (bf16[8,96,1024]{2,1,0:T(8,128)(2,1)}, bf16[8,96,1024]{2,1,0:T(8,128)(2,1)}, u32[]{:S(2)}, u32[]{:S(2)}) collective-permute-start(bf16[8,96,1024]{2,1,0:T(8,128)(2,1)} %pad_maximum_fusion.13.refs_0_), channel_id=1, source_target_pairs={{0,2},{1,3},{2,0},{3,1},{4,6},{5,7},{6,4},{7,5},{8,10},{9,11},{10,... | collective-permute-start | bytes 4718600 | tf_op jit(solution)/shard_map/ppermute | solution.py:33
  371.9 57.5 %collective-permute-start.45 = (bf16[8,64,1536]{2,1,0:T(8,128)(2,1)}, bf16[8,64,1536]{2,1,0:T(8,128)(2,1)}, u32[]{:S(2)}, u32[]{:S(2)}) collective-permute-start(bf16[8,64,1536]{2,1,0:T(8,128)(2,1)} %pad_maximum_fusion.14.refs_2_), channel_id=1, source_target_pairs={{0,4},{1,5},{2,6},{3,7},{4,0},{5,1},{6,2},{7,3},{8,12},{9,13},{10,... | collective-permute-start | bytes 4718600 | tf_op jit(solution)/shard_map/ppermute | solution.py:33
  373.2 68.5 %collective-permute-start.46 = (bf16[8,96,1024]{2,1,0:T(8,128)(2,1)}, bf16[8,96,1024]{2,1,0:T(8,128)(2,1)}, u32[]{:S(2)}, u32[]{:S(2)}) collective-permute-start(bf16[8,96,1024]{2,1,0:T(8,128)(2,1)} %get-tuple-element.395), channel_id=1, source_target_pairs={{0,2},{1,3},{2,0},{3,1},{4,6},{5,7},{6,4},{7,5},{8,10},{9,11},{10,... | collective-permute-start | bytes 4718600 | tf_op jit(solution)/shard_map/ppermute | solution.py:33
  374.6 67.9 %collective-permute-start.47 = (bf16[8,64,1536]{2,1,0:T(8,128)(2,1)}, bf16[8,64,1536]{2,1,0:T(8,128)(2,1)}, u32[]{:S(2)}, u32[]{:S(2)}) collective-permute-start(bf16[8,64,1536]{2,1,0:T(8,128)(2,1)} %get-tuple-element.396), channel_id=1, source_target_pairs={{0,4},{1,5},{2,6},{3,7},{4,0},{5,1},{6,2},{7,3},{8,12},{9,13},{10,... | collective-permute-start | bytes 4718600 | tf_op jit(solution)/shard_map/ppermute | solution.py:33
  449.3 58.7 %collective-permute-start.53 = (bf16[2,4,128,1536]{3,2,1,0:T(8,128)(2,1)}, bf16[2,4,128,1536]{3,2,1,0:T(8,128)(2,1)}, u32[]{:S(2)}, u32[]{:S(2)}) collective-permute-start(bf16[2,4,128,1536]{3,2,1,0:T(8,128)(2,1)} %get-tuple-element.419), channel_id=1, source_target_pairs={{0,1},{1,0},{2,3},{3,2},{4,5},{5,4},{6,7},{7,6},{8,9},{9,8},{10,11... | collective-permute-start | bytes 9437192 | tf_op jit(solution)/shard_map/ppermute | solution.py:33
  449.3 58.6 %collective-permute-start.49 = (bf16[4,96,1024]{2,1,0:T(8,128)(2,1)}, bf16[4,96,1024]{2,1,0:T(8,128)(2,1)}, u32[]{:S(2)}, u32[]{:S(2)}) collective-permute-start(bf16[4,96,1024]{2,1,0:T(8,128)(2,1)} %get-tuple-element.415), channel_id=1, source_target_pairs={{0,4},{1,5},{2,6},{3,7},{4,0},{5,1},{6,2},{7,3},{8,12},{9,13},{10,... | collective-permute-start | bytes 2359304 | tf_op jit(solution)/shard_map/ppermute | solution.py:33
  450.5 57.4 %collective-permute-start.50 = (bf16[4,64,1536]{2,1,0:T(8,128)(2,1)}, bf16[4,64,1536]{2,1,0:T(8,128)(2,1)}, u32[]{:S(2)}, u32[]{:S(2)}) collective-permute-start(bf16[4,64,1536]{2,1,0:T(8,128)(2,1)} %get-tuple-element.416), channel_id=1, source_target_pairs={{0,2},{1,3},{2,0},{3,1},{4,6},{5,7},{6,4},{7,5},{8,10},{9,11},{10,... | collective-permute-start | bytes 2359304 | tf_op jit(solution)/shard_map/ppermute | solution.py:33
  452.0 56.0 %collective-permute-start.51 = (bf16[8,96,1024]{2,1,0:T(8,128)(2,1)}, bf16[8,96,1024]{2,1,0:T(8,128)(2,1)}, u32[]{:S(2)}, u32[]{:S(2)}) collective-permute-start(bf16[8,96,1024]{2,1,0:T(8,128)(2,1)} %get-tuple-element.417), channel_id=1, source_target_pairs={{0,2},{1,3},{2,0},{3,1},{4,6},{5,7},{6,4},{7,5},{8,10},{9,11},{10,... | collective-permute-start | bytes 4718600 | tf_op jit(solution)/shard_map/ppermute | solution.py:33
  452.5 55.4 %collective-permute-start.52 = (bf16[8,64,1536]{2,1,0:T(8,128)(2,1)}, bf16[8,64,1536]{2,1,0:T(8,128)(2,1)}, u32[]{:S(2)}, u32[]{:S(2)}) collective-permute-start(bf16[8,64,1536]{2,1,0:T(8,128)(2,1)} %get-tuple-element.418), channel_id=1, source_target_pairs={{0,4},{1,5},{2,6},{3,7},{4,0},{5,1},{6,2},{7,3},{8,12},{9,13},{10,... | collective-permute-start | bytes 4718600 | tf_op jit(solution)/shard_map/ppermute | solution.py:33
  511.3 37.1 %collective-permute-start.56 = (bf16[8,96,1024]{2,1,0:T(8,128)(2,1)}, bf16[8,96,1024]{2,1,0:T(8,128)(2,1)}, u32[]{:S(2)}, u32[]{:S(2)}) collective-permute-start(bf16[8,96,1024]{2,1,0:T(8,128)(2,1)} %get-tuple-element.437), channel_id=1, source_target_pairs={{0,2},{1,3},{2,0},{3,1},{4,6},{5,7},{6,4},{7,5},{8,10},{9,11},{10,... | collective-permute-start | bytes 4718600 | tf_op jit(solution)/shard_map/ppermute | solution.py:33
  512.3 36.7 %collective-permute-start.57 = (bf16[8,64,1536]{2,1,0:T(8,128)(2,1)}, bf16[8,64,1536]{2,1,0:T(8,128)(2,1)}, u32[]{:S(2)}, u32[]{:S(2)}) collective-permute-start(bf16[8,64,1536]{2,1,0:T(8,128)(2,1)} %get-tuple-element.438), channel_id=1, source_target_pairs={{0,4},{1,5},{2,6},{3,7},{4,0},{5,1},{6,2},{7,3},{8,12},{9,13},{10,... | collective-permute-start | bytes 4718600 | tf_op jit(solution)/shard_map/ppermute | solution.py:33
  581.6 44.1 %collective-permute-start.64 = (bf16[2,2,2,48,1536]{4,3,1,0,2:T(8,128)(2,1)}, bf16[2,2,2,48,1536]{4,3,1,0,2:T(8,128)(2,1)}, u32[]{:S(2)}, u32[]{:S(2)}) collective-permute-start(bf16[2,2,2,48,1536]{4,3,1,0,2:T(8,128)(2,1)} %copy_bitcast_fusion.2), channel_id=1, source_target_pairs={{0,2},{1,3},{2,0},{3,1},{4,6},{5,7},{6,4},{7,5},{8,10},{9,11},{10,... | collective-permute-start | bytes 3538952 | tf_op jit(solution)/shard_map/ppermute | solution.py:33
  583.4 42.3 %collective-permute-start.68 = (bf16[4,64,1536]{2,1,0:T(8,128)(2,1)}, bf16[4,64,1536]{2,1,0:T(8,128)(2,1)}, u32[]{:S(2)}, u32[]{:S(2)}) collective-permute-start(bf16[4,64,1536]{2,1,0:T(8,128)(2,1)} %get-tuple-element.478), channel_id=1, source_target_pairs={{0,2},{1,3},{2,0},{3,1},{4,6},{5,7},{6,4},{7,5},{8,10},{9,11},{10,... | collective-permute-start | bytes 2359304 | tf_op jit(solution)/shard_map/ppermute | solution.py:33
  653.5 41.7 %collective-permute-start.76 = (bf16[576,1536]{1,0:T(8,128)(2,1)}, bf16[576,1536]{1,0:T(8,128)(2,1)}, u32[]{:S(2)}, u32[]{:S(2)}) collective-permute-start(bf16[576,1536]{1,0:T(8,128)(2,1)} %bitcast.55), channel_id=1, source_target_pairs={{0,1},{1,0},{2,3},{3,2},{4,5},{5,4},{6,7},{7,6},{8,9},{9,8},{10,11... | collective-permute-start | bytes 5308424 | tf_op jit(solution)/shard_map/ppermute | solution.py:33
  661.7 41.3 %collective-permute-start.72 = (bf16[2,2,2,96,1152]{4,3,0,1,2:T(8,128)(2,1)}, bf16[2,2,2,96,1152]{4,3,0,1,2:T(8,128)(2,1)}, u32[]{:S(2)}, u32[]{:S(2)}) collective-permute-start(bf16[2,2,2,96,1152]{4,3,0,1,2:T(8,128)(2,1)} %copy_bitcast_fusion.1), channel_id=1, source_target_pairs={{0,2},{1,3},{2,0},{3,1},{4,6},{5,7},{6,4},{7,5},{8,10},{9,11},{10,... | collective-permute-start | bytes 5308424 | tf_op jit(solution)/shard_map/ppermute | solution.py:33
  662.8 41.0 %collective-permute-start.73 = (bf16[2,2,2,96,1152]{4,3,0,1,2:T(8,128)(2,1)}, bf16[2,2,2,96,1152]{4,3,0,1,2:T(8,128)(2,1)}, u32[]{:S(2)}, u32[]{:S(2)}) collective-permute-start(bf16[2,2,2,96,1152]{4,3,0,1,2:T(8,128)(2,1)} %copy_bitcast_fusion), channel_id=1, source_target_pairs={{0,4},{1,5},{2,6},{3,7},{4,0},{5,1},{6,2},{7,3},{8,12},{9,13},{10,... | collective-permute-start | bytes 5308424 | tf_op jit(solution)/shard_map/ppermute | solution.py:33
  710.7 33.4 %collective-permute-start.77 = (bf16[2,2,96,1152]{3,2,0,1:T(8,128)(2,1)}, bf16[2,2,96,1152]{3,2,0,1:T(8,128)(2,1)}, u32[]{:S(2)}, u32[]{:S(2)}) collective-permute-start(bf16[2,2,96,1152]{3,2,0,1:T(8,128)(2,1)} %fusion.4), channel_id=1, source_target_pairs={{0,4},{1,5},{2,6},{3,7},{4,0},{5,1},{6,2},{7,3},{8,12},{9,13},{10,... | collective-permute-start | bytes 2654216 | tf_op jit(solution)/shard_map/ppermute | solution.py:33
  (180 other events, 2063.9 us)

commit v12 on v11

--- a/solution.py
+++ b/solution.py
@@ -1305,25 +1305,25 @@
         return row_split(up_all.transpose(0, 2, 1, 3), 2).reshape(part, -1)
 
     slot.finish([proj_flow])
-    proj_share = proj_flow.result
-    up_share = slot([qkv_flow, mods_flow, tap_flow], split_up)
+
+    def last_work():
+        proj_share = lax.ppermute(proj_flow.result, AXES, proj_back)
+        return run(mods_flow), run(tap_flow), split_up(), proj_share
+
+    grad_mods_all, tap_share, up_share, proj_share = slot([qkv_flow], last_work)
     slot.finish([qkv_flow])
     qkv_share = qkv_flow.result
 
     def split_qkv():
         qkv_all = qkv_share.reshape(2 * part, pairs, 3, 128).transpose(0, 2, 1, 3)
-        qkv_out = row_split(qkv_all, 2).reshape(part, -1)
-        return qkv_out, lax.ppermute(proj_share, AXES, proj_back)
-
-    qkv_out, proj_share = slot([mods_flow, tap_flow], split_qkv)
-    slot.finish([mods_flow, tap_flow])
+        return row_split(qkv_all, 2).reshape(part, -1)
+
+    qkv_out = split_qkv()
     down_share = jnp.concatenate(down_shares, axis=0)
 
-    grad_mods_all = mods_flow.result
     mod_grad = jnp.dot(lifted.T, grad_mods_all, preferred_element_type=full)
     (cond_grad,) = lift_pull(jnp.dot(grad_mods_all, mod_weight.T, preferred_element_type=full))
     table_grad = jnp.dot(picks.astype(full).T, cond_grad, precision=highest)
-    tap_share = tap_flow.result
     ffn_share = tap_share[: 9 * share].reshape(9, share)
     kernel_share = tap_share[9 * share :].reshape(9, part)
 

time: 837 us -> 830 us (level)
  waiting for transfers between devices: 155 us -> 145 us
    ppermute x96, waiting for transfers between devices: 155 us -> 145 us  [swap(): lax.ppermute(x, AXES, [(i, i ^ 1 << bit) for i in range(device_count())])]
  transfers between devices with their start and end apart: 98 -> 98, of which waited for: 30 -> 33; matrix products, arithmetic and copies ran while one was open for 21% -> 21% of each run, Pallas kernels for 36% -> 37%
where the time goes in v12:
time: 830 us; the launch traced here: 824 us
  Pallas kernels  301 us (36%)
  waiting for transfers between devices  145 us (17%)
  other arithmetic  124 us (15%)
  starting transfers between devices  107 us (13%)
  local copies, waits for them, and re-layouts  94 us (11%)
  matrix products  49.5 us (6%)
    pallas_call x3, Pallas kernels, feed_forward(): pl.pallas_call(functools.partial(feed_body, spread), grid_spec=pltpu.Pref...  164 us
    ppermute x96, waiting for transfers between devices, swap(): lax.ppermute(x, AXES, [(i, i ^ 1 << bit) for i in range(device_count())])  145 us
    ppermute x96, starting transfers between devices, swap(): lax.ppermute(x, AXES, [(i, i ^ 1 << bit) for i in range(device_count())])  104 us
    concatenate x17, other arithmetic, join(): return [jnp.concatenate(pair, axis=0) for pair in zip(held, arriving)]  32.9 us
    convert_element_type x18, other arithmetic, halving_steps(): (staying[at].astype(full) + arriving[at].astype(full)).astype(low)  32.2 us
    pallas_call x1, Pallas kernels, attend_back(): pl.pallas_call(attend_back_body, grid=(pairs,), in_specs=[pl.BlockSpec((P...  28.9 us
    pallas_call x1, Pallas kernels, conv_in(): pl.pallas_call(conv_in_body, grid=(model // TILE,), in_specs=[pl.BlockSpe...  23.1 us
    pallas_call x1, Pallas kernels, conv_back(): pl.pallas_call(conv_back_body, grid_spec=pltpu.PrefetchScalarGridSpec(num...  21.2 us
  transfers between devices with their start and end apart: 98, of which 33 were waited for; matrix products, arithmetic and copies ran while one was open for 21% of the time, Pallas kernels for 37%

profile of v12, /device:TPU:0, one launch (start us, length us, event | category | flops | bytes accessed | tf_op | source)
XLA Modules:
  0.0 823.9 jit_solution(7683697855842459599)
XLA Ops:
  17.0 4.6 reshape_squeeze.6
  23.3 4.5 reshape_squeeze.7
  68.8 8.9 %collective-permute-done.7 = bf16[1,48,1536]{2,1,0:T(8,128)(2,1)S(1)} collective-permute-done((bf16[1,48,1536]{2,1,0:T(8,128)(2,1)S(1)}, bf16[1,48,1536]{2,1,0:T(8,128)(2,1)S(1)}, u32[]{:S(2)}, u32[]{:S(2)}) %collective-permute-start.7) | collective-permute-done | bytes 147488 | tf_op jit(solution)/shard_map/ppermute | solution.py:33
  105.7 7.7 collective-permute-done.13
  128.7 4.6 collective-permute-done.25
  139.0 23.1 %conv_in.1 = bf16[1024,1536]{1,0:T(8,128)(2,1)} custom-call(bf16[1024,1536]{1,0:T(8,128)(2,1)} %bitcast.293, f32[16,1536]{1,0:T(8,128)} %pad_convert_fusion.1.kernel_ref, f32[8,1536]{1,0:T(8,128)} %maximum_maximum_fusion.mods_ref), custom_call_target="tpu_custom_call" | custom-call | flops 47185920 | bytes 6291456 | tf_op jit(solution)/shard_map/conv_in/pallas_call | solution.py:731
  162.2 13.9 %collective-permute-done.17 = bf16[4,48,1536]{2,1,0:T(8,128)(2,1)} collective-permute-done((bf16[4,48,1536]{2,1,0:T(8,128)(2,1)}, bf16[4,48,1536]{2,1,0:T(8,128)(2,1)}, u32[]{:S(2)}, u32[]{:S(2)}) %collective-permute-start.17) | collective-permute-done | bytes 589856 | tf_op jit(solution)/shard_map/ppermute | solution.py:33
  188.3 5.6 assemble.4
  194.0 5.6 assemble.3
  199.6 12.7 %convolution_convert_fusion.2.qkv_ref = bf16[1024,2304]{1,0:T(8,128)(2,1)} fusion(bf16[1024,1536]{1,0:T(8,128)(2,1)} %conv_in.1, bf16[1536,1152]{1,0:T(8,128)(2,1)} %bitcast.299, bf16[1536,1152]{1,0:T(8,128)(2,1)} %bitcast.301), kind=kOutput, calls=%fused_computation.3 | convolution fusion | flops 7264272384 | bytes 14942208 | tf_op jit(solution)/shard_map/dot_general | solution.py:1156
  212.3 5.4 pad_maximum_fusion
  237.7 5.0 assemble.5
  242.7 15.4 %attend.1 = bf16[1024,768]{1,0:T(8,128)(2,1)} custom-call(f32[256,256]{1,0:T(8,128)} %compare_convert_fusion.mask_ref, bf16[1024,2304]{1,0:T(8,128)(2,1)} %convolution_convert_fusion.2.qkv_ref), custom_call_target="tpu_custom_call" | custom-call | flops 3221225472 | bytes 6291456 | tf_op jit(solution)/shard_map/attend/pallas_call | solution.py:365
  258.1 8.3 %collective-permute-done.35 = bf16[2,128,1536]{2,1,0:T(8,128)(2,1)} collective-permute-done((bf16[2,128,1536]{2,1,0:T(8,128)(2,1)}, bf16[2,128,1536]{2,1,0:T(8,128)(2,1)}, u32[]{:S(2)}, u32[]{:S(2)}) %collective-permute-start.35) | collective-permute-done | bytes 786464 | tf_op jit(solution)/shard_map/ppermute | solution.py:33
  266.3 6.4 convolution_convert_fusion.4.part_ref
  285.4 17.6 %enter_feed.1 = (bf16[1024,1536]{1,0:T(8,128)(2,1)}, bf16[1536,1024]{1,0:T(8,128)(2,1)}, bf16[1024,1536]{1,0:T(8,128)(2,1)}) custom-call(bf16[1024,1536]{1,0:T(8,128)(2,1)} %bitcast.294, bf16[1024,1536]{1,0:T(8,128)(2,1)} %convolution_convert_fusion.4.part_ref, bf16[1024,1536]{1,0:T(8,128)(2,1)} %collective-permute-done.38.other_ref, ...), custom_call_target="tpu_custom_call" | custom-call | flops 1000 | bytes 1000 | tf_op jit(solution)/shard_map/enter_feed/pallas_call | solution.py:956
  312.2 54.8 %feed_forward.3 = (bf16[2,4,128,1536]{3,2,1,0:T(8,128)(2,1)}, bf16[2,4,128,1536]{3,2,1,0:T(8,128)(2,1)}, bf16[8,96,1024]{2,1,0:T(8,128)(2,1)}, bf16[8,96,1024]{2...) custom-call(s32[49]{0:T(128)} %pad_add_fusion.1.words_ref, ...), custom_call_target="tpu_custom_call" | custom-call | flops 19327352832 | bytes 28311552 | tf_op jit(solution)/shard_map/feed_forward/pallas_call | solution.py:623
  376.4 54.4 %feed_forward.4 = (bf16[2,4,128,1536]{3,2,1,0:T(8,128)(2,1)}, bf16[2,4,128,1536]{3,2,1,0:T(8,128)(2,1)}, bf16[8,96,1024]{2,1,0:T(8,128)(2,1)}, bf16[8,96,1024]{2...) custom-call(s32[49]{0:T(128)} %pad_add_fusion.1.words_ref, ...), custom_call_target="tpu_custom_call" | custom-call | flops 19327352832 | bytes 28311552 | tf_op jit(solution)/shard_map/feed_forward/pallas_call | solution.py:623
  430.8 12.4 %collective-permute-done.46 = bf16[8,96,1024]{2,1,0:T(8,128)(2,1)} collective-permute-done((bf16[8,96,1024]{2,1,0:T(8,128)(2,1)}, bf16[8,96,1024]{2,1,0:T(8,128)(2,1)}, u32[]{:S(2)}, u32[]{:S(2)}) %collective-permute-start.46) | collective-permute-done | bytes 1572896 | tf_op jit(solution)/shard_map/ppermute | solution.py:33
  454.8 54.6 %feed_forward.5 = (bf16[2,4,128,1536]{3,2,1,0:T(8,128)(2,1)}, bf16[2,4,128,1536]{3,2,1,0:T(8,128)(2,1)}, bf16[8,96,1024]{2,1,0:T(8,128)(2,1)}, bf16[8,96,1024]{2...) custom-call(s32[49]{0:T(128)} %pad_add_fusion.1.words_ref, ...), custom_call_target="tpu_custom_call" | custom-call | flops 19327352832 | bytes 28311552 | tf_op jit(solution)/shard_map/feed_forward/pallas_call | solution.py:623
  520.2 15.4 %leave_feed.1 = (bf16[512,1536]{1,0:T(8,128)(2,1)}, f32[512,1536]{1,0:T(8,128)}, bf16[512,1536]{1,0:T(8,128)(2,1)}, f32[8,1536]{1,0:T(8,128)}) custom-call(s32[1]{0:T(128)} %bitcast.31.words_ref.core_ref, bf16[1024,1536]{1,0:T(8,128)(2,1)} %bitcast.295, bf16[1024,1536]{1,0:T(8,128)(2,1)} %convolution_convert_fusion.4.part_ref, ...), custom_call_target="tpu_custom_call" | custom-call | flops 1000 | bytes 1000 | tf_op jit(solution)/shard_map/leave_feed/pallas_call | solution.py:1012
  535.6 14.2 %collective-permute-done.56 = bf16[8,96,1024]{2,1,0:T(8,128)(2,1)} collective-permute-done((bf16[8,96,1024]{2,1,0:T(8,128)(2,1)}, bf16[8,96,1024]{2,1,0:T(8,128)(2,1)}, u32[]{:S(2)}, u32[]{:S(2)}) %collective-permute-start.56) | collective-permute-done | bytes 1572896 | tf_op jit(solution)/shard_map/ppermute | solution.py:33
  587.6 28.9 %attend_back.1 = bf16[1024,2304]{1,0:T(8,128)(2,1)} custom-call(f32[256,256]{1,0:T(8,128)} %compare_convert_fusion.mask_ref, bf16[1024,2304]{1,0:T(8,128)(2,1)} %convolution_convert_fusion.2.qkv_ref, bf16[1024,768]{1,0:T(8,128)(2,1)} %convolution_convert_fusion.7.grad_ref), custom_call_target="tpu_custom_call" | custom-call | flops 8053063680 | bytes 11010048 | tf_op jit(solution)/shard_map/attend_back/pallas_call | solution.py:386
  616.6 10.6 %collective-permute-done.68 = bf16[4,64,1536]{2,1,0:T(8,128)(2,1)} collective-permute-done((bf16[4,64,1536]{2,1,0:T(8,128)(2,1)}, bf16[4,64,1536]{2,1,0:T(8,128)(2,1)}, u32[]{:S(2)}, u32[]{:S(2)}) %collective-permute-start.68) | collective-permute-done | bytes 786464 | tf_op jit(solution)/shard_map/ppermute | solution.py:33
  634.6 10.3 %convolution_convert_fusion = bf16[1536,2304]{1,0:T(8,128)(2,1)S(1)} fusion(bf16[1024,1536]{1,0:T(8,128)(2,1)S(1)} %copy-done.14, bf16[1024,2304]{1,0:T(8,128)(2,1)} %attend_back.1), kind=kOutput, calls=%fused_computation | convolution fusion | flops 7251296256 | bytes 14942208 | tf_op jit(solution)/shard_map/dot_general | solution.py:1249
  645.0 7.7 convolution_convert_fusion.3
  681.7 6.3 collective-permute-done.74
  688.0 7.3 collective-permute-done.75
  695.3 9.2 %collective-permute-done.72 = bf16[2,2,2,96,1152]{4,3,1,0,2:T(8,128)(2,1)} collective-permute-done((bf16[2,2,2,96,1152]{4,3,1,0,2:T(8,128)(2,1)}, bf16[2,2,2,96,1152]{4,3,1,0,2:T(8,128)(2,1)}, u32[]{:S(2)}, u32[]{:S(2)}) %collective-permute-start.72) | collective-permute-done | bytes 1769504 | tf_op jit(solution)/shard_map/ppermute | solution.py:33
  724.2 21.2 %conv_back.1 = (f32[512,1536]{1,0:T(8,128)}, f32[16,1536]{1,0:T(8,128)}, f32[8,1536]{1,0:T(8,128)}) custom-call(s32[1]{0:T(128)} %bitcast.31.words_ref.core_ref, bf16[576,1536]{1,0:T(8,128)(2,1)} %bitcast.312, bf16[576,1536]{1,0:T(8,128)(2,1)} %bitcast.313, bf16[576,1536]{1,0:T(8,128)(2,1)} %collective-permute-done.76.arriving_ref, ...), custom_call_target="tpu_custom_call" | custom-call | flops 55050240 | bytes 11010048 | tf_op jit(solution)/shard_map/conv_back/pallas_call | solution.py:889
  794.7 5.3 collective-permute-done.93
  806.4 4.8 reshape.342
  (622 shorter events, 354.3 us)
Async XLA Ops:
  81.2 34.2 %collective-permute-start.9 = (bf16[4,96,1152]{2,1,0:T(8,128)(2,1)S(1)}, bf16[4,96,1152]{2,1,0:T(8,128)(2,1)}, u32[]{:S(2)}, u32[]{:S(2)}) collective-permute-start(bf16[4,96,1152]{2,1,0:T(8,128)(2,1)S(1)} %get-tuple-element.282), channel_id=1, source_target_pairs={{0,4},{1,5},{2,6},{3,7},{4,0},{5,1},{6,2},{7,3},{8,12},{9,13},{10,... | collective-permute-start | bytes 2654216 | tf_op jit(solution)/shard_map/ppermute | solution.py:33
  82.8 33.3 %collective-permute-start.10 = (bf16[4,96,1152]{2,1,0:T(8,128)(2,1)S(1)}, bf16[4,96,1152]{2,1,0:T(8,128)(2,1)}, u32[]{:S(2)}, u32[]{:S(2)}) collective-permute-start(bf16[4,96,1152]{2,1,0:T(8,128)(2,1)S(1)} %get-tuple-element.283), channel_id=1, source_target_pairs={{0,2},{1,3},{2,0},{3,1},{4,6},{5,7},{6,4},{7,5},{8,10},{9,11},{10,... | collective-permute-start | bytes 2654216 | tf_op jit(solution)/shard_map/ppermute | solution.py:33
  124.6 51.4 %collective-permute-start.15 = (bf16[8,96,1152]{2,1,0:T(8,128)(2,1)S(1)}, bf16[8,96,1152]{2,1,0:T(8,128)(2,1)}, u32[]{:S(2)}, u32[]{:S(2)}) collective-permute-start(bf16[8,96,1152]{2,1,0:T(8,128)(2,1)S(1)} %pad_maximum_fusion.6.refs_0_), channel_id=1, source_target_pairs={{0,2},{1,3},{2,0},{3,1},{4,6},{5,7},{6,4},{7,5},{8,10},{9,11},{10,... | collective-permute-start | bytes 5308424 | tf_op jit(solution)/shard_map/ppermute | solution.py:33
  125.3 50.7 %collective-permute-start.16 = (bf16[8,96,1152]{2,1,0:T(8,128)(2,1)}, bf16[8,96,1152]{2,1,0:T(8,128)(2,1)}, u32[]{:S(2)}, u32[]{:S(2)}) collective-permute-start(bf16[8,96,1152]{2,1,0:T(8,128)(2,1)} %pad_maximum_fusion.7.refs_0_), channel_id=1, source_target_pairs={{0,4},{1,5},{2,6},{3,7},{4,0},{5,1},{6,2},{7,3},{8,12},{9,13},{10,... | collective-permute-start | bytes 5308424 | tf_op jit(solution)/shard_map/ppermute | solution.py:33
  135.8 40.2 %collective-permute-start.17 = (bf16[4,48,1536]{2,1,0:T(8,128)(2,1)}, bf16[4,48,1536]{2,1,0:T(8,128)(2,1)}, u32[]{:S(2)}, u32[]{:S(2)}) collective-permute-start(bf16[4,48,1536]{2,1,0:T(8,128)(2,1)} %pad_maximum_fusion.23), channel_id=1, source_target_pairs={{0,4},{1,5},{2,6},{3,7},{4,0},{5,1},{6,2},{7,3},{8,12},{9,13},{10,... | collective-permute-start | bytes 1769480 | tf_op jit(solution)/shard_map/ppermute | solution.py:33
  181.6 41.2 %collective-permute-start.27 = (bf16[8,48,1536]{2,1,0:T(8,128)(2,1)S(1)}, bf16[8,48,1536]{2,1,0:T(8,128)(2,1)}, u32[]{:S(2)}, u32[]{:S(2)}) collective-permute-start(bf16[8,48,1536]{2,1,0:T(8,128)(2,1)S(1)} %pad_maximum_fusion.15.refs_0_), channel_id=1, source_target_pairs={{0,2},{1,3},{2,0},{3,1},{4,6},{5,7},{6,4},{7,5},{8,10},{9,11},{10,... | collective-permute-start | bytes 3538952 | tf_op jit(solution)/shard_map/ppermute | solution.py:33
  182.9 35.6 %collective-permute-start.28 = (bf16[4,96,1024]{2,1,0:T(8,128)(2,1)}, bf16[4,96,1024]{2,1,0:T(8,128)(2,1)}, u32[]{:S(2)}, u32[]{:S(2)}) collective-permute-start(bf16[4,96,1024]{2,1,0:T(8,128)(2,1)} %pad_maximum_fusion.19), channel_id=1, source_target_pairs={{0,4},{1,5},{2,6},{3,7},{4,0},{5,1},{6,2},{7,3},{8,12},{9,13},{10,... | collective-permute-start | bytes 2359304 | tf_op jit(solution)/shard_map/ppermute | solution.py:33
  184.1 38.8 %collective-permute-start.29 = (bf16[4,64,1536]{2,1,0:T(8,128)(2,1)}, bf16[4,64,1536]{2,1,0:T(8,128)(2,1)}, u32[]{:S(2)}, u32[]{:S(2)}) collective-permute-start(bf16[4,64,1536]{2,1,0:T(8,128)(2,1)} %pad_maximum_fusion.20), channel_id=1, source_target_pairs={{0,2},{1,3},{2,0},{3,1},{4,6},{5,7},{6,4},{7,5},{8,10},{9,11},{10,... | collective-permute-start | bytes 2359304 | tf_op jit(solution)/shard_map/ppermute | solution.py:33
  232.0 34.3 %collective-permute-start.32 = (bf16[8,96,1024]{2,1,0:T(8,128)(2,1)}, bf16[8,96,1024]{2,1,0:T(8,128)(2,1)}, u32[]{:S(2)}, u32[]{:S(2)}) collective-permute-start(bf16[8,96,1024]{2,1,0:T(8,128)(2,1)} %pad_maximum_fusion.8.refs_0_), channel_id=1, source_target_pairs={{0,2},{1,3},{2,0},{3,1},{4,6},{5,7},{6,4},{7,5},{8,10},{9,11},{10,... | collective-permute-start | bytes 4718600 | tf_op jit(solution)/shard_map/ppermute | solution.py:33
  233.2 33.2 %collective-permute-start.33 = (bf16[8,64,1536]{2,1,0:T(8,128)(2,1)}, bf16[8,64,1536]{2,1,0:T(8,128)(2,1)}, u32[]{:S(2)}, u32[]{:S(2)}) collective-permute-start(bf16[8,64,1536]{2,1,0:T(8,128)(2,1)} %pad_maximum_fusion.9.refs_2_), channel_id=1, source_target_pairs={{0,4},{1,5},{2,6},{3,7},{4,0},{5,1},{6,2},{7,3},{8,12},{9,13},{10,... | collective-permute-start | bytes 4718600 | tf_op jit(solution)/shard_map/ppermute | solution.py:33
  308.1 58.9 %collective-permute-start.40 = (bf16[8,96,1024]{2,1,0:T(8,128)(2,1)}, bf16[8,96,1024]{2,1,0:T(8,128)(2,1)}, u32[]{:S(2)}, u32[]{:S(2)}) collective-permute-start(bf16[8,96,1024]{2,1,0:T(8,128)(2,1)} %pad_maximum_fusion.11.refs_0_), channel_id=1, source_target_pairs={{0,2},{1,3},{2,0},{3,1},{4,6},{5,7},{6,4},{7,5},{8,10},{9,11},{10,... | collective-permute-start | bytes 4718600 | tf_op jit(solution)/shard_map/ppermute | solution.py:33
  309.2 57.8 %collective-permute-start.41 = (bf16[8,64,1536]{2,1,0:T(8,128)(2,1)}, bf16[8,64,1536]{2,1,0:T(8,128)(2,1)}, u32[]{:S(2)}, u32[]{:S(2)}) collective-permute-start(bf16[8,64,1536]{2,1,0:T(8,128)(2,1)} %pad_maximum_fusion.12.refs_2_), channel_id=1, source_target_pairs={{0,4},{1,5},{2,6},{3,7},{4,0},{5,1},{6,2},{7,3},{8,12},{9,13},{10,... | collective-permute-start | bytes 4718600 | tf_op jit(solution)/shard_map/ppermute | solution.py:33
  310.5 56.5 %collective-permute-start.42 = (bf16[4,96,1024]{2,1,0:T(8,128)(2,1)}, bf16[4,96,1024]{2,1,0:T(8,128)(2,1)}, u32[]{:S(2)}, u32[]{:S(2)}) collective-permute-start(bf16[4,96,1024]{2,1,0:T(8,128)(2,1)} %get-tuple-element.349), channel_id=1, source_target_pairs={{0,4},{1,5},{2,6},{3,7},{4,0},{5,1},{6,2},{7,3},{8,12},{9,13},{10,... | collective-permute-start | bytes 2359304 | tf_op jit(solution)/shard_map/ppermute | solution.py:33
  311.2 55.8 %collective-permute-start.43 = (bf16[4,64,1536]{2,1,0:T(8,128)(2,1)}, bf16[4,64,1536]{2,1,0:T(8,128)(2,1)}, u32[]{:S(2)}, u32[]{:S(2)}) collective-permute-start(bf16[4,64,1536]{2,1,0:T(8,128)(2,1)} %get-tuple-element.350), channel_id=1, source_target_pairs={{0,2},{1,3},{2,0},{3,1},{4,6},{5,7},{6,4},{7,5},{8,10},{9,11},{10,... | collective-permute-start | bytes 2359304 | tf_op jit(solution)/shard_map/ppermute | solution.py:33
  372.3 71.6 %collective-permute-start.48 = (bf16[2,4,128,1536]{3,2,1,0:T(8,128)(2,1)}, bf16[2,4,128,1536]{3,2,1,0:T(8,128)(2,1)}, u32[]{:S(2)}, u32[]{:S(2)}) collective-permute-start(bf16[2,4,128,1536]{3,2,1,0:T(8,128)(2,1)} %get-tuple-element.375), channel_id=1, source_target_pairs={{0,1},{1,0},{2,3},{3,2},{4,5},{5,4},{6,7},{7,6},{8,9},{9,8},{10,11... | collective-permute-start | bytes 9437192 | tf_op jit(solution)/shard_map/ppermute | solution.py:33
  372.3 58.4 %collective-permute-start.44 = (bf16[8,96,1024]{2,1,0:T(8,128)(2,1)}, bf16[8,96,1024]{2,1,0:T(8,128)(2,1)}, u32[]{:S(2)}, u32[]{:S(2)}) collective-permute-start(bf16[8,96,1024]{2,1,0:T(8,128)(2,1)} %pad_maximum_fusion.13.refs_0_), channel_id=1, source_target_pairs={{0,2},{1,3},{2,0},{3,1},{4,6},{5,7},{6,4},{7,5},{8,10},{9,11},{10,... | collective-permute-start | bytes 4718600 | tf_op jit(solution)/shard_map/ppermute | solution.py:33
  373.4 57.4 %collective-permute-start.45 = (bf16[8,64,1536]{2,1,0:T(8,128)(2,1)}, bf16[8,64,1536]{2,1,0:T(8,128)(2,1)}, u32[]{:S(2)}, u32[]{:S(2)}) collective-permute-start(bf16[8,64,1536]{2,1,0:T(8,128)(2,1)} %pad_maximum_fusion.14.refs_2_), channel_id=1, source_target_pairs={{0,4},{1,5},{2,6},{3,7},{4,0},{5,1},{6,2},{7,3},{8,12},{9,13},{10,... | collective-permute-start | bytes 4718600 | tf_op jit(solution)/shard_map/ppermute | solution.py:33
  374.8 68.4 %collective-permute-start.46 = (bf16[8,96,1024]{2,1,0:T(8,128)(2,1)}, bf16[8,96,1024]{2,1,0:T(8,128)(2,1)}, u32[]{:S(2)}, u32[]{:S(2)}) collective-permute-start(bf16[8,96,1024]{2,1,0:T(8,128)(2,1)} %get-tuple-element.373), channel_id=1, source_target_pairs={{0,2},{1,3},{2,0},{3,1},{4,6},{5,7},{6,4},{7,5},{8,10},{9,11},{10,... | collective-permute-start | bytes 4718600 | tf_op jit(solution)/shard_map/ppermute | solution.py:33
  376.1 67.8 %collective-permute-start.47 = (bf16[8,64,1536]{2,1,0:T(8,128)(2,1)}, bf16[8,64,1536]{2,1,0:T(8,128)(2,1)}, u32[]{:S(2)}, u32[]{:S(2)}) collective-permute-start(bf16[8,64,1536]{2,1,0:T(8,128)(2,1)} %get-tuple-element.374), channel_id=1, source_target_pairs={{0,4},{1,5},{2,6},{3,7},{4,0},{5,1},{6,2},{7,3},{8,12},{9,13},{10,... | collective-permute-start | bytes 4718600 | tf_op jit(solution)/shard_map/ppermute | solution.py:33
  450.7 58.7 %collective-permute-start.53 = (bf16[2,4,128,1536]{3,2,1,0:T(8,128)(2,1)}, bf16[2,4,128,1536]{3,2,1,0:T(8,128)(2,1)}, u32[]{:S(2)}, u32[]{:S(2)}) collective-permute-start(bf16[2,4,128,1536]{3,2,1,0:T(8,128)(2,1)} %get-tuple-element.397), channel_id=1, source_target_pairs={{0,1},{1,0},{2,3},{3,2},{4,5},{5,4},{6,7},{7,6},{8,9},{9,8},{10,11... | collective-permute-start | bytes 9437192 | tf_op jit(solution)/shard_map/ppermute | solution.py:33
  450.8 58.6 %collective-permute-start.49 = (bf16[4,96,1024]{2,1,0:T(8,128)(2,1)}, bf16[4,96,1024]{2,1,0:T(8,128)(2,1)}, u32[]{:S(2)}, u32[]{:S(2)}) collective-permute-start(bf16[4,96,1024]{2,1,0:T(8,128)(2,1)} %get-tuple-element.393), channel_id=1, source_target_pairs={{0,4},{1,5},{2,6},{3,7},{4,0},{5,1},{6,2},{7,3},{8,12},{9,13},{10,... | collective-permute-start | bytes 2359304 | tf_op jit(solution)/shard_map/ppermute | solution.py:33
  452.1 57.3 %collective-permute-start.50 = (bf16[4,64,1536]{2,1,0:T(8,128)(2,1)}, bf16[4,64,1536]{2,1,0:T(8,128)(2,1)}, u32[]{:S(2)}, u32[]{:S(2)}) collective-permute-start(bf16[4,64,1536]{2,1,0:T(8,128)(2,1)} %get-tuple-element.394), channel_id=1, source_target_pairs={{0,2},{1,3},{2,0},{3,1},{4,6},{5,7},{6,4},{7,5},{8,10},{9,11},{10,... | collective-permute-start | bytes 2359304 | tf_op jit(solution)/shard_map/ppermute | solution.py:33
  453.5 55.9 %collective-permute-start.51 = (bf16[8,96,1024]{2,1,0:T(8,128)(2,1)}, bf16[8,96,1024]{2,1,0:T(8,128)(2,1)}, u32[]{:S(2)}, u32[]{:S(2)}) collective-permute-start(bf16[8,96,1024]{2,1,0:T(8,128)(2,1)} %get-tuple-element.395), channel_id=1, source_target_pairs={{0,2},{1,3},{2,0},{3,1},{4,6},{5,7},{6,4},{7,5},{8,10},{9,11},{10,... | collective-permute-start | bytes 4718600 | tf_op jit(solution)/shard_map/ppermute | solution.py:33
  454.1 55.3 %collective-permute-start.52 = (bf16[8,64,1536]{2,1,0:T(8,128)(2,1)}, bf16[8,64,1536]{2,1,0:T(8,128)(2,1)}, u32[]{:S(2)}, u32[]{:S(2)}) collective-permute-start(bf16[8,64,1536]{2,1,0:T(8,128)(2,1)} %get-tuple-element.396), channel_id=1, source_target_pairs={{0,4},{1,5},{2,6},{3,7},{4,0},{5,1},{6,2},{7,3},{8,12},{9,13},{10,... | collective-permute-start | bytes 4718600 | tf_op jit(solution)/shard_map/ppermute | solution.py:33
  512.8 37.1 %collective-permute-start.56 = (bf16[8,96,1024]{2,1,0:T(8,128)(2,1)}, bf16[8,96,1024]{2,1,0:T(8,128)(2,1)}, u32[]{:S(2)}, u32[]{:S(2)}) collective-permute-start(bf16[8,96,1024]{2,1,0:T(8,128)(2,1)} %get-tuple-element.415), channel_id=1, source_target_pairs={{0,2},{1,3},{2,0},{3,1},{4,6},{5,7},{6,4},{7,5},{8,10},{9,11},{10,... | collective-permute-start | bytes 4718600 | tf_op jit(solution)/shard_map/ppermute | solution.py:33
  513.8 36.7 %collective-permute-start.57 = (bf16[8,64,1536]{2,1,0:T(8,128)(2,1)}, bf16[8,64,1536]{2,1,0:T(8,128)(2,1)}, u32[]{:S(2)}, u32[]{:S(2)}) collective-permute-start(bf16[8,64,1536]{2,1,0:T(8,128)(2,1)} %get-tuple-element.416), channel_id=1, source_target_pairs={{0,4},{1,5},{2,6},{3,7},{4,0},{5,1},{6,2},{7,3},{8,12},{9,13},{10,... | collective-permute-start | bytes 4718600 | tf_op jit(solution)/shard_map/ppermute | solution.py:33
  583.0 44.1 %collective-permute-start.64 = (bf16[2,2,2,48,1536]{4,3,1,0,2:T(8,128)(2,1)}, bf16[2,2,2,48,1536]{4,3,1,0,2:T(8,128)(2,1)}, u32[]{:S(2)}, u32[]{:S(2)}) collective-permute-start(bf16[2,2,2,48,1536]{4,3,1,0,2:T(8,128)(2,1)} %copy_bitcast_fusion.2), channel_id=1, source_target_pairs={{0,2},{1,3},{2,0},{3,1},{4,6},{5,7},{6,4},{7,5},{8,10},{9,11},{10,... | collective-permute-start | bytes 3538952 | tf_op jit(solution)/shard_map/ppermute | solution.py:33
  584.9 42.3 %collective-permute-start.68 = (bf16[4,64,1536]{2,1,0:T(8,128)(2,1)}, bf16[4,64,1536]{2,1,0:T(8,128)(2,1)}, u32[]{:S(2)}, u32[]{:S(2)}) collective-permute-start(bf16[4,64,1536]{2,1,0:T(8,128)(2,1)} %get-tuple-element.454), channel_id=1, source_target_pairs={{0,2},{1,3},{2,0},{3,1},{4,6},{5,7},{6,4},{7,5},{8,10},{9,11},{10,... | collective-permute-start | bytes 2359304 | tf_op jit(solution)/shard_map/ppermute | solution.py:33
  654.8 40.5 %collective-permute-start.76 = (bf16[576,1536]{1,0:T(8,128)(2,1)}, bf16[576,1536]{1,0:T(8,128)(2,1)}, u32[]{:S(2)}, u32[]{:S(2)}) collective-permute-start(bf16[576,1536]{1,0:T(8,128)(2,1)} %bitcast.55), channel_id=1, source_target_pairs={{0,1},{1,0},{2,3},{3,2},{4,5},{5,4},{6,7},{7,6},{8,9},{9,8},{10,11... | collective-permute-start | bytes 5308424 | tf_op jit(solution)/shard_map/ppermute | solution.py:33
  663.3 41.3 %collective-permute-start.72 = (bf16[2,2,2,96,1152]{4,3,1,0,2:T(8,128)(2,1)}, bf16[2,2,2,96,1152]{4,3,1,0,2:T(8,128)(2,1)}, u32[]{:S(2)}, u32[]{:S(2)}) collective-permute-start(bf16[2,2,2,96,1152]{4,3,1,0,2:T(8,128)(2,1)} %copy_bitcast_fusion.1), channel_id=1, source_target_pairs={{0,2},{1,3},{2,0},{3,1},{4,6},{5,7},{6,4},{7,5},{8,10},{9,11},{10,... | collective-permute-start | bytes 5308424 | tf_op jit(solution)/shard_map/ppermute | solution.py:33
  664.6 41.0 %collective-permute-start.73 = (bf16[2,2,2,96,1152]{4,3,1,0,2:T(8,128)(2,1)}, bf16[2,2,2,96,1152]{4,3,1,0,2:T(8,128)(2,1)}, u32[]{:S(2)}, u32[]{:S(2)}) collective-permute-start(bf16[2,2,2,96,1152]{4,3,1,0,2:T(8,128)(2,1)} %copy_bitcast_fusion), channel_id=1, source_target_pairs={{0,4},{1,5},{2,6},{3,7},{4,0},{5,1},{6,2},{7,3},{8,12},{9,13},{10,... | collective-permute-start | bytes 5308424 | tf_op jit(solution)/shard_map/ppermute | solution.py:33
  780.0 33.7 %collective-permute-start.86 = (bf16[96,2304]{1,0:T(8,128)(2,1)S(1)}, bf16[96,2304]{1,0:T(8,128)(2,1)}, u32[]{:S(2)}, u32[]{:S(2)}) collective-permute-start(bf16[96,2304]{1,0:T(8,128)(2,1)S(1)} %fusion.13), channel_id=1, source_target_pairs={{0,16},{1,17},{2,18},{3,19},{4,20},{5,21},{6,22},{7,23},{8,24},{9,... | collective-permute-start | bytes 1327112 | tf_op jit(solution)/shard_map/ppermute | solution.py:33
  (176 other events, 2099.7 us)
